TPU v7x, 32 devices: a whole 2x2x4 slice. The times are simulated.
32 devices in a mesh: dp: 16 (over z, y, core), mp: 2 (over x).
Axes of the slice: x: 2, y: 2, z: 4, core: 2. Of those that a mesh axis runs over, the one named last changes fastest.
Arguments:
- tokens: bfloat16 [16384, 1024], P('dp', 'mp'), may hold values from -6 to 6
- cotangent: bfloat16 [16384, 1024], P('dp', 'mp'), may hold values from -6 to 6
- route: int32 [16384], P('dp'), may hold values from 0 to 16383, as said below
- seq_lengths: int32 [16, 4], P('dp'), may hold values from 1 to 512, 1024 in all within a row
- norm1_gain: float32 [1024], replicated, may hold values from 0.25 to 1.75
- in_weight: bfloat16 [3, 1024, 1024], P(None, None, 'mp'), may hold values from -0.1875 to 0.1875
- conv_weight: float32 [3, 1024], P(None, 'mp'), may hold values from -3 to 3
- out_weight: bfloat16 [1024, 1024], P('mp'), may hold values from -0.1875 to 0.1875
- norm2_gain: float32 [1024], replicated, may hold values from 0.25 to 1.75
- gate_weight: bfloat16 [1024, 4608], P(None, 'mp'), may hold values from -0.1875 to 0.1875
- up_weight: bfloat16 [1024, 4608], P(None, 'mp'), may hold values from -0.1875 to 0.1875
- down_weight: bfloat16 [4608, 1024], P('mp'), may hold values from -0.09375 to 0.09375
Outputs:
- block_out: bfloat16 [16384, 1024], P('dp', 'mp')
- tokens_grad: float32 [16384, 1024], P('dp', 'mp')
- norm1_gain_grad: float32 [1024], replicated
- in_weight_grad: float32 [3, 1024, 1024], P(None, None, 'mp')
- conv_weight_grad: float32 [3, 1024], P(None, 'mp')
- out_weight_grad: float32 [1024, 1024], P('mp')
- norm2_gain_grad: float32 [1024], replicated
- gate_weight_grad: float32 [1024, 4608], P(None, 'mp')
- up_weight_grad: float32 [1024, 4608], P(None, 'mp')
- down_weight_grad: float32 [4608, 1024], P('mp')
Inputs may be any that keep to these rules, and one draw needn't show every extreme that they name: route is a permutation of the packed places; the 1024 arrival rows of one dp shard go 96 to one group, 32 to another and 64 to each other group, which groups drawn from the seed. `seq_lengths`: each row sums to 1024.
All inputs are finite; a program needn't handle non-finite values.
Results may differ from a plain program's by a relative error of at most 0.011.
Values may be sent and summed in bfloat16 or wider, within the bound.
No kernel may reach another device: no remote copies, remote signals or barrier semaphores. Data moves between devices by JAX's collectives and lax.ppermute only.
A program may use at most 192 MiB of HBM per device.

v0:
```python
import jax
import jax.numpy as jnp
from jax import lax
from jax.sharding import PartitionSpec as P

epsilon = 1e-05


def lag_rows(values, shift):
    return jnp.concatenate(
        [jnp.zeros((shift, values.shape[1]), values.dtype), values[:-shift]], axis=0
    )


def lead_rows(values, shift):
    return jnp.concatenate(
        [values[shift:], jnp.zeros((shift, values.shape[1]), values.dtype)], axis=0
    )


def seq_masks(lengths, row_count):
    starts = jnp.cumsum(lengths, dtype=jnp.int32) - lengths
    position = jnp.arange(row_count, dtype=jnp.int32)
    started = position[:, None] >= starts[None, :]
    seq_first = jnp.max(jnp.where(started, starts[None, :], 0), axis=1)
    offset = position - seq_first
    return ((offset >= 1).astype(jnp.float32)[:, None], (offset >= 2).astype(jnp.float32)[:, None])


def padded_piece(piece, start, model_width):
    return lax.dynamic_update_slice_in_dim(jnp.zeros((model_width,), jnp.float32), piece, start, 0)


def on_device(
    tokens,
    cotangent,
    route,
    seq_lengths,
    norm1_gain,
    in_weight,
    conv_weight,
    out_weight,
    norm2_gain,
    gate_weight,
    up_weight,
    down_weight,
):
    dp_size = lax.axis_size("dp")
    mp_index = lax.axis_index("mp")
    row_count = tokens.shape[0]
    narrow = tokens.shape[1]
    model_width = norm1_gain.shape[0]
    pair_share = row_count // dp_size
    slot_count = pair_share + pair_share // 2
    ordering = jnp.argsort(route)
    target = route[ordering] // row_count
    members = jnp.arange(dp_size, dtype=jnp.int32)
    counts = jnp.sum(
        (target[:, None] == members[None, :]).astype(jnp.int32), axis=0, dtype=jnp.int32
    )
    begins = jnp.cumsum(counts, dtype=jnp.int32) - counts
    slot_ids = jnp.arange(slot_count, dtype=jnp.int32)
    filled = slot_ids[None, :] < counts[:, None]
    sources = ordering[jnp.clip(begins[:, None] + slot_ids[None, :], 0, row_count - 1)]
    pulled_rows = tokens[sources]
    pulled_seeds = cotangent[sources]
    send_rows = jnp.where(filled[:, :, None], pulled_rows, jnp.zeros_like(pulled_rows))
    send_seeds = jnp.where(filled[:, :, None], pulled_seeds, jnp.zeros_like(pulled_seeds))
    send_places = jnp.where(filled, route[sources] % row_count, row_count)
    got_rows, got_seeds, got_places = (
        lax.all_to_all(send_rows, "dp", split_axis=0, concat_axis=0, tiled=True),
        lax.all_to_all(send_seeds, "dp", split_axis=0, concat_axis=0, tiled=True),
        lax.all_to_all(send_places, "dp", split_axis=0, concat_axis=0, tiled=True),
    )
    flat_places = got_places.reshape(-1)
    input_piece = (
        jnp.zeros((row_count, narrow), tokens.dtype)
        .at[flat_places]
        .set(got_rows.reshape(-1, narrow), mode="drop")
    )
    seed_piece = (
        jnp.zeros((row_count, narrow), cotangent.dtype)
        .at[flat_places]
        .set(got_seeds.reshape(-1, narrow), mode="drop")
    )
    input_full, seed_full = (
        lax.all_gather(input_piece, "mp", axis=1, tiled=True),
        lax.all_gather(seed_piece, "mp", axis=1, tiled=True),
    )
    first_mask, second_mask = seq_masks(seq_lengths[0], row_count)
    column_start = mp_index * narrow
    gain_one = lax.dynamic_slice_in_dim(norm1_gain, column_start, narrow)
    gain_two = lax.dynamic_slice_in_dim(norm2_gain, column_start, narrow)
    residual = input_full.astype(jnp.float32)
    residual_piece = input_piece.astype(jnp.float32)
    scale_one = lax.rsqrt(jnp.mean(residual * residual, axis=1) + epsilon)
    normed_one = (residual * scale_one[:, None] * norm1_gain).astype(jnp.bfloat16)
    projected = jnp.einsum("rd,kdc->krc", normed_one, in_weight, preferred_element_type=jnp.float32)
    in_gate, out_gate, value_part = (projected[0], projected[1], projected[2])
    mixed = in_gate * value_part
    lag_one = lag_rows(mixed, 1) * first_mask
    lag_two = lag_rows(mixed, 2) * second_mask
    convolved = conv_weight[2] * mixed + conv_weight[1] * lag_one + conv_weight[0] * lag_two
    gated = (out_gate * convolved).astype(jnp.bfloat16)
    mix_terms = jnp.dot(gated, out_weight, preferred_element_type=jnp.float32)
    middle = residual_piece + lax.psum_scatter(mix_terms, "mp", scatter_dimension=1, tiled=True)
    square_sum = lax.psum(jnp.sum(middle * middle, axis=1), "mp")
    scale_two = lax.rsqrt(square_sum / model_width + epsilon)
    normed_piece = (middle * scale_two[:, None] * gain_two).astype(jnp.bfloat16)
    normed_two = lax.all_gather(normed_piece, "mp", axis=1, tiled=True)
    gate_val = jnp.dot(normed_two, gate_weight, preferred_element_type=jnp.float32)
    up_val = jnp.dot(normed_two, up_weight, preferred_element_type=jnp.float32)
    sigmoid_val = jax.nn.sigmoid(gate_val)
    silu_val = gate_val * sigmoid_val
    hidden = (silu_val * up_val).astype(jnp.bfloat16)
    down_terms = jnp.dot(hidden, down_weight, preferred_element_type=jnp.float32)
    block_piece = middle + lax.psum_scatter(down_terms, "mp", scatter_dimension=1, tiled=True)
    seed_local = seed_piece.astype(jnp.float32)
    grad_down = jnp.einsum("rf,rd->fd", hidden, seed_full, preferred_element_type=jnp.float32)
    grad_hidden = jnp.einsum(
        "rd,fd->rf", seed_full, down_weight, preferred_element_type=jnp.float32
    )
    grad_gate_val = (
        grad_hidden * up_val * sigmoid_val * (1.0 + gate_val * (1.0 - sigmoid_val))
    ).astype(jnp.bfloat16)
    grad_up_val = (grad_hidden * silu_val).astype(jnp.bfloat16)
    grad_gate = jnp.einsum(
        "rd,rf->df", normed_two, grad_gate_val, preferred_element_type=jnp.float32
    )
    grad_up = jnp.einsum("rd,rf->df", normed_two, grad_up_val, preferred_element_type=jnp.float32)
    normed_terms = jnp.einsum(
        "rf,df->rd", grad_gate_val, gate_weight, preferred_element_type=jnp.float32
    ) + jnp.einsum("rf,df->rd", grad_up_val, up_weight, preferred_element_type=jnp.float32)
    grad_normed_two = lax.psum_scatter(normed_terms, "mp", scatter_dimension=1, tiled=True)
    gain_two_piece = jnp.sum(grad_normed_two * middle * scale_two[:, None], axis=0)
    dot_two, grad_gain_two = lax.psum(
        (
            jnp.sum(gain_two * grad_normed_two * middle, axis=1),
            padded_piece(gain_two_piece, column_start, model_width),
        ),
        "mp",
    )
    grad_middle = (
        seed_local
        + scale_two[:, None] * gain_two * grad_normed_two
        - middle * (scale_two * scale_two * scale_two * dot_two / model_width)[:, None]
    )
    grad_mix_piece = grad_middle.astype(jnp.bfloat16)
    grad_mix = lax.all_gather(grad_mix_piece, "mp", axis=1, tiled=True)
    grad_out_weight = jnp.einsum("rc,rd->cd", gated, grad_mix, preferred_element_type=jnp.float32)
    grad_gated = jnp.einsum("rd,cd->rc", grad_mix, out_weight, preferred_element_type=jnp.float32)
    grad_conv = grad_gated * out_gate
    grad_conv_weight = jnp.stack(
        [
            jnp.sum(grad_conv * lag_two, axis=0),
            jnp.sum(grad_conv * lag_one, axis=0),
            jnp.sum(grad_conv * mixed, axis=0),
        ],
        axis=0,
    )
    grad_mixed = (
        conv_weight[2] * grad_conv
        + conv_weight[1] * lead_rows(grad_conv * first_mask, 1)
        + conv_weight[0] * lead_rows(grad_conv * second_mask, 2)
    )
    grad_parts = jnp.stack(
        [grad_mixed * value_part, grad_gated * convolved, grad_mixed * in_gate], axis=0
    ).astype(jnp.bfloat16)
    grad_in_weight = jnp.einsum(
        "rd,krc->kdc", normed_one, grad_parts, preferred_element_type=jnp.float32
    )
    first_terms = jnp.einsum(
        "krc,kdc->rd", grad_parts, in_weight, preferred_element_type=jnp.float32
    )
    grad_normed_one = lax.psum_scatter(first_terms, "mp", scatter_dimension=1, tiled=True)
    gain_one_piece = jnp.sum(grad_normed_one * residual_piece * scale_one[:, None], axis=0)
    dot_one, grad_gain_one = lax.psum(
        (
            jnp.sum(gain_one * grad_normed_one * residual_piece, axis=1),
            padded_piece(gain_one_piece, column_start, model_width),
        ),
        "mp",
    )
    input_grad = (
        grad_middle
        + scale_one[:, None] * gain_one * grad_normed_one
        - residual_piece * (scale_one * scale_one * scale_one * dot_one / model_width)[:, None]
    )
    summed = lax.psum(
        (
            grad_gain_one,
            grad_in_weight,
            grad_conv_weight,
            grad_out_weight,
            grad_gain_two,
            grad_gate,
            grad_up,
            grad_down,
        ),
        "dp",
    )
    local_ids = jnp.clip(got_places, 0, row_count - 1)
    back_out, back_grad = (
        lax.all_to_all(block_piece[local_ids], "dp", split_axis=0, concat_axis=0, tiled=True),
        lax.all_to_all(input_grad[local_ids], "dp", split_axis=0, concat_axis=0, tiled=True),
    )
    home = jnp.where(filled, sources, row_count).reshape(-1)
    block_out = (
        jnp.zeros((row_count, narrow), jnp.float32)
        .at[home]
        .set(back_out.reshape(-1, narrow), mode="drop")
        .astype(jnp.bfloat16)
    )
    tokens_grad = (
        jnp.zeros((row_count, narrow), jnp.float32)
        .at[home]
        .set(back_grad.reshape(-1, narrow), mode="drop")
    )
    return (
        block_out,
        tokens_grad,
        summed[0],
        summed[1],
        summed[2],
        summed[3],
        summed[4],
        summed[5],
        summed[6],
        summed[7],
    )


def solution(mesh):
    in_specs = (
        P("dp", "mp"),
        P("dp", "mp"),
        P("dp"),
        P("dp", None),
        P(),
        P(None, None, "mp"),
        P(None, "mp"),
        P("mp", None),
        P(),
        P(None, "mp"),
        P(None, "mp"),
        P("mp", None),
    )
    out_specs = (
        P("dp", "mp"),
        P("dp", "mp"),
        P(),
        P(None, None, "mp"),
        P(None, "mp"),
        P("mp", None),
        P(),
        P(None, "mp"),
        P(None, "mp"),
        P("mp", None),
    )
    return jax.shard_map(
        on_device, mesh=mesh, in_specs=in_specs, out_specs=out_specs, check_vma=False
    )
```

profile of v0, /device:TPU:0, one launch (start us, length us, event | category | flops | bytes accessed | tf_op | source)
XLA Modules:
  0.0 1352.7 jit_solution(5558362743720589754)
XLA Ops:
  7.2 5.2 sort.17
  12.4 4.5 gather_fusion
  17.5 5.9 gather_fusion.1
  24.1 5.9 gather_fusion.2
  30.7 7.4 all-to-all-start
  38.2 6.8 gather_fusion.5
  45.0 6.8 gather_fusion.3
  55.1 6.2 all-to-all-start.1
  63.2 30.1 %all-to-all-done.1 = bf16[16,96,512]{2,1,0:T(8,128)(2,1)} async-done(((bf16[16,96,512]{2,1,0:T(8,128)(2,1)}), bf16[16,96,512]{2,1,0:T(8,128)(2,1)}, u32[]{:S(2)}, u32[]{:S(2)}) %all-to-all-start.1) | async-done | bytes 1572896 | tf_op jit(solution)/shard_map/all_to_all | solution.py:71
  93.3 8.7 scatter_custom_fusion
  102.6 37.1 %all-gather.5.cloned.1.call-done = bf16[1024,1024]{1,0:T(8,128)(2,1)} async-done(((bf16[1024,512]{1,0:T(8,128)(2,1)}), bf16[1024,1024]{1,0:T(8,128)(2,1)}) %all-gather.5.cloned.1.call-update) | async-done | bytes 2097168 | tf_op jit(solution)/shard_map/all_gather | solution.py:87
  155.0 5.7 all-to-all-start.3
  160.9 48.6 %reduce-scatter.5.cloned.1.call-done = f32[1024,512]{1,0:T(8,128)} async-done(((f32[1024,1024]{1,0:T(8,128)}), f32[1024,512]{1,0:T(8,128)}) %reduce-scatter.5.cloned.1.call-update) | async-done | bytes 2097168 | tf_op jit(solution)/shard_map/reduce_scatter | solution.py:106
  212.9 4.9 psum.91
  220.8 8.7 scatter_custom_fusion.2
  229.8 24.2 %all-gather.7.cloned.1.call-done = bf16[1024,1024]{1,0:T(8,128)(2,1)} async-done(((bf16[1024,512]{1,0:T(8,128)(2,1)}), bf16[1024,1024]{1,0:T(8,128)(2,1)}) %all-gather.7.cloned.1.call-update) | async-done | bytes 2097168 | tf_op jit(solution)/shard_map/all_gather | solution.py:110
  254.0 10.2 fusion.41
  264.2 9.9 fusion.40
  274.1 14.5 %all-gather.9.cloned.1.call-done = bf16[1024,1024]{1,0:T(8,128)(2,1)} async-done(((bf16[1024,512]{1,0:T(8,128)(2,1)}), bf16[1024,1024]{1,0:T(8,128)(2,1)}) %all-gather.9.cloned.1.call-update) | async-done | bytes 2097168 | tf_op jit(solution)/shard_map/all_gather | solution.py:88
  288.6 17.8 %multiply_convert_fusion = (bf16[1024,2304]{1,0:T(8,128)(2,1)}, bf16[1024,2304]{1,0:T(8,128)(2,1)}, bf16[1024,2304]{1,0:T(8,128)(2,1)}) fusion(f32[1024,2304]{1,0:T(8,128)} %fusion.40, f32[1024,2304]{1,0:T(8,128)} %fusion.41, bf16[1024,1024]{1,0:T(8,128)(2,1)} %all-gather.9.cloned.1.call-done, bf16[2304,1024]{1,0:T(8,128)(2,1)} %param.23), kind=kOutput, calls=%fused_computation.11 | convolution fusion | flops 4867227648 | bytes 39845888 | tf_op jit(solution)/shard_map/rd,fd->rf/dot_general | solution.py:120
  306.4 8.5 fusion.43
  314.9 9.0 convolution_add_fusion
  324.0 54.4 %reduce-scatter.9.cloned.1.call-done = f32[1024,512]{1,0:T(8,128)} async-done(((f32[1024,1024]{1,0:T(8,128)}), f32[1024,512]{1,0:T(8,128)}) %reduce-scatter.9.cloned.1.call-update) | async-done | bytes 2097168 | tf_op jit(solution)/shard_map/reduce_scatter | solution.py:134
  381.2 5.3 psum.92
  390.8 33.1 %all-gather.11.cloned.1.call-done = bf16[1024,1024]{1,0:T(8,128)(2,1)} async-done(((bf16[1024,512]{1,0:T(8,128)(2,1)}), bf16[1024,1024]{1,0:T(8,128)(2,1)}) %all-gather.11.cloned.1.call-update) | async-done | bytes 2097168 | tf_op jit(solution)/shard_map/all_gather | solution.py:149
  423.9 7.0 multiply_reduce_fusion.3
  437.5 5.0 convolution_bitcast_fusion.2
  442.6 9.7 fusion.42
  452.6 10.3 fusion.47
  462.9 10.2 fusion.46
  473.1 10.3 fusion.45
  486.5 5.7 convolution_bitcast_fusion
  499.8 7.1 all-reduce.6
  506.9 46.9 %reduce-scatter.7.cloned.1.call-done = f32[1024,512]{1,0:T(8,128)} async-done(((f32[1024,1024]{1,0:T(8,128)}), f32[1024,512]{1,0:T(8,128)}) %reduce-scatter.7.cloned.1.call-update) | async-done | bytes 2097168 | tf_op jit(solution)/shard_map/reduce_scatter | solution.py:117
  553.8 5.3 fusion.5
  559.1 7.3 gather_fusion.4
  566.4 5.7 all-to-all-start.2
  572.1 5.0 gather_fusion.6
  577.0 91.2 %all-to-all-done.2 = f32[16,96,512]{2,1,0:T(8,128)} async-done(((f32[16,96,512]{2,1,0:T(8,128)}), f32[16,96,512]{2,1,0:T(8,128)}, u32[]{:S(2)}, u32[]{:S(2)}) %all-to-all-start.2) | async-done | bytes 3145760 | tf_op jit(solution)/shard_map/all_to_all | solution.py:204
  668.2 12.8 all-to-all-start.4
  681.3 143.8 %all-reduce.4 = (f32[1024]{0:T(1024)}, f32[3,512]{1,0:T(4,128)}, f32[1024]{0:T(1024)}) all-reduce(f32[1024]{0:T(1024)S(1)} %get-tuple-element.68, f32[3,512]{1,0:T(4,128)S(1)} %pad_maximum_fusion.3, f32[1024]{0:T(1024)S(1)} %get-tuple-element.69), channel_id=1, replica_groups=mesh['dp'=16,'mp'=2] {'dp'}, use_global_device_ids=true, to_apply=%region_22.23 | all-reduce | flops 3584 | bytes 28672 | tf_op jit(solution)/shard_map/psum | solution.py:189
  825.1 8.1 scatter_custom_fusion.1
  834.3 9.0 scatter_custom_fusion.3
  843.3 473.7 %all-reduce.9.cloned.1.call-done = (f32[3,1024,512]{1,2,0:T(8,128)}, f32[512,1024]{1,0:T(8,128)}, f32[1024,2304]{1,0:T(8,128)}, f32[1024,2304]{1,0:T(8,128)}, f32[2304,1024]{1,0:T(8,128)}) async-done(((f32[3,1024,512]{1,2,0:T(8,128)}, f32[512,1024]{1,0:T(8,128)}, f32[1024,2304]{1,0:T(8,128)}, f32[1024,2304]{1,0:T(8,128)}, f32[2304,1024]{1,0:T(8,128)}), (f32[3,1024,512]{1,2,0:T(8,128)}, ...) | async-done | bytes 36700176 | tf_op jit(solution)/shard_map/psum | solution.py:189
  1317.1 6.7 copy.33
  1325.1 8.4 copy.45
  1333.5 8.1 copy.46
  1341.6 4.2 copy.47
  (162 shorter events, 57.0 us)
Async XLA Ops:
  7.2 134.9 %copy-start = (bf16[3,1024,512]{2,1,0:T(8,128)(2,1)S(1)}, bf16[3,1024,512]{2,1,0:T(8,128)(2,1)}, u32[]{:S(2)}) copy-start(bf16[3,1024,512]{2,1,0:T(8,128)(2,1)} %param.17) | copy-start | bytes 9437188
  7.2 5.2 copy-start.2
  17.1 21.0 %copy-start.24 = (s32[16]{0:T(128)}, s32[16]{0:T(128)S(1)}, u32[]{:S(2)}) copy-start(s32[16]{0:T(128)S(1)} %convert_reduce_fusion) | copy-start | bytes 196
  30.7 24.4 %all-to-all-start = ((s32[16,1,96]{2,1,0:T(1,128)}), s32[16,1,96]{2,1,0:T(1,128)S(1)}, u32[]{:S(2)}, u32[]{:S(2)}) async-start(s32[16,1,96]{2,1,0:T(1,128)} %compare_select_fusion.4), calls=%async_computation | async-start | bytes 16384 | tf_op jit(solution)/shard_map/all_to_all | solution.py:73
  55.1 47.2 %copy-start.32 = (s32[1,4]{1,0:T(1,128)S(1)}, s32[1,4]{1,0:T(1,128)}, u32[]{:S(2)}) copy-start(s32[1,4]{1,0:T(1,128)} %param.15) | copy-start | bytes 52
  55.1 47.5 %copy-start.26 = (f32[3,512]{1,0:T(4,128)S(1)}, f32[3,512]{1,0:T(4,128)}, u32[]{:S(2)}) copy-start(f32[3,512]{1,0:T(4,128)} %param.18) | copy-start | bytes 18436
  55.1 38.2 %all-to-all-start.1 = ((bf16[16,96,512]{2,1,0:T(8,128)(2,1)}), bf16[16,96,512]{2,1,0:T(8,128)(2,1)}, u32[]{:S(2)}, u32[]{:S(2)}) async-start(bf16[16,96,512]{2,1,0:T(8,128)(2,1)} %get-tuple-element.91), calls=%async_computation.1 | async-start | bytes 3145728 | tf_op jit(solution)/shard_map/all_to_all | solution.py:71
  61.3 78.5 %all-gather.5.cloned.1.call-start = ((), (), s32[]{:S(2)}) async-start(), calls=%async_computation.9 | async-start | bytes 3145728 | tf_op jit(solution)/shard_map/all_gather | solution.py:87
  93.3 48.7 %copy-start.28 = (f32[1024]{0:T(1024)S(1)}, f32[1024]{0:T(1024)}, u32[]{:S(2)}) copy-start(f32[1024]{0:T(1024)} %param.16) | copy-start | bytes 12292
  102.1 107.4 %reduce-scatter.5.cloned.1.call-start = ((), (), s32[]{:S(2)}) async-start(), calls=%async_computation.10 | async-start | bytes 6291456 | tf_op jit(solution)/shard_map/reduce_scatter | solution.py:106
  139.8 2.3 copy-start.9
  142.0 3.6 copy-start.21
  145.6 2.7 copy-start.4
  146.1 4.6 copy-start.3
  148.3 3.4 copy-start.12
  150.7 1.0 copy-start.7
  155.0 5.8 copy-start.27
  155.0 65.7 %all-to-all-start.3 = ((bf16[16,96,512]{2,1,0:T(8,128)(2,1)}), bf16[16,96,512]{2,1,0:T(8,128)(2,1)}, u32[]{:S(2)}, u32[]{:S(2)}) async-start(bf16[16,96,512]{2,1,0:T(8,128)(2,1)} %get-tuple-element.90), calls=%async_computation.5 | async-start | bytes 3145728 | tf_op jit(solution)/shard_map/all_to_all | solution.py:72
  160.7 93.3 %all-gather.7.cloned.1.call-start = ((), (), s32[]{:S(2)}) async-start(), calls=%async_computation.11 | async-start | bytes 3145728 | tf_op jit(solution)/shard_map/all_gather | solution.py:110
  220.7 67.9 %all-gather.9.cloned.1.call-start = ((), (), s32[]{:S(2)}) async-start(), calls=%async_computation.13 | async-start | bytes 3145728 | tf_op jit(solution)/shard_map/all_gather | solution.py:88
  229.5 148.9 %reduce-scatter.9.cloned.1.call-start = ((), (), s32[]{:S(2)}) async-start(), calls=%async_computation.14 | async-start | bytes 6291456 | tf_op jit(solution)/shard_map/reduce_scatter | solution.py:134
  254.0 10.2 copy-start.29
  306.4 8.5 copy-start.33
  323.9 99.9 %all-gather.11.cloned.1.call-start = ((), (), s32[]{:S(2)}) async-start(), calls=%async_computation.15 | async-start | bytes 3145728 | tf_op jit(solution)/shard_map/all_gather | solution.py:149
  390.6 106.5 %reduce-scatter.11.cloned.1.call-start = ((), (), s32[]{:S(2)}) async-start(), calls=%async_computation.16 | async-start | bytes 6291456 | tf_op jit(solution)/shard_map/reduce_scatter | solution.py:175
  430.9 5.7 copy-start.13
  434.2 2.4 copy-start.15
  442.6 111.2 %reduce-scatter.7.cloned.1.call-start = ((), (), s32[]{:S(2)}) async-start(), calls=%async_computation.12 | async-start | bytes 6291456 | tf_op jit(solution)/shard_map/reduce_scatter | solution.py:117
  452.3 10.5 copy-start.30
  452.4 864.7 %all-reduce.9.cloned.1.call-start = ((), (), s32[]{:S(2)}) async-start(), calls=%async_computation.17 | async-start | bytes 73400320 | tf_op jit(solution)/shard_map/psum | solution.py:189
  462.9 10.2 copy-start.31
  473.1 10.3 copy-start.6
  473.1 10.3 copy-start.8
  483.4 2.6 copy-start.10
  483.4 2.6 copy-start.14
  483.4 2.6 copy-start.16
  483.4 3.1 copy-start.18
  492.2 4.9 copy-start.5
  492.2 14.6 %copy-start.22 = (f32[1024]{0:T(1024)S(1)}, f32[1024]{0:T(1024)}, u32[]{:S(2)}) copy-start(f32[1024]{0:T(1024)} %copy-done.21) | copy-start | bytes 12292
  566.4 101.8 %all-to-all-start.2 = ((f32[16,96,512]{2,1,0:T(8,128)}), f32[16,96,512]{2,1,0:T(8,128)}, u32[]{:S(2)}, u32[]{:S(2)}) async-start(f32[16,96,512]{2,1,0:T(8,128)} %bitcast.104), calls=%async_computation.4 | async-start | bytes 6291456 | tf_op jit(solution)/shard_map/all_to_all | solution.py:204
  668.2 12.8 copy-start.20
  668.2 12.9 copy-start.25
  668.2 166.1 %all-to-all-start.4 = ((f32[16,96,512]{2,1,0:T(8,128)}), f32[16,96,512]{2,1,0:T(8,128)}, u32[]{:S(2)}, u32[]{:S(2)}) async-start(f32[16,96,512]{2,1,0:T(8,128)} %bitcast.103), calls=%async_computation.8 | async-start | bytes 6291456 | tf_op jit(solution)/shard_map/all_to_all | solution.py:205
  1317.1 6.7 copy-start.11
  1325.1 16.5 %slice-start = ((s8[9437184]{0:T(1024)(128)(4,1)}), s8[4194304]{0:T(1024)(128)(4,1)S(1)}, s32[]{:S(2)}) async-start(s8[9437184]{0:T(1024)(128)(4,1)} %bitcast.105), calls=%async_computation.18 | async-start | bytes 8388608
  1325.1 16.5 %slice-start.1 = ((s8[9437184]{0:T(1024)(128)(4,1)}), s8[4194304]{0:T(1024)(128)(4,1)S(1)}, s32[]{:S(2)}) async-start(s8[9437184]{0:T(1024)(128)(4,1)} %bitcast.105), calls=%async_computation.19 | async-start | bytes 8388608
  1333.5 8.1 slice-start.2
  1341.6 4.3 copy-start.1
  (3 other events, 2.3 us)
Sparse Core Ops, SparseCore 0:
  102.2 37.5 all-gather.4
  155.1 54.2 reduce-scatter.4
  220.8 33.1 all-gather.6
  255.5 33.1 all-gather.8
  324.1 54.3 reduce-scatter.8
  390.7 33.1 all-gather.10
  442.7 54.3 reduce-scatter.10
  499.5 54.2 reduce-scatter.6
  560.2 756.7 all-reduce.8
where the time goes:
time: 1360 us; the launch traced here: 1350 us
  waiting for transfers between devices  858 us (63%)
  blocking collectives  161 us (12%)
  matrix products  123 us (9%)
  local copies, waits for them, and re-layouts  113 us (8%)
  other arithmetic  44 us (3%)
  starting transfers between devices  38.6 us (3%)
  between operations  14.6 us (1%)
    psum x1, waiting for transfers between devices, on_device(): lax.psum((grad_gain_one, grad_in_weight, grad_conv_weight, grad_out_weigh...  474 us
    psum x1, blocking collectives, on_device(): lax.psum((grad_gain_one, grad_in_weight, grad_conv_weight, grad_out_weigh...  144 us
    all_to_all x1, waiting for transfers between devices, on_device(): lax.all_to_all(block_piece[local_ids], 'dp', split_axis=0, concat_axis=0,...  91.2 us
    reduce_scatter x1, waiting for transfers between devices, on_device(): lax.psum_scatter(normed_terms, 'mp', scatter_dimension=1, tiled=True)  54.4 us
    reduce_scatter x1, waiting for transfers between devices, on_device(): lax.psum_scatter(mix_terms, 'mp', scatter_dimension=1, tiled=True)  48.6 us
    reduce_scatter x1, waiting for transfers between devices, on_device(): lax.psum_scatter(down_terms, 'mp', scatter_dimension=1, tiled=True)  46.9 us
    all_gather x1, waiting for transfers between devices, on_device(): lax.all_gather(input_piece, 'mp', axis=1, tiled=True)  37.1 us
    unnamed x79, local copies, waits for them, and re-layouts  34.7 us
  transfers between devices with their start and end apart: 14, of which 11 were waited for; matrix products, arithmetic and copies ran while one was open for 11% of the time, Pallas kernels for 0%

commit v1 on v0

v1 whole, which is shorter than its diff:
```python
import jax
import jax.numpy as jnp
from jax import lax
from jax.experimental import pallas as pl
from jax.experimental.pallas import tpu as pltpu
from jax.sharding import PartitionSpec as P

epsilon = 1e-05
f32 = jnp.float32
bf16 = jnp.bfloat16


def lag_rows(values, shift):
    return jnp.concatenate(
        [jnp.zeros((shift, values.shape[1]), values.dtype), values[:-shift]], axis=0
    )


def lead_rows(values, shift):
    return jnp.concatenate(
        [values[shift:], jnp.zeros((shift, values.shape[1]), values.dtype)], axis=0
    )


def seq_masks(lengths, row_count):
    count = lengths.shape[0]
    before = jnp.arange(count)[:, None] < jnp.arange(count)[None, :]
    starts = jnp.sum(jnp.where(before, lengths[:, None], 0), axis=0, dtype=jnp.int32)
    position = jnp.arange(row_count, dtype=jnp.int32)
    started = position[:, None] >= starts[None, :]
    seq_first = jnp.max(jnp.where(started, starts[None, :], 0), axis=1)
    offset = position - seq_first
    return ((offset >= 1).astype(f32)[:, None], (offset >= 2).astype(f32)[:, None])


def pack_kernel(rows, slots, route_ref, x_ref, g_ref, sx_ref, sg_ref, place_ref, slot_ref):
    j = pl.program_id(0)
    members = pl.num_programs(0)
    width = min(rows, 512)

    @pl.when(j == 0)
    def _():
        route = route_ref[...]
        target = route // rows
        owner = lax.broadcasted_iota(jnp.int32, (members, rows), 0)
        one_hot = jnp.where(owner == target, 1.0, 0.0)
        for start in range(0, rows, width):
            first = lax.broadcasted_iota(jnp.int32, (rows, width), 0)
            second = lax.broadcasted_iota(jnp.int32, (rows, width), 1) + start
            earlier = jnp.where(first < second, 1.0, 0.0).astype(bf16)
            rank = jnp.dot(one_hot.astype(bf16), earlier, preferred_element_type=f32)
            piece = one_hot[:, start : start + width]
            mine = jnp.sum(rank * piece, axis=0, keepdims=True).astype(jnp.int32)
            slot_ref[:, start : start + width] = (
                target[:, start : start + width] * slots + mine
            )

    ids = lax.broadcasted_iota(jnp.int32, (slots, rows), 0) + j * slots
    pick = jnp.where(slot_ref[...] == ids, 1.0, 0.0).astype(bf16)
    sx_ref[...] = jnp.dot(pick, x_ref[...], preferred_element_type=f32).astype(bf16)
    sg_ref[...] = jnp.dot(pick, g_ref[...], preferred_element_type=f32).astype(bf16)
    place = route_ref[...] % rows
    row = lax.broadcasted_iota(jnp.int32, (16, rows), 0)
    digits = jnp.where(
        row == 0,
        (place // 64).astype(f32),
        jnp.where(row == 1, (place % 64).astype(f32), 1.0),
    ).astype(bf16)
    sent = lax.dot_general(
        digits, pick, (((1,), (1,)), ((), ())), preferred_element_type=f32
    )
    value = sent[0:1] * 64.0 + sent[1:2] + (1.0 - sent[2:3]) * rows
    place_ref[...] = jnp.broadcast_to(value, (8, slots)).astype(jnp.int32)


def pack(route, tokens, cotangent, members, slots):
    rows, width = tokens.shape
    whole = lambda j: (0, 0)
    return pl.pallas_call(
        lambda *refs: pack_kernel(rows, slots, *refs),
        grid=(members,),
        in_specs=[
            pl.BlockSpec((1, rows), whole),
            pl.BlockSpec((rows, width), whole),
            pl.BlockSpec((rows, width), whole),
        ],
        out_specs=[
            pl.BlockSpec((None, slots, width), lambda j: (j, 0, 0)),
            pl.BlockSpec((None, slots, width), lambda j: (j, 0, 0)),
            pl.BlockSpec((None, 8, slots), lambda j: (j, 0, 0)),
            pl.BlockSpec((1, rows), whole),
        ],
        out_shape=[
            jax.ShapeDtypeStruct((members, slots, width), bf16),
            jax.ShapeDtypeStruct((members, slots, width), bf16),
            jax.ShapeDtypeStruct((members, 8, slots), jnp.int32),
            jax.ShapeDtypeStruct((1, rows), jnp.int32),
        ],
        compiler_params=pltpu.CompilerParams(vmem_limit_bytes=56 << 20),
        name="pack",
    )(route.reshape(1, rows), tokens, cotangent)


def place_kernel(block, places_ref, got_ref, out_ref):
    base = pl.program_id(0) * block
    ids = lax.broadcasted_iota(jnp.int32, (block, places_ref.shape[1]), 0) + base
    pick = jnp.where(places_ref[...] == ids, 1.0, 0.0).astype(bf16)
    out_ref[...] = jnp.dot(pick, got_ref[...], preferred_element_type=f32).astype(bf16)


def place_rows(places, got, rows):
    total, width = got.shape
    block = min(rows, 256)
    return pl.pallas_call(
        lambda *refs: place_kernel(block, *refs),
        grid=(rows // block,),
        in_specs=[
            pl.BlockSpec((1, total), lambda i: (0, 0)),
            pl.BlockSpec((total, width), lambda i: (0, 0)),
        ],
        out_specs=pl.BlockSpec((block, width), lambda i: (i, 0)),
        out_shape=jax.ShapeDtypeStruct((rows, width), bf16),
        compiler_params=pltpu.CompilerParams(vmem_limit_bytes=56 << 20),
        name="place_rows",
    )(places, got)


def take_kernel(ids_ref, from_ref, out_ref):
    cols = lax.broadcasted_iota(jnp.int32, (out_ref.shape[0], from_ref.shape[0]), 1)
    pick = jnp.where(ids_ref[...] == cols, 1.0, 0.0).astype(bf16)
    out_ref[...] = jnp.dot(
        pick, from_ref[...].astype(bf16), preferred_element_type=f32
    ).astype(out_ref.dtype)


def take_rows(ids, source, block, dtype):
    count = ids.shape[0]
    total, width = source.shape
    return pl.pallas_call(
        take_kernel,
        grid=(count // block,),
        in_specs=[
            pl.BlockSpec((block, 1), lambda i: (i, 0)),
            pl.BlockSpec((total, width), lambda i: (0, 0)),
        ],
        out_specs=pl.BlockSpec((block, width), lambda i: (i, 0)),
        out_shape=jax.ShapeDtypeStruct((count, width), dtype),
        compiler_params=pltpu.CompilerParams(vmem_limit_bytes=56 << 20),
        name="take_rows",
    )(ids, source)


def swap_mp(value):
    return lax.ppermute(value, "mp", [(0, 1), (1, 0)])


def gather_features(piece, members, index):
    if members != 2:
        return lax.all_gather(piece, "mp", axis=1, tiled=True)
    other = swap_mp(piece)
    return jnp.where(
        index == 0,
        jnp.concatenate([piece, other], axis=1),
        jnp.concatenate([other, piece], axis=1),
    )


def sum_mp(partial, members):
    if members != 2:
        return lax.psum(partial, "mp")
    return partial + swap_mp(partial.astype(bf16)).astype(f32)


def sum_features(partial, members, index):
    if members != 2:
        return lax.psum_scatter(partial, "mp", scatter_dimension=1, tiled=True)
    narrow = partial.shape[1] // 2
    low, high = partial[:, :narrow], partial[:, narrow:]
    sent = jnp.where(index == 0, high, low).astype(bf16)
    kept = jnp.where(index == 0, low, high)
    return kept + swap_mp(sent).astype(f32)


def flip(value, bit, size):
    return lax.ppermute(value, "dp", [(i, i ^ bit) for i in range(size)])


def sum_dp(partial, size, index):
    bits = []
    bit = 1
    while bit < size:
        bits.append(bit)
        bit *= 2
    value = partial
    for bit in bits:
        half = value.shape[0] // 2
        side = (index // bit) % 2
        sent = lax.dynamic_slice_in_dim(value, (1 - side) * half, half, 0)
        kept = lax.dynamic_slice_in_dim(value, side * half, half, 0)
        value = (kept.astype(f32) + flip(sent, bit, size).astype(f32)).astype(bf16)
    for bit in reversed(bits):
        side = (index // bit) % 2
        other = flip(value, bit, size)
        value = jnp.where(
            side == 0,
            jnp.concatenate([value, other], axis=0),
            jnp.concatenate([other, value], axis=0),
        )
    return value


def on_device(
    tokens,
    cotangent,
    route,
    seq_lengths,
    norm1_gain,
    in_weight,
    conv_weight,
    out_weight,
    norm2_gain,
    gate_weight,
    up_weight,
    down_weight,
):
    dp_size = lax.axis_size("dp")
    mp_size = lax.axis_size("mp")
    dp_index = lax.axis_index("dp")
    mp_index = lax.axis_index("mp")
    row_count = tokens.shape[0]
    narrow = tokens.shape[1]
    model_width = norm1_gain.shape[0]
    pair_share = row_count // dp_size
    slot_count = pair_share + pair_share // 2
    slot_total = dp_size * slot_count

    send_rows, send_seeds, send_places, slots = pack(
        route, tokens, cotangent, dp_size, slot_count
    )
    got_places = lax.all_to_all(
        send_places[:, 0, :], "dp", split_axis=0, concat_axis=0, tiled=True
    )
    got_rows = lax.all_to_all(send_rows, "dp", split_axis=0, concat_axis=0, tiled=True)
    got_seeds = lax.all_to_all(send_seeds, "dp", split_axis=0, concat_axis=0, tiled=True)
    places = got_places.reshape(1, slot_total)
    place_ids = got_places.reshape(slot_total, 1)
    slot_of = slots.reshape(row_count, 1)

    input_piece = place_rows(places, got_rows.reshape(slot_total, narrow), row_count)
    seed_piece = place_rows(places, got_seeds.reshape(slot_total, narrow), row_count)
    input_full = gather_features(input_piece, mp_size, mp_index)
    seed_full = gather_features(seed_piece, mp_size, mp_index)

    first_mask, second_mask = seq_masks(seq_lengths[0], row_count)
    column_start = mp_index * narrow
    gain_one = lax.dynamic_slice_in_dim(norm1_gain, column_start, narrow)
    residual = input_full.astype(f32)
    scale_one = lax.rsqrt(jnp.mean(residual * residual, axis=1) + epsilon)
    normed_one = (residual * scale_one[:, None] * norm1_gain).astype(bf16)
    projected = jnp.einsum("rd,kdc->krc", normed_one, in_weight, preferred_element_type=f32)
    in_gate, out_gate, value_part = (projected[0], projected[1], projected[2])
    mixed = in_gate * value_part
    lag_one = lag_rows(mixed, 1) * first_mask
    lag_two = lag_rows(mixed, 2) * second_mask
    convolved = conv_weight[2] * mixed + conv_weight[1] * lag_one + conv_weight[0] * lag_two
    gated = (out_gate * convolved).astype(bf16)
    mix_terms = jnp.dot(gated, out_weight, preferred_element_type=f32)
    middle = residual + sum_mp(mix_terms, mp_size)
    scale_two = lax.rsqrt(jnp.mean(middle * middle, axis=1) + epsilon)
    normed_two = (middle * scale_two[:, None] * norm2_gain).astype(bf16)

    gate_val = jnp.dot(normed_two, gate_weight, preferred_element_type=f32)
    up_val = jnp.dot(normed_two, up_weight, preferred_element_type=f32)
    sigmoid_val = jax.nn.sigmoid(gate_val)
    silu_val = gate_val * sigmoid_val
    hidden = (silu_val * up_val).astype(bf16)
    grad_hidden = jnp.einsum("rd,fd->rf", seed_full, down_weight, preferred_element_type=f32)
    grad_gate_val = (
        grad_hidden * up_val * sigmoid_val * (1.0 + gate_val * (1.0 - sigmoid_val))
    ).astype(bf16)
    grad_up_val = (grad_hidden * silu_val).astype(bf16)
    normed_terms = jnp.einsum(
        "rf,df->rd", grad_gate_val, gate_weight, preferred_element_type=f32
    ) + jnp.einsum("rf,df->rd", grad_up_val, up_weight, preferred_element_type=f32)
    grad_normed_two = sum_mp(normed_terms, mp_size)

    down_terms = jnp.dot(hidden, down_weight, preferred_element_type=f32)
    middle_piece = lax.dynamic_slice_in_dim(middle, column_start, narrow, 1)
    block_piece = middle_piece + sum_features(down_terms, mp_size, mp_index)

    grad_down = jnp.einsum("rf,rd->fd", hidden, seed_full, preferred_element_type=f32)
    grad_gate = jnp.einsum("rd,rf->df", normed_two, grad_gate_val, preferred_element_type=f32)
    grad_up = jnp.einsum("rd,rf->df", normed_two, grad_up_val, preferred_element_type=f32)
    total_down = sum_dp(grad_down.astype(bf16), dp_size, dp_index)
    total_gate = sum_dp(grad_gate.astype(bf16), dp_size, dp_index)
    total_up = sum_dp(grad_up.astype(bf16), dp_size, dp_index)

    grad_gain_two = jnp.sum(grad_normed_two * middle * scale_two[:, None], axis=0)
    dot_two = jnp.sum(norm2_gain * grad_normed_two * middle, axis=1)
    grad_middle = (
        seed_full.astype(f32)
        + scale_two[:, None] * norm2_gain * grad_normed_two
        - middle * (scale_two * scale_two * scale_two * dot_two / model_width)[:, None]
    )
    grad_mix = grad_middle.astype(bf16)
    grad_out_weight = jnp.einsum("rc,rd->cd", gated, grad_mix, preferred_element_type=f32)
    grad_gated = jnp.einsum("rd,cd->rc", grad_mix, out_weight, preferred_element_type=f32)
    grad_conv = grad_gated * out_gate
    grad_conv_weight = jnp.stack(
        [
            jnp.sum(grad_conv * lag_two, axis=0),
            jnp.sum(grad_conv * lag_one, axis=0),
            jnp.sum(grad_conv * mixed, axis=0),
        ],
        axis=0,
    )
    grad_mixed = (
        conv_weight[2] * grad_conv
        + conv_weight[1] * lead_rows(grad_conv * first_mask, 1)
        + conv_weight[0] * lead_rows(grad_conv * second_mask, 2)
    )
    grad_parts = jnp.stack(
        [grad_mixed * value_part, grad_gated * convolved, grad_mixed * in_gate], axis=0
    ).astype(bf16)
    first_terms = jnp.einsum("krc,kdc->rd", grad_parts, in_weight, preferred_element_type=f32)
    grad_in_weight = jnp.einsum("rd,krc->kdc", normed_one, grad_parts, preferred_element_type=f32)
    total_in = sum_dp(
        grad_in_weight.astype(bf16).reshape(-1, narrow), dp_size, dp_index
    ).reshape(in_weight.shape)
    total_out = sum_dp(grad_out_weight.astype(bf16), dp_size, dp_index)

    grad_normed_one = sum_features(first_terms, mp_size, mp_index)
    dot_one = jnp.sum(norm1_gain * first_terms * residual, axis=1)
    dot_one = dot_one + swap_mp(dot_one) if mp_size == 2 else lax.psum(dot_one, "mp")
    residual_piece = input_piece.astype(f32)
    gain_one_piece = jnp.sum(grad_normed_one * residual_piece * scale_one[:, None], axis=0)
    grad_middle_piece = lax.dynamic_slice_in_dim(grad_middle, column_start, narrow, 1)
    input_grad = (
        grad_middle_piece
        + scale_one[:, None] * gain_one * grad_normed_one
        - residual_piece * (scale_one * scale_one * scale_one * dot_one / model_width)[:, None]
    )

    small = lax.psum(
        jnp.concatenate(
            [gain_one_piece, grad_gain_two, grad_conv_weight.reshape(-1)], axis=0
        ),
        "dp",
    )
    total_gain_one = lax.all_gather(small[:narrow], "mp", axis=0, tiled=True)
    total_gain_two = small[narrow : narrow + model_width]
    total_conv = small[narrow + model_width :].reshape(conv_weight.shape)

    back_out = take_rows(place_ids, block_piece.astype(bf16), slot_count, bf16)
    back_grad = take_rows(place_ids, input_grad.astype(bf16), slot_count, bf16)
    shape = (dp_size, slot_count, narrow)
    home_out = lax.all_to_all(
        back_out.reshape(shape), "dp", split_axis=0, concat_axis=0, tiled=True
    )
    home_grad = lax.all_to_all(
        back_grad.reshape(shape), "dp", split_axis=0, concat_axis=0, tiled=True
    )
    block_rows = min(row_count, 256)
    block_out = take_rows(slot_of, home_out.reshape(slot_total, narrow), block_rows, bf16)
    tokens_grad = take_rows(slot_of, home_grad.reshape(slot_total, narrow), block_rows, f32)
    return (
        block_out,
        tokens_grad,
        total_gain_one,
        total_in.astype(f32),
        total_conv,
        total_out.astype(f32),
        total_gain_two,
        total_gate.astype(f32),
        total_up.astype(f32),
        total_down.astype(f32),
    )


def solution(mesh):
    in_specs = (
        P("dp", "mp"),
        P("dp", "mp"),
        P("dp"),
        P("dp", None),
        P(),
        P(None, None, "mp"),
        P(None, "mp"),
        P("mp", None),
        P(),
        P(None, "mp"),
        P(None, "mp"),
        P("mp", None),
    )
    out_specs = (
        P("dp", "mp"),
        P("dp", "mp"),
        P(),
        P(None, None, "mp"),
        P(None, "mp"),
        P("mp", None),
        P(),
        P(None, "mp"),
        P(None, "mp"),
        P("mp", None),
    )
    return jax.shard_map(
        on_device, mesh=mesh, in_specs=in_specs, out_specs=out_specs, check_vma=False
    )
```

time: 1360 us -> 783 us (0.58)
  waiting for transfers between devices: 858 us -> 309 us
  blocking collectives: 161 us -> 77.4 us
  local copies, waits for them, and re-layouts: 113 us -> 35.7 us
  other arithmetic: 44 us -> 108 us
  Pallas kernels: 0 us -> 54.4 us
  starting transfers between devices: 38.6 us -> 71.1 us
    psum x1 -> x0, waiting for transfers between devices: 474 us -> none  [on_device(): lax.psum((grad_gain_one, grad_in_weight, grad_conv_weight, grad_out_weigh...]
    ppermute x0 -> x47, waiting for transfers between devices: none -> 278 us  [the longest x40 211 us: flip(): return lax.ppermute(value, 'dp', [(i, i ^ bit) for i in range(size)])]
    reduce_scatter x4 -> x0, waiting for transfers between devices: 154 us -> none  [the longest x1 54.4 us: on_device(): lax.psum_scatter(normed_terms, 'mp', scatter_dimension=1, tiled=True)]
    all_gather x4 -> x0, waiting for transfers between devices: 109 us -> none  [the longest x1 37.1 us: on_device(): lax.all_gather(input_piece, 'mp', axis=1, tiled=True)]
    psum x4 -> x1, blocking collectives: 161 us -> 59.5 us  [on_device(): lax.psum(jnp.concatenate([gain_one_piece, grad_gain_two, grad_conv_weight...]
    all_to_all x3 -> x2, waiting for transfers between devices: 91.2 us -> 0.01 us  [the longest x1 0.01 us: on_device(): lax.all_to_all(back_out.reshape(shape), 'dp', split_axis=0, concat_axis=0...]
    pallas_call x0 -> x7, Pallas kernels: none -> 54.4 us  [the longest x4 33.5 us: take_rows(): pl.pallas_call(take_kernel, grid=(count // block,), in_specs=[pl.BlockSpe...]
    ppermute x0 -> x47, starting transfers between devices: none -> 43.3 us  [the longest x40 35.6 us: flip(): return lax.ppermute(value, 'dp', [(i, i ^ bit) for i in range(size)])]
  transfers between devices with their start and end apart: 14 -> 51, of which waited for: 11 -> 20; matrix products, arithmetic and copies ran while one was open for 11% -> 25% of each run, Pallas kernels for 0% -> 5%
where the time goes in v1:
time: 783 us; the launch traced here: 771 us
  waiting for transfers between devices  309 us (39%)
  matrix products  112 us (14%)
  other arithmetic  108 us (14%)
  blocking collectives  77.4 us (10%)
  starting transfers between devices  71.1 us (9%)
  Pallas kernels  54.4 us (7%)
  local copies, waits for them, and re-layouts  35.7 us (5%)
    ppermute x40, waiting for transfers between devices, flip(): return lax.ppermute(value, 'dp', [(i, i ^ bit) for i in range(size)])  211 us
    ppermute x7, waiting for transfers between devices, swap_mp(): return lax.ppermute(value, 'mp', [(0, 1), (1, 0)])  67.3 us
    psum x1, blocking collectives, on_device(): lax.psum(jnp.concatenate([gain_one_piece, grad_gain_two, grad_conv_weight...  59.5 us
    ppermute x40, starting transfers between devices, flip(): return lax.ppermute(value, 'dp', [(i, i ^ bit) for i in range(size)])  35.6 us
    pallas_call x4, Pallas kernels, take_rows(): pl.pallas_call(take_kernel, grid=(count // block,), in_specs=[pl.BlockSpe...  33.5 us
    all_to_all x1, waiting for transfers between devices, on_device(): lax.all_to_all(send_rows, 'dp', split_axis=0, concat_axis=0, tiled=True)  31.3 us
    select_n x16, other arithmetic, sum_dp(): jnp.where(side == 0, jnp.concatenate([value, other], axis=0), jnp.concate...  29.9 us
    dot_general x1, matrix products, on_device(): jnp.einsum('rd,fd->rf', seed_full, down_weight, preferred_element_type=f32)  17.2 us
  transfers between devices with their start and end apart: 51, of which 20 were waited for; matrix products, arithmetic and copies ran while one was open for 25% of the time, Pallas kernels for 5%

profile of v1, /device:TPU:0, one launch (start us, length us, event | category | flops | bytes accessed | tf_op | source)
XLA Modules:
  0.0 770.8 jit_solution(16009150559126508043)
XLA Ops:
  0.7 11.7 %pack.1 = (bf16[16,96,512]{2,1,0:T(8,128)(2,1)}, bf16[16,96,512]{2,1,0:T(8,128)(2,1)}, s32[16,8,96]{2,1,0:T(8,128)}, s32[1,1024]{1,0:T(1,128)}) custom-call(s32[1,1024]{1,0:T(1,128)} %bitcast.115, bf16[1024,512]{1,0:T(8,128)(2,1)} %refs_1_.1, bf16[1024,512]{1,0:T(8,128)(2,1)} %refs_2_.1), custom_call_target="tpu_custom_call" | custom-call | tf_op jit(solution)/shard_map/pack/pallas_call | solution.py:79
  13.2 13.6 %all_to_all.26 = s32[16,1,96]{2,1,0:T(1,128)S(1)} all-to-all(s32[16,1,96]{2,1,0:T(1,128)S(1)} %slice.67), channel_id=1, replica_groups=mesh['dp'=16,'mp'=2] {'dp'}, dimensions={0} | all-to-all | bytes 12288 | tf_op jit(solution)/shard_map/all_to_all | solution.py:240
  31.9 31.3 %all-to-all-done.1 = bf16[16,96,512]{2,1,0:T(8,128)(2,1)} async-done(((bf16[16,96,512]{2,1,0:T(8,128)(2,1)}), bf16[16,96,512]{2,1,0:T(8,128)(2,1)}, u32[]{:S(2)}, u32[]{:S(2)}) %all-to-all-start.1) | async-done | bytes 1572896 | tf_op jit(solution)/shard_map/all_to_all | solution.py:243
  63.2 4.6 place_rows.2
  69.3 9.3 %all-to-all-start.3 = ((bf16[16,96,512]{2,1,0:T(8,128)(2,1)}), bf16[16,96,512]{2,1,0:T(8,128)(2,1)}, u32[]{:S(2)}, u32[]{:S(2)}) async-start(bf16[16,96,512]{2,1,0:T(8,128)(2,1)} %get-tuple-element.17), calls=%async_computation.3 | async-start | bytes 3145728 | tf_op jit(solution)/shard_map/all_to_all | solution.py:244
  78.8 15.2 %collective-permute-done = bf16[1024,512]{1,0:T(8,128)(2,1)} collective-permute-done((bf16[1024,512]{1,0:T(8,128)(2,1)}, bf16[1024,512]{1,0:T(8,128)(2,1)}, u32[]{:S(2)}, u32[]{:S(2)}) %collective-permute-start) | collective-permute-done | bytes 1048608 | tf_op jit(solution)/shard_map/ppermute | solution.py:154
  97.6 6.1 convolution_bitcast_fusion
  118.0 4.7 place_rows.3
  123.2 38.5 %collective-permute-done.1 = bf16[1024,1024]{1,0:T(8,128)(2,1)} collective-permute-done((bf16[1024,1024]{1,0:T(8,128)(2,1)}, bf16[1024,1024]{1,0:T(8,128)(2,1)}, u32[]{:S(2)}, u32[]{:S(2)}) %collective-permute-start.1) | collective-permute-done | bytes 2097184 | tf_op jit(solution)/shard_map/ppermute | solution.py:154
  161.7 4.7 multiply_reduce_fusion.2
  168.9 10.8 %fusion.37 = f32[1024,2304]{1,0:T(8,128)} fusion(bf16[1024,1024]{1,0:T(8,128)(2,1)S(1)} %multiply_convert_fusion.3, bf16[1024,2304]{1,0:T(8,128)(2,1)} %param.21), kind=kOutput, calls=%fused_computation.152 | convolution fusion | flops 4831838208 | bytes 16252928 | tf_op jit(solution)/shard_map/dot_general | solution.py:272
  179.6 7.4 fusion.38
  187.1 17.2 %multiply_convert_fusion = (bf16[1024,2304]{1,0:T(8,128)(2,1)}, bf16[1024,2304]{1,0:T(8,128)(2,1)}, bf16[1024,2304]{1,0:T(8,128)(2,1)}) fusion(f32[1024,2304]{1,0:T(8,128)} %fusion.37, f32[1024,2304]{1,0:T(8,128)} %fusion.38, bf16[2304,1024]{1,0:T(8,128)(2,1)} %param.23, bf16[1024,512]{1,0:T(8,128)(2,1)} %collective-permute-done.3, ...), kind=kOutput, calls=%fused_computation | convolution fusion | flops 4876664832 | bytes 39845888 | tf_op jit(solution)/shard_map/rd,fd->rf/dot_general | solution.py:277
  204.3 9.9 %fusion.40 = f32[1024,1024]{1,0:T(8,128)} fusion(bf16[1024,2304]{1,0:T(8,128)(2,1)} %get-tuple-element.31, bf16[1024,2304]{1,0:T(8,128)(2,1)} %param.21), kind=kOutput, calls=%fused_computation.155 | convolution fusion | flops 4831838208 | bytes 13631488 | tf_op jit(solution)/shard_map/rf,df->rd/dot_general | solution.py:282
  214.2 5.6 convolution_convert_fusion.2
  219.9 8.6 %fusion.39 = f32[1024,1024]{1,0:T(8,128)S(1)} fusion(bf16[1024,2304]{1,0:T(8,128)(2,1)S(1)} %copy-done.39, bf16[2304,1024]{1,0:T(8,128)(2,1)} %param.23), kind=kOutput, calls=%fused_computation.154 | convolution fusion | flops 4831838208 | bytes 13631488 | tf_op jit(solution)/shard_map/dot_general | solution.py:287
  230.3 5.7 convolution_convert_fusion.1
  236.0 10.2 %fusion.34 = (bf16[1024,1024]{1,0:T(8,128)(2,1)}, f32[1024,1024]{1,0:T(8,128)}) fusion(f32[1024,1024]{1,0:T(8,128)} %fusion.40, bf16[1024,2304]{1,0:T(8,128)(2,1)S(1)} %bitcast.123, bf16[1024,2304]{1,0:T(8,128)(2,1)S(1)} %bitcast.120), kind=kOutput, calls=%fused_computation.151 | convolution fusion | flops 4833935360 | bytes 19922944 | tf_op jit(solution)/shard_map/rf,df->rd/dot_general | solution.py:284
  250.3 8.4 %convolution_convert_fusion = bf16[2304,1024]{1,0:T(8,128)(2,1)S(1)} fusion(bf16[1024,2304]{1,0:T(8,128)(2,1)} %get-tuple-element.32, bf16[1024,512]{1,0:T(8,128)(2,1)} %collective-permute-done.3, bf16[1024,512]{1,0:T(8,128)(2,1)S(1)} %copy-done.26, pred[]{:T(512)S(6)} %eq.77), kind=kOutput, calls=%fused_computation.9 | convolution fusion | flops 4843634688 | bytes 11534337 | tf_op jit(solution)/shard_map/rf,rd->fd/dot_general | solution.py:291
  265.3 11.3 %take_rows.4 = bf16[1536,512]{1,0:T(8,128)(2,1)} custom-call(s32[1536,1]{1,0:T(8,128)} %reshape.132.ids_ref, bf16[1024,512]{1,0:T(8,128)(2,1)} %add_convert_fusion.7.from_ref), custom_call_target="tpu_custom_call" | custom-call | tf_op jit(solution)/shard_map/take_rows/pallas_call | solution.py:139
  276.6 8.9 %all-to-all-start.2 = ((bf16[16,96,512]{2,1,0:T(8,128)(2,1)}), bf16[16,96,512]{2,1,0:T(8,128)(2,1)}, u32[]{:S(2)}, u32[]{:S(2)}) async-start(bf16[16,96,512]{2,1,0:T(8,128)(2,1)} %bitcast.97), calls=%async_computation.2 | async-start | bytes 3145728 | tf_op jit(solution)/shard_map/all_to_all | solution.py:357
  285.5 11.4 %collective-permute-done.4 = bf16[1024,1024]{1,0:T(8,128)(2,1)} collective-permute-done((bf16[1024,1024]{1,0:T(8,128)(2,1)}, bf16[1024,1024]{1,0:T(8,128)(2,1)}, u32[]{:S(2)}, u32[]{:S(2)}) %collective-permute-start.4) | collective-permute-done | bytes 2097184 | tf_op jit(solution)/shard_map/ppermute | solution.py:154
  296.9 5.5 multiply_reduce_fusion
  313.8 5.7 fusion.7
  324.7 7.1 convert_bitcast_fusion
  331.8 4.7 copy.48
  356.8 27.7 %collective-permute-done.16 = bf16[128,1024]{1,0:T(8,128)(2,1)S(1)} collective-permute-done((bf16[128,1024]{1,0:T(8,128)(2,1)S(1)}, bf16[128,1024]{1,0:T(8,128)(2,1)S(1)}, u32[]{:S(2)}, u32[]{:S(2)}) %collective-permute-start.16) | collective-permute-done | bytes 262176 | tf_op jit(solution)/shard_map/ppermute | solution.py:185
  403.3 11.5 %take_rows.6 = bf16[1536,512]{1,0:T(8,128)(2,1)} custom-call(s32[1536,1]{1,0:T(8,128)} %reshape.132.ids_ref, bf16[1024,512]{1,0:T(8,128)(2,1)} %get-tuple-element.34.from_ref), custom_call_target="tpu_custom_call" | custom-call | tf_op jit(solution)/shard_map/take_rows/pallas_call | solution.py:139
  420.5 17.0 %collective-permute-done.40 = bf16[576,1024]{1,0:T(8,128)(2,1)} collective-permute-done((bf16[576,1024]{1,0:T(8,128)(2,1)}, bf16[576,1024]{1,0:T(8,128)(2,1)}, u32[]{:S(2)}, u32[]{:S(2)}) %collective-permute-start.40) | collective-permute-done | bytes 1179680 | tf_op jit(solution)/shard_map/ppermute | solution.py:185
  448.6 15.3 %collective-permute-done.41 = bf16[288,1024]{1,0:T(8,128)(2,1)S(1)} collective-permute-done((bf16[288,1024]{1,0:T(8,128)(2,1)S(1)}, bf16[288,1024]{1,0:T(8,128)(2,1)S(1)}, u32[]{:S(2)}, u32[]{:S(2)}) %collective-permute-start.41) | collective-permute-done | bytes 589856 | tf_op jit(solution)/shard_map/ppermute | solution.py:185
  466.1 18.6 %collective-permute-done.26 = bf16[64,2304]{1,0:T(8,128)(2,1)S(1)} collective-permute-done((bf16[64,2304]{1,0:T(8,128)(2,1)S(1)}, bf16[64,2304]{1,0:T(8,128)(2,1)S(1)}, u32[]{:S(2)}, u32[]{:S(2)}) %collective-permute-start.26) | collective-permute-done | bytes 294944 | tf_op jit(solution)/shard_map/ppermute | solution.py:185
  484.8 12.5 %collective-permute-done.34 = bf16[64,2304]{1,0:T(8,128)(2,1)S(1)} collective-permute-done((bf16[64,2304]{1,0:T(8,128)(2,1)S(1)}, bf16[64,2304]{1,0:T(8,128)(2,1)S(1)}, u32[]{:S(2)}, u32[]{:S(2)}) %collective-permute-start.34) | collective-permute-done | bytes 294944 | tf_op jit(solution)/shard_map/ppermute | solution.py:185
  497.9 5.9 collective-permute-done.42
  504.0 6.2 collective-permute-done.27
  510.3 21.6 %collective-permute-done.9 = bf16[384,512]{1,0:T(8,128)(2,1)S(1)} collective-permute-done((bf16[384,512]{1,0:T(8,128)(2,1)S(1)}, bf16[384,512]{1,0:T(8,128)(2,1)S(1)}, u32[]{:S(2)}, u32[]{:S(2)}) %collective-permute-start.9) | collective-permute-done | bytes 393248 | tf_op jit(solution)/shard_map/ppermute | solution.py:185
  533.1 6.7 collective-permute-done.10
  539.9 8.9 %collective-permute-done.28 = bf16[128,2304]{1,0:T(8,128)(2,1)S(1)} collective-permute-done((bf16[128,2304]{1,0:T(8,128)(2,1)S(1)}, bf16[128,2304]{1,0:T(8,128)(2,1)S(1)}, u32[]{:S(2)}, u32[]{:S(2)}) %collective-permute-start.28) | collective-permute-done | bytes 589856 | tf_op jit(solution)/shard_map/ppermute | solution.py:185
  556.7 5.3 all-to-all-start.4
  566.8 15.8 %collective-permute-done.12 = bf16[384,512]{1,0:T(8,128)(2,1)} collective-permute-done((bf16[384,512]{1,0:T(8,128)(2,1)S(1)}, bf16[384,512]{1,0:T(8,128)(2,1)}, u32[]{:S(2)}, u32[]{:S(2)}) %collective-permute-start.12) | collective-permute-done | bytes 393248 | tf_op jit(solution)/shard_map/ppermute | solution.py:185
  588.1 14.2 %collective-permute-done.44 = bf16[288,1024]{1,0:T(8,128)(2,1)} collective-permute-done((bf16[288,1024]{1,0:T(8,128)(2,1)}, bf16[288,1024]{1,0:T(8,128)(2,1)}, u32[]{:S(2)}, u32[]{:S(2)}) %collective-permute-start.44) | collective-permute-done | bytes 589856 | tf_op jit(solution)/shard_map/ppermute | solution.py:185
  610.0 17.6 %collective-permute-done.13 = bf16[768,512]{1,0:T(8,128)(2,1)} collective-permute-done((bf16[768,512]{1,0:T(8,128)(2,1)}, bf16[768,512]{1,0:T(8,128)(2,1)}, u32[]{:S(2)}, u32[]{:S(2)}) %collective-permute-start.13) | collective-permute-done | bytes 786464 | tf_op jit(solution)/shard_map/ppermute | solution.py:185
  636.2 20.1 %collective-permute-done.45 = bf16[576,1024]{1,0:T(8,128)(2,1)S(1)} collective-permute-done((bf16[576,1024]{1,0:T(8,128)(2,1)S(1)}, bf16[576,1024]{1,0:T(8,128)(2,1)S(1)}, u32[]{:S(2)}, u32[]{:S(2)}) %collective-permute-start.45) | collective-permute-done | bytes 1179680 | tf_op jit(solution)/shard_map/ppermute | solution.py:185
  659.8 59.5 %psum.7 = f32[3072]{0:T(1024)S(1)} all-reduce(f32[3072]{0:T(1024)S(1)} %pad_maximum_fusion.3), channel_id=1, replica_groups=mesh['dp'=16,'mp'=2] {'dp'}, use_global_device_ids=true, to_apply=%region_11.12 | all-reduce | flops 3072 | bytes 24576 | tf_op jit(solution)/shard_map/psum | solution.py:344
  724.9 5.4 take_rows.5
  733.6 5.3 take_rows.7
  745.8 8.5 %fusion.1 = f32[1024,2304]{1,0:T(8,128)} fusion(bf16[512,2304]{1,0:T(8,128)(2,1)} %collective-permute-done.30, bf16[512,2304]{1,0:T(8,128)(2,1)} %maximum_select_fusion.4, pred[]{:T(512)S(6)} %eq.78), kind=kLoop, calls=%fused_computation.13 | loop fusion | flops 23592960 | bytes 14155777 | tf_op jit(solution)/shard_map/convert_element_type | solution.py:374
  754.3 8.5 %fusion.2 = f32[1024,2304]{1,0:T(8,128)} fusion(bf16[512,2304]{1,0:T(8,128)(2,1)} %collective-permute-done.38, bf16[512,2304]{1,0:T(8,128)(2,1)} %maximum_select_fusion.5, pred[]{:T(512)S(6)} %eq.78), kind=kLoop, calls=%fused_computation.15 | loop fusion | flops 23592960 | bytes 14155777 | tf_op jit(solution)/shard_map/convert_element_type | solution.py:375
  762.8 6.9 fusion.3
  (291 shorter events, 171.7 us)
Async XLA Ops:
  26.8 36.4 %all-to-all-start.1 = ((bf16[16,96,512]{2,1,0:T(8,128)(2,1)}), bf16[16,96,512]{2,1,0:T(8,128)(2,1)}, u32[]{:S(2)}, u32[]{:S(2)}) async-start(bf16[16,96,512]{2,1,0:T(8,128)(2,1)} %get-tuple-element.16), calls=%async_computation.1 | async-start | bytes 3145728 | tf_op jit(solution)/shard_map/all_to_all | solution.py:243
  67.8 26.2 %collective-permute-start = (bf16[1024,512]{1,0:T(8,128)(2,1)}, bf16[1024,512]{1,0:T(8,128)(2,1)}, u32[]{:S(2)}, u32[]{:S(2)}) collective-permute-start(bf16[1024,512]{1,0:T(8,128)(2,1)} %place_rows.2), channel_id=1, source_target_pairs={{0,1},{1,0},{2,3},{3,2},{4,5},{5,4},{6,7},{7,6},{8,9},{9,8},{10,11... | collective-permute-start | bytes 3145736 | tf_op jit(solution)/shard_map/ppermute | solution.py:154
  69.3 48.7 %all-to-all-start.3 = ((bf16[16,96,512]{2,1,0:T(8,128)(2,1)}), bf16[16,96,512]{2,1,0:T(8,128)(2,1)}, u32[]{:S(2)}, u32[]{:S(2)}) async-start(bf16[16,96,512]{2,1,0:T(8,128)(2,1)} %get-tuple-element.17), calls=%async_computation.3 | async-start | bytes 3145728 | tf_op jit(solution)/shard_map/all_to_all | solution.py:244
  112.9 48.8 %collective-permute-start.1 = (bf16[1024,1024]{1,0:T(8,128)(2,1)}, bf16[1024,1024]{1,0:T(8,128)(2,1)}, u32[]{:S(2)}, u32[]{:S(2)}) collective-permute-start(bf16[1024,1024]{1,0:T(8,128)(2,1)} %get-tuple-element.41), channel_id=1, source_target_pairs={{0,1},{1,0},{2,3},{3,2},{4,5},{5,4},{6,7},{7,6},{8,9},{9,8},{10,11... | collective-permute-start | bytes 6291464 | tf_op jit(solution)/shard_map/ppermute | solution.py:154
  122.7 64.4 %collective-permute-start.3 = (bf16[1024,512]{1,0:T(8,128)(2,1)}, bf16[1024,512]{1,0:T(8,128)(2,1)}, u32[]{:S(2)}, u32[]{:S(2)}) collective-permute-start(bf16[1024,512]{1,0:T(8,128)(2,1)} %place_rows.3), channel_id=1, source_target_pairs={{0,1},{1,0},{2,3},{3,2},{4,5},{5,4},{6,7},{7,6},{8,9},{9,8},{10,11... | collective-permute-start | bytes 3145736 | tf_op jit(solution)/shard_map/ppermute | solution.py:154
  228.7 33.6 %collective-permute-start.2 = (bf16[1024,512]{1,0:T(8,128)(2,1)S(1)}, bf16[1024,512]{1,0:T(8,128)(2,1)S(1)}, u32[]{:S(2)}, u32[]{:S(2)}) collective-permute-start(bf16[1024,512]{1,0:T(8,128)(2,1)S(1)} %select_convert_fusion.1), channel_id=1, source_target_pairs={{0,1},{1,0},{2,3},{3,2},{4,5},{5,4},{6,7},{7,6},{8,9},{9,8},{10,11... | collective-permute-start | bytes 3145736 | tf_op jit(solution)/shard_map/ppermute | solution.py:154
  246.2 50.7 %collective-permute-start.4 = (bf16[1024,1024]{1,0:T(8,128)(2,1)}, bf16[1024,1024]{1,0:T(8,128)(2,1)}, u32[]{:S(2)}, u32[]{:S(2)}) collective-permute-start(bf16[1024,1024]{1,0:T(8,128)(2,1)} %get-tuple-element.43), channel_id=1, source_target_pairs={{0,1},{1,0},{2,3},{3,2},{4,5},{5,4},{6,7},{7,6},{8,9},{9,8},{10,11... | collective-permute-start | bytes 6291464 | tf_op jit(solution)/shard_map/ppermute | solution.py:154
  248.2 97.0 %collective-permute-start.23 = (bf16[512,2304]{1,0:T(8,128)(2,1)}, bf16[512,2304]{1,0:T(8,128)(2,1)}, u32[]{:S(2)}, u32[]{:S(2)}) collective-permute-start(bf16[512,2304]{1,0:T(8,128)(2,1)} %constant_dynamic-slice_fusion.11), channel_id=1, source_target_pairs={{0,2},{2,0},{4,6},{6,4},{8,10},{10,8},{12,14},{14,12},{16,18},{18,... | collective-permute-start | bytes 7077896 | tf_op jit(solution)/shard_map/ppermute | solution.py:185
  249.8 100.0 %collective-permute-start.31 = (bf16[512,2304]{1,0:T(8,128)(2,1)}, bf16[512,2304]{1,0:T(8,128)(2,1)}, u32[]{:S(2)}, u32[]{:S(2)}) collective-permute-start(bf16[512,2304]{1,0:T(8,128)(2,1)} %constant_dynamic-slice_fusion.7), channel_id=1, source_target_pairs={{0,2},{2,0},{4,6},{6,4},{8,10},{10,8},{12,14},{14,12},{16,18},{18,... | collective-permute-start | bytes 7077896 | tf_op jit(solution)/shard_map/ppermute | solution.py:185
  262.3 124.1 %collective-permute-start.39 = (bf16[1152,1024]{1,0:T(8,128)(2,1)}, bf16[1152,1024]{1,0:T(8,128)(2,1)}, u32[]{:S(2)}, u32[]{:S(2)}) collective-permute-start(bf16[1152,1024]{1,0:T(8,128)(2,1)} %constant_dynamic-slice_fusion.3), channel_id=1, source_target_pairs={{0,2},{2,0},{4,6},{6,4},{8,10},{10,8},{12,14},{14,12},{16,18},{18,... | collective-permute-start | bytes 7077896 | tf_op jit(solution)/shard_map/ppermute | solution.py:185
  276.6 280.1 %all-to-all-start.2 = ((bf16[16,96,512]{2,1,0:T(8,128)(2,1)}), bf16[16,96,512]{2,1,0:T(8,128)(2,1)}, u32[]{:S(2)}, u32[]{:S(2)}) async-start(bf16[16,96,512]{2,1,0:T(8,128)(2,1)} %bitcast.97), calls=%async_computation.2 | async-start | bytes 3145728 | tf_op jit(solution)/shard_map/all_to_all | solution.py:357
  322.7 76.2 %collective-permute-start.5 = (bf16[1024,512]{1,0:T(8,128)(2,1)}, bf16[1024,512]{1,0:T(8,128)(2,1)}, u32[]{:S(2)}, u32[]{:S(2)}) collective-permute-start(bf16[1024,512]{1,0:T(8,128)(2,1)} %select_convert_fusion), channel_id=1, source_target_pairs={{0,1},{1,0},{2,3},{3,2},{4,5},{5,4},{6,7},{7,6},{8,9},{9,8},{10,11... | collective-permute-start | bytes 3145736 | tf_op jit(solution)/shard_map/ppermute | solution.py:154
  324.2 21.0 %collective-permute-start.6 = (f32[1024]{0:T(1024)S(1)}, f32[1024]{0:T(1024)S(1)}, u32[]{:S(2)}, u32[]{:S(2)}) collective-permute-start(f32[1024]{0:T(1024)S(1)} %get-tuple-element.45), channel_id=1, source_target_pairs={{0,1},{1,0},{2,3},{3,2},{4,5},{5,4},{6,7},{7,6},{8,9},{9,8},{10,11... | collective-permute-start | bytes 12296 | tf_op jit(solution)/shard_map/ppermute | solution.py:154
  345.2 97.7 %collective-permute-start.7 = (bf16[1536,512]{1,0:T(8,128)(2,1)}, bf16[1536,512]{1,0:T(8,128)(2,1)}, u32[]{:S(2)}, u32[]{:S(2)}) collective-permute-start(bf16[1536,512]{1,0:T(8,128)(2,1)} %constant_dynamic-slice_fusion.19), channel_id=1, source_target_pairs={{0,2},{2,0},{4,6},{6,4},{8,10},{10,8},{12,14},{14,12},{16,18},{18,... | collective-permute-start | bytes 4718600 | tf_op jit(solution)/shard_map/ppermute | solution.py:185
  345.2 9.5 %collective-permute-start.15 = (bf16[256,1024]{1,0:T(8,128)(2,1)S(1)}, bf16[256,1024]{1,0:T(8,128)(2,1)S(1)}, u32[]{:S(2)}, u32[]{:S(2)}) collective-permute-start(bf16[256,1024]{1,0:T(8,128)(2,1)S(1)} %constant_dynamic-slice_fusion.15), channel_id=1, source_target_pairs={{0,2},{2,0},{4,6},{6,4},{8,10},{10,8},{12,14},{14,12},{16,18},{18,... | collective-permute-start | bytes 1572872 | tf_op jit(solution)/shard_map/ppermute | solution.py:185
  349.9 64.9 %collective-permute-start.24 = (bf16[256,2304]{1,0:T(8,128)(2,1)}, bf16[256,2304]{1,0:T(8,128)(2,1)}, u32[]{:S(2)}, u32[]{:S(2)}) collective-permute-start(bf16[256,2304]{1,0:T(8,128)(2,1)} %constant_dynamic-slice_fusion.10), channel_id=1, source_target_pairs={{0,4},{2,6},{4,0},{6,2},{8,12},{10,14},{12,8},{14,10},{16,20},{18,... | collective-permute-start | bytes 3538952 | tf_op jit(solution)/shard_map/ppermute | solution.py:185
  355.0 29.5 %collective-permute-start.16 = (bf16[128,1024]{1,0:T(8,128)(2,1)S(1)}, bf16[128,1024]{1,0:T(8,128)(2,1)S(1)}, u32[]{:S(2)}, u32[]{:S(2)}) collective-permute-start(bf16[128,1024]{1,0:T(8,128)(2,1)S(1)} %constant_dynamic-slice_fusion.14), channel_id=1, source_target_pairs={{0,4},{2,6},{4,0},{6,2},{8,12},{10,14},{12,8},{14,10},{16,20},{18,... | collective-permute-start | bytes 786440 | tf_op jit(solution)/shard_map/ppermute | solution.py:185
  384.5 34.1 %collective-permute-start.32 = (bf16[256,2304]{1,0:T(8,128)(2,1)}, bf16[256,2304]{1,0:T(8,128)(2,1)}, u32[]{:S(2)}, u32[]{:S(2)}) collective-permute-start(bf16[256,2304]{1,0:T(8,128)(2,1)} %constant_dynamic-slice_fusion.6), channel_id=1, source_target_pairs={{0,4},{2,6},{4,0},{6,2},{8,12},{10,14},{12,8},{14,10},{16,20},{18,... | collective-permute-start | bytes 3538952 | tf_op jit(solution)/shard_map/ppermute | solution.py:185
  397.2 40.3 %collective-permute-start.40 = (bf16[576,1024]{1,0:T(8,128)(2,1)}, bf16[576,1024]{1,0:T(8,128)(2,1)}, u32[]{:S(2)}, u32[]{:S(2)}) collective-permute-start(bf16[576,1024]{1,0:T(8,128)(2,1)} %constant_dynamic-slice_fusion.2), channel_id=1, source_target_pairs={{0,4},{2,6},{4,0},{6,2},{8,12},{10,14},{12,8},{14,10},{16,20},{18,... | collective-permute-start | bytes 3538952 | tf_op jit(solution)/shard_map/ppermute | solution.py:185
  399.0 152.9 %collective-permute-start.19 = (bf16[32,1024]{1,0:T(8,128)(2,1)S(1)}, bf16[32,1024]{1,0:T(8,128)(2,1)S(1)}, u32[]{:S(2)}, u32[]{:S(2)}) collective-permute-start(bf16[32,1024]{1,0:T(8,128)(2,1)S(1)} %add_convert_fusion.20), channel_id=1, source_target_pairs={{0,16},{2,18},{4,20},{6,22},{8,24},{10,26},{12,28},{14,30},{16,0},... | collective-permute-start | bytes 196616 | tf_op jit(solution)/shard_map/ppermute | solution.py:185
  416.4 28.7 %collective-permute-start.25 = (bf16[128,2304]{1,0:T(8,128)(2,1)S(1)}, bf16[128,2304]{1,0:T(8,128)(2,1)S(1)}, u32[]{:S(2)}, u32[]{:S(2)}) collective-permute-start(bf16[128,2304]{1,0:T(8,128)(2,1)S(1)} %constant_dynamic-slice_fusion.9), channel_id=1, source_target_pairs={{0,8},{2,10},{4,12},{6,14},{8,0},{10,2},{12,4},{14,6},{16,24},{18,... | collective-permute-start | bytes 1769480 | tf_op jit(solution)/shard_map/ppermute | solution.py:185
  420.3 26.6 %collective-permute-start.33 = (bf16[128,2304]{1,0:T(8,128)(2,1)S(1)}, bf16[128,2304]{1,0:T(8,128)(2,1)S(1)}, u32[]{:S(2)}, u32[]{:S(2)}) collective-permute-start(bf16[128,2304]{1,0:T(8,128)(2,1)S(1)} %constant_dynamic-slice_fusion.5), channel_id=1, source_target_pairs={{0,8},{2,10},{4,12},{6,14},{8,0},{10,2},{12,4},{14,6},{16,24},{18,... | collective-permute-start | bytes 1769480 | tf_op jit(solution)/shard_map/ppermute | solution.py:185
  439.3 24.6 %collective-permute-start.41 = (bf16[288,1024]{1,0:T(8,128)(2,1)S(1)}, bf16[288,1024]{1,0:T(8,128)(2,1)S(1)}, u32[]{:S(2)}, u32[]{:S(2)}) collective-permute-start(bf16[288,1024]{1,0:T(8,128)(2,1)S(1)} %constant_dynamic-slice_fusion.1), channel_id=1, source_target_pairs={{0,8},{2,10},{4,12},{6,14},{8,0},{10,2},{12,4},{14,6},{16,24},{18,... | collective-permute-start | bytes 1769480 | tf_op jit(solution)/shard_map/ppermute | solution.py:185
  444.8 52.7 %collective-permute-start.8 = (bf16[768,512]{1,0:T(8,128)(2,1)S(1)}, bf16[768,512]{1,0:T(8,128)(2,1)S(1)}, u32[]{:S(2)}, u32[]{:S(2)}) collective-permute-start(bf16[768,512]{1,0:T(8,128)(2,1)S(1)} %constant_dynamic-slice_fusion.18), channel_id=1, source_target_pairs={{0,4},{2,6},{4,0},{6,2},{8,12},{10,14},{12,8},{14,10},{16,20},{18,... | collective-permute-start | bytes 2359304 | tf_op jit(solution)/shard_map/ppermute | solution.py:185
  445.3 39.4 %collective-permute-start.26 = (bf16[64,2304]{1,0:T(8,128)(2,1)S(1)}, bf16[64,2304]{1,0:T(8,128)(2,1)S(1)}, u32[]{:S(2)}, u32[]{:S(2)}) collective-permute-start(bf16[64,2304]{1,0:T(8,128)(2,1)S(1)} %constant_dynamic-slice_fusion.8), channel_id=1, source_target_pairs={{0,16},{2,18},{4,20},{6,22},{8,24},{10,26},{12,28},{14,30},{16,0},... | collective-permute-start | bytes 884744 | tf_op jit(solution)/shard_map/ppermute | solution.py:185
  447.0 50.4 %collective-permute-start.34 = (bf16[64,2304]{1,0:T(8,128)(2,1)S(1)}, bf16[64,2304]{1,0:T(8,128)(2,1)S(1)}, u32[]{:S(2)}, u32[]{:S(2)}) collective-permute-start(bf16[64,2304]{1,0:T(8,128)(2,1)S(1)} %constant_dynamic-slice_fusion.4), channel_id=1, source_target_pairs={{0,16},{2,18},{4,20},{6,22},{8,24},{10,26},{12,28},{14,30},{16,0},... | collective-permute-start | bytes 884744 | tf_op jit(solution)/shard_map/ppermute | solution.py:185
  464.1 39.7 %collective-permute-start.42 = (bf16[144,1024]{1,0:T(8,128)(2,1)S(1)}, bf16[144,1024]{1,0:T(8,128)(2,1)S(1)}, u32[]{:S(2)}, u32[]{:S(2)}) collective-permute-start(bf16[144,1024]{1,0:T(8,128)(2,1)S(1)} %constant_dynamic-slice_fusion), channel_id=1, source_target_pairs={{0,16},{2,18},{4,20},{6,22},{8,24},{10,26},{12,28},{14,30},{16,0},... | collective-permute-start | bytes 884744 | tf_op jit(solution)/shard_map/ppermute | solution.py:185
  484.8 25.3 %collective-permute-start.27 = (bf16[64,2304]{1,0:T(8,128)(2,1)S(1)}, bf16[64,2304]{1,0:T(8,128)(2,1)S(1)}, u32[]{:S(2)}, u32[]{:S(2)}) collective-permute-start(bf16[64,2304]{1,0:T(8,128)(2,1)S(1)} %add_convert_fusion.16), channel_id=1, source_target_pairs={{0,16},{2,18},{4,20},{6,22},{8,24},{10,26},{12,28},{14,30},{16,0},... | collective-permute-start | bytes 884744 | tf_op jit(solution)/shard_map/ppermute | solution.py:185
  497.4 34.7 %collective-permute-start.35 = (bf16[64,2304]{1,0:T(8,128)(2,1)S(1)}, bf16[64,2304]{1,0:T(8,128)(2,1)S(1)}, u32[]{:S(2)}, u32[]{:S(2)}) collective-permute-start(bf16[64,2304]{1,0:T(8,128)(2,1)S(1)} %add_convert_fusion.15), channel_id=1, source_target_pairs={{0,16},{2,18},{4,20},{6,22},{8,24},{10,26},{12,28},{14,30},{16,0},... | collective-permute-start | bytes 884744 | tf_op jit(solution)/shard_map/ppermute | solution.py:185
  497.8 34.1 %collective-permute-start.9 = (bf16[384,512]{1,0:T(8,128)(2,1)S(1)}, bf16[384,512]{1,0:T(8,128)(2,1)S(1)}, u32[]{:S(2)}, u32[]{:S(2)}) collective-permute-start(bf16[384,512]{1,0:T(8,128)(2,1)S(1)} %constant_dynamic-slice_fusion.17), channel_id=1, source_target_pairs={{0,8},{2,10},{4,12},{6,14},{8,0},{10,2},{12,4},{14,6},{16,24},{18,... | collective-permute-start | bytes 1179656 | tf_op jit(solution)/shard_map/ppermute | solution.py:185
  503.9 51.8 %collective-permute-start.43 = (bf16[144,1024]{1,0:T(8,128)(2,1)S(1)}, bf16[144,1024]{1,0:T(8,128)(2,1)S(1)}, u32[]{:S(2)}, u32[]{:S(2)}) collective-permute-start(bf16[144,1024]{1,0:T(8,128)(2,1)S(1)} %add_convert_fusion.14), channel_id=1, source_target_pairs={{0,16},{2,18},{4,20},{6,22},{8,24},{10,26},{12,28},{14,30},{16,0},... | collective-permute-start | bytes 884744 | tf_op jit(solution)/shard_map/ppermute | solution.py:185
  510.2 38.6 %collective-permute-start.28 = (bf16[128,2304]{1,0:T(8,128)(2,1)S(1)}, bf16[128,2304]{1,0:T(8,128)(2,1)S(1)}, u32[]{:S(2)}, u32[]{:S(2)}) collective-permute-start(bf16[128,2304]{1,0:T(8,128)(2,1)S(1)} %maximum_select_fusion.15), channel_id=1, source_target_pairs={{0,8},{2,10},{4,12},{6,14},{8,0},{10,2},{12,4},{14,6},{16,24},{18,... | collective-permute-start | bytes 1769480 | tf_op jit(solution)/shard_map/ppermute | solution.py:185
  533.1 28.9 %collective-permute-start.36 = (bf16[128,2304]{1,0:T(8,128)(2,1)}, bf16[128,2304]{1,0:T(8,128)(2,1)}, u32[]{:S(2)}, u32[]{:S(2)}) collective-permute-start(bf16[128,2304]{1,0:T(8,128)(2,1)} %maximum_select_fusion.16), channel_id=1, source_target_pairs={{0,8},{2,10},{4,12},{6,14},{8,0},{10,2},{12,4},{14,6},{16,24},{18,... | collective-permute-start | bytes 1769480 | tf_op jit(solution)/shard_map/ppermute | solution.py:185
  539.8 12.8 %collective-permute-start.11 = (bf16[192,512]{1,0:T(8,128)(2,1)S(1)}, bf16[192,512]{1,0:T(8,128)(2,1)S(1)}, u32[]{:S(2)}, u32[]{:S(2)}) collective-permute-start(bf16[192,512]{1,0:T(8,128)(2,1)S(1)} %add_convert_fusion.18), channel_id=1, source_target_pairs={{0,16},{2,18},{4,20},{6,22},{8,24},{10,26},{12,28},{14,30},{16,0},... | collective-permute-start | bytes 589832 | tf_op jit(solution)/shard_map/ppermute | solution.py:185
  550.0 56.4 %collective-permute-start.29 = (bf16[256,2304]{1,0:T(8,128)(2,1)}, bf16[256,2304]{1,0:T(8,128)(2,1)}, u32[]{:S(2)}, u32[]{:S(2)}) collective-permute-start(bf16[256,2304]{1,0:T(8,128)(2,1)} %maximum_select_fusion.10), channel_id=1, source_target_pairs={{0,4},{2,6},{4,0},{6,2},{8,12},{10,14},{12,8},{14,10},{16,20},{18,... | collective-permute-start | bytes 3538952 | tf_op jit(solution)/shard_map/ppermute | solution.py:185
  552.6 32.4 %collective-permute-start.20 = (bf16[64,1024]{1,0:T(8,128)(2,1)}, bf16[64,1024]{1,0:T(8,128)(2,1)}, u32[]{:S(2)}, u32[]{:S(2)}) collective-permute-start(bf16[64,1024]{1,0:T(8,128)(2,1)} %maximum_select_fusion.21), channel_id=1, source_target_pairs={{0,8},{2,10},{4,12},{6,14},{8,0},{10,2},{12,4},{14,6},{16,24},{18,... | collective-permute-start | bytes 393224 | tf_op jit(solution)/shard_map/ppermute | solution.py:185
  552.7 29.8 %collective-permute-start.12 = (bf16[384,512]{1,0:T(8,128)(2,1)S(1)}, bf16[384,512]{1,0:T(8,128)(2,1)}, u32[]{:S(2)}, u32[]{:S(2)}) collective-permute-start(bf16[384,512]{1,0:T(8,128)(2,1)S(1)} %maximum_select_fusion.19), channel_id=1, source_target_pairs={{0,8},{2,10},{4,12},{6,14},{8,0},{10,2},{12,4},{14,6},{16,24},{18,... | collective-permute-start | bytes 1179656 | tf_op jit(solution)/shard_map/ppermute | solution.py:185
  556.6 45.6 %collective-permute-start.44 = (bf16[288,1024]{1,0:T(8,128)(2,1)}, bf16[288,1024]{1,0:T(8,128)(2,1)}, u32[]{:S(2)}, u32[]{:S(2)}) collective-permute-start(bf16[288,1024]{1,0:T(8,128)(2,1)} %maximum_select_fusion.17), channel_id=1, source_target_pairs={{0,8},{2,10},{4,12},{6,14},{8,0},{10,2},{12,4},{14,6},{16,24},{18,... | collective-permute-start | bytes 1769480 | tf_op jit(solution)/shard_map/ppermute | solution.py:185
  556.7 176.9 %all-to-all-start.4 = ((bf16[16,96,512]{2,1,0:T(8,128)(2,1)}), bf16[16,96,512]{2,1,0:T(8,128)(2,1)}, u32[]{:S(2)}, u32[]{:S(2)}) async-start(bf16[16,96,512]{2,1,0:T(8,128)(2,1)} %bitcast.98), calls=%async_computation.4 | async-start | bytes 3145728 | tf_op jit(solution)/shard_map/all_to_all | solution.py:360
  564.9 66.2 %collective-permute-start.37 = (bf16[256,2304]{1,0:T(8,128)(2,1)}, bf16[256,2304]{1,0:T(8,128)(2,1)}, u32[]{:S(2)}, u32[]{:S(2)}) collective-permute-start(bf16[256,2304]{1,0:T(8,128)(2,1)} %maximum_select_fusion.11), channel_id=1, source_target_pairs={{0,4},{2,6},{4,0},{6,2},{8,12},{10,14},{12,8},{14,10},{16,20},{18,... | collective-permute-start | bytes 3538952 | tf_op jit(solution)/shard_map/ppermute | solution.py:185
  584.8 42.8 %collective-permute-start.13 = (bf16[768,512]{1,0:T(8,128)(2,1)}, bf16[768,512]{1,0:T(8,128)(2,1)}, u32[]{:S(2)}, u32[]{:S(2)}) collective-permute-start(bf16[768,512]{1,0:T(8,128)(2,1)} %maximum_select_fusion.14), channel_id=1, source_target_pairs={{0,4},{2,6},{4,0},{6,2},{8,12},{10,14},{12,8},{14,10},{16,20},{18,... | collective-permute-start | bytes 2359304 | tf_op jit(solution)/shard_map/ppermute | solution.py:185
  586.2 49.1 %collective-permute-start.21 = (bf16[128,1024]{1,0:T(8,128)(2,1)S(1)}, bf16[128,1024]{1,0:T(8,128)(2,1)S(1)}, u32[]{:S(2)}, u32[]{:S(2)}) collective-permute-start(bf16[128,1024]{1,0:T(8,128)(2,1)S(1)} %maximum_select_fusion.20), channel_id=1, source_target_pairs={{0,4},{2,6},{4,0},{6,2},{8,12},{10,14},{12,8},{14,10},{16,20},{18,... | collective-permute-start | bytes 786440 | tf_op jit(solution)/shard_map/ppermute | solution.py:185
  604.5 51.9 %collective-permute-start.45 = (bf16[576,1024]{1,0:T(8,128)(2,1)S(1)}, bf16[576,1024]{1,0:T(8,128)(2,1)S(1)}, u32[]{:S(2)}, u32[]{:S(2)}) collective-permute-start(bf16[576,1024]{1,0:T(8,128)(2,1)S(1)} %maximum_select_fusion.12), channel_id=1, source_target_pairs={{0,4},{2,6},{4,0},{6,2},{8,12},{10,14},{12,8},{14,10},{16,20},{18,... | collective-permute-start | bytes 3538952 | tf_op jit(solution)/shard_map/ppermute | solution.py:185
  610.0 135.8 %collective-permute-start.30 = (bf16[512,2304]{1,0:T(8,128)(2,1)}, bf16[512,2304]{1,0:T(8,128)(2,1)}, u32[]{:S(2)}, u32[]{:S(2)}) collective-permute-start(bf16[512,2304]{1,0:T(8,128)(2,1)} %maximum_select_fusion.4), channel_id=1, source_target_pairs={{0,2},{2,0},{4,6},{6,4},{8,10},{10,8},{12,14},{14,12},{16,18},{18,... | collective-permute-start | bytes 7077896 | tf_op jit(solution)/shard_map/ppermute | solution.py:185
  631.1 107.8 %collective-permute-start.14 = (bf16[1536,512]{1,0:T(8,128)(2,1)}, bf16[1536,512]{1,0:T(8,128)(2,1)}, u32[]{:S(2)}, u32[]{:S(2)}) collective-permute-start(bf16[1536,512]{1,0:T(8,128)(2,1)} %maximum_select_fusion.9), channel_id=1, source_target_pairs={{0,2},{2,0},{4,6},{6,4},{8,10},{10,8},{12,14},{14,12},{16,18},{18,... | collective-permute-start | bytes 4718600 | tf_op jit(solution)/shard_map/ppermute | solution.py:185
  634.8 119.5 %collective-permute-start.38 = (bf16[512,2304]{1,0:T(8,128)(2,1)}, bf16[512,2304]{1,0:T(8,128)(2,1)}, u32[]{:S(2)}, u32[]{:S(2)}) collective-permute-start(bf16[512,2304]{1,0:T(8,128)(2,1)} %maximum_select_fusion.5), channel_id=1, source_target_pairs={{0,2},{2,0},{4,6},{6,4},{8,10},{10,8},{12,14},{14,12},{16,18},{18,... | collective-permute-start | bytes 7077896 | tf_op jit(solution)/shard_map/ppermute | solution.py:185
  636.2 94.0 %collective-permute-start.22 = (bf16[256,1024]{1,0:T(8,128)(2,1)}, bf16[256,1024]{1,0:T(8,128)(2,1)}, u32[]{:S(2)}, u32[]{:S(2)}) collective-permute-start(bf16[256,1024]{1,0:T(8,128)(2,1)} %maximum_select_fusion.18), channel_id=1, source_target_pairs={{0,2},{2,0},{4,6},{6,4},{8,10},{10,8},{12,14},{14,12},{16,18},{18,... | collective-permute-start | bytes 1572872 | tf_op jit(solution)/shard_map/ppermute | solution.py:185
  658.7 104.1 %collective-permute-start.46 = (bf16[1152,1024]{1,0:T(8,128)(2,1)}, bf16[1152,1024]{1,0:T(8,128)(2,1)}, u32[]{:S(2)}, u32[]{:S(2)}) collective-permute-start(bf16[1152,1024]{1,0:T(8,128)(2,1)} %maximum_select_fusion.6), channel_id=1, source_target_pairs={{0,2},{2,0},{4,6},{6,4},{8,10},{10,8},{12,14},{14,12},{16,18},{18,... | collective-permute-start | bytes 7077896 | tf_op jit(solution)/shard_map/ppermute | solution.py:185
  (55 other events, 710.5 us)

commit v2 on v1

v2 whole, which is shorter than its diff:
```python
import jax
import jax.numpy as jnp
from jax import lax
from jax.experimental import pallas as pl
from jax.experimental.pallas import tpu as pltpu
from jax.sharding import PartitionSpec as P

epsilon = 1e-05
f32 = jnp.float32
bf16 = jnp.bfloat16
halo = 8
spare = 8
big_vmem = pltpu.CompilerParams(vmem_limit_bytes=58 << 20)


def cost(flops, moved, transcendentals=0):
    return pl.CostEstimate(
        flops=int(flops), bytes_accessed=int(moved), transcendentals=int(transcendentals)
    )


def lag_rows(values, shift):
    return jnp.concatenate(
        [jnp.zeros((shift, values.shape[1]), values.dtype), values[:-shift]], axis=0
    )


def lead_rows(values, shift):
    return jnp.concatenate(
        [values[shift:], jnp.zeros((shift, values.shape[1]), values.dtype)], axis=0
    )


def seq_masks(lengths, positions, row_count):
    count = lengths.shape[0]
    before = jnp.arange(count)[:, None] < jnp.arange(count)[None, :]
    starts = jnp.sum(jnp.where(before, lengths[:, None], 0), axis=0, dtype=jnp.int32)
    started = positions[:, None] >= starts[None, :]
    seq_first = jnp.max(jnp.where(started, starts[None, :], 0), axis=1)
    offset = positions - seq_first
    inside = (positions >= 0) & (positions < row_count)
    return (
        ((offset >= 1) & inside).astype(f32)[:, None],
        ((offset >= 2) & inside).astype(f32)[:, None],
    )


def nt_dot(left, right):
    return lax.dot_general(
        left, right, (((1,), (1,)), ((), ())), preferred_element_type=f32
    )


def tn_dot(left, right):
    return lax.dot_general(
        left, right, (((0,), (0,)), ((), ())), preferred_element_type=f32
    )


def rank_kernel(rows, members, slots, route_ref, slot_ref):
    target = route_ref[...] // rows
    width = min(rows, 512)
    owner = lax.broadcasted_iota(jnp.int32, (members, rows), 0)
    one_hot = jnp.where(owner == target, 1.0, 0.0)
    left = one_hot.astype(bf16)
    for start in range(0, rows, width):
        first = lax.broadcasted_iota(jnp.int32, (rows, width), 0)
        second = lax.broadcasted_iota(jnp.int32, (rows, width), 1) + start
        earlier = jnp.where(first < second, 1.0, 0.0).astype(bf16)
        rank = jnp.dot(left, earlier, preferred_element_type=f32)
        piece = one_hot[:, start : start + width]
        mine = jnp.sum(rank * piece, axis=0, keepdims=True).astype(jnp.int32)
        slot_ref[:, start : start + width] = (
            target[:, start : start + width] * slots + mine
        )


def pack_kernel(rows, members, slots, route_ref, x_ref, sx_ref, digit_ref, slot_ref):
    step = pl.program_id(0)
    group = sx_ref.shape[0]

    @pl.when(step == 0)
    def _():
        rank_kernel(rows, members, slots, route_ref, slot_ref)

    place = route_ref[...] % rows
    row = lax.broadcasted_iota(jnp.int32, (8, rows), 0)
    digits = jnp.where(
        row == 0,
        (place // 64).astype(f32),
        jnp.where(row == 1, (place % 64).astype(f32), 1.0),
    ).astype(bf16)
    ids = lax.broadcasted_iota(jnp.int32, (group * slots, rows), 0)
    pick = jnp.where(slot_ref[...] == ids + step * group * slots, 1.0, 0.0).astype(bf16)
    sent = jnp.dot(pick, x_ref[...], preferred_element_type=f32).astype(bf16)
    for k in range(group):
        here = slice(k * slots, (k + 1) * slots)
        sx_ref[k, 0:slots] = sent[here]
        coded = nt_dot(digits, pick[here]).astype(bf16)
        if sx_ref.shape[1] > slots:
            sx_ref[k, slots : slots + spare] = jnp.zeros((spare, sx_ref.shape[2]), bf16)
            sx_ref[k, slots : slots + spare, 0:slots] = coded
        else:
            digit_ref[k] = jnp.zeros(digit_ref.shape[1:], bf16)
            digit_ref[k, :, 0:slots] = coded


def pack(route, tokens, members, slots):
    rows, width = tokens.shape
    group = min(members, 4)
    inside = slots <= width
    span = slots + spare if inside else slots
    whole = lambda j: (0, 0)
    block = lambda *tail: pl.BlockSpec((group, *tail), lambda j: (j, 0, 0))
    lanes = 8 if inside else 256
    return pl.pallas_call(
        lambda *refs: pack_kernel(rows, members, slots, *refs),
        grid=(members // group,),
        in_specs=[pl.BlockSpec((1, rows), whole), pl.BlockSpec((rows, width), whole)],
        out_specs=[block(span, width), block(8, lanes), pl.BlockSpec((1, rows), whole)],
        out_shape=[
            jax.ShapeDtypeStruct((members, span, width), bf16),
            jax.ShapeDtypeStruct((members, 8, lanes), bf16),
            jax.ShapeDtypeStruct((1, rows), jnp.int32),
        ],
        compiler_params=big_vmem,
        cost_estimate=cost(2 * members * slots * rows * width, 5 * rows * width),
        name="pack",
    )(route.reshape(1, rows), tokens)


def send_kernel(slots, slot_ref, x_ref, out_ref):
    group = out_ref.shape[0]
    count = group * slots
    ids = lax.broadcasted_iota(jnp.int32, (count, x_ref.shape[0]), 0)
    pick = jnp.where(slot_ref[...] == ids + pl.program_id(0) * count, 1.0, 0.0)
    sent = jnp.dot(pick.astype(bf16), x_ref[...], preferred_element_type=f32)
    for k in range(group):
        out_ref[k] = sent[k * slots : (k + 1) * slots].astype(bf16)


def send_rows(slot_of, source, members, slots):
    rows, width = source.shape
    group = min(members, 8)
    return pl.pallas_call(
        lambda *refs: send_kernel(slots, *refs),
        grid=(members // group,),
        in_specs=[
            pl.BlockSpec((1, rows), lambda j: (0, 0)),
            pl.BlockSpec((rows, width), lambda j: (0, 0)),
        ],
        out_specs=pl.BlockSpec((group, slots, width), lambda j: (j, 0, 0)),
        out_shape=jax.ShapeDtypeStruct((members, slots, width), bf16),
        compiler_params=big_vmem,
        cost_estimate=cost(2 * members * slots * rows * width, 5 * rows * width),
        name="send_rows",
    )(slot_of, source)


def place_kernel(rows, bases_ref, digit_ref, got_ref, out_ref, place_ref, src, pick):
    members, slots = got_ref.shape[0], got_ref.shape[1]
    count = out_ref.shape[0]
    span = src.shape[0] // members
    base = bases_ref[pl.program_id(0)]
    ids = lax.broadcasted_iota(jnp.int32, (count, span), 0) + base

    @pl.when(pl.program_id(0) == 0)
    def _():
        for j in range(members):
            src[j * span : j * span + slots] = got_ref[j]
            if span > slots:
                src[j * span + slots : (j + 1) * span] = jnp.zeros(
                    (span - slots, src.shape[1]), bf16
                )

    for j in range(members):
        coded = digit_ref[j].astype(f32)[:, 0:span]
        value = coded[0:1] * 64.0 + coded[1:2]
        places = jnp.where(coded[2:3] > 0.5, value, 4.0 * rows).astype(jnp.int32)
        pick[:, j * span : (j + 1) * span] = jnp.where(places == ids, 1.0, 0.0).astype(bf16)
        place_ref[j : j + 1, :] = places[:, 0:slots]
    out_ref[...] = jnp.dot(pick[...], src[...], preferred_element_type=f32).astype(bf16)


def place_rows(bases, digits, got, slots, rows, count):
    members, width = got.shape[0], got.shape[2]
    at = digits.shape[1] // 8 - 1
    span = -(-slots // 128) * 128
    return pl.pallas_call(
        lambda *refs: place_kernel(rows, *refs),
        grid_spec=pltpu.PrefetchScalarGridSpec(
            num_scalar_prefetch=1,
            grid=(bases.shape[0],),
            in_specs=[
                pl.BlockSpec((members, 8, digits.shape[2]), lambda i, b: (0, at, 0)),
                pl.BlockSpec((members, slots, width), lambda i, b: (0, 0, 0)),
            ],
            out_specs=[
                pl.BlockSpec((None, count, width), lambda i, b: (i, 0, 0)),
                pl.BlockSpec((members, slots), lambda i, b: (0, 0)),
            ],
            scratch_shapes=[
                pltpu.VMEM((members * span, width), bf16),
                pltpu.VMEM((count, members * span), bf16),
            ],
        ),
        out_shape=[
            jax.ShapeDtypeStruct((bases.shape[0], count, width), bf16),
            jax.ShapeDtypeStruct((members, slots), jnp.int32),
        ],
        compiler_params=big_vmem,
        cost_estimate=cost(0, (bases.shape[0] * count + members * slots) * width // 8),
        name="place_rows",
    )(bases, digits, got)


def take_kernel(ids_ref, from_ref, out_ref):
    cols = lax.broadcasted_iota(jnp.int32, (out_ref.shape[0], from_ref.shape[0]), 1)
    pick = jnp.where(ids_ref[...] == cols, 1.0, 0.0).astype(bf16)
    out_ref[...] = jnp.dot(pick, from_ref[...], preferred_element_type=f32).astype(
        out_ref.dtype
    )


def take_rows(ids, source, block, dtype):
    count = ids.shape[0]
    total, width = source.shape
    return pl.pallas_call(
        take_kernel,
        grid=(count // block,),
        in_specs=[
            pl.BlockSpec((block, 1), lambda i: (i, 0)),
            pl.BlockSpec((total, width), lambda i: (0, 0)),
        ],
        out_specs=pl.BlockSpec((block, width), lambda i: (i, 0)),
        out_shape=jax.ShapeDtypeStruct((count, width), dtype),
        compiler_params=big_vmem,
        cost_estimate=cost(2 * count * total * width, 2 * (count + total) * width),
        name="take_rows",
    )(ids, source)


def swap_mp(value):
    return lax.ppermute(value, "mp", [(0, 1), (1, 0)])


def side_by_side(mine, other, index):
    return jnp.where(
        index == 0,
        jnp.concatenate([mine, other], axis=1),
        jnp.concatenate([other, mine], axis=1),
    )


def rolled(full, shift):
    return jnp.roll(full, shift, axis=0)


def flip(value, bit):
    size = lax.axis_size("dp")
    return lax.ppermute(value, "dp", [(i, i ^ bit) for i in range(size)])


def dp_bits():
    return [1 << k for k in range(lax.axis_size("dp").bit_length() - 1)]


def halve(value, bit):
    half = value.shape[0] // 2
    side = (lax.axis_index("dp") // bit) % 2
    sent = lax.dynamic_slice_in_dim(value, (1 - side) * half, half, 0)
    kept = lax.dynamic_slice_in_dim(value, side * half, half, 0)
    return (kept.astype(f32) + flip(sent, bit).astype(f32)).astype(bf16)


def double(value, bit):
    side = (lax.axis_index("dp") // bit) % 2
    other = flip(value, bit)
    return jnp.where(
        side == 0,
        jnp.concatenate([value, other], axis=0),
        jnp.concatenate([other, value], axis=0),
    )


def sum_dp(value):
    bits = dp_bits()
    for bit in bits:
        value = halve(value, bit)
    for bit in reversed(bits):
        value = double(value, bit)
    return value


def after(value, *others):
    return lax.optimization_barrier((value, *others))[0]


class Ring:
    def __init__(self, parts):
        self.parts = parts
        self.nodes = nodes = lax.axis_size("dp") // 2
        chip = lax.axis_index("dp") // 2
        self.here = jnp.where(chip % 2 == 0, chip // 2, nodes - 1 - chip // 2)
        top = nodes // 2
        self.chips = [2 * p if p < top else 2 * (nodes - 1 - p) + 1 for p in range(nodes)]
        self.half = parts[0].shape[1] // 2
        self.held = {way: self.terms(self.here, way).astype(bf16) for way in (1, -1)}
        self.pieces = {1: [], -1: []}
        self.steps = 0

    def send(self, value, way):
        pairs = [
            (2 * self.chips[p] + c, 2 * self.chips[(p + way) % self.nodes] + c)
            for p in range(self.nodes)
            for c in range(2)
        ]
        return lax.ppermute(value, "dp", pairs)

    def terms(self, block, way):
        at = (block % self.nodes, 0 if way == 1 else self.half, 0)
        size = (1, self.half, self.parts[0].shape[2])
        pieces = [lax.dynamic_slice(v, at, size) for v in self.parts]
        return sum(piece.astype(f32) for piece in pieces)

    def step(self, *gates):
        count = self.steps
        if count == 2 * self.nodes - 2:
            return
        self.steps += 1
        adding = count < self.nodes - 1
        if gates:
            both = lax.optimization_barrier((self.held[1], self.held[-1], *gates))
            self.held = {1: both[0], -1: both[1]}
        for way in (1, -1):
            if count == self.nodes - 1:
                self.pieces[way].append(self.held[way])
            came = self.send(self.held[way], way)
            if adding:
                own = self.terms(self.here - way * (count + 1) + self.nodes, way)
                came = (came.astype(f32) + own).astype(bf16)
            else:
                self.pieces[way].append(came)
            self.held[way] = came

    def first(self, value):
        return after(value, *self.held.values())

    def total(self):
        return gather_pieces([p[0] for way in (1, -1) for p in self.pieces[way]])

    def order(self):
        block = jnp.arange(self.nodes, dtype=jnp.int32)
        up = (self.here + 1 - block + self.nodes) % self.nodes
        down = (block - self.here + 1 + self.nodes) % self.nodes + self.nodes
        core = lax.axis_index("dp")[None] % 2
        return jnp.concatenate([up, down, core]).astype(jnp.int32)


def gather_kernel(*refs):
    *sources, out_ref = refs
    for k, ref in enumerate(sources):
        out_ref[k] = ref[...]


def gather_pieces(pieces):
    count = len(pieces)
    vmem = pl.BlockSpec(memory_space=pltpu.VMEM)
    return pl.pallas_call(
        gather_kernel,
        in_specs=[vmem] * count,
        out_specs=vmem,
        out_shape=jax.ShapeDtypeStruct((count, *pieces[0].shape), bf16),
        compiler_params=big_vmem,
        cost_estimate=cost(0, 4 * count * pieces[0].size),
        name="gather_pieces",
    )(*pieces)


def core_parts(value):
    count = value.shape[0] // 2
    core = lax.axis_index("dp") % 2
    sent = lax.dynamic_slice_in_dim(value, (1 - core) * count, count, 0)
    kept = lax.dynamic_slice_in_dim(value, core * count, count, 0)
    return kept, flip(sent, 1)


def ff_kernel(sub, x_ref, g_ref, wg_ref, wu_ref, wd_ref, gx_ref, y_ref, h_ref, gg_ref, gu_ref):
    step = pl.program_id(0)
    for at in range(0, wg_ref.shape[1], sub):
        c = slice(at, at + sub)
        gate = jnp.dot(x_ref[...], wg_ref[:, c], preferred_element_type=f32)
        up = jnp.dot(x_ref[...], wu_ref[:, c], preferred_element_type=f32)
        grad = nt_dot(g_ref[...], wd_ref[c])
        sig = 1.0 / (1.0 + jnp.exp(-gate))
        silu = gate * sig
        h_ref[:, c] = (silu * up).astype(bf16)
        gg_ref[:, c] = (grad * up * (sig + silu * (1.0 - sig))).astype(bf16)
        gu_ref[:, c] = (grad * silu).astype(bf16)
    def back(first):
        w = 256
        for at in range(0, gx_ref.shape[1], w):
            c = slice(at, at + w)
            gx = nt_dot(gg_ref[...], wg_ref[c, :]) + nt_dot(gu_ref[...], wu_ref[c, :])
            y = jnp.dot(h_ref[...], wd_ref[:, c], preferred_element_type=f32)
            if first:
                gx_ref[:, c] = gx
                y_ref[:, c] = y
            else:
                gx_ref[:, c] += gx
                y_ref[:, c] += y
    pl.when(step == 0)(lambda: back(True))
    pl.when(step > 0)(lambda: back(False))

def feed_forward(x, g, wg, wu, wd, sub=384):
    r, d = x.shape
    hid = wg.shape[1]
    chunk = hid // 3
    whole = pl.BlockSpec((r, d), lambda i: (0, 0))
    tall = pl.BlockSpec((d, chunk), lambda i: (0, i))
    wide = pl.BlockSpec((r, chunk), lambda i: (0, i))
    return pl.pallas_call(
        lambda *refs: ff_kernel(sub, *refs),
        grid=(hid // chunk,),
        in_specs=[
            whole,
            whole,
            tall,
            tall,
            pl.BlockSpec((chunk, d), lambda i: (i, 0)),
        ],
        out_specs=[whole, whole, wide, wide, wide],
        out_shape=[jax.ShapeDtypeStruct((r, d), f32)] * 2 + [jax.ShapeDtypeStruct((r, hid), bf16)] * 3,
        compiler_params=big_vmem,
        cost_estimate=cost(24 * r * d * hid, 6 * (d + r) * hid + 12 * r * d, 2 * r * hid),
        name="feed_forward",
    )(x, g, wg, wu, wd)

def grads_kernel(x0, x1, gg0, gg1, gu0, gu1, h0, h1, g0, g1, out_ref, xt, ht):
    step = pl.program_id(0)
    nodes, count, lanes = out_ref.shape
    rows = x0.shape[1] // nodes
    deep = h0.shape[1] // nodes
    r = x0.shape[0]
    @pl.when(step == 0)
    def _():
        xt[:, :r] = x0[...].T
        xt[:, r:] = x1[...].T
    @pl.when(step == 5)
    def _():
        ht[:, :r] = h0[...].T
        ht[:, r:] = h1[...].T
    def put(c, d, at):
        v = jnp.dot(xt[:, :r], c[...], preferred_element_type=f32) + jnp.dot(xt[:, r:], d[...], preferred_element_type=f32)
        out_ref[:, pl.ds(pl.multiple_of(at, 64), rows)] = v.astype(bf16).reshape(nodes, rows, lanes)
    @pl.when(step < 3)
    def _(): put(gg0, gg1, step * rows)
    @pl.when((step >= 3) & (step < 6))
    def _(): put(gu0, gu1, step * rows)
    @pl.when(step == 6)
    def _():
        v = jnp.dot(ht[:, :r], g0[:, :lanes], preferred_element_type=f32) + jnp.dot(ht[:, r:], g1[:, :lanes], preferred_element_type=f32)
        out_ref[:, 6 * rows : 6 * rows + deep] = v.astype(bf16).reshape(nodes, deep, lanes)
        v = jnp.dot(ht[:, :r], g0[:, lanes:], preferred_element_type=f32) + jnp.dot(ht[:, r:], g1[:, lanes:], preferred_element_type=f32)
        v = v.astype(bf16).reshape(nodes, deep, v.shape[1])
        short, rest = deep // 3, v.shape[2]
        for k in range(3):
            out_ref[:, 6 * rows + deep :, k * rest : (k + 1) * rest] = v[:, k * short : (k + 1) * short]

def ff_grads(side, nodes, x0, x1, gg0, gg1, gu0, gu1, h0, h1, g0, g1):
    r, d = x0.shape
    hid = gg0.shape[1]
    lanes = hid // 3
    rows, deep = d // (2 * nodes), hid // (2 * nodes)
    count = 6 * rows + deep + deep // 3
    half = lambda n: pl.BlockSpec((r, n), lambda i, s: (0, s[0]))
    first = pl.BlockSpec((r, lanes), lambda i, s: (0, jnp.minimum(i, 2)))
    second = pl.BlockSpec((r, lanes), lambda i, s: (0, jnp.clip(i - 3, 0, 2)))
    whole = pl.BlockSpec((r, d), lambda i, s: (0, 0))
    return pl.pallas_call(
        lambda s, *refs: grads_kernel(*refs),
        grid_spec=pltpu.PrefetchScalarGridSpec(
            num_scalar_prefetch=1, grid=(7,),
            in_specs=[half(d // 2)] * 2 + [first] * 2 + [second] * 2 + [half(hid // 2)] * 2 + [whole] * 2,
            out_specs=pl.BlockSpec((nodes, count, lanes), lambda i, s: (0, 0, 0)),
            scratch_shapes=[pltpu.VMEM((d // 2, 2 * r), bf16), pltpu.VMEM((hid // 2, 2 * r), bf16)],
        ),
        out_shape=jax.ShapeDtypeStruct((nodes, count, lanes), bf16),
        compiler_params=big_vmem,
        cost_estimate=cost(12 * r * d * hid, 6 * r * hid + 5 * d * hid),
        name="ff_grads",
    )(side.astype(jnp.int32).reshape(1), x0, x1, gg0, gg1, gu0, gu1, h0, h1, g0, g1)


def open_specs(nodes, group, half, lanes):
    specs = []
    for _ in range(2):
        for b in range(group):
            for at in (0, nodes):
                specs.append(
                    pl.BlockSpec(
                        (None, half, lanes),
                        lambda j, h, order, b=b, at=at: (order[at + j * group + b], 0, 0),
                    )
                )
    return specs


def open_blocks(group, order_ref, refs, write):
    core = order_ref[order_ref.shape[0] - 1]
    half = refs[0].shape[0]

    def reader(first, second):
        def read(start, stop):
            if stop <= half:
                return first[start:stop].astype(f32)
            if start >= half:
                return second[start - half : stop - half].astype(f32)
            pieces = [first[start:half], second[0 : stop - half]]
            return jnp.concatenate([p.astype(f32) for p in pieces], axis=0)

        return read

    def hand(refs):
        for b in range(group):
            write(b, reader(refs[2 * b], refs[2 * b + 1]))

    own = pl.program_id(1) == core
    pl.when(own)(lambda: hand(refs[: 2 * group]))
    pl.when(jnp.logical_not(own))(lambda: hand(refs[2 * group :]))


def open_ff_kernel(group, order_ref, *refs):
    *pieces, gate_ref, up_ref, down_ref = refs
    lanes = pieces[0].shape[1]
    rows, deep = gate_ref.shape[0] // group, down_ref.shape[0] // group
    rest = down_ref.shape[1] - lanes
    short = deep // 3

    def write(b, read):
        here = slice(b * rows, (b + 1) * rows)
        for k, out in enumerate((gate_ref, up_ref)):
            for c in range(3):
                part = read((3 * k + c) * rows, (3 * k + c + 1) * rows)
                out[here, c * lanes : (c + 1) * lanes] = part
        low, at = b * deep, 6 * rows
        down_ref[low : low + deep, :lanes] = read(at, at + deep)
        for c in range(3):
            part = read(at + deep, at + deep + short)[:, c * rest : (c + 1) * rest]
            down_ref[low + c * short : low + (c + 1) * short, lanes:] = part

    open_blocks(group, order_ref, pieces, write)


def open_ff(ring, width, hidden):
    mine = ring.total()
    other = flip(mine, 1)
    _, half, lanes = mine.shape
    nodes, group = ring.nodes, 2
    steps = nodes // group
    rows, deep = width // (2 * nodes), hidden // (2 * nodes)
    out = lambda tall, wide: pl.BlockSpec(
        (group * tall, wide), lambda j, h, order: (h * steps + j, 0)
    )
    return pl.pallas_call(
        lambda *refs: open_ff_kernel(group, *refs),
        grid_spec=pltpu.PrefetchScalarGridSpec(
            num_scalar_prefetch=1,
            grid=(steps, 2),
            in_specs=open_specs(nodes, group, half, lanes),
            out_specs=[out(rows, hidden), out(rows, hidden), out(deep, width)],
        ),
        out_shape=[
            jax.ShapeDtypeStruct((width, hidden), f32),
            jax.ShapeDtypeStruct((width, hidden), f32),
            jax.ShapeDtypeStruct((hidden, width), f32),
        ],
        compiler_params=big_vmem,
        cost_estimate=cost(0, 24 * width * hidden),
        name="open_ff",
    )(ring.order(), *[mine] * (2 * group), *[other] * (2 * group))


def pack_conv_kernel(in_ref, out_w_ref, tail_ref, out_ref):
    blocks = out_ref.shape[0]
    rows = in_ref.shape[0] // (2 * blocks)
    deep = out_w_ref.shape[0] // blocks
    lanes = in_ref.shape[1]
    for k in range(blocks):
        out_ref[k, 0:rows, 0:lanes] = in_ref[2 * k * rows : (2 * k + 1) * rows]
        out_ref[k, 0:rows, lanes:] = in_ref[(2 * k + 1) * rows : (2 * k + 2) * rows]
        out_ref[k, rows : rows + deep] = out_w_ref[k * deep : (k + 1) * deep]
        out_ref[k, rows + deep :] = tail_ref[...]


def pack_conv(grad_in, grad_out, tail, blocks):
    total, lanes = grad_in.shape
    rows, deep, spared = total // blocks, grad_out.shape[0] // blocks, tail.shape[0]
    count = rows // 2 + deep + spared
    return pl.pallas_call(
        pack_conv_kernel,
        grid=(4,),
        in_specs=[
            pl.BlockSpec((total // 4, lanes), lambda i: (i, 0)),
            pl.BlockSpec((grad_out.shape[0] // 4, 2 * lanes), lambda i: (i, 0)),
            pl.BlockSpec((spared, 2 * lanes), lambda i: (0, 0)),
        ],
        out_specs=pl.BlockSpec((blocks // 4, count, 2 * lanes), lambda i: (i, 0, 0)),
        out_shape=jax.ShapeDtypeStruct((blocks, count, 2 * lanes), bf16),
        compiler_params=big_vmem,
        cost_estimate=cost(0, 4 * (grad_in.size + grad_out.size)),
        name="pack_conv",
    )(grad_in, grad_out, tail)


def open_conv_kernel(group, order_ref, *refs):
    *pieces, in_ref, out_w_ref, tail_ref = refs
    rows, lanes = in_ref.shape[0] // (2 * group), in_ref.shape[1]
    deep = out_w_ref.shape[0] // group

    def write(b, read):
        low = 2 * b * rows
        in_ref[low : low + rows] = read(0, rows)[:, :lanes]
        in_ref[low + rows : low + 2 * rows] = read(0, rows)[:, lanes:]
        out_w_ref[b * deep : (b + 1) * deep] = read(rows, rows + deep)
        tail_ref[b] = read(rows + deep, rows + deep + tail_ref.shape[1])

    open_blocks(group, order_ref, pieces, write)


def open_conv(ring, gate, total, deep_total):
    mine = after(ring.total(), gate)
    other = flip(mine, 1)
    _, half, width = mine.shape
    nodes, group = ring.nodes, ring.nodes // 2
    blocks = 2 * nodes
    steps = nodes // group
    rows, deep = total // blocks, deep_total // blocks
    spared = 2 * half - rows // 2 - deep
    at = lambda j, h, order: (h * steps + j, 0)
    return pl.pallas_call(
        lambda *refs: open_conv_kernel(group, *refs),
        grid_spec=pltpu.PrefetchScalarGridSpec(
            num_scalar_prefetch=1,
            grid=(steps, 2),
            in_specs=open_specs(nodes, group, half, width),
            out_specs=[
                pl.BlockSpec((group * rows, width // 2), at),
                pl.BlockSpec((group * deep, width), at),
                pl.BlockSpec(
                    (group, spared, width), lambda j, h, order: (h * steps + j, 0, 0)
                ),
            ],
        ),
        out_shape=[
            jax.ShapeDtypeStruct((total, width // 2), f32),
            jax.ShapeDtypeStruct((deep_total, width), f32),
            jax.ShapeDtypeStruct((blocks, spared, width), f32),
        ],
        compiler_params=big_vmem,
        cost_estimate=cost(0, 8 * (total + deep_total) * width),
        name="open_conv",
    )(ring.order(), *[mine] * (2 * group), *[other] * (2 * group))


def on_device(
    tokens,
    cotangent,
    route,
    seq_lengths,
    norm1_gain,
    in_weight,
    conv_weight,
    out_weight,
    norm2_gain,
    gate_weight,
    up_weight,
    down_weight,
):
    dp_size = lax.axis_size("dp")
    mp_size = lax.axis_size("mp")
    dp_index = lax.axis_index("dp")
    mp_index = lax.axis_index("mp")
    rows = tokens.shape[0]
    narrow = tokens.shape[1]
    width = norm1_gain.shape[0]
    own = rows // mp_size
    start = mp_index * own
    column = mp_index * narrow
    pair_share = rows // dp_size
    slots = pair_share + pair_share // 2
    paired = mp_size == 2

    if paired:
        core = dp_index % 2
        deep = width // 2
        part_in = lax.dynamic_slice_in_dim(in_weight, core * deep, deep, 1)
        part_out = lax.dynamic_slice_in_dim(out_weight, core * deep, deep, 1)
        part = jnp.concatenate([part_in, part_out.reshape(1, deep, deep)], axis=0)
        there = swap_mp(part)
        route = after(route, part)
        taps = jnp.concatenate([conv_weight, swap_mp(conv_weight)], axis=1)
    else:
        full_in = lax.all_gather(in_weight, "mp", axis=2, tiled=True)
        full_out = lax.all_gather(out_weight, "mp", axis=0, tiled=True)
        taps = lax.all_gather(conv_weight, "mp", axis=1, tiled=True)

    sent_rows, digits, slot_of = pack(route, tokens, dp_size, slots)
    sent_seeds = send_rows(after(slot_of, sent_rows), cotangent, dp_size, slots)
    over = dict(split_axis=0, concat_axis=0, tiled=True)
    got_rows = lax.all_to_all(sent_rows, "dp", **over)
    digits = got_rows if slots <= narrow else lax.all_to_all(digits, "dp", **over)
    got_rows, sent_seeds = lax.optimization_barrier((got_rows, sent_seeds))
    got_seeds = lax.all_to_all(sent_seeds, "dp", **over)
    slot_of = slot_of.reshape(rows, 1)
    window = own + 2 * halo
    if paired:
        bases = jnp.stack([start, own - start]).astype(jnp.int32)
        digits = got_rows if slots <= narrow else digits
        pieces, places = place_rows(bases - halo, digits, got_rows, slots, rows, window)
        there, _ = lax.optimization_barrier((there, pieces))
        here = flip(there, 1)
        both = [jnp.where(core == k, there, here) for k in range(2)]
        other_in = jnp.concatenate([v[:3] for v in both], axis=1)
        other_out = jnp.concatenate([v[3] for v in both], axis=1)
        full_in = jnp.concatenate([in_weight, other_in], axis=2)
        full_out = jnp.concatenate([out_weight, other_out], axis=0)
        input_rows = side_by_side(pieces[0], swap_mp(pieces[1]), mp_index)
        pieces, _ = place_rows(bases, digits, got_seeds, slots, rows, own)
        input_rows = after(input_rows, pieces)
        came = swap_mp(pieces[1])
        seeds_own = side_by_side(pieces[0], came, mp_index)
        seeds_other = side_by_side(pieces[1], swap_mp(after(pieces[0], came)), mp_index)
        place_ids = ((places - start) % rows).reshape(-1, 1)
    else:
        bases = (jnp.arange(mp_size) * own).astype(jnp.int32)
        pieces, places = place_rows(bases, digits, got_rows, slots, rows, own)
        full = lax.all_gather(pieces.reshape(rows, narrow), "mp", axis=1, tiled=True)
        full = jnp.pad(full, ((halo, halo), (0, 0)))
        input_rows = lax.dynamic_slice_in_dim(full, start, window, 0)
        pieces, _ = place_rows(bases, digits, got_seeds, slots, rows, own)
        full = lax.all_gather(pieces.reshape(rows, narrow), "mp", axis=1, tiled=True)
        seeds = rolled(full, -start)
        seeds_own, seeds_other = seeds[:own], seeds[own:]
        place_ids = places.reshape(-1, 1)

    positions = start - halo + jnp.arange(window, dtype=jnp.int32)
    first_mask, second_mask = seq_masks(seq_lengths[0], positions, rows)
    residual = input_rows.astype(f32)
    scale_one = lax.rsqrt(jnp.mean(residual * residual, axis=1) + epsilon)[:, None]
    normed_one = (residual * scale_one * norm1_gain).astype(bf16)
    projected = jnp.einsum("rd,kdc->krc", normed_one, full_in, preferred_element_type=f32)
    in_gate, out_gate, value_part = (projected[0], projected[1], projected[2])
    mixed = in_gate * value_part
    lag_one = lag_rows(mixed, 1) * first_mask
    lag_two = lag_rows(mixed, 2) * second_mask
    convolved = taps[2] * mixed + taps[1] * lag_one + taps[0] * lag_two
    gated = (out_gate * convolved).astype(bf16)
    gated = after(gated, seeds_own)
    middle = (residual + jnp.dot(gated, full_out, preferred_element_type=f32))[halo:]
    scale_two = lax.rsqrt(jnp.mean(middle * middle, axis=1) + epsilon)[:, None]
    normed_own = (middle[:own] * scale_two[:own] * norm2_gain).astype(bf16)

    weights = (gate_weight, up_weight, down_weight)
    if paired:
        normed_other = swap_mp(normed_own)
        first = feed_forward(normed_own, seeds_own, *weights)
        second = feed_forward(normed_other, seeds_other, *weights)
        sent = jnp.concatenate([second[0], first[0][:halo]], axis=0).astype(bf16)
        came = swap_mp(sent)
        saved = (normed_other, first[3], second[3], first[4], second[4])
        saved += (first[2], second[2], seeds_own, seeds_other)
        away = ff_grads(1 - core, dp_size // 2, after(normed_own, sent), *saved)
        kept = ff_grads(core, dp_size // 2, after(normed_own, away), *saved)
        away = flip(away, 1)
        came, _ = lax.optimization_barrier((came, kept))
        grad_normed_two = jnp.concatenate([first[0], second[0][:halo]], axis=0)
        grad_normed_two = grad_normed_two + came.astype(f32)
        down_came = swap_mp(after(second[1].astype(bf16), came))
        ring = Ring((kept, away))
        grad_normed_two = ring.first(grad_normed_two)
        ring.step()
    else:
        normed_two = rolled(lax.all_gather(normed_own, "mp", axis=0, tiled=True), -start)
        gate_val = jnp.dot(normed_two, gate_weight, preferred_element_type=f32)
        up_val = jnp.dot(normed_two, up_weight, preferred_element_type=f32)
        sigmoid_val = jax.nn.sigmoid(gate_val)
        silu_val = gate_val * sigmoid_val
        hidden = (silu_val * up_val).astype(bf16)
        grad_hidden = nt_dot(seeds, down_weight)
        grad_gate_val = (
            grad_hidden * up_val * sigmoid_val * (1.0 + gate_val * (1.0 - sigmoid_val))
        ).astype(bf16)
        grad_up_val = (grad_hidden * silu_val).astype(bf16)
        normed_terms = nt_dot(grad_gate_val, gate_weight) + nt_dot(grad_up_val, up_weight)
        down_terms = jnp.dot(hidden, down_weight, preferred_element_type=f32)
        full = rolled(lax.psum(rolled(normed_terms, start), "mp"), -start)
        grad_normed_two = full[: own + halo]
        down_sum = rolled(lax.psum(rolled(down_terms, start), "mp"), -start)[:own]
        total_gate = sum_dp(tn_dot(normed_two, grad_gate_val).astype(bf16)).astype(f32)
        total_up = sum_dp(tn_dot(normed_two, grad_up_val).astype(bf16)).astype(f32)
        total_down = sum_dp(tn_dot(hidden, seeds).astype(bf16)).astype(f32)

    gain_two_term = jnp.sum((grad_normed_two * middle * scale_two)[:own], axis=0)
    dot_two = jnp.sum(norm2_gain * grad_normed_two * middle, axis=1, keepdims=True)
    grad_middle = (
        jnp.concatenate([seeds_own, seeds_other[:halo]], axis=0).astype(f32)
        + scale_two * norm2_gain * grad_normed_two
        - middle * (scale_two * scale_two * scale_two * dot_two / width)
    )
    grad_mix = grad_middle.astype(bf16)
    grad_gated = jnp.einsum("rd,cd->rc", grad_mix, full_out, preferred_element_type=f32)
    if paired:
        grad_gated = ring.first(grad_gated)
        ring.step()
    grad_conv = grad_gated * out_gate[halo:]
    inner = slice(halo, halo + own)
    conv_terms = jnp.stack(
        [
            jnp.sum(grad_conv[:own] * lag_two[inner], axis=0),
            jnp.sum(grad_conv[:own] * lag_one[inner], axis=0),
            jnp.sum(grad_conv[:own] * mixed[inner], axis=0),
        ],
        axis=0,
    )
    grad_mixed = (
        taps[2] * grad_conv
        + taps[1] * lead_rows(grad_conv * first_mask[halo:], 1)
        + taps[0] * lead_rows(grad_conv * second_mask[halo:], 2)
    )[:own]
    grad_parts = jnp.stack(
        [
            grad_mixed * value_part[inner],
            grad_gated[:own] * convolved[inner],
            grad_mixed * in_gate[inner],
        ],
        axis=0,
    ).astype(bf16)
    parts_late = grad_parts
    if paired:
        grad_parts = ring.first(grad_parts)
        ring.step()
        ring.step()
        parts_late = ring.first(grad_parts)
    grad_normed_one = jnp.einsum("krc,kdc->rd", parts_late, full_in, preferred_element_type=f32)
    residual_own = residual[inner]
    scale_own = scale_one[inner]
    gain_one_term = jnp.sum(grad_normed_one * residual_own * scale_own, axis=0)
    dot_one = jnp.sum(norm1_gain * grad_normed_one * residual_own, axis=1, keepdims=True)
    input_own = (
        grad_middle[:own]
        + scale_own * norm1_gain * grad_normed_one
        - residual_own * (scale_own * scale_own * scale_own * dot_one / width)
    ).astype(bf16)

    grad_in = jnp.einsum(
        "rd,krc->kdc", normed_one[inner], grad_parts, preferred_element_type=f32
    ).astype(bf16)
    grad_out = jnp.einsum(
        "rc,rd->cd", gated[inner], grad_mix[:own], preferred_element_type=f32
    ).astype(bf16)
    if paired:
        down_sum = first[1] + after(down_came, grad_parts).astype(f32)
    block_own = (middle[:own] + down_sum).astype(bf16)
    gains = jnp.stack([gain_one_term, gain_two_term], axis=0)
    count = 2 + conv_weight.shape[0]

    def to_features(mine):
        if not paired:
            full = lax.all_gather(mine, "mp", axis=0, tiled=True)
            return lax.dynamic_slice_in_dim(full, column, narrow, 1)
        low, high = mine[:, :narrow], mine[:, narrow:]
        other = swap_mp(jnp.where(mp_index == 0, high, low))
        return jnp.concatenate([jnp.where(mp_index == 0, low, high), other], axis=0)

    shape = (dp_size, slots, narrow)
    back_block = min(8 * slots, slots * dp_size)
    home_block = min(rows, 512)

    def leave(piece):
        back = take_rows(place_ids, piece, back_block, bf16)
        return lax.all_to_all(back.reshape(shape), "dp", **over)

    def arrive(home, dtype):
        return take_rows(slot_of, home.reshape(-1, narrow), home_block, dtype)

    if paired:
        def packed_half(k, parts):
            lanes = slice(k * narrow, (k + 1) * narrow)
            terms = jnp.pad(conv_terms[:, lanes], ((0, 16 - count), (0, width - narrow)))
            ends = jnp.concatenate([gains, terms], axis=0).astype(bf16)
            lane_in = parts[:, :, lanes].reshape(-1, narrow)
            return core_parts(pack_conv(lane_in, grad_out[lanes], ends, dp_size))

        other = packed_half(1, grad_in)
        passed = (other[0].astype(f32) + other[1].astype(f32)).astype(bf16)
        gate_in = ring.first(after(grad_in, passed))
        passed = swap_mp(passed)
        block_piece = to_features(block_own)
        out_home = leave(block_piece)
        ring.step(block_piece)
        mine = packed_half(0, gate_in)
        input_piece = to_features(input_own)
        ring.step()
        ring.step(input_piece)
        grad_home = leave(after(input_piece, out_home))
        ring.step(out_home)
        ring.step(mine[1])
        ring.step()
        ring.step(grad_home)
        second = Ring((*mine, passed))
        while ring.steps < 2 * ring.nodes - 2:
            ring.step(*second.held.values())
            second.step()
        for _ in range(4):
            second.step()
        ring_done = open_ff(ring, width, gate_weight.shape[1])
        total_gate, total_up, total_down = ring_done
        while second.steps < 2 * second.nodes - 3:
            second.step()
        second.step(total_gate)
        total_in, total_out, ends = open_conv(
            second, total_gate, grad_in.size // (2 * narrow), narrow
        )
        tail = ends[0]
    else:
        out_home = leave(to_features(block_own))
        grad_home = leave(to_features(input_own))
        total_in = lax.psum_scatter(
            grad_in.astype(f32), "mp", scatter_dimension=2, tiled=True
        )
        total_in = sum_dp(total_in.astype(bf16).reshape(-1, narrow)).astype(f32)
        total_out = lax.psum_scatter(
            grad_out.astype(f32), "mp", scatter_dimension=0, tiled=True
        )
        total_out = sum_dp(total_out.astype(bf16)).astype(f32)
        gains = lax.psum(gains, ("dp", "mp"))
        terms = lax.psum_scatter(conv_terms, "mp", scatter_dimension=1, tiled=True)
        terms = jnp.pad(lax.psum(terms, "dp"), ((0, 0), (0, width - narrow)))
        tail = jnp.concatenate([gains, terms], axis=0)
    total_taps = tail[2:count, :narrow]
    block_out = arrive(out_home, bf16)
    tokens_grad = arrive(grad_home, f32)
    return (
        block_out,
        tokens_grad,
        tail[0],
        total_in.reshape(in_weight.shape),
        total_taps,
        total_out,
        tail[1],
        total_gate,
        total_up,
        total_down,
    )


def solution(mesh):
    in_specs = (
        P("dp", "mp"),
        P("dp", "mp"),
        P("dp"),
        P("dp", None),
        P(),
        P(None, None, "mp"),
        P(None, "mp"),
        P("mp", None),
        P(),
        P(None, "mp"),
        P(None, "mp"),
        P("mp", None),
    )
    out_specs = (
        P("dp", "mp"),
        P("dp", "mp"),
        P(),
        P(None, None, "mp"),
        P(None, "mp"),
        P("mp", None),
        P(),
        P(None, "mp"),
        P(None, "mp"),
        P("mp", None),
    )
    return jax.shard_map(
        on_device, mesh=mesh, in_specs=in_specs, out_specs=out_specs, check_vma=False
    )
```

time: 783 us -> 639 us (0.82); the launches traced: 771 us -> 635 us
  Pallas kernels: 54.4 us -> 172 us
  matrix products: 112 us -> 16.4 us
  waiting for transfers between devices: 309 us -> 219 us
  blocking collectives: 77.4 us -> 0 us
  starting transfers between devices: 71.1 us -> 113 us
  other arithmetic: 108 us -> 67.4 us
  local copies, waits for them, and re-layouts: 35.7 us -> 44.3 us
    ppermute x40 -> x6, waiting for transfers between devices: 211 us -> 0.02 us  [flip(): return lax.ppermute(value, 'dp', [(i, i ^ bit) for i in range(size)])]
    ppermute x0 -> x56, waiting for transfers between devices: none -> 151 us  [send(): return lax.ppermute(value, 'dp', pairs)]
    pallas_call x3 -> x14, Pallas kernels: 21 us -> 154 us  [the longest x2 50.2 us: feed_forward(): pl.pallas_call(lambda *refs: ff_kernel(sub, *refs), grid=(hid // chunk,),...]
    dot_general x15 -> x6, matrix products: 112 us -> 16.4 us  [the longest x1 4.96 us: on_device(): jnp.einsum('krc,kdc->rd', parts_late, full_in, preferred_element_type=f32)]
    ppermute x0 -> x56, starting transfers between devices: none -> 68.9 us  [send(): return lax.ppermute(value, 'dp', pairs)]
    psum x1 -> x0, blocking collectives: 59.5 us -> none  [on_device(): lax.psum(jnp.concatenate([gain_one_piece, grad_gain_two, grad_conv_weight...]
    ppermute x7 -> x11, waiting for transfers between devices: 67.3 us -> 27.9 us  [swap_mp(): return lax.ppermute(value, 'mp', [(0, 1), (1, 0)])]
    ppermute x40 -> x6, starting transfers between devices: 35.6 us -> 0.58 us  [flip(): return lax.ppermute(value, 'dp', [(i, i ^ bit) for i in range(size)])]
  transfers between devices with their start and end apart: 51 -> 77, of which waited for: 20 -> 46; matrix products, arithmetic and copies ran while one was open for 25% -> 14% of each run, Pallas kernels for 5% -> 15%
where the time goes in v2:
time: 639 us; the launch traced here: 635 us
  waiting for transfers between devices  219 us (34%)
  Pallas kernels  172 us (27%)
  starting transfers between devices  113 us (18%)
  other arithmetic  67.4 us (11%)
  local copies, waits for them, and re-layouts  44.3 us (7%)
  matrix products  16.4 us (3%)
    ppermute x56, waiting for transfers between devices, send(): return lax.ppermute(value, 'dp', pairs)  151 us
    ppermute x56, starting transfers between devices, send(): return lax.ppermute(value, 'dp', pairs)  68.9 us
    pallas_call x2, Pallas kernels, feed_forward(): pl.pallas_call(lambda *refs: ff_kernel(sub, *refs), grid=(hid // chunk,),...  50.2 us
    pallas_call x2, Pallas kernels, ff_grads(): pl.pallas_call(lambda s, *refs: grads_kernel(*refs), grid_spec=pltpu.Pref...  35.4 us
    all_to_all x1, waiting for transfers between devices, on_device(): got_rows = lax.all_to_all(sent_rows, 'dp', **over)  28.6 us
    ppermute x11, waiting for transfers between devices, swap_mp(): return lax.ppermute(value, 'mp', [(0, 1), (1, 0)])  27.9 us
    convert_element_type x14, other arithmetic, step(): came = (came.astype(f32) + own).astype(bf16)  24.5 us
    pallas_call x1, Pallas kernels, open_ff(): pl.pallas_call(lambda *refs: open_ff_kernel(group, *refs), grid_spec=pltp...  19.9 us
  transfers between devices with their start and end apart: 77, of which 46 were waited for; matrix products, arithmetic and copies ran while one was open for 14% of the time, Pallas kernels for 15%

profile of v2, /device:TPU:0, one launch (start us, length us, event | category | flops | bytes accessed | tf_op | source)
XLA Modules:
  0.0 634.8 jit_solution(9453817276762782016)
XLA Ops:
  4.8 5.4 pack.1
  10.2 7.4 %all-to-all-start = ((bf16[16,104,512]{2,1,0:T(8,128)(2,1)}), bf16[16,104,512]{2,1,0:T(8,128)(2,1)S(1)}, u32[]{:S(2)}, u32[]{:S(2)}) async-start(bf16[16,104,512]{2,1,0:T(8,128)(2,1)} %get-tuple-element.72), calls=%async_computation | async-start | bytes 3407872 | tf_op jit(solution)/shard_map/all_to_all | solution.py:711
  19.1 4.1 send_rows.1
  23.2 28.6 %all-to-all-done.refs_1_.refs_2_ = bf16[16,104,512]{2,1,0:T(8,128)(2,1)S(1)} async-done(((bf16[16,104,512]{2,1,0:T(8,128)(2,1)}), bf16[16,104,512]{2,1,0:T(8,128)(2,1)S(1)}, u32[]{:S(2)}, u32[]{:S(2)}) %all-to-all-start) | async-done | bytes 1703968 | tf_op jit(solution)/shard_map/all_to_all | solution.py:711
  51.8 10.2 %all-to-all-start.1 = ((bf16[16,96,512]{2,1,0:T(8,128)(2,1)}), bf16[16,96,512]{2,1,0:T(8,128)(2,1)}, u32[]{:S(2)}, u32[]{:S(2)}) async-start(bf16[16,96,512]{2,1,0:T(8,128)(2,1)} %send_rows.1), calls=%async_computation.1 | async-start | bytes 3145728 | tf_op jit(solution)/shard_map/all_to_all | solution.py:714
  62.7 5.8 place_rows.2
  72.6 13.3 %collective-permute-done = bf16[528,512]{1,0:T(8,128)(2,1)S(1)} collective-permute-done((bf16[528,512]{1,0:T(8,128)(2,1)S(1)}, bf16[528,512]{1,0:T(8,128)(2,1)S(1)}, u32[]{:S(2)}, u32[]{:S(2)}) %collective-permute-start) | collective-permute-done | bytes 540704 | tf_op jit(solution)/shard_map/ppermute | solution.py:244
  94.1 5.7 place_rows.3
  103.4 3.5 convolution_bitcast_fusion
  110.4 3.4 fusion.2
  122.7 25.1 %feed_forward.2 = (f32[512,1024]{1,0:T(8,128)}, f32[512,1024]{1,0:T(8,128)}, bf16[512,2304]{1,0:T(8,128)(2,1)}, bf16[512,2304]{1,0:T(8,128)(2,1)}, bf16[512,2304]{1,0:T(8,128)(2,1)}) custom-call(bf16[512,1024]{1,0:T(8,128)(2,1)} %copy-done.29, bf16[512,1024]{1,0:T(8,128)(2,1)} %maximum_select_fusion.1.refs_1_.refs_8_, bf16[1024,2304]{1,0:T(8,128)(2,1)} %refs_2_.3, ...), custom_call_target="tpu_custom_call" | custom-call | flops 28991029248 | bytes 27525120 | tf_op jit(solution)/shard_map/feed_forward/pallas_call | solution.py:422
  152.1 25.1 %feed_forward.3 = (f32[512,1024]{1,0:T(8,128)}, f32[512,1024]{1,0:T(8,128)}, bf16[512,2304]{1,0:T(8,128)(2,1)}, bf16[512,2304]{1,0:T(8,128)(2,1)}, bf16[512,2304]{1,0:T(8,128)(2,1)}) custom-call(bf16[512,1024]{1,0:T(8,128)(2,1)} %collective-permute-done.5.refs_0_.refs_1_, bf16[512,1024]{1,0:T(8,128)(2,1)} %maximum_select_fusion.2.refs_1_.refs_9_, ...), custom_call_target="tpu_custom_call" | custom-call | flops 28991029248 | bytes 27525120 | tf_op jit(solution)/shard_map/feed_forward/pallas_call | solution.py:422
  180.1 17.9 %ff_grads.2 = bf16[8,576,768]{2,1,0:T(8,128)(2,1)} custom-call(s32[1]{0:T(128)} %bitcast.22.s, bf16[512,1024]{1,0:T(8,128)(2,1)} %copy-done.29, bf16[512,1024]{1,0:T(8,128)(2,1)} %collective-permute-done.5.refs_0_.refs_1_, bf16[512,2304]{1,0:T(8,128)(2,1)} %get-tuple-element.88.refs_2_, bf16[512,2304]{1,0:T(8,128)(2,1)} %get-tuple-element.89.refs_3_, ...), custom_call_target="tpu_custom_call" | custom-call | flops 14495514624 | bytes 18874368 | tf_op jit(solution)/shard_map/ff_grads/pallas_call | solution.py:480
  204.3 17.5 %ff_grads.3 = bf16[8,576,768]{2,1,0:T(8,128)(2,1)} custom-call(s32[1]{0:T(128)} %bitcast.21.s, bf16[512,1024]{1,0:T(8,128)(2,1)} %copy-done.29, bf16[512,1024]{1,0:T(8,128)(2,1)} %collective-permute-done.5.refs_0_.refs_1_, bf16[512,2304]{1,0:T(8,128)(2,1)} %get-tuple-element.88.refs_2_, bf16[512,2304]{1,0:T(8,128)(2,1)} %get-tuple-element.89.refs_3_, ...), custom_call_target="tpu_custom_call" | custom-call | flops 14495514624 | bytes 18874368 | tf_op jit(solution)/shard_map/ff_grads/pallas_call | solution.py:480
  221.8 5.8 collective-permute-done.7
  267.9 5.3 collective-permute-done.17
  277.3 4.0 convert_bitcast_fusion
  289.7 5.0 fusion.24
  295.4 4.9 pack_conv.2
  300.3 3.3 constant_dynamic-slice_fusion.1
  303.6 4.3 take_rows.4
  307.8 4.5 all-to-all-start.2
  317.9 3.6 add_convert_fusion
  321.4 3.9 slice.268
  325.3 5.0 pack_conv.3
  335.7 8.8 %all-to-all-done.2 = bf16[16,96,512]{2,1,0:T(8,128)(2,1)} async-done(((bf16[16,96,512]{2,1,0:T(8,128)(2,1)}), bf16[16,96,512]{2,1,0:T(8,128)(2,1)}, u32[]{:S(2)}, u32[]{:S(2)}) %all-to-all-start.2) | async-done | bytes 1572896 | tf_op jit(solution)/shard_map/all_to_all | solution.py:882
  344.5 4.3 take_rows.6
  348.8 9.4 %all-to-all-start.3 = ((bf16[16,96,512]{2,1,0:T(8,128)(2,1)}), bf16[16,96,512]{2,1,0:T(8,128)(2,1)}, u32[]{:S(2)}, u32[]{:S(2)}) async-start(bf16[16,96,512]{2,1,0:T(8,128)(2,1)} %bitcast.156), calls=%async_computation.3 | async-start | bytes 3145728 | tf_op jit(solution)/shard_map/all_to_all | solution.py:882
  363.1 33.1 %collective-permute-done.52 = bf16[1,288,768]{2,1,0:T(8,128)(2,1)S(1)} collective-permute-done((bf16[1,288,768]{2,1,0:T(8,128)(2,1)}, bf16[1,288,768]{2,1,0:T(8,128)(2,1)S(1)}, u32[]{:S(2)}, u32[]{:S(2)}) %collective-permute-start.52) | collective-permute-done | bytes 442400 | tf_op jit(solution)/shard_map/ppermute | solution.py:318
  398.7 10.0 %collective-permute-start.53 = (bf16[1,288,768]{2,1,0:T(8,128)(2,1)}, bf16[1,288,768]{2,1,0:T(8,128)(2,1)S(1)}, u32[]{:S(2)}, u32[]{:S(2)}) collective-permute-start(bf16[1,288,768]{2,1,0:T(8,128)(2,1)} %get-tuple-element.107), channel_id=1, source_target_pairs={{0,8},{2,10},{8,16},{10,18},{16,24},{18,26},{24,28},{26,30},{28,20... | collective-permute-start | bytes 1327112 | tf_op jit(solution)/shard_map/ppermute | solution.py:318
  409.5 8.7 %collective-permute-done.53 = bf16[1,288,768]{2,1,0:T(8,128)(2,1)S(1)} collective-permute-done((bf16[1,288,768]{2,1,0:T(8,128)(2,1)}, bf16[1,288,768]{2,1,0:T(8,128)(2,1)S(1)}, u32[]{:S(2)}, u32[]{:S(2)}) %collective-permute-start.53) | collective-permute-done | bytes 442400 | tf_op jit(solution)/shard_map/ppermute | solution.py:318
  424.6 8.5 %collective-permute-done.55 = bf16[1,288,768]{2,1,0:T(8,128)(2,1)S(1)} collective-permute-done((bf16[1,288,768]{2,1,0:T(8,128)(2,1)S(1)}, bf16[1,288,768]{2,1,0:T(8,128)(2,1)S(1)}, u32[]{:S(2)}, u32[]{:S(2)}) %collective-permute-start.55) | collective-permute-done | bytes 442400 | tf_op jit(solution)/shard_map/ppermute | solution.py:318
  436.2 8.0 %collective-permute-done.57 = bf16[1,288,768]{2,1,0:T(8,128)(2,1)} collective-permute-done((bf16[1,288,768]{2,1,0:T(8,128)(2,1)S(1)}, bf16[1,288,768]{2,1,0:T(8,128)(2,1)}, u32[]{:S(2)}, u32[]{:S(2)}) %collective-permute-start.57) | collective-permute-done | bytes 442400 | tf_op jit(solution)/shard_map/ppermute | solution.py:318
  446.2 8.3 %collective-permute-done.58 = bf16[1,288,768]{2,1,0:T(8,128)(2,1)} collective-permute-done((bf16[1,288,768]{2,1,0:T(8,128)(2,1)}, bf16[1,288,768]{2,1,0:T(8,128)(2,1)}, u32[]{:S(2)}, u32[]{:S(2)}) %collective-permute-start.58) | collective-permute-done | bytes 442400 | tf_op jit(solution)/shard_map/ppermute | solution.py:318
  457.3 4.3 collective-permute-done.22
  468.8 9.3 %collective-permute-done.36 = bf16[1,72,1024]{2,1,0:T(8,128)(2,1)S(1)} collective-permute-done((bf16[1,72,1024]{2,1,0:T(8,128)(2,1)S(1)}, bf16[1,72,1024]{2,1,0:T(8,128)(2,1)S(1)}, u32[]{:S(2)}, u32[]{:S(2)}) %collective-permute-start.36) | collective-permute-done | bytes 147488 | tf_op jit(solution)/shard_map/ppermute | solution.py:318
  483.7 8.3 %collective-permute-done.37 = bf16[1,72,1024]{2,1,0:T(8,128)(2,1)S(1)} collective-permute-done((bf16[1,72,1024]{2,1,0:T(8,128)(2,1)S(1)}, bf16[1,72,1024]{2,1,0:T(8,128)(2,1)S(1)}, u32[]{:S(2)}, u32[]{:S(2)}) %collective-permute-start.37) | collective-permute-done | bytes 147488 | tf_op jit(solution)/shard_map/ppermute | solution.py:318
  495.6 6.3 collective-permute-done.67
  503.1 6.4 %gather_pieces.2.refs_1_.refs_2_.refs_3_.refs_4_ = bf16[16,288,768]{2,1,0:T(8,128)(2,1)} custom-call(bf16[288,768]{1,0:T(8,128)(2,1)} %bitcast.155, bf16[288,768]{1,0:T(8,128)(2,1)} %bitcast.160, bf16[288,768]{1,0:T(8,128)(2,1)} %bitcast.52.refs_2_, bf16[288,768]{1,0:T(8,128)(2,1)} %bitcast.53.refs_3_, bf16[288,768]{1,0:T(8,128)(2,1)} %bitcast.54.refs_4_, ...), custom_call_target="tpu_custom_call" | custom-call | bytes 14155776 | tf_op jit(solution)/shard_map/gather_pieces/pallas_call | solution.py:369
  511.7 4.2 collective-permute-done.38
  543.8 3.7 collective-permute-done.42
  553.8 4.6 collective-permute-done.43
  560.4 3.7 collective-permute-done.44
  582.3 19.9 %open_ff.1 = (f32[1024,2304]{1,0:T(8,128)}, f32[1024,2304]{1,0:T(8,128)}, f32[2304,1024]{1,0:T(8,128)}) custom-call(s32[17]{0:T(128)} %pad_add_fusion.1.refs_0_, bf16[16,288,768]{2,1,0:T(8,128)(2,1)} %gather_pieces.2.refs_1_.refs_2_.refs_3_.refs_4_, bf16[16,288,768]{2,1,0:T(8,128)(2,1)} %gather_pieces.2.refs_1_.refs_2_.refs_3_.refs_4_, ...), custom_call_target="tpu_custom_call" | custom-call | bytes 56623104 | tf_op jit(solution)/shard_map/open_ff/pallas_call | solution.py:565
  608.6 3.3 gather_pieces.3.refs_1_.refs_2_.refs_3_.refs_4_.refs_5_.refs_6_.refs_7_.refs_8_
  612.9 4.4 take_rows.5
  617.3 4.5 take_rows.7
  623.3 8.5 %open_conv.1 = (f32[3072,512]{1,0:T(8,128)}, f32[512,1024]{1,0:T(8,128)}, f32[16,16,1024]{2,1,0:T(8,128)}) custom-call(s32[17]{0:T(128)} %pad_add_fusion.1.refs_0_, bf16[16,72,1024]{2,1,0:T(8,128)(2,1)} %gather_pieces.3.refs_1_.refs_2_.refs_3_.refs_4_.refs_5_.refs_6_.refs_7_.refs_8_, ...), custom_call_target="tpu_custom_call" | custom-call | bytes 29360128 | tf_op jit(solution)/shard_map/open_conv/pallas_call | solution.py:641
  (373 shorter events, 219.7 us)
Async XLA Ops:
  10.2 41.7 %all-to-all-start = ((bf16[16,104,512]{2,1,0:T(8,128)(2,1)}), bf16[16,104,512]{2,1,0:T(8,128)(2,1)S(1)}, u32[]{:S(2)}, u32[]{:S(2)}) async-start(bf16[16,104,512]{2,1,0:T(8,128)(2,1)} %get-tuple-element.72), calls=%async_computation | async-start | bytes 3407872 | tf_op jit(solution)/shard_map/all_to_all | solution.py:711
  17.6 50.9 %collective-permute-start.1 = (bf16[4,512,512]{2,1,0:T(8,128)(2,1)}, bf16[4,512,512]{2,1,0:T(8,128)(2,1)}, u32[]{:S(2)}, u32[]{:S(2)}) collective-permute-start(bf16[4,512,512]{2,1,0:T(8,128)(2,1)} %pad_maximum_fusion.1), channel_id=1, source_target_pairs={{0,1},{1,0},{2,3},{3,2},{4,5},{5,4},{6,7},{7,6},{8,9},{9,8},{10,11... | collective-permute-start | bytes 6291464 | tf_op jit(solution)/shard_map/ppermute | solution.py:244
  51.8 42.2 %all-to-all-start.1 = ((bf16[16,96,512]{2,1,0:T(8,128)(2,1)}), bf16[16,96,512]{2,1,0:T(8,128)(2,1)}, u32[]{:S(2)}, u32[]{:S(2)}) async-start(bf16[16,96,512]{2,1,0:T(8,128)(2,1)} %send_rows.1), calls=%async_computation.1 | async-start | bytes 3145728 | tf_op jit(solution)/shard_map/all_to_all | solution.py:714
  68.4 17.8 %collective-permute-start.2 = (bf16[4,512,512]{2,1,0:T(8,128)(2,1)}, bf16[4,512,512]{2,1,0:T(8,128)(2,1)}, u32[]{:S(2)}, u32[]{:S(2)}) collective-permute-start(bf16[4,512,512]{2,1,0:T(8,128)(2,1)} %collective-permute-done.1), channel_id=1, source_target_pairs={{0,2},{2,0},{4,6},{6,4},{8,10},{10,8},{12,14},{14,12},{16,18},{18,... | collective-permute-start | bytes 6291464 | tf_op jit(solution)/shard_map/ppermute | solution.py:261
  71.9 14.0 %collective-permute-start = (bf16[528,512]{1,0:T(8,128)(2,1)S(1)}, bf16[528,512]{1,0:T(8,128)(2,1)S(1)}, u32[]{:S(2)}, u32[]{:S(2)}) collective-permute-start(bf16[528,512]{1,0:T(8,128)(2,1)S(1)} %get-tuple-element.186), channel_id=1, source_target_pairs={{0,1},{1,0},{2,3},{3,2},{4,5},{5,4},{6,7},{7,6},{8,9},{9,8},{10,11... | collective-permute-start | bytes 1622024 | tf_op jit(solution)/shard_map/ppermute | solution.py:244
  101.2 14.7 %collective-permute-start.4 = (bf16[512,512]{1,0:T(8,128)(2,1)S(1)}, bf16[512,512]{1,0:T(8,128)(2,1)S(1)}, u32[]{:S(2)}, u32[]{:S(2)}) collective-permute-start(bf16[512,512]{1,0:T(8,128)(2,1)S(1)} %get-tuple-element.194), channel_id=1, source_target_pairs={{0,1},{1,0},{2,3},{3,2},{4,5},{5,4},{6,7},{7,6},{8,9},{9,8},{10,11... | collective-permute-start | bytes 1572872 | tf_op jit(solution)/shard_map/ppermute | solution.py:244
  115.8 32.7 %collective-permute-start.6 = (bf16[512,512]{1,0:T(8,128)(2,1)S(1)}, bf16[512,512]{1,0:T(8,128)(2,1)S(1)}, u32[]{:S(2)}, u32[]{:S(2)}) collective-permute-start(bf16[512,512]{1,0:T(8,128)(2,1)S(1)} %get-tuple-element.83), channel_id=1, source_target_pairs={{0,1},{1,0},{2,3},{3,2},{4,5},{5,4},{6,7},{7,6},{8,9},{9,8},{10,11... | collective-permute-start | bytes 1572872 | tf_op jit(solution)/shard_map/ppermute | solution.py:244
  121.7 30.4 %collective-permute-start.5 = (bf16[512,1024]{1,0:T(8,128)(2,1)S(1)}, bf16[512,1024]{1,0:T(8,128)(2,1)}, u32[]{:S(2)}, u32[]{:S(2)}) collective-permute-start(bf16[512,1024]{1,0:T(8,128)(2,1)S(1)} %multiply_convert_fusion.1.refs_0_), channel_id=1, source_target_pairs={{0,1},{1,0},{2,3},{3,2},{4,5},{5,4},{6,7},{7,6},{8,9},{9,8},{10,11... | collective-permute-start | bytes 3145736 | tf_op jit(solution)/shard_map/ppermute | solution.py:244
  198.0 33.2 %collective-permute-start.9 = (bf16[8,576,768]{2,1,0:T(8,128)(2,1)}, bf16[8,576,768]{2,1,0:T(8,128)(2,1)}, u32[]{:S(2)}, u32[]{:S(2)}) collective-permute-start(bf16[8,576,768]{2,1,0:T(8,128)(2,1)} %ff_grads.2), channel_id=1, source_target_pairs={{0,2},{2,0},{4,6},{6,4},{8,10},{10,8},{12,14},{14,12},{16,18},{18,... | collective-permute-start | bytes 21233672 | tf_op jit(solution)/shard_map/ppermute | solution.py:261
  201.7 25.9 %collective-permute-start.7 = (bf16[520,1024]{1,0:T(8,128)(2,1)}, bf16[520,1024]{1,0:T(8,128)(2,1)S(1)}, u32[]{:S(2)}, u32[]{:S(2)}) collective-permute-start(bf16[520,1024]{1,0:T(8,128)(2,1)} %pad_maximum_fusion.2), channel_id=1, source_target_pairs={{0,1},{1,0},{2,3},{3,2},{4,5},{5,4},{6,7},{7,6},{8,9},{9,8},{10,11... | collective-permute-start | bytes 3194888 | tf_op jit(solution)/shard_map/ppermute | solution.py:244
  227.6 37.8 %collective-permute-start.8 = (bf16[512,1024]{1,0:T(8,128)(2,1)}, bf16[512,1024]{1,0:T(8,128)(2,1)}, u32[]{:S(2)}, u32[]{:S(2)}) collective-permute-start(bf16[512,1024]{1,0:T(8,128)(2,1)} %convert_element_type.498), channel_id=1, source_target_pairs={{0,1},{1,0},{2,3},{3,2},{4,5},{5,4},{6,7},{7,6},{8,9},{9,8},{10,11... | collective-permute-start | bytes 3145736 | tf_op jit(solution)/shard_map/ppermute | solution.py:244
  232.8 14.3 %collective-permute-start.11 = (bf16[1,288,768]{2,1,0:T(8,128)(2,1)S(1)}, bf16[1,288,768]{2,1,0:T(8,128)(2,1)S(1)}, u32[]{:S(2)}, u32[]{:S(2)}) collective-permute-start(bf16[1,288,768]{2,1,0:T(8,128)(2,1)S(1)} %get-tuple-element.159), channel_id=1, source_target_pairs={{0,4},{2,6},{8,0},{10,2},{16,8},{18,10},{24,16},{26,18},{28,24},{3... | collective-permute-start | bytes 1327112 | tf_op jit(solution)/shard_map/ppermute | solution.py:318
  235.5 13.1 %collective-permute-start.10 = (bf16[1,288,768]{2,1,0:T(8,128)(2,1)S(1)}, bf16[1,288,768]{2,1,0:T(8,128)(2,1)S(1)}, u32[]{:S(2)}, u32[]{:S(2)}) collective-permute-start(bf16[1,288,768]{2,1,0:T(8,128)(2,1)S(1)} %get-tuple-element.160), channel_id=1, source_target_pairs={{0,8},{2,10},{8,16},{10,18},{16,24},{18,26},{24,28},{26,30},{28,20... | collective-permute-start | bytes 1327112 | tf_op jit(solution)/shard_map/ppermute | solution.py:318
  250.1 10.5 %collective-permute-start.13 = (bf16[1,288,768]{2,1,0:T(8,128)(2,1)S(1)}, bf16[1,288,768]{2,1,0:T(8,128)(2,1)S(1)}, u32[]{:S(2)}, u32[]{:S(2)}) collective-permute-start(bf16[1,288,768]{2,1,0:T(8,128)(2,1)S(1)} %get-tuple-element.157), channel_id=1, source_target_pairs={{0,4},{2,6},{8,0},{10,2},{16,8},{18,10},{24,16},{26,18},{28,24},{3... | collective-permute-start | bytes 1327112 | tf_op jit(solution)/shard_map/ppermute | solution.py:318
  251.9 9.9 %collective-permute-start.12 = (bf16[1,288,768]{2,1,0:T(8,128)(2,1)S(1)}, bf16[1,288,768]{2,1,0:T(8,128)(2,1)S(1)}, u32[]{:S(2)}, u32[]{:S(2)}) collective-permute-start(bf16[1,288,768]{2,1,0:T(8,128)(2,1)S(1)} %get-tuple-element.158), channel_id=1, source_target_pairs={{0,8},{2,10},{8,16},{10,18},{16,24},{18,26},{24,28},{26,30},{28,20... | collective-permute-start | bytes 1327112 | tf_op jit(solution)/shard_map/ppermute | solution.py:318
  263.3 9.9 %collective-permute-start.17 = (bf16[1,288,768]{2,1,0:T(8,128)(2,1)S(1)}, bf16[1,288,768]{2,1,0:T(8,128)(2,1)S(1)}, u32[]{:S(2)}, u32[]{:S(2)}) collective-permute-start(bf16[1,288,768]{2,1,0:T(8,128)(2,1)S(1)} %get-tuple-element.155), channel_id=1, source_target_pairs={{0,4},{2,6},{8,0},{10,2},{16,8},{18,10},{24,16},{26,18},{28,24},{3... | collective-permute-start | bytes 1327112 | tf_op jit(solution)/shard_map/ppermute | solution.py:318
  267.3 18.7 %collective-permute-start.14 = (bf16[512,512]{1,0:T(8,128)(2,1)S(1)}, bf16[512,512]{1,0:T(8,128)(2,1)S(1)}, u32[]{:S(2)}, u32[]{:S(2)}) collective-permute-start(bf16[512,512]{1,0:T(8,128)(2,1)S(1)} %get-tuple-element.192), channel_id=1, source_target_pairs={{0,1},{1,0},{2,3},{3,2},{4,5},{5,4},{6,7},{7,6},{8,9},{9,8},{10,11... | collective-permute-start | bytes 1572872 | tf_op jit(solution)/shard_map/ppermute | solution.py:244
  275.1 12.0 %collective-permute-start.18 = (bf16[1,288,768]{2,1,0:T(8,128)(2,1)S(1)}, bf16[1,288,768]{2,1,0:T(8,128)(2,1)S(1)}, u32[]{:S(2)}, u32[]{:S(2)}) collective-permute-start(bf16[1,288,768]{2,1,0:T(8,128)(2,1)S(1)} %get-tuple-element.153), channel_id=1, source_target_pairs={{0,4},{2,6},{8,0},{10,2},{16,8},{18,10},{24,16},{26,18},{28,24},{3... | collective-permute-start | bytes 1327112 | tf_op jit(solution)/shard_map/ppermute | solution.py:318
  276.5 10.7 %collective-permute-start.16 = (bf16[1,288,768]{2,1,0:T(8,128)(2,1)S(1)}, bf16[1,288,768]{2,1,0:T(8,128)(2,1)S(1)}, u32[]{:S(2)}, u32[]{:S(2)}) collective-permute-start(bf16[1,288,768]{2,1,0:T(8,128)(2,1)S(1)} %get-tuple-element.154), channel_id=1, source_target_pairs={{0,8},{2,10},{8,16},{10,18},{16,24},{18,26},{24,28},{26,30},{28,20... | collective-permute-start | bytes 1327112 | tf_op jit(solution)/shard_map/ppermute | solution.py:318
  303.6 14.3 %collective-permute-start.20 = (bf16[8,144,1024]{2,1,0:T(8,128)(2,1)}, bf16[8,144,1024]{2,1,0:T(8,128)(2,1)}, u32[]{:S(2)}, u32[]{:S(2)}) collective-permute-start(bf16[8,144,1024]{2,1,0:T(8,128)(2,1)} %constant_dynamic-slice_fusion.1), channel_id=1, source_target_pairs={{0,2},{2,0},{4,6},{6,4},{8,10},{10,8},{12,14},{14,12},{16,18},{18,... | collective-permute-start | bytes 7077896 | tf_op jit(solution)/shard_map/ppermute | solution.py:261
  307.8 36.6 %all-to-all-start.2 = ((bf16[16,96,512]{2,1,0:T(8,128)(2,1)}), bf16[16,96,512]{2,1,0:T(8,128)(2,1)}, u32[]{:S(2)}, u32[]{:S(2)}) async-start(bf16[16,96,512]{2,1,0:T(8,128)(2,1)} %bitcast.157), calls=%async_computation.2 | async-start | bytes 3145728 | tf_op jit(solution)/shard_map/all_to_all | solution.py:882
  315.2 18.4 %collective-permute-start.19 = (bf16[512,512]{1,0:T(8,128)(2,1)S(1)}, bf16[512,512]{1,0:T(8,128)(2,1)}, u32[]{:S(2)}, u32[]{:S(2)}) collective-permute-start(bf16[512,512]{1,0:T(8,128)(2,1)S(1)} %get-tuple-element.190), channel_id=1, source_target_pairs={{0,1},{1,0},{2,3},{3,2},{4,5},{5,4},{6,7},{7,6},{8,9},{9,8},{10,11... | collective-permute-start | bytes 1572872 | tf_op jit(solution)/shard_map/ppermute | solution.py:244
  315.8 42.4 %collective-permute-start.49 = (bf16[1,288,768]{2,1,0:T(8,128)(2,1)}, bf16[1,288,768]{2,1,0:T(8,128)(2,1)}, u32[]{:S(2)}, u32[]{:S(2)}) collective-permute-start(bf16[1,288,768]{2,1,0:T(8,128)(2,1)} %get-tuple-element.105), channel_id=1, source_target_pairs={{0,8},{2,10},{8,16},{10,18},{16,24},{18,26},{24,28},{26,30},{28,20... | collective-permute-start | bytes 1327112 | tf_op jit(solution)/shard_map/ppermute | solution.py:318
  317.6 40.6 %collective-permute-start.51 = (bf16[1,288,768]{2,1,0:T(8,128)(2,1)}, bf16[1,288,768]{2,1,0:T(8,128)(2,1)}, u32[]{:S(2)}, u32[]{:S(2)}) collective-permute-start(bf16[1,288,768]{2,1,0:T(8,128)(2,1)} %get-tuple-element.106), channel_id=1, source_target_pairs={{0,4},{2,6},{8,0},{10,2},{16,8},{18,10},{24,16},{26,18},{28,24},{3... | collective-permute-start | bytes 1327112 | tf_op jit(solution)/shard_map/ppermute | solution.py:318
  333.6 100.5 %collective-permute-start.21 = (bf16[8,144,1024]{2,1,0:T(8,128)(2,1)}, bf16[8,144,1024]{2,1,0:T(8,128)(2,1)}, u32[]{:S(2)}, u32[]{:S(2)}) collective-permute-start(bf16[8,144,1024]{2,1,0:T(8,128)(2,1)} %constant_dynamic-slice_fusion), channel_id=1, source_target_pairs={{0,2},{2,0},{4,6},{6,4},{8,10},{10,8},{12,14},{14,12},{16,18},{18,... | collective-permute-start | bytes 7077896 | tf_op jit(solution)/shard_map/ppermute | solution.py:261
  348.8 97.5 %all-to-all-start.3 = ((bf16[16,96,512]{2,1,0:T(8,128)(2,1)}), bf16[16,96,512]{2,1,0:T(8,128)(2,1)}, u32[]{:S(2)}, u32[]{:S(2)}) async-start(bf16[16,96,512]{2,1,0:T(8,128)(2,1)} %bitcast.156), calls=%async_computation.3 | async-start | bytes 3145728 | tf_op jit(solution)/shard_map/all_to_all | solution.py:882
  361.0 35.1 %collective-permute-start.52 = (bf16[1,288,768]{2,1,0:T(8,128)(2,1)}, bf16[1,288,768]{2,1,0:T(8,128)(2,1)S(1)}, u32[]{:S(2)}, u32[]{:S(2)}) collective-permute-start(bf16[1,288,768]{2,1,0:T(8,128)(2,1)} %get-tuple-element.149), channel_id=1, source_target_pairs={{0,4},{2,6},{8,0},{10,2},{16,8},{18,10},{24,16},{26,18},{28,24},{3... | collective-permute-start | bytes 1327112 | tf_op jit(solution)/shard_map/ppermute | solution.py:318
  362.9 33.2 %collective-permute-start.50 = (bf16[1,288,768]{2,1,0:T(8,128)(2,1)S(1)}, bf16[1,288,768]{2,1,0:T(8,128)(2,1)}, u32[]{:S(2)}, u32[]{:S(2)}) collective-permute-start(bf16[1,288,768]{2,1,0:T(8,128)(2,1)S(1)} %get-tuple-element.150), channel_id=1, source_target_pairs={{0,8},{2,10},{8,16},{10,18},{16,24},{18,26},{24,28},{26,30},{28,20... | collective-permute-start | bytes 1327112 | tf_op jit(solution)/shard_map/ppermute | solution.py:318
  398.7 19.5 %collective-permute-start.53 = (bf16[1,288,768]{2,1,0:T(8,128)(2,1)}, bf16[1,288,768]{2,1,0:T(8,128)(2,1)S(1)}, u32[]{:S(2)}, u32[]{:S(2)}) collective-permute-start(bf16[1,288,768]{2,1,0:T(8,128)(2,1)} %get-tuple-element.107), channel_id=1, source_target_pairs={{0,8},{2,10},{8,16},{10,18},{16,24},{18,26},{24,28},{26,30},{28,20... | collective-permute-start | bytes 1327112 | tf_op jit(solution)/shard_map/ppermute | solution.py:318
  408.7 11.7 %collective-permute-start.54 = (bf16[1,288,768]{2,1,0:T(8,128)(2,1)S(1)}, bf16[1,288,768]{2,1,0:T(8,128)(2,1)}, u32[]{:S(2)}, u32[]{:S(2)}) collective-permute-start(bf16[1,288,768]{2,1,0:T(8,128)(2,1)S(1)} %get-tuple-element.108), channel_id=1, source_target_pairs={{0,4},{2,6},{8,0},{10,2},{16,8},{18,10},{24,16},{26,18},{28,24},{3... | collective-permute-start | bytes 1327112 | tf_op jit(solution)/shard_map/ppermute | solution.py:318
  408.9 52.7 %collective-permute-start.22 = (bf16[8,144,1024]{2,1,0:T(8,128)(2,1)S(1)}, bf16[8,144,1024]{2,1,0:T(8,128)(2,1)}, u32[]{:S(2)}, u32[]{:S(2)}) collective-permute-start(bf16[8,144,1024]{2,1,0:T(8,128)(2,1)S(1)} %add_convert_fusion), channel_id=1, source_target_pairs={{0,1},{1,0},{2,3},{3,2},{4,5},{5,4},{6,7},{7,6},{8,9},{9,8},{10,11... | collective-permute-start | bytes 7077896 | tf_op jit(solution)/shard_map/ppermute | solution.py:244
  422.5 10.6 %collective-permute-start.55 = (bf16[1,288,768]{2,1,0:T(8,128)(2,1)S(1)}, bf16[1,288,768]{2,1,0:T(8,128)(2,1)S(1)}, u32[]{:S(2)}, u32[]{:S(2)}) collective-permute-start(bf16[1,288,768]{2,1,0:T(8,128)(2,1)S(1)} %get-tuple-element.109), channel_id=1, source_target_pairs={{0,8},{2,10},{8,16},{10,18},{16,24},{18,26},{24,28},{26,30},{28,20... | collective-permute-start | bytes 1327112 | tf_op jit(solution)/shard_map/ppermute | solution.py:318
  423.5 10.6 %collective-permute-start.56 = (bf16[1,288,768]{2,1,0:T(8,128)(2,1)S(1)}, bf16[1,288,768]{2,1,0:T(8,128)(2,1)S(1)}, u32[]{:S(2)}, u32[]{:S(2)}) collective-permute-start(bf16[1,288,768]{2,1,0:T(8,128)(2,1)S(1)} %get-tuple-element.110), channel_id=1, source_target_pairs={{0,4},{2,6},{8,0},{10,2},{16,8},{18,10},{24,16},{26,18},{28,24},{3... | collective-permute-start | bytes 1327112 | tf_op jit(solution)/shard_map/ppermute | solution.py:318
  434.1 10.0 %collective-permute-start.57 = (bf16[1,288,768]{2,1,0:T(8,128)(2,1)S(1)}, bf16[1,288,768]{2,1,0:T(8,128)(2,1)}, u32[]{:S(2)}, u32[]{:S(2)}) collective-permute-start(bf16[1,288,768]{2,1,0:T(8,128)(2,1)S(1)} %collective-permute-done.55), channel_id=1, source_target_pairs={{0,8},{2,10},{8,16},{10,18},{16,24},{18,26},{24,28},{26,30},{28,20... | collective-permute-start | bytes 1327112 | tf_op jit(solution)/shard_map/ppermute | solution.py:318
  435.2 10.2 %collective-permute-start.59 = (bf16[1,288,768]{2,1,0:T(8,128)(2,1)S(1)}, bf16[1,288,768]{2,1,0:T(8,128)(2,1)}, u32[]{:S(2)}, u32[]{:S(2)}) collective-permute-start(bf16[1,288,768]{2,1,0:T(8,128)(2,1)S(1)} %collective-permute-done.56), channel_id=1, source_target_pairs={{0,4},{2,6},{8,0},{10,2},{16,8},{18,10},{24,16},{26,18},{28,24},{3... | collective-permute-start | bytes 1327112 | tf_op jit(solution)/shard_map/ppermute | solution.py:318
  444.2 10.3 %collective-permute-start.58 = (bf16[1,288,768]{2,1,0:T(8,128)(2,1)}, bf16[1,288,768]{2,1,0:T(8,128)(2,1)}, u32[]{:S(2)}, u32[]{:S(2)}) collective-permute-start(bf16[1,288,768]{2,1,0:T(8,128)(2,1)} %collective-permute-done.57), channel_id=1, source_target_pairs={{0,8},{2,10},{8,16},{10,18},{16,24},{18,26},{24,28},{26,30},{28,20... | collective-permute-start | bytes 1327112 | tf_op jit(solution)/shard_map/ppermute | solution.py:318
  445.4 9.9 %collective-permute-start.60 = (bf16[1,288,768]{2,1,0:T(8,128)(2,1)}, bf16[1,288,768]{2,1,0:T(8,128)(2,1)}, u32[]{:S(2)}, u32[]{:S(2)}) collective-permute-start(bf16[1,288,768]{2,1,0:T(8,128)(2,1)} %collective-permute-done.59), channel_id=1, source_target_pairs={{0,4},{2,6},{8,0},{10,2},{16,8},{18,10},{24,16},{26,18},{28,24},{3... | collective-permute-start | bytes 1327112 | tf_op jit(solution)/shard_map/ppermute | solution.py:318
  464.8 14.8 %collective-permute-start.63 = (bf16[1,288,768]{2,1,0:T(8,128)(2,1)}, bf16[1,288,768]{2,1,0:T(8,128)(2,1)S(1)}, u32[]{:S(2)}, u32[]{:S(2)}) collective-permute-start(bf16[1,288,768]{2,1,0:T(8,128)(2,1)} %collective-permute-done.61), channel_id=1, source_target_pairs={{0,8},{2,10},{8,16},{10,18},{16,24},{18,26},{24,28},{26,30},{28,20... | collective-permute-start | bytes 1327112 | tf_op jit(solution)/shard_map/ppermute | solution.py:318
  465.0 14.5 %collective-permute-start.64 = (bf16[1,288,768]{2,1,0:T(8,128)(2,1)}, bf16[1,288,768]{2,1,0:T(8,128)(2,1)S(1)}, u32[]{:S(2)}, u32[]{:S(2)}) collective-permute-start(bf16[1,288,768]{2,1,0:T(8,128)(2,1)} %collective-permute-done.62), channel_id=1, source_target_pairs={{0,4},{2,6},{8,0},{10,2},{16,8},{18,10},{24,16},{26,18},{28,24},{3... | collective-permute-start | bytes 1327112 | tf_op jit(solution)/shard_map/ppermute | solution.py:318
  466.8 11.3 %collective-permute-start.36 = (bf16[1,72,1024]{2,1,0:T(8,128)(2,1)S(1)}, bf16[1,72,1024]{2,1,0:T(8,128)(2,1)S(1)}, u32[]{:S(2)}, u32[]{:S(2)}) collective-permute-start(bf16[1,72,1024]{2,1,0:T(8,128)(2,1)S(1)} %get-tuple-element.175), channel_id=1, source_target_pairs={{0,4},{2,6},{8,0},{10,2},{16,8},{18,10},{24,16},{26,18},{28,24},{3... | collective-permute-start | bytes 442376 | tf_op jit(solution)/shard_map/ppermute | solution.py:318
  468.0 10.1 %collective-permute-start.23 = (bf16[1,72,1024]{2,1,0:T(8,128)(2,1)S(1)}, bf16[1,72,1024]{2,1,0:T(8,128)(2,1)S(1)}, u32[]{:S(2)}, u32[]{:S(2)}) collective-permute-start(bf16[1,72,1024]{2,1,0:T(8,128)(2,1)S(1)} %get-tuple-element.176), channel_id=1, source_target_pairs={{0,8},{2,10},{8,16},{10,18},{16,24},{18,26},{24,28},{26,30},{28,20... | collective-permute-start | bytes 442376 | tf_op jit(solution)/shard_map/ppermute | solution.py:318
  479.6 13.9 %collective-permute-start.65 = (bf16[1,288,768]{2,1,0:T(8,128)(2,1)S(1)}, bf16[1,288,768]{2,1,0:T(8,128)(2,1)S(1)}, u32[]{:S(2)}, u32[]{:S(2)}) collective-permute-start(bf16[1,288,768]{2,1,0:T(8,128)(2,1)S(1)} %collective-permute-done.63), channel_id=1, source_target_pairs={{0,8},{2,10},{8,16},{10,18},{16,24},{18,26},{24,28},{26,30},{28,20... | collective-permute-start | bytes 1327112 | tf_op jit(solution)/shard_map/ppermute | solution.py:318
  480.3 13.1 %collective-permute-start.66 = (bf16[1,288,768]{2,1,0:T(8,128)(2,1)S(1)}, bf16[1,288,768]{2,1,0:T(8,128)(2,1)S(1)}, u32[]{:S(2)}, u32[]{:S(2)}) collective-permute-start(bf16[1,288,768]{2,1,0:T(8,128)(2,1)S(1)} %collective-permute-done.64), channel_id=1, source_target_pairs={{0,4},{2,6},{8,0},{10,2},{16,8},{18,10},{24,16},{26,18},{28,24},{3... | collective-permute-start | bytes 1327112 | tf_op jit(solution)/shard_map/ppermute | solution.py:318
  481.6 10.3 %collective-permute-start.37 = (bf16[1,72,1024]{2,1,0:T(8,128)(2,1)S(1)}, bf16[1,72,1024]{2,1,0:T(8,128)(2,1)S(1)}, u32[]{:S(2)}, u32[]{:S(2)}) collective-permute-start(bf16[1,72,1024]{2,1,0:T(8,128)(2,1)S(1)} %get-tuple-element.173), channel_id=1, source_target_pairs={{0,4},{2,6},{8,0},{10,2},{16,8},{18,10},{24,16},{26,18},{28,24},{3... | collective-permute-start | bytes 442376 | tf_op jit(solution)/shard_map/ppermute | solution.py:318
  509.6 72.7 %collective-permute-start.69 = (bf16[16,288,768]{2,1,0:T(8,128)(2,1)}, bf16[16,288,768]{2,1,0:T(8,128)(2,1)}, u32[]{:S(2)}, u32[]{:S(2)}) collective-permute-start(bf16[16,288,768]{2,1,0:T(8,128)(2,1)} %gather_pieces.2.refs_1_.refs_2_.refs_3_.refs_4_), channel_id=1, source_target_pairs={{0,2},{2,0},{4,6},{6,4},{8,10},{10,8},{12,14},{14,12},{16,18},{18,... | collective-permute-start | bytes 21233672 | tf_op jit(solution)/shard_map/ppermute | solution.py:261
  579.6 22.7 %collective-permute-start.48 = (bf16[1,72,1024]{2,1,0:T(8,128)(2,1)S(1)}, bf16[1,72,1024]{2,1,0:T(8,128)(2,1)S(1)}, u32[]{:S(2)}, u32[]{:S(2)}) collective-permute-start(bf16[1,72,1024]{2,1,0:T(8,128)(2,1)S(1)} %collective-permute-done.47), channel_id=1, source_target_pairs={{0,4},{2,6},{8,0},{10,2},{16,8},{18,10},{24,16},{26,18},{28,24},{3... | collective-permute-start | bytes 442376 | tf_op jit(solution)/shard_map/ppermute | solution.py:318
  579.9 22.4 %collective-permute-start.35 = (bf16[1,72,1024]{2,1,0:T(8,128)(2,1)S(1)}, bf16[1,72,1024]{2,1,0:T(8,128)(2,1)S(1)}, u32[]{:S(2)}, u32[]{:S(2)}) collective-permute-start(bf16[1,72,1024]{2,1,0:T(8,128)(2,1)S(1)} %collective-permute-done.34), channel_id=1, source_target_pairs={{0,8},{2,10},{8,16},{10,18},{16,24},{18,26},{24,28},{26,30},{28,20... | collective-permute-start | bytes 442376 | tf_op jit(solution)/shard_map/ppermute | solution.py:318
  611.9 9.9 %collective-permute-start.72 = (bf16[16,72,1024]{2,1,0:T(8,128)(2,1)}, bf16[16,72,1024]{2,1,0:T(8,128)(2,1)S(1)}, u32[]{:S(2)}, u32[]{:S(2)}) collective-permute-start(bf16[16,72,1024]{2,1,0:T(8,128)(2,1)} %gather_pieces.3.refs_1_.refs_2_.refs_3_.refs_4_.refs_5_.refs_6_.refs_7_.refs_8_), channel_id=1, source_target_pairs={{0,2},{2,0},{4,6},{6,4},{8,10},{10,8},{12,14},{14,12},{16,18},{18,... | collective-permute-start | bytes 7077896 | tf_op jit(solution)/shard_map/ppermute | solution.py:261
  (102 other events, 1186.9 us)

commit v3 on v2

--- a/solution.py
+++ b/solution.py
@@ -377,14 +377,6 @@
     )(*pieces)
 
 
-def core_parts(value):
-    count = value.shape[0] // 2
-    core = lax.axis_index("dp") % 2
-    sent = lax.dynamic_slice_in_dim(value, (1 - core) * count, count, 0)
-    kept = lax.dynamic_slice_in_dim(value, core * count, count, 0)
-    return kept, flip(sent, 1)
-
-
 def ff_kernel(sub, x_ref, g_ref, wg_ref, wu_ref, wd_ref, gx_ref, y_ref, h_ref, gg_ref, gu_ref):
     step = pl.program_id(0)
     for at in range(0, wg_ref.shape[1], sub):
@@ -492,7 +484,7 @@
     )(side.astype(jnp.int32).reshape(1), x0, x1, gg0, gg1, gu0, gu1, h0, h1, g0, g1)
 
 
-def open_specs(nodes, group, half, lanes):
+def open_specs(nodes, group, half, lanes, first=0):
     specs = []
     for _ in range(2):
         for b in range(group):
@@ -500,7 +492,11 @@
                 specs.append(
                     pl.BlockSpec(
                         (None, half, lanes),
-                        lambda j, h, order, b=b, at=at: (order[at + j * group + b], 0, 0),
+                        lambda j, h, order, b=b, at=at: (
+                            order[at + (first + j) * group + b],
+                            0,
+                            0,
+                        ),
                     )
                 )
     return specs
@@ -552,65 +548,78 @@
     open_blocks(group, order_ref, pieces, write)
 
 
-def open_ff(ring, width, hidden):
-    mine = ring.total()
-    other = flip(mine, 1)
-    _, half, lanes = mine.shape
-    nodes, group = ring.nodes, 2
+def open_ff(pieces, order, at, so_far, width, hidden):
+    mine, other = pieces
+    half, lanes = mine.shape[1:]
+    nodes, group = mine.shape[0] // 2, 2
     steps = nodes // group
     rows, deep = width // (2 * nodes), hidden // (2 * nodes)
     out = lambda tall, wide: pl.BlockSpec(
-        (group * tall, wide), lambda j, h, order: (h * steps + j, 0)
+        (group * tall, wide), lambda j, h, order: (h * steps + at, 0)
+    )
+    specs = open_specs(nodes, group, half, lanes, at)
+    shapes = [(width, hidden), (width, hidden), (hidden, width)]
+    kernel = lambda order, *refs: open_ff_kernel(
+        group, order, *refs[: 4 * group], *refs[4 * group + len(so_far) :]
     )
     return pl.pallas_call(
-        lambda *refs: open_ff_kernel(group, *refs),
+        kernel,
         grid_spec=pltpu.PrefetchScalarGridSpec(
             num_scalar_prefetch=1,
-            grid=(steps, 2),
-            in_specs=open_specs(nodes, group, half, lanes),
+            grid=(1, 2),
+            in_specs=specs + [pl.BlockSpec(memory_space=pl.ANY)] * len(so_far),
             out_specs=[out(rows, hidden), out(rows, hidden), out(deep, width)],
         ),
-        out_shape=[
-            jax.ShapeDtypeStruct((width, hidden), f32),
-            jax.ShapeDtypeStruct((width, hidden), f32),
-            jax.ShapeDtypeStruct((hidden, width), f32),
-        ],
+        out_shape=[jax.ShapeDtypeStruct(shape, f32) for shape in shapes],
+        input_output_aliases={1 + 4 * group + k: k for k in range(len(so_far))},
         compiler_params=big_vmem,
-        cost_estimate=cost(0, 24 * width * hidden),
+        cost_estimate=cost(0, 24 * width * hidden // steps),
         name="open_ff",
-    )(ring.order(), *[mine] * (2 * group), *[other] * (2 * group))
-
-
-def pack_conv_kernel(in_ref, out_w_ref, tail_ref, out_ref):
-    blocks = out_ref.shape[0]
+    )(order, *[mine] * (2 * group), *[other] * (2 * group), *so_far)
+
+
+def pack_conv_kernel(core_ref, in_ref, out_w_ref, tail_ref, away_ref, own_ref):
+    blocks, _, width = own_ref.shape
     rows = in_ref.shape[0] // (2 * blocks)
     deep = out_w_ref.shape[0] // blocks
-    lanes = in_ref.shape[1]
-    for k in range(blocks):
-        out_ref[k, 0:rows, 0:lanes] = in_ref[2 * k * rows : (2 * k + 1) * rows]
-        out_ref[k, 0:rows, lanes:] = in_ref[(2 * k + 1) * rows : (2 * k + 2) * rows]
-        out_ref[k, rows : rows + deep] = out_w_ref[k * deep : (k + 1) * deep]
-        out_ref[k, rows + deep :] = tail_ref[...]
-
-
-def pack_conv(grad_in, grad_out, tail, blocks):
-    total, lanes = grad_in.shape
-    rows, deep, spared = total // blocks, grad_out.shape[0] // blocks, tail.shape[0]
-    count = rows // 2 + deep + spared
+    lanes = width // 2
+
+    def write(ref):
+        for k in range(blocks):
+            ref[k, 0:rows, 0:lanes] = in_ref[2 * k * rows : (2 * k + 1) * rows]
+            ref[k, 0:rows, lanes:] = in_ref[(2 * k + 1) * rows : (2 * k + 2) * rows]
+            ref[k, rows : rows + deep] = out_w_ref[k * deep : (k + 1) * deep]
+            ref[k, rows + deep :] = tail_ref[...]
+
+    pl.when(pl.program_id(0) == 0)(lambda: write(away_ref))
+    pl.when(pl.program_id(0) == 1)(lambda: write(own_ref))
+
+
+def pack_conv(grad_in, grad_out, tail, part, nodes):
+    total, width = grad_in.shape
+    half_in, half_out = total // 2, grad_out.shape[0] // 4
+    spared = tail.shape[0]
+    count = half_in // (2 * nodes) + half_out // nodes + spared
+    core = (lax.axis_index("dp") % 2).astype(jnp.int32).reshape(1)
+    side = lambda i, c: jnp.where(i == 0, 1 - c[0], c[0])
+    out = pl.BlockSpec((nodes, count, width), lambda i, c: (0, 0, 0))
     return pl.pallas_call(
         pack_conv_kernel,
-        grid=(4,),
-        in_specs=[
-            pl.BlockSpec((total // 4, lanes), lambda i: (i, 0)),
-            pl.BlockSpec((grad_out.shape[0] // 4, 2 * lanes), lambda i: (i, 0)),
-            pl.BlockSpec((spared, 2 * lanes), lambda i: (0, 0)),
-        ],
-        out_specs=pl.BlockSpec((blocks // 4, count, 2 * lanes), lambda i: (i, 0, 0)),
-        out_shape=jax.ShapeDtypeStruct((blocks, count, 2 * lanes), bf16),
+        grid_spec=pltpu.PrefetchScalarGridSpec(
+            num_scalar_prefetch=1,
+            grid=(2,),
+            in_specs=[
+                pl.BlockSpec((half_in, width // 2), lambda i, c: (side(i, c), part)),
+                pl.BlockSpec((half_out, width), lambda i, c: (2 * part + side(i, c), 0)),
+                pl.BlockSpec((spared, width), lambda i, c: (0, 0)),
+            ],
+            out_specs=[out, out],
+        ),
+        out_shape=[jax.ShapeDtypeStruct((nodes, count, width), bf16)] * 2,
         compiler_params=big_vmem,
-        cost_estimate=cost(0, 4 * (grad_in.size + grad_out.size)),
+        cost_estimate=cost(0, 2 * (grad_in.size + grad_out.size)),
         name="pack_conv",
-    )(grad_in, grad_out, tail)
+    )(core, grad_in, grad_out, tail)
 
 
 def open_conv_kernel(group, order_ref, *refs):
@@ -800,6 +809,28 @@
         total_gate = sum_dp(tn_dot(normed_two, grad_gate_val).astype(bf16)).astype(f32)
         total_up = sum_dp(tn_dot(normed_two, grad_up_val).astype(bf16)).astype(f32)
         total_down = sum_dp(tn_dot(hidden, seeds).astype(bf16)).astype(f32)
+        block_own = (middle[:own] + down_sum).astype(bf16)
+
+    def to_features(mine):
+        if not paired:
+            full = lax.all_gather(mine, "mp", axis=0, tiled=True)
+            return lax.dynamic_slice_in_dim(full, column, narrow, 1)
+        low, high = mine[:, :narrow], mine[:, narrow:]
+        other = swap_mp(jnp.where(mp_index == 0, high, low))
+        return jnp.concatenate([jnp.where(mp_index == 0, low, high), other], axis=0)
+
+    shape = (dp_size, slots, narrow)
+    back_block = min(8 * slots, slots * dp_size)
+    home_block = min(rows, 512)
+
+    def leave(piece):
+        return take_rows(place_ids, piece, back_block, bf16).reshape(shape)
+
+    def to_home(back):
+        return lax.all_to_all(back, "dp", **over)
+
+    def arrive(home, dtype):
+        return take_rows(slot_of, home.reshape(-1, narrow), home_block, dtype)
 
     gain_two_term = jnp.sum((grad_normed_two * middle * scale_two)[:own], axis=0)
     dot_two = jnp.sum(norm2_gain * grad_normed_two * middle, axis=1, keepdims=True)
@@ -836,10 +867,16 @@
         ],
         axis=0,
     ).astype(bf16)
+    grad_in = jnp.einsum(
+        "rd,krc->kdc", normed_one[inner], grad_parts, preferred_element_type=f32
+    ).astype(bf16)
+    grad_out = jnp.einsum(
+        "rc,rd->cd", gated[inner], grad_mix[:own], preferred_element_type=f32
+    ).astype(bf16)
+    taps_end = 2 + conv_weight.shape[0]
+
     parts_late = grad_parts
     if paired:
-        grad_parts = ring.first(grad_parts)
-        ring.step()
         ring.step()
         parts_late = ring.first(grad_parts)
     grad_normed_one = jnp.einsum("krc,kdc->rd", parts_late, full_in, preferred_element_type=f32)
@@ -853,79 +890,58 @@
         - residual_own * (scale_own * scale_own * scale_own * dot_one / width)
     ).astype(bf16)
 
-    grad_in = jnp.einsum(
-        "rd,krc->kdc", normed_one[inner], grad_parts, preferred_element_type=f32
-    ).astype(bf16)
-    grad_out = jnp.einsum(
-        "rc,rd->cd", gated[inner], grad_mix[:own], preferred_element_type=f32
-    ).astype(bf16)
+    def packed_half(k, *gates):
+        lanes = slice(k * narrow, (k + 1) * narrow)
+        terms = jnp.pad(conv_terms[:, lanes], ((0, 16 - taps_end), (0, width - narrow)))
+        gains = jnp.stack([gain_one_term, gain_two_term], axis=0)
+        ends = after(jnp.concatenate([gains, terms], axis=0).astype(bf16), *gates)
+        return pack_conv(grad_in.reshape(-1, width), grad_out, ends, k, dp_size // 2)
+
     if paired:
-        down_sum = first[1] + after(down_came, grad_parts).astype(f32)
-    block_own = (middle[:own] + down_sum).astype(bf16)
-    gains = jnp.stack([gain_one_term, gain_two_term], axis=0)
-    count = 2 + conv_weight.shape[0]
-
-    def to_features(mine):
-        if not paired:
-            full = lax.all_gather(mine, "mp", axis=0, tiled=True)
-            return lax.dynamic_slice_in_dim(full, column, narrow, 1)
-        low, high = mine[:, :narrow], mine[:, narrow:]
-        other = swap_mp(jnp.where(mp_index == 0, high, low))
-        return jnp.concatenate([jnp.where(mp_index == 0, low, high), other], axis=0)
-
-    shape = (dp_size, slots, narrow)
-    back_block = min(8 * slots, slots * dp_size)
-    home_block = min(rows, 512)
-
-    def leave(piece):
-        back = take_rows(place_ids, piece, back_block, bf16)
-        return lax.all_to_all(back.reshape(shape), "dp", **over)
-
-    def arrive(home, dtype):
-        return take_rows(slot_of, home.reshape(-1, narrow), home_block, dtype)
-
-    if paired:
-        def packed_half(k, parts):
-            lanes = slice(k * narrow, (k + 1) * narrow)
-            terms = jnp.pad(conv_terms[:, lanes], ((0, 16 - count), (0, width - narrow)))
-            ends = jnp.concatenate([gains, terms], axis=0).astype(bf16)
-            lane_in = parts[:, :, lanes].reshape(-1, narrow)
-            return core_parts(pack_conv(lane_in, grad_out[lanes], ends, dp_size))
-
-        other = packed_half(1, grad_in)
-        passed = (other[0].astype(f32) + other[1].astype(f32)).astype(bf16)
-        gate_in = ring.first(after(grad_in, passed))
+        away, other = packed_half(1)
+        passed = (other.astype(f32) + flip(away, 1).astype(f32)).astype(bf16)
+        down_came = after(down_came, grad_parts)
+        block_own = (middle[:own] + (first[1] + down_came.astype(f32))).astype(bf16)
+        block_piece = to_features(block_own)
+        block_back = leave(block_piece)
+        out_home = to_home(block_back)
+        ring.step(block_piece)
+        away, own_half = packed_half(0, passed, *ring.held.values())
         passed = swap_mp(passed)
-        block_piece = to_features(block_own)
-        out_home = leave(block_piece)
-        ring.step(block_piece)
-        mine = packed_half(0, gate_in)
         input_piece = to_features(input_own)
         ring.step()
         ring.step(input_piece)
-        grad_home = leave(after(input_piece, out_home))
+        input_back = leave(after(input_piece, out_home))
+        grad_home = to_home(input_back)
         ring.step(out_home)
-        ring.step(mine[1])
+        ring.step(away)
+        block_out = arrive(out_home, bf16)
         ring.step()
-        ring.step(grad_home)
-        second = Ring((*mine, passed))
+        second = Ring((own_half, flip(away, 1), passed))
+        ring.step(*second.held.values(), grad_home)
+        second.step()
+        tokens_grad = arrive(grad_home, f32)
         while ring.steps < 2 * ring.nodes - 2:
             ring.step(*second.held.values())
             second.step()
-        for _ in range(4):
+        mine = ring.total()
+        pieces = (mine, flip(mine, 1))
+        second.step(mine)
+        second.step(tokens_grad)
+        totals = ()
+        for at in range(ring.nodes // 2):
+            totals = open_ff(pieces, ring.order(), at, totals, width, gate_weight.shape[1])
+            second.step(*totals)
+        while second.steps < 2 * second.nodes - 2:
             second.step()
-        ring_done = open_ff(ring, width, gate_weight.shape[1])
-        total_gate, total_up, total_down = ring_done
-        while second.steps < 2 * second.nodes - 3:
-            second.step()
-        second.step(total_gate)
+        total_gate, total_up, total_down = totals
         total_in, total_out, ends = open_conv(
             second, total_gate, grad_in.size // (2 * narrow), narrow
         )
         tail = ends[0]
     else:
-        out_home = leave(to_features(block_own))
-        grad_home = leave(to_features(input_own))
+        block_out = arrive(to_home(leave(to_features(block_own))), bf16)
+        tokens_grad = arrive(to_home(leave(to_features(input_own))), f32)
         total_in = lax.psum_scatter(
             grad_in.astype(f32), "mp", scatter_dimension=2, tiled=True
         )
@@ -934,13 +950,11 @@
             grad_out.astype(f32), "mp", scatter_dimension=0, tiled=True
         )
         total_out = sum_dp(total_out.astype(bf16)).astype(f32)
-        gains = lax.psum(gains, ("dp", "mp"))
+        gains = lax.psum(jnp.stack([gain_one_term, gain_two_term]), ("dp", "mp"))
         terms = lax.psum_scatter(conv_terms, "mp", scatter_dimension=1, tiled=True)
         terms = jnp.pad(lax.psum(terms, "dp"), ((0, 0), (0, width - narrow)))
         tail = jnp.concatenate([gains, terms], axis=0)
-    total_taps = tail[2:count, :narrow]
-    block_out = arrive(out_home, bf16)
-    tokens_grad = arrive(grad_home, f32)
+    total_taps = tail[2:taps_end, :narrow]
     return (
         block_out,
         tokens_grad,

time: 639 us -> 606 us (0.948)
  waiting for transfers between devices: 219 us -> 190 us
  local copies, waits for them, and re-layouts: 44.3 us -> 27.6 us
    ppermute x56, waiting for transfers between devices: 151 us -> 134 us  [send(): return lax.ppermute(value, 'dp', pairs)]
    all_to_all x2, waiting for transfers between devices: 8.8 us -> 0.01 us  [to_home(): return lax.all_to_all(back, 'dp', **over)]
    ppermute x56, starting transfers between devices: 68.9 us -> 76.6 us  [send(): return lax.ppermute(value, 'dp', pairs)]
    slice x4 -> x1, local copies, waits for them, and re-layouts: 8.14 us -> 0.6 us  [on_device(): total_taps = tail[2:taps_end, :narrow]]
    dynamic_slice x2 -> x0, local copies, waits for them, and re-layouts: 6.55 us -> none  [core_parts(): sent = lax.dynamic_slice_in_dim(value, (1 - core) * count, count, 0)]
    pallas_call x3 -> x6, Pallas kernels: 29.8 us -> 32.7 us  [the longest x4 23.4 us: open_ff(): pl.pallas_call(kernel, grid_spec=pltpu.PrefetchScalarGridSpec(num_scalar_...]
    unnamed x145 -> x151, local copies, waits for them, and re-layouts: 14.3 us -> 12.1 us
  transfers between devices with their start and end apart: 77 -> 77, of which waited for: 46 -> 34; matrix products, arithmetic and copies ran while one was open for 14% -> 16% of each run, Pallas kernels for 15% -> 16%
where the time goes in v3:
time: 606 us; the launch traced here: 602 us
  waiting for transfers between devices  190 us (31%)
  Pallas kernels  175 us (29%)
  starting transfers between devices  116 us (19%)
  other arithmetic  68.9 us (11%)
  local copies, waits for them, and re-layouts  27.6 us (5%)
  matrix products  21.8 us (4%)
    ppermute x56, waiting for transfers between devices, send(): return lax.ppermute(value, 'dp', pairs)  134 us
    ppermute x56, starting transfers between devices, send(): return lax.ppermute(value, 'dp', pairs)  76.6 us
    pallas_call x2, Pallas kernels, feed_forward(): pl.pallas_call(lambda *refs: ff_kernel(sub, *refs), grid=(hid // chunk,),...  50.2 us
    pallas_call x2, Pallas kernels, ff_grads(): pl.pallas_call(lambda s, *refs: grads_kernel(*refs), grid_spec=pltpu.Pref...  35.4 us
    all_to_all x1, waiting for transfers between devices, on_device(): got_rows = lax.all_to_all(sent_rows, 'dp', **over)  28.6 us
    convert_element_type x14, other arithmetic, step(): came = (came.astype(f32) + own).astype(bf16)  27.2 us
    ppermute x11, waiting for transfers between devices, swap_mp(): return lax.ppermute(value, 'mp', [(0, 1), (1, 0)])  24.4 us
    pallas_call x4, Pallas kernels, open_ff(): pl.pallas_call(kernel, grid_spec=pltpu.PrefetchScalarGridSpec(num_scalar_...  23.4 us
  transfers between devices with their start and end apart: 77, of which 34 were waited for; matrix products, arithmetic and copies ran while one was open for 16% of the time, Pallas kernels for 16%

profile of v3, /device:TPU:0, one launch (start us, length us, event | category | flops | bytes accessed | tf_op | source)
XLA Modules:
  0.0 602.0 jit_solution(16340193166302806876)
XLA Ops:
  4.8 5.4 pack.1
  10.2 7.4 %all-to-all-start = ((bf16[16,104,512]{2,1,0:T(8,128)(2,1)}), bf16[16,104,512]{2,1,0:T(8,128)(2,1)S(1)}, u32[]{:S(2)}, u32[]{:S(2)}) async-start(bf16[16,104,512]{2,1,0:T(8,128)(2,1)} %get-tuple-element.95), calls=%async_computation | async-start | bytes 3407872 | tf_op jit(solution)/shard_map/all_to_all | solution.py:720
  19.1 4.1 send_rows.1
  23.2 28.6 %all-to-all-done.refs_1_.refs_2_ = bf16[16,104,512]{2,1,0:T(8,128)(2,1)S(1)} async-done(((bf16[16,104,512]{2,1,0:T(8,128)(2,1)}), bf16[16,104,512]{2,1,0:T(8,128)(2,1)S(1)}, u32[]{:S(2)}, u32[]{:S(2)}) %all-to-all-start) | async-done | bytes 1703968 | tf_op jit(solution)/shard_map/all_to_all | solution.py:720
  51.8 10.2 %all-to-all-start.1 = ((bf16[16,96,512]{2,1,0:T(8,128)(2,1)}), bf16[16,96,512]{2,1,0:T(8,128)(2,1)}, u32[]{:S(2)}, u32[]{:S(2)}) async-start(bf16[16,96,512]{2,1,0:T(8,128)(2,1)} %send_rows.1), calls=%async_computation.1 | async-start | bytes 3145728 | tf_op jit(solution)/shard_map/all_to_all | solution.py:723
  62.7 5.8 place_rows.2
  72.6 13.3 %collective-permute-done = bf16[528,512]{1,0:T(8,128)(2,1)S(1)} collective-permute-done((bf16[528,512]{1,0:T(8,128)(2,1)S(1)}, bf16[528,512]{1,0:T(8,128)(2,1)S(1)}, u32[]{:S(2)}, u32[]{:S(2)}) %collective-permute-start) | collective-permute-done | bytes 540704 | tf_op jit(solution)/shard_map/ppermute | solution.py:244
  94.1 5.7 place_rows.3
  103.4 3.5 convolution_bitcast_fusion
  110.4 3.4 fusion.2
  122.7 25.1 %feed_forward.2 = (f32[512,1024]{1,0:T(8,128)}, f32[512,1024]{1,0:T(8,128)}, bf16[512,2304]{1,0:T(8,128)(2,1)}, bf16[512,2304]{1,0:T(8,128)(2,1)}, bf16[512,2304]{1,0:T(8,128)(2,1)}) custom-call(bf16[512,1024]{1,0:T(8,128)(2,1)} %copy-done.26, bf16[512,1024]{1,0:T(8,128)(2,1)} %maximum_select_fusion.1.refs_1_.refs_8_, bf16[1024,2304]{1,0:T(8,128)(2,1)} %refs_2_.3, ...), custom_call_target="tpu_custom_call" | custom-call | flops 28991029248 | bytes 27525120 | tf_op jit(solution)/shard_map/feed_forward/pallas_call | solution.py:414
  152.1 25.1 %feed_forward.3 = (f32[512,1024]{1,0:T(8,128)}, f32[512,1024]{1,0:T(8,128)}, bf16[512,2304]{1,0:T(8,128)(2,1)}, bf16[512,2304]{1,0:T(8,128)(2,1)}, bf16[512,2304]{1,0:T(8,128)(2,1)}) custom-call(bf16[512,1024]{1,0:T(8,128)(2,1)} %collective-permute-done.5.refs_0_.refs_1_, bf16[512,1024]{1,0:T(8,128)(2,1)} %maximum_select_fusion.2.refs_1_.refs_9_, ...), custom_call_target="tpu_custom_call" | custom-call | flops 28991029248 | bytes 27525120 | tf_op jit(solution)/shard_map/feed_forward/pallas_call | solution.py:414
  180.0 17.8 %ff_grads.2 = bf16[8,576,768]{2,1,0:T(8,128)(2,1)} custom-call(s32[1]{0:T(128)} %bitcast.22.s, bf16[512,1024]{1,0:T(8,128)(2,1)} %copy-done.26, bf16[512,1024]{1,0:T(8,128)(2,1)} %collective-permute-done.5.refs_0_.refs_1_, bf16[512,2304]{1,0:T(8,128)(2,1)} %get-tuple-element.111.refs_2_, bf16[512,2304]{1,0:T(8,128)(2,1)} %get-tuple-element.112.refs_3_, ...), custom_call_target="tpu_custom_call" | custom-call | flops 14495514624 | bytes 18874368 | tf_op jit(solution)/shard_map/ff_grads/pallas_call | solution.py:472
  204.9 17.6 %ff_grads.3 = bf16[8,576,768]{2,1,0:T(8,128)(2,1)} custom-call(s32[1]{0:T(128)} %bitcast.21.s.core_ref, bf16[512,1024]{1,0:T(8,128)(2,1)} %copy-done.26, bf16[512,1024]{1,0:T(8,128)(2,1)} %collective-permute-done.5.refs_0_.refs_1_, bf16[512,2304]{1,0:T(8,128)(2,1)} %get-tuple-element.111.refs_2_, bf16[512,2304]{1,0:T(8,128)(2,1)} %get-tuple-element.112.refs_3_, ...), custom_call_target="tpu_custom_call" | custom-call | flops 14495514624 | bytes 18874368 | tf_op jit(solution)/shard_map/ff_grads/pallas_call | solution.py:472
  222.5 5.7 collective-permute-done.7
  262.0 5.4 convolution_convert_fusion
  274.1 4.3 take_rows.4
  278.4 4.7 all-to-all-start.2
  286.2 7.7 %fusion.24 = (bf16[1024]{0:T(1024)(128)(2,1)S(1)}, f32[512]{0:T(512)S(1)}, f32[512,1024,1]{1,0,2:T(8,128)}) fusion(f32[528,1024]{1,0:T(8,128)S(1)} %copy-done.8, f32[512]{0:T(512)S(1)} %slice.240, f32[1024]{0:T(1024)S(1)} %copy-done.68, bf16[3,512,1024]{2,1,0:T(8,128)(2,1)} %pad_maximum_fusion, bf16[3,512,512]{2,1,0:T(8,128)(2,1)} %slice.260, ...), kind=kOutput, calls=%fused_computation.60 | convolution fusion | flops 3243244032 | bytes 13641728 | tf_op jit(solution)/shard_map/krc,kdc->rd/dot_general | solution.py:882
  294.6 4.7 pack_conv.2
  304.4 14.5 %collective-permute-done.19 = bf16[1,288,768]{2,1,0:T(8,128)(2,1)S(1)} collective-permute-done((bf16[1,288,768]{2,1,0:T(8,128)(2,1)S(1)}, bf16[1,288,768]{2,1,0:T(8,128)(2,1)S(1)}, u32[]{:S(2)}, u32[]{:S(2)}) %collective-permute-start.19) | collective-permute-done | bytes 442400 | tf_op jit(solution)/shard_map/ppermute | solution.py:318
  325.0 8.7 %collective-permute-start.33 = (bf16[1,288,768]{2,1,0:T(8,128)(2,1)}, bf16[1,288,768]{2,1,0:T(8,128)(2,1)}, u32[]{:S(2)}, u32[]{:S(2)}) collective-permute-start(bf16[1,288,768]{2,1,0:T(8,128)(2,1)} %get-tuple-element.198), channel_id=1, source_target_pairs={{0,8},{2,10},{8,16},{10,18},{16,24},{18,26},{24,28},{26,30},{28,20... | collective-permute-start | bytes 1327112 | tf_op jit(solution)/shard_map/ppermute | solution.py:318
  334.8 4.3 take_rows.6
  339.1 4.4 all-to-all-start.3
  343.5 3.5 add_convert_fusion
  347.7 4.6 pack_conv.3
  357.1 22.5 %collective-permute-done.35 = bf16[1,288,768]{2,1,0:T(8,128)(2,1)S(1)} collective-permute-done((bf16[1,288,768]{2,1,0:T(8,128)(2,1)}, bf16[1,288,768]{2,1,0:T(8,128)(2,1)S(1)}, u32[]{:S(2)}, u32[]{:S(2)}) %collective-permute-start.35) | collective-permute-done | bytes 442400 | tf_op jit(solution)/shard_map/ppermute | solution.py:318
  384.2 10.0 %collective-permute-start.37 = (bf16[1,288,768]{2,1,0:T(8,128)(2,1)}, bf16[1,288,768]{2,1,0:T(8,128)(2,1)S(1)}, u32[]{:S(2)}, u32[]{:S(2)}) collective-permute-start(bf16[1,288,768]{2,1,0:T(8,128)(2,1)} %get-tuple-element.134), channel_id=1, source_target_pairs={{0,8},{2,10},{8,16},{10,18},{16,24},{18,26},{24,28},{26,30},{28,20... | collective-permute-start | bytes 1327112 | tf_op jit(solution)/shard_map/ppermute | solution.py:318
  394.2 9.5 %collective-permute-done.37 = bf16[1,288,768]{2,1,0:T(8,128)(2,1)S(1)} collective-permute-done((bf16[1,288,768]{2,1,0:T(8,128)(2,1)}, bf16[1,288,768]{2,1,0:T(8,128)(2,1)S(1)}, u32[]{:S(2)}, u32[]{:S(2)}) %collective-permute-start.37) | collective-permute-done | bytes 442400 | tf_op jit(solution)/shard_map/ppermute | solution.py:318
  409.9 9.3 %collective-permute-done.39 = bf16[1,288,768]{2,1,0:T(8,128)(2,1)S(1)} collective-permute-done((bf16[1,288,768]{2,1,0:T(8,128)(2,1)S(1)}, bf16[1,288,768]{2,1,0:T(8,128)(2,1)S(1)}, u32[]{:S(2)}, u32[]{:S(2)}) %collective-permute-start.39) | collective-permute-done | bytes 442400 | tf_op jit(solution)/shard_map/ppermute | solution.py:318
  422.6 7.0 %collective-permute-done.40 = bf16[1,288,768]{2,1,0:T(8,128)(2,1)S(1)} collective-permute-done((bf16[1,288,768]{2,1,0:T(8,128)(2,1)S(1)}, bf16[1,288,768]{2,1,0:T(8,128)(2,1)S(1)}, u32[]{:S(2)}, u32[]{:S(2)}) %collective-permute-start.40) | collective-permute-done | bytes 442400 | tf_op jit(solution)/shard_map/ppermute | solution.py:318
  434.5 9.0 %collective-permute-done.28 = bf16[1,72,1024]{2,1,0:T(8,128)(2,1)S(1)} collective-permute-done((bf16[1,72,1024]{2,1,0:T(8,128)(2,1)S(1)}, bf16[1,72,1024]{2,1,0:T(8,128)(2,1)S(1)}, u32[]{:S(2)}, u32[]{:S(2)}) %collective-permute-start.28) | collective-permute-done | bytes 147488 | tf_op jit(solution)/shard_map/ppermute | solution.py:318
  449.1 8.2 %collective-permute-done.29 = bf16[1,72,1024]{2,1,0:T(8,128)(2,1)S(1)} collective-permute-done((bf16[1,72,1024]{2,1,0:T(8,128)(2,1)S(1)}, bf16[1,72,1024]{2,1,0:T(8,128)(2,1)S(1)}, u32[]{:S(2)}, u32[]{:S(2)}) %collective-permute-start.29) | collective-permute-done | bytes 147488 | tf_op jit(solution)/shard_map/ppermute | solution.py:318
  462.9 8.7 %collective-permute-done.30 = bf16[1,72,1024]{2,1,0:T(8,128)(2,1)S(1)} collective-permute-done((bf16[1,72,1024]{2,1,0:T(8,128)(2,1)S(1)}, bf16[1,72,1024]{2,1,0:T(8,128)(2,1)S(1)}, u32[]{:S(2)}, u32[]{:S(2)}) %collective-permute-start.30) | collective-permute-done | bytes 147488 | tf_op jit(solution)/shard_map/ppermute | solution.py:318
  477.2 9.7 %collective-permute-done.31 = bf16[1,72,1024]{2,1,0:T(8,128)(2,1)S(1)} collective-permute-done((bf16[1,72,1024]{2,1,0:T(8,128)(2,1)S(1)}, bf16[1,72,1024]{2,1,0:T(8,128)(2,1)S(1)}, u32[]{:S(2)}, u32[]{:S(2)}) %collective-permute-start.31) | collective-permute-done | bytes 147488 | tf_op jit(solution)/shard_map/ppermute | solution.py:318
  490.4 6.3 %collective-permute-done.51 = bf16[1,288,768]{2,1,0:T(8,128)(2,1)S(1)} collective-permute-done((bf16[1,288,768]{2,1,0:T(8,128)(2,1)S(1)}, bf16[1,288,768]{2,1,0:T(8,128)(2,1)S(1)}, u32[]{:S(2)}, u32[]{:S(2)}) %collective-permute-start.51) | collective-permute-done | bytes 442400 | tf_op jit(solution)/shard_map/ppermute | solution.py:318
  497.6 6.5 %gather_pieces.2.refs_0_.refs_1_.refs_2_.refs_3_ = bf16[16,288,768]{2,1,0:T(8,128)(2,1)} custom-call(bf16[288,768]{1,0:T(8,128)(2,1)} %bitcast.151, bf16[288,768]{1,0:T(8,128)(2,1)} %bitcast.156, bf16[288,768]{1,0:T(8,128)(2,1)} %bitcast.158, bf16[288,768]{1,0:T(8,128)(2,1)} %bitcast.159, bf16[288,768]{1,0:T(8,128)(2,1)} %bitcast.161, ...), custom_call_target="tpu_custom_call" | custom-call | bytes 14155776 | tf_op jit(solution)/shard_map/gather_pieces/pallas_call | solution.py:369
  507.2 3.1 collective-permute-done.32
  515.3 4.5 take_rows.7
  528.0 5.9 open_ff.4
  536.1 5.8 open_ff.5
  544.1 5.8 open_ff.6
  552.1 5.8 open_ff.7
  560.1 3.8 collective-permute-done.64
  565.8 3.1 collective-permute-done.65
  580.9 3.3 gather_pieces.3.refs_1_.refs_2_.refs_3_.refs_4_.refs_5_.refs_6_.refs_7_.refs_8_
  584.2 4.4 take_rows.5
  590.4 8.4 %open_conv.1 = (f32[3072,512]{1,0:T(8,128)}, f32[512,1024]{1,0:T(8,128)}, f32[16,16,1024]{2,1,0:T(8,128)}) custom-call(s32[17]{0:T(128)} %pad_add_fusion.1.order.refs_0_, bf16[16,72,1024]{2,1,0:T(8,128)(2,1)} %gather_pieces.3.refs_1_.refs_2_.refs_3_.refs_4_.refs_5_.refs_6_.refs_7_.refs_8_, ...), custom_call_target="tpu_custom_call" | custom-call | bytes 29360128 | tf_op jit(solution)/shard_map/open_conv/pallas_call | solution.py:650
  (376 shorter events, 193.6 us)
Async XLA Ops:
  10.2 41.6 %all-to-all-start = ((bf16[16,104,512]{2,1,0:T(8,128)(2,1)}), bf16[16,104,512]{2,1,0:T(8,128)(2,1)S(1)}, u32[]{:S(2)}, u32[]{:S(2)}) async-start(bf16[16,104,512]{2,1,0:T(8,128)(2,1)} %get-tuple-element.95), calls=%async_computation | async-start | bytes 3407872 | tf_op jit(solution)/shard_map/all_to_all | solution.py:720
  17.6 50.9 %collective-permute-start.1 = (bf16[4,512,512]{2,1,0:T(8,128)(2,1)}, bf16[4,512,512]{2,1,0:T(8,128)(2,1)}, u32[]{:S(2)}, u32[]{:S(2)}) collective-permute-start(bf16[4,512,512]{2,1,0:T(8,128)(2,1)} %pad_maximum_fusion.1), channel_id=1, source_target_pairs={{0,1},{1,0},{2,3},{3,2},{4,5},{5,4},{6,7},{7,6},{8,9},{9,8},{10,11... | collective-permute-start | bytes 6291464 | tf_op jit(solution)/shard_map/ppermute | solution.py:244
  51.8 42.2 %all-to-all-start.1 = ((bf16[16,96,512]{2,1,0:T(8,128)(2,1)}), bf16[16,96,512]{2,1,0:T(8,128)(2,1)}, u32[]{:S(2)}, u32[]{:S(2)}) async-start(bf16[16,96,512]{2,1,0:T(8,128)(2,1)} %send_rows.1), calls=%async_computation.1 | async-start | bytes 3145728 | tf_op jit(solution)/shard_map/all_to_all | solution.py:723
  68.4 17.8 %collective-permute-start.2 = (bf16[4,512,512]{2,1,0:T(8,128)(2,1)}, bf16[4,512,512]{2,1,0:T(8,128)(2,1)}, u32[]{:S(2)}, u32[]{:S(2)}) collective-permute-start(bf16[4,512,512]{2,1,0:T(8,128)(2,1)} %collective-permute-done.1), channel_id=1, source_target_pairs={{0,2},{2,0},{4,6},{6,4},{8,10},{10,8},{12,14},{14,12},{16,18},{18,... | collective-permute-start | bytes 6291464 | tf_op jit(solution)/shard_map/ppermute | solution.py:261
  71.9 14.0 %collective-permute-start = (bf16[528,512]{1,0:T(8,128)(2,1)S(1)}, bf16[528,512]{1,0:T(8,128)(2,1)S(1)}, u32[]{:S(2)}, u32[]{:S(2)}) collective-permute-start(bf16[528,512]{1,0:T(8,128)(2,1)S(1)} %get-tuple-element.230), channel_id=1, source_target_pairs={{0,1},{1,0},{2,3},{3,2},{4,5},{5,4},{6,7},{7,6},{8,9},{9,8},{10,11... | collective-permute-start | bytes 1622024 | tf_op jit(solution)/shard_map/ppermute | solution.py:244
  101.2 14.7 %collective-permute-start.4 = (bf16[512,512]{1,0:T(8,128)(2,1)S(1)}, bf16[512,512]{1,0:T(8,128)(2,1)S(1)}, u32[]{:S(2)}, u32[]{:S(2)}) collective-permute-start(bf16[512,512]{1,0:T(8,128)(2,1)S(1)} %get-tuple-element.238), channel_id=1, source_target_pairs={{0,1},{1,0},{2,3},{3,2},{4,5},{5,4},{6,7},{7,6},{8,9},{9,8},{10,11... | collective-permute-start | bytes 1572872 | tf_op jit(solution)/shard_map/ppermute | solution.py:244
  115.8 32.7 %collective-permute-start.6 = (bf16[512,512]{1,0:T(8,128)(2,1)S(1)}, bf16[512,512]{1,0:T(8,128)(2,1)S(1)}, u32[]{:S(2)}, u32[]{:S(2)}) collective-permute-start(bf16[512,512]{1,0:T(8,128)(2,1)S(1)} %get-tuple-element.106), channel_id=1, source_target_pairs={{0,1},{1,0},{2,3},{3,2},{4,5},{5,4},{6,7},{7,6},{8,9},{9,8},{10,11... | collective-permute-start | bytes 1572872 | tf_op jit(solution)/shard_map/ppermute | solution.py:244
  121.7 30.4 %collective-permute-start.5 = (bf16[512,1024]{1,0:T(8,128)(2,1)S(1)}, bf16[512,1024]{1,0:T(8,128)(2,1)}, u32[]{:S(2)}, u32[]{:S(2)}) collective-permute-start(bf16[512,1024]{1,0:T(8,128)(2,1)S(1)} %multiply_convert_fusion.1.refs_0_), channel_id=1, source_target_pairs={{0,1},{1,0},{2,3},{3,2},{4,5},{5,4},{6,7},{7,6},{8,9},{9,8},{10,11... | collective-permute-start | bytes 3145736 | tf_op jit(solution)/shard_map/ppermute | solution.py:244
  197.9 32.3 %collective-permute-start.9 = (bf16[8,576,768]{2,1,0:T(8,128)(2,1)}, bf16[8,576,768]{2,1,0:T(8,128)(2,1)}, u32[]{:S(2)}, u32[]{:S(2)}) collective-permute-start(bf16[8,576,768]{2,1,0:T(8,128)(2,1)} %ff_grads.2), channel_id=1, source_target_pairs={{0,2},{2,0},{4,6},{6,4},{8,10},{10,8},{12,14},{14,12},{16,18},{18,... | collective-permute-start | bytes 21233672 | tf_op jit(solution)/shard_map/ppermute | solution.py:261
  202.3 25.9 %collective-permute-start.7 = (bf16[520,1024]{1,0:T(8,128)(2,1)}, bf16[520,1024]{1,0:T(8,128)(2,1)S(1)}, u32[]{:S(2)}, u32[]{:S(2)}) collective-permute-start(bf16[520,1024]{1,0:T(8,128)(2,1)} %pad_maximum_fusion.2), channel_id=1, source_target_pairs={{0,1},{1,0},{2,3},{3,2},{4,5},{5,4},{6,7},{7,6},{8,9},{9,8},{10,11... | collective-permute-start | bytes 3194888 | tf_op jit(solution)/shard_map/ppermute | solution.py:244
  228.2 32.3 %collective-permute-start.8 = (bf16[512,1024]{1,0:T(8,128)(2,1)}, bf16[512,1024]{1,0:T(8,128)(2,1)S(1)}, u32[]{:S(2)}, u32[]{:S(2)}) collective-permute-start(bf16[512,1024]{1,0:T(8,128)(2,1)} %convert_element_type.498), channel_id=1, source_target_pairs={{0,1},{1,0},{2,3},{3,2},{4,5},{5,4},{6,7},{7,6},{8,9},{9,8},{10,11... | collective-permute-start | bytes 3145736 | tf_op jit(solution)/shard_map/ppermute | solution.py:244
  231.8 14.4 %collective-permute-start.11 = (bf16[1,288,768]{2,1,0:T(8,128)(2,1)S(1)}, bf16[1,288,768]{2,1,0:T(8,128)(2,1)S(1)}, u32[]{:S(2)}, u32[]{:S(2)}) collective-permute-start(bf16[1,288,768]{2,1,0:T(8,128)(2,1)S(1)} %get-tuple-element.205), channel_id=1, source_target_pairs={{0,4},{2,6},{8,0},{10,2},{16,8},{18,10},{24,16},{26,18},{28,24},{3... | collective-permute-start | bytes 1327112 | tf_op jit(solution)/shard_map/ppermute | solution.py:318
  234.6 13.2 %collective-permute-start.10 = (bf16[1,288,768]{2,1,0:T(8,128)(2,1)S(1)}, bf16[1,288,768]{2,1,0:T(8,128)(2,1)S(1)}, u32[]{:S(2)}, u32[]{:S(2)}) collective-permute-start(bf16[1,288,768]{2,1,0:T(8,128)(2,1)S(1)} %get-tuple-element.206), channel_id=1, source_target_pairs={{0,8},{2,10},{8,16},{10,18},{16,24},{18,26},{24,28},{26,30},{28,20... | collective-permute-start | bytes 1327112 | tf_op jit(solution)/shard_map/ppermute | solution.py:318
  249.5 17.9 %collective-permute-start.15 = (bf16[1,288,768]{2,1,0:T(8,128)(2,1)S(1)}, bf16[1,288,768]{2,1,0:T(8,128)(2,1)S(1)}, u32[]{:S(2)}, u32[]{:S(2)}) collective-permute-start(bf16[1,288,768]{2,1,0:T(8,128)(2,1)S(1)} %get-tuple-element.203), channel_id=1, source_target_pairs={{0,4},{2,6},{8,0},{10,2},{16,8},{18,10},{24,16},{26,18},{28,24},{3... | collective-permute-start | bytes 1327112 | tf_op jit(solution)/shard_map/ppermute | solution.py:318
  251.3 16.2 %collective-permute-start.13 = (bf16[1,288,768]{2,1,0:T(8,128)(2,1)S(1)}, bf16[1,288,768]{2,1,0:T(8,128)(2,1)S(1)}, u32[]{:S(2)}, u32[]{:S(2)}) collective-permute-start(bf16[1,288,768]{2,1,0:T(8,128)(2,1)S(1)} %get-tuple-element.204), channel_id=1, source_target_pairs={{0,8},{2,10},{8,16},{10,18},{16,24},{18,26},{24,28},{26,30},{28,20... | collective-permute-start | bytes 1327112 | tf_op jit(solution)/shard_map/ppermute | solution.py:318
  261.4 11.6 %collective-permute-start.12 = (bf16[512,512]{1,0:T(8,128)(2,1)S(1)}, bf16[512,512]{1,0:T(8,128)(2,1)S(1)}, u32[]{:S(2)}, u32[]{:S(2)}) collective-permute-start(bf16[512,512]{1,0:T(8,128)(2,1)S(1)} %get-tuple-element.236), channel_id=1, source_target_pairs={{0,1},{1,0},{2,3},{3,2},{4,5},{5,4},{6,7},{7,6},{8,9},{9,8},{10,11... | collective-permute-start | bytes 1572872 | tf_op jit(solution)/shard_map/ppermute | solution.py:244
  270.1 13.0 %collective-permute-start.16 = (bf16[1,288,768]{2,1,0:T(8,128)(2,1)}, bf16[1,288,768]{2,1,0:T(8,128)(2,1)}, u32[]{:S(2)}, u32[]{:S(2)}) collective-permute-start(bf16[1,288,768]{2,1,0:T(8,128)(2,1)} %get-tuple-element.201), channel_id=1, source_target_pairs={{0,4},{2,6},{8,0},{10,2},{16,8},{18,10},{24,16},{26,18},{28,24},{3... | collective-permute-start | bytes 1327112 | tf_op jit(solution)/shard_map/ppermute | solution.py:318
  271.8 11.3 %collective-permute-start.14 = (bf16[1,288,768]{2,1,0:T(8,128)(2,1)}, bf16[1,288,768]{2,1,0:T(8,128)(2,1)}, u32[]{:S(2)}, u32[]{:S(2)}) collective-permute-start(bf16[1,288,768]{2,1,0:T(8,128)(2,1)} %get-tuple-element.202), channel_id=1, source_target_pairs={{0,8},{2,10},{8,16},{10,18},{16,24},{18,26},{24,28},{26,30},{28,20... | collective-permute-start | bytes 1327112 | tf_op jit(solution)/shard_map/ppermute | solution.py:318
  278.4 56.4 %all-to-all-start.2 = ((bf16[16,96,512]{2,1,0:T(8,128)(2,1)}), bf16[16,96,512]{2,1,0:T(8,128)(2,1)}, u32[]{:S(2)}, u32[]{:S(2)}) async-start(bf16[16,96,512]{2,1,0:T(8,128)(2,1)} %bitcast.153), calls=%async_computation.2 | async-start | bytes 3145728 | tf_op jit(solution)/shard_map/all_to_all | solution.py:830
  299.3 44.3 %collective-permute-start.18 = (bf16[8,144,1024]{2,1,0:T(8,128)(2,1)}, bf16[8,144,1024]{2,1,0:T(8,128)(2,1)}, u32[]{:S(2)}, u32[]{:S(2)}) collective-permute-start(bf16[8,144,1024]{2,1,0:T(8,128)(2,1)} %get-tuple-element.126), channel_id=1, source_target_pairs={{0,2},{2,0},{4,6},{6,4},{8,10},{10,8},{12,14},{14,12},{16,18},{18,... | collective-permute-start | bytes 7077896 | tf_op jit(solution)/shard_map/ppermute | solution.py:261
  299.5 19.4 %collective-permute-start.19 = (bf16[1,288,768]{2,1,0:T(8,128)(2,1)S(1)}, bf16[1,288,768]{2,1,0:T(8,128)(2,1)S(1)}, u32[]{:S(2)}, u32[]{:S(2)}) collective-permute-start(bf16[1,288,768]{2,1,0:T(8,128)(2,1)S(1)} %copy-done.47), channel_id=1, source_target_pairs={{0,8},{2,10},{8,16},{10,18},{16,24},{18,26},{24,28},{26,30},{28,20... | collective-permute-start | bytes 1327112 | tf_op jit(solution)/shard_map/ppermute | solution.py:318
  301.2 19.7 %collective-permute-start.20 = (bf16[1,288,768]{2,1,0:T(8,128)(2,1)S(1)}, bf16[1,288,768]{2,1,0:T(8,128)(2,1)S(1)}, u32[]{:S(2)}, u32[]{:S(2)}) collective-permute-start(bf16[1,288,768]{2,1,0:T(8,128)(2,1)S(1)} %copy-done.46), channel_id=1, source_target_pairs={{0,4},{2,6},{8,0},{10,2},{16,8},{18,10},{24,16},{26,18},{28,24},{3... | collective-permute-start | bytes 1327112 | tf_op jit(solution)/shard_map/ppermute | solution.py:318
  303.7 30.0 %collective-permute-start.17 = (bf16[512,512]{1,0:T(8,128)(2,1)S(1)}, bf16[512,512]{1,0:T(8,128)(2,1)S(1)}, u32[]{:S(2)}, u32[]{:S(2)}) collective-permute-start(bf16[512,512]{1,0:T(8,128)(2,1)S(1)} %get-tuple-element.234), channel_id=1, source_target_pairs={{0,1},{1,0},{2,3},{3,2},{4,5},{5,4},{6,7},{7,6},{8,9},{9,8},{10,11... | collective-permute-start | bytes 1572872 | tf_op jit(solution)/shard_map/ppermute | solution.py:244
  323.5 28.9 %collective-permute-start.34 = (bf16[1,288,768]{2,1,0:T(8,128)(2,1)}, bf16[1,288,768]{2,1,0:T(8,128)(2,1)S(1)}, u32[]{:S(2)}, u32[]{:S(2)}) collective-permute-start(bf16[1,288,768]{2,1,0:T(8,128)(2,1)} %get-tuple-element.197), channel_id=1, source_target_pairs={{0,4},{2,6},{8,0},{10,2},{16,8},{18,10},{24,16},{26,18},{28,24},{3... | collective-permute-start | bytes 1327112 | tf_op jit(solution)/shard_map/ppermute | solution.py:318
  325.0 27.4 %collective-permute-start.33 = (bf16[1,288,768]{2,1,0:T(8,128)(2,1)}, bf16[1,288,768]{2,1,0:T(8,128)(2,1)}, u32[]{:S(2)}, u32[]{:S(2)}) collective-permute-start(bf16[1,288,768]{2,1,0:T(8,128)(2,1)} %get-tuple-element.198), channel_id=1, source_target_pairs={{0,8},{2,10},{8,16},{10,18},{16,24},{18,26},{24,28},{26,30},{28,20... | collective-permute-start | bytes 1327112 | tf_op jit(solution)/shard_map/ppermute | solution.py:318
  339.1 91.3 %all-to-all-start.3 = ((bf16[16,96,512]{2,1,0:T(8,128)(2,1)}), bf16[16,96,512]{2,1,0:T(8,128)(2,1)}, u32[]{:S(2)}, u32[]{:S(2)}) async-start(bf16[16,96,512]{2,1,0:T(8,128)(2,1)} %bitcast.152), calls=%async_computation.3 | async-start | bytes 3145728 | tf_op jit(solution)/shard_map/all_to_all | solution.py:830
  347.1 74.1 %collective-permute-start.22 = (bf16[8,144,1024]{2,1,0:T(8,128)(2,1)S(1)}, bf16[8,144,1024]{2,1,0:T(8,128)(2,1)}, u32[]{:S(2)}, u32[]{:S(2)}) collective-permute-start(bf16[8,144,1024]{2,1,0:T(8,128)(2,1)S(1)} %add_convert_fusion), channel_id=1, source_target_pairs={{0,1},{1,0},{2,3},{3,2},{4,5},{5,4},{6,7},{7,6},{8,9},{9,8},{10,11... | collective-permute-start | bytes 7077896 | tf_op jit(solution)/shard_map/ppermute | solution.py:244
  352.3 68.8 %collective-permute-start.21 = (bf16[8,144,1024]{2,1,0:T(8,128)(2,1)}, bf16[8,144,1024]{2,1,0:T(8,128)(2,1)}, u32[]{:S(2)}, u32[]{:S(2)}) collective-permute-start(bf16[8,144,1024]{2,1,0:T(8,128)(2,1)} %get-tuple-element.131), channel_id=1, source_target_pairs={{0,2},{2,0},{4,6},{6,4},{8,10},{10,8},{12,14},{14,12},{16,18},{18,... | collective-permute-start | bytes 7077896 | tf_op jit(solution)/shard_map/ppermute | solution.py:261
  355.0 24.5 %collective-permute-start.35 = (bf16[1,288,768]{2,1,0:T(8,128)(2,1)}, bf16[1,288,768]{2,1,0:T(8,128)(2,1)S(1)}, u32[]{:S(2)}, u32[]{:S(2)}) collective-permute-start(bf16[1,288,768]{2,1,0:T(8,128)(2,1)} %get-tuple-element.132), channel_id=1, source_target_pairs={{0,8},{2,10},{8,16},{10,18},{16,24},{18,26},{24,28},{26,30},{28,20... | collective-permute-start | bytes 1327112 | tf_op jit(solution)/shard_map/ppermute | solution.py:318
  356.9 24.6 %collective-permute-start.36 = (bf16[1,288,768]{2,1,0:T(8,128)(2,1)S(1)}, bf16[1,288,768]{2,1,0:T(8,128)(2,1)}, u32[]{:S(2)}, u32[]{:S(2)}) collective-permute-start(bf16[1,288,768]{2,1,0:T(8,128)(2,1)S(1)} %get-tuple-element.133), channel_id=1, source_target_pairs={{0,4},{2,6},{8,0},{10,2},{16,8},{18,10},{24,16},{26,18},{28,24},{3... | collective-permute-start | bytes 1327112 | tf_op jit(solution)/shard_map/ppermute | solution.py:318
  384.2 19.5 %collective-permute-start.37 = (bf16[1,288,768]{2,1,0:T(8,128)(2,1)}, bf16[1,288,768]{2,1,0:T(8,128)(2,1)S(1)}, u32[]{:S(2)}, u32[]{:S(2)}) collective-permute-start(bf16[1,288,768]{2,1,0:T(8,128)(2,1)} %get-tuple-element.134), channel_id=1, source_target_pairs={{0,8},{2,10},{8,16},{10,18},{16,24},{18,26},{24,28},{26,30},{28,20... | collective-permute-start | bytes 1327112 | tf_op jit(solution)/shard_map/ppermute | solution.py:318
  394.2 11.5 %collective-permute-start.38 = (bf16[1,288,768]{2,1,0:T(8,128)(2,1)S(1)}, bf16[1,288,768]{2,1,0:T(8,128)(2,1)}, u32[]{:S(2)}, u32[]{:S(2)}) collective-permute-start(bf16[1,288,768]{2,1,0:T(8,128)(2,1)S(1)} %get-tuple-element.135), channel_id=1, source_target_pairs={{0,4},{2,6},{8,0},{10,2},{16,8},{18,10},{24,16},{26,18},{28,24},{3... | collective-permute-start | bytes 1327112 | tf_op jit(solution)/shard_map/ppermute | solution.py:318
  407.8 11.4 %collective-permute-start.39 = (bf16[1,288,768]{2,1,0:T(8,128)(2,1)S(1)}, bf16[1,288,768]{2,1,0:T(8,128)(2,1)S(1)}, u32[]{:S(2)}, u32[]{:S(2)}) collective-permute-start(bf16[1,288,768]{2,1,0:T(8,128)(2,1)S(1)} %get-tuple-element.136), channel_id=1, source_target_pairs={{0,8},{2,10},{8,16},{10,18},{16,24},{18,26},{24,28},{26,30},{28,20... | collective-permute-start | bytes 1327112 | tf_op jit(solution)/shard_map/ppermute | solution.py:318
  409.2 10.7 %collective-permute-start.41 = (bf16[1,288,768]{2,1,0:T(8,128)(2,1)S(1)}, bf16[1,288,768]{2,1,0:T(8,128)(2,1)S(1)}, u32[]{:S(2)}, u32[]{:S(2)}) collective-permute-start(bf16[1,288,768]{2,1,0:T(8,128)(2,1)S(1)} %get-tuple-element.137), channel_id=1, source_target_pairs={{0,4},{2,6},{8,0},{10,2},{16,8},{18,10},{24,16},{26,18},{28,24},{3... | collective-permute-start | bytes 1327112 | tf_op jit(solution)/shard_map/ppermute | solution.py:318
  419.2 10.4 %collective-permute-start.40 = (bf16[1,288,768]{2,1,0:T(8,128)(2,1)S(1)}, bf16[1,288,768]{2,1,0:T(8,128)(2,1)S(1)}, u32[]{:S(2)}, u32[]{:S(2)}) collective-permute-start(bf16[1,288,768]{2,1,0:T(8,128)(2,1)S(1)} %collective-permute-done.39), channel_id=1, source_target_pairs={{0,8},{2,10},{8,16},{10,18},{16,24},{18,26},{24,28},{26,30},{28,20... | collective-permute-start | bytes 1327112 | tf_op jit(solution)/shard_map/ppermute | solution.py:318
  430.4 14.5 %collective-permute-start.43 = (bf16[1,288,768]{2,1,0:T(8,128)(2,1)}, bf16[1,288,768]{2,1,0:T(8,128)(2,1)S(1)}, u32[]{:S(2)}, u32[]{:S(2)}) collective-permute-start(bf16[1,288,768]{2,1,0:T(8,128)(2,1)} %copy-done.35), channel_id=1, source_target_pairs={{0,8},{2,10},{8,16},{10,18},{16,24},{18,26},{24,28},{26,30},{28,20... | collective-permute-start | bytes 1327112 | tf_op jit(solution)/shard_map/ppermute | solution.py:318
  431.4 13.6 %collective-permute-start.44 = (bf16[1,288,768]{2,1,0:T(8,128)(2,1)}, bf16[1,288,768]{2,1,0:T(8,128)(2,1)S(1)}, u32[]{:S(2)}, u32[]{:S(2)}) collective-permute-start(bf16[1,288,768]{2,1,0:T(8,128)(2,1)} %collective-permute-done.42), channel_id=1, source_target_pairs={{0,4},{2,6},{8,0},{10,2},{16,8},{18,10},{24,16},{26,18},{28,24},{3... | collective-permute-start | bytes 1327112 | tf_op jit(solution)/shard_map/ppermute | solution.py:318
  432.4 11.0 %collective-permute-start.28 = (bf16[1,72,1024]{2,1,0:T(8,128)(2,1)S(1)}, bf16[1,72,1024]{2,1,0:T(8,128)(2,1)S(1)}, u32[]{:S(2)}, u32[]{:S(2)}) collective-permute-start(bf16[1,72,1024]{2,1,0:T(8,128)(2,1)S(1)} %get-tuple-element.221), channel_id=1, source_target_pairs={{0,4},{2,6},{8,0},{10,2},{16,8},{18,10},{24,16},{26,18},{28,24},{3... | collective-permute-start | bytes 442376 | tf_op jit(solution)/shard_map/ppermute | solution.py:318
  445.0 13.8 %collective-permute-start.45 = (bf16[1,288,768]{2,1,0:T(8,128)(2,1)S(1)}, bf16[1,288,768]{2,1,0:T(8,128)(2,1)S(1)}, u32[]{:S(2)}, u32[]{:S(2)}) collective-permute-start(bf16[1,288,768]{2,1,0:T(8,128)(2,1)S(1)} %collective-permute-done.43), channel_id=1, source_target_pairs={{0,8},{2,10},{8,16},{10,18},{16,24},{18,26},{24,28},{26,30},{28,20... | collective-permute-start | bytes 1327112 | tf_op jit(solution)/shard_map/ppermute | solution.py:318
  446.3 12.4 %collective-permute-start.46 = (bf16[1,288,768]{2,1,0:T(8,128)(2,1)S(1)}, bf16[1,288,768]{2,1,0:T(8,128)(2,1)S(1)}, u32[]{:S(2)}, u32[]{:S(2)}) collective-permute-start(bf16[1,288,768]{2,1,0:T(8,128)(2,1)S(1)} %collective-permute-done.44), channel_id=1, source_target_pairs={{0,4},{2,6},{8,0},{10,2},{16,8},{18,10},{24,16},{26,18},{28,24},{3... | collective-permute-start | bytes 1327112 | tf_op jit(solution)/shard_map/ppermute | solution.py:318
  458.8 14.3 %collective-permute-start.47 = (bf16[1,288,768]{2,1,0:T(8,128)(2,1)S(1)}, bf16[1,288,768]{2,1,0:T(8,128)(2,1)S(1)}, u32[]{:S(2)}, u32[]{:S(2)}) collective-permute-start(bf16[1,288,768]{2,1,0:T(8,128)(2,1)S(1)} %collective-permute-done.45), channel_id=1, source_target_pairs={{0,8},{2,10},{8,16},{10,18},{16,24},{18,26},{24,28},{26,30},{28,20... | collective-permute-start | bytes 1327112 | tf_op jit(solution)/shard_map/ppermute | solution.py:318
  460.7 12.4 %collective-permute-start.48 = (bf16[1,288,768]{2,1,0:T(8,128)(2,1)S(1)}, bf16[1,288,768]{2,1,0:T(8,128)(2,1)S(1)}, u32[]{:S(2)}, u32[]{:S(2)}) collective-permute-start(bf16[1,288,768]{2,1,0:T(8,128)(2,1)S(1)} %collective-permute-done.46), channel_id=1, source_target_pairs={{0,4},{2,6},{8,0},{10,2},{16,8},{18,10},{24,16},{26,18},{28,24},{3... | collective-permute-start | bytes 1327112 | tf_op jit(solution)/shard_map/ppermute | solution.py:318
  460.8 10.8 %collective-permute-start.30 = (bf16[1,72,1024]{2,1,0:T(8,128)(2,1)S(1)}, bf16[1,72,1024]{2,1,0:T(8,128)(2,1)S(1)}, u32[]{:S(2)}, u32[]{:S(2)}) collective-permute-start(bf16[1,72,1024]{2,1,0:T(8,128)(2,1)S(1)} %get-tuple-element.217), channel_id=1, source_target_pairs={{0,4},{2,6},{8,0},{10,2},{16,8},{18,10},{24,16},{26,18},{28,24},{3... | collective-permute-start | bytes 442376 | tf_op jit(solution)/shard_map/ppermute | solution.py:318
  473.1 15.1 %collective-permute-start.49 = (bf16[1,288,768]{2,1,0:T(8,128)(2,1)S(1)}, bf16[1,288,768]{2,1,0:T(8,128)(2,1)S(1)}, u32[]{:S(2)}, u32[]{:S(2)}) collective-permute-start(bf16[1,288,768]{2,1,0:T(8,128)(2,1)S(1)} %collective-permute-done.47), channel_id=1, source_target_pairs={{0,8},{2,10},{8,16},{10,18},{16,24},{18,26},{24,28},{26,30},{28,20... | collective-permute-start | bytes 1327112 | tf_op jit(solution)/shard_map/ppermute | solution.py:318
  474.3 14.0 %collective-permute-start.50 = (bf16[1,288,768]{2,1,0:T(8,128)(2,1)S(1)}, bf16[1,288,768]{2,1,0:T(8,128)(2,1)S(1)}, u32[]{:S(2)}, u32[]{:S(2)}) collective-permute-start(bf16[1,288,768]{2,1,0:T(8,128)(2,1)S(1)} %collective-permute-done.48), channel_id=1, source_target_pairs={{0,4},{2,6},{8,0},{10,2},{16,8},{18,10},{24,16},{26,18},{28,24},{3... | collective-permute-start | bytes 1327112 | tf_op jit(solution)/shard_map/ppermute | solution.py:318
  475.2 11.7 %collective-permute-start.31 = (bf16[1,72,1024]{2,1,0:T(8,128)(2,1)S(1)}, bf16[1,72,1024]{2,1,0:T(8,128)(2,1)S(1)}, u32[]{:S(2)}, u32[]{:S(2)}) collective-permute-start(bf16[1,72,1024]{2,1,0:T(8,128)(2,1)S(1)} %get-tuple-element.215), channel_id=1, source_target_pairs={{0,4},{2,6},{8,0},{10,2},{16,8},{18,10},{24,16},{26,18},{28,24},{3... | collective-permute-start | bytes 442376 | tf_op jit(solution)/shard_map/ppermute | solution.py:318
  475.9 11.0 %collective-permute-start.26 = (bf16[1,72,1024]{2,1,0:T(8,128)(2,1)S(1)}, bf16[1,72,1024]{2,1,0:T(8,128)(2,1)S(1)}, u32[]{:S(2)}, u32[]{:S(2)}) collective-permute-start(bf16[1,72,1024]{2,1,0:T(8,128)(2,1)S(1)} %get-tuple-element.216), channel_id=1, source_target_pairs={{0,8},{2,10},{8,16},{10,18},{16,24},{18,26},{24,28},{26,30},{28,20... | collective-permute-start | bytes 442376 | tf_op jit(solution)/shard_map/ppermute | solution.py:318
  504.1 23.9 %collective-permute-start.57 = (bf16[16,288,768]{2,1,0:T(8,128)(2,1)}, bf16[16,288,768]{2,1,0:T(8,128)(2,1)}, u32[]{:S(2)}, u32[]{:S(2)}) collective-permute-start(bf16[16,288,768]{2,1,0:T(8,128)(2,1)} %gather_pieces.2.refs_0_.refs_1_.refs_2_.refs_3_), channel_id=1, source_target_pairs={{0,2},{2,0},{4,6},{6,4},{8,10},{10,8},{12,14},{14,12},{16,18},{18,... | collective-permute-start | bytes 21233672 | tf_op jit(solution)/shard_map/ppermute | solution.py:261
  (105 other events, 1006.0 us)

commit v4 on v3

--- a/solution.py
+++ b/solution.py
@@ -738,6 +738,7 @@
         pieces, _ = place_rows(bases, digits, got_seeds, slots, rows, own)
         input_rows = after(input_rows, pieces)
         came = swap_mp(pieces[1])
+        seeds_here = came
         seeds_own = side_by_side(pieces[0], came, mp_index)
         seeds_other = side_by_side(pieces[1], swap_mp(after(pieces[0], came)), mp_index)
         place_ids = ((places - start) % rows).reshape(-1, 1)
@@ -751,6 +752,7 @@
         full = lax.all_gather(pieces.reshape(rows, narrow), "mp", axis=1, tiled=True)
         seeds = rolled(full, -start)
         seeds_own, seeds_other = seeds[:own], seeds[own:]
+        seeds_here = seeds_own
         place_ids = places.reshape(-1, 1)
 
     positions = start - halo + jnp.arange(window, dtype=jnp.int32)
@@ -759,13 +761,13 @@
     scale_one = lax.rsqrt(jnp.mean(residual * residual, axis=1) + epsilon)[:, None]
     normed_one = (residual * scale_one * norm1_gain).astype(bf16)
     projected = jnp.einsum("rd,kdc->krc", normed_one, full_in, preferred_element_type=f32)
+    projected = after(projected, seeds_here)
     in_gate, out_gate, value_part = (projected[0], projected[1], projected[2])
     mixed = in_gate * value_part
     lag_one = lag_rows(mixed, 1) * first_mask
     lag_two = lag_rows(mixed, 2) * second_mask
     convolved = taps[2] * mixed + taps[1] * lag_one + taps[0] * lag_two
     gated = (out_gate * convolved).astype(bf16)
-    gated = after(gated, seeds_own)
     middle = (residual + jnp.dot(gated, full_out, preferred_element_type=f32))[halo:]
     scale_two = lax.rsqrt(jnp.mean(middle * middle, axis=1) + epsilon)[:, None]
     normed_own = (middle[:own] * scale_two[:own] * norm2_gain).astype(bf16)
@@ -906,28 +908,30 @@
         block_back = leave(block_piece)
         out_home = to_home(block_back)
         ring.step(block_piece)
-        away, own_half = packed_half(0, passed, *ring.held.values())
+        ring.step(passed)
+        away, own_half = packed_half(0, passed)
         passed = swap_mp(passed)
         input_piece = to_features(input_own)
-        ring.step()
         ring.step(input_piece)
         input_back = leave(after(input_piece, out_home))
         grad_home = to_home(input_back)
-        ring.step(out_home)
-        ring.step(away)
+        second = Ring((own_half, flip(away, 1), passed))
+        ring.step(*second.held.values(), out_home)
+        second.step()
         block_out = arrive(out_home, bf16)
-        ring.step()
-        second = Ring((own_half, flip(away, 1), passed))
         ring.step(*second.held.values(), grad_home)
+        second.step(block_out)
+        tokens_grad = arrive(grad_home, f32)
+        ring.step(*second.held.values())
         second.step()
-        tokens_grad = arrive(grad_home, f32)
+        ring.step(*second.held.values(), tokens_grad)
+        second.step()
         while ring.steps < 2 * ring.nodes - 2:
             ring.step(*second.held.values())
             second.step()
         mine = ring.total()
         pieces = (mine, flip(mine, 1))
         second.step(mine)
-        second.step(tokens_grad)
         totals = ()
         for at in range(ring.nodes // 2):
             totals = open_ff(pieces, ring.order(), at, totals, width, gate_weight.shape[1])

time: 606 us -> 603 us (level)
    ppermute x56, waiting for transfers between devices: 134 us -> 118 us  [send(): return lax.ppermute(value, 'dp', pairs)]
    ppermute x11, waiting for transfers between devices: 24.4 us -> 39.9 us  [swap_mp(): return lax.ppermute(value, 'mp', [(0, 1), (1, 0)])]
    ppermute x56, starting transfers between devices: 76.6 us -> 69.3 us  [send(): return lax.ppermute(value, 'dp', pairs)]
  transfers between devices with their start and end apart: 77 -> 77, of which waited for: 34 -> 40; matrix products, arithmetic and copies ran while one was open for 16% -> 14% of each run, Pallas kernels for 16% -> 17%
where the time goes in v4:
time: 603 us; the launch traced here: 598 us
  waiting for transfers between devices  195 us (32%)
  Pallas kernels  175 us (29%)
  starting transfers between devices  112 us (19%)
  other arithmetic  67.5 us (11%)
  local copies, waits for them, and re-layouts  24.3 us (4%)
  matrix products  21.8 us (4%)
    ppermute x56, waiting for transfers between devices, send(): return lax.ppermute(value, 'dp', pairs)  118 us
    ppermute x56, starting transfers between devices, send(): return lax.ppermute(value, 'dp', pairs)  69.3 us
    pallas_call x2, Pallas kernels, feed_forward(): pl.pallas_call(lambda *refs: ff_kernel(sub, *refs), grid=(hid // chunk,),...  50.2 us
    ppermute x11, waiting for transfers between devices, swap_mp(): return lax.ppermute(value, 'mp', [(0, 1), (1, 0)])  39.9 us
    pallas_call x2, Pallas kernels, ff_grads(): pl.pallas_call(lambda s, *refs: grads_kernel(*refs), grid_spec=pltpu.Pref...  35.4 us
    all_to_all x1, waiting for transfers between devices, on_device(): got_rows = lax.all_to_all(sent_rows, 'dp', **over)  28.6 us
    convert_element_type x14, other arithmetic, step(): came = (came.astype(f32) + own).astype(bf16)  26.8 us
    pallas_call x4, Pallas kernels, open_ff(): pl.pallas_call(kernel, grid_spec=pltpu.PrefetchScalarGridSpec(num_scalar_...  23.4 us
  transfers between devices with their start and end apart: 77, of which 40 were waited for; matrix products, arithmetic and copies ran while one was open for 14% of the time, Pallas kernels for 17%

profile of v4, /device:TPU:0, one launch (start us, length us, event | category | flops | bytes accessed | tf_op | source)
XLA Modules:
  0.0 598.4 jit_solution(8550579887784145266)
XLA Ops:
  3.9 5.4 pack.1
  9.3 7.4 %all-to-all-start = ((bf16[16,104,512]{2,1,0:T(8,128)(2,1)}), bf16[16,104,512]{2,1,0:T(8,128)(2,1)S(1)}, u32[]{:S(2)}, u32[]{:S(2)}) async-start(bf16[16,104,512]{2,1,0:T(8,128)(2,1)} %get-tuple-element.99), calls=%async_computation | async-start | bytes 3407872 | tf_op jit(solution)/shard_map/all_to_all | solution.py:720
  18.2 4.1 send_rows.1
  22.3 28.6 %all-to-all-done.refs_1_.refs_2_ = bf16[16,104,512]{2,1,0:T(8,128)(2,1)S(1)} async-done(((bf16[16,104,512]{2,1,0:T(8,128)(2,1)}), bf16[16,104,512]{2,1,0:T(8,128)(2,1)S(1)}, u32[]{:S(2)}, u32[]{:S(2)}) %all-to-all-start) | async-done | bytes 1703968 | tf_op jit(solution)/shard_map/all_to_all | solution.py:720
  50.9 10.2 %all-to-all-start.1 = ((bf16[16,96,512]{2,1,0:T(8,128)(2,1)}), bf16[16,96,512]{2,1,0:T(8,128)(2,1)}, u32[]{:S(2)}, u32[]{:S(2)}) async-start(bf16[16,96,512]{2,1,0:T(8,128)(2,1)} %send_rows.1), calls=%async_computation.1 | async-start | bytes 3145728 | tf_op jit(solution)/shard_map/all_to_all | solution.py:723
  61.8 5.8 place_rows.2
  71.7 13.3 %collective-permute-done = bf16[528,512]{1,0:T(8,128)(2,1)S(1)} collective-permute-done((bf16[528,512]{1,0:T(8,128)(2,1)S(1)}, bf16[528,512]{1,0:T(8,128)(2,1)S(1)}, u32[]{:S(2)}, u32[]{:S(2)}) %collective-permute-start) | collective-permute-done | bytes 540704 | tf_op jit(solution)/shard_map/ppermute | solution.py:244
  93.2 5.7 place_rows.3
  102.5 3.5 convolution_bitcast_fusion
  106.0 9.2 %collective-permute-done.3 = bf16[512,512]{1,0:T(8,128)(2,1)S(1)} collective-permute-done((bf16[512,512]{1,0:T(8,128)(2,1)S(1)}, bf16[512,512]{1,0:T(8,128)(2,1)S(1)}, u32[]{:S(2)}, u32[]{:S(2)}) %collective-permute-start.3) | collective-permute-done | bytes 524320 | tf_op jit(solution)/shard_map/ppermute | solution.py:244
  117.4 3.4 fusion.3
  127.3 25.1 %feed_forward.2 = (f32[512,1024]{1,0:T(8,128)}, f32[512,1024]{1,0:T(8,128)}, bf16[512,2304]{1,0:T(8,128)(2,1)}, bf16[512,2304]{1,0:T(8,128)(2,1)}, bf16[512,2304]{1,0:T(8,128)(2,1)}) custom-call(bf16[512,1024]{1,0:T(8,128)(2,1)} %copy-done.27, bf16[512,1024]{1,0:T(8,128)(2,1)} %maximum_select_fusion.1.refs_1_.refs_8_, bf16[1024,2304]{1,0:T(8,128)(2,1)} %refs_2_.3, ...), custom_call_target="tpu_custom_call" | custom-call | flops 28991029248 | bytes 27525120 | tf_op jit(solution)/shard_map/feed_forward/pallas_call | solution.py:414
  153.1 7.1 %collective-permute-done.6 = bf16[512,512]{1,0:T(8,128)(2,1)} collective-permute-done((bf16[512,512]{1,0:T(8,128)(2,1)S(1)}, bf16[512,512]{1,0:T(8,128)(2,1)}, u32[]{:S(2)}, u32[]{:S(2)}) %collective-permute-start.6) | collective-permute-done | bytes 524320 | tf_op jit(solution)/shard_map/ppermute | solution.py:244
  162.7 25.1 %feed_forward.3 = (f32[512,1024]{1,0:T(8,128)}, f32[512,1024]{1,0:T(8,128)}, bf16[512,2304]{1,0:T(8,128)(2,1)}, bf16[512,2304]{1,0:T(8,128)(2,1)}, bf16[512,2304]{1,0:T(8,128)(2,1)}) custom-call(bf16[512,1024]{1,0:T(8,128)(2,1)} %collective-permute-done.5.refs_0_.refs_1_, bf16[512,1024]{1,0:T(8,128)(2,1)} %maximum_select_fusion.2.refs_1_.refs_9_, ...), custom_call_target="tpu_custom_call" | custom-call | flops 28991029248 | bytes 27525120 | tf_op jit(solution)/shard_map/feed_forward/pallas_call | solution.py:414
  190.7 17.8 %ff_grads.2 = bf16[8,576,768]{2,1,0:T(8,128)(2,1)} custom-call(s32[1]{0:T(128)} %bitcast.22.s, bf16[512,1024]{1,0:T(8,128)(2,1)} %copy-done.27, bf16[512,1024]{1,0:T(8,128)(2,1)} %collective-permute-done.5.refs_0_.refs_1_, bf16[512,2304]{1,0:T(8,128)(2,1)} %get-tuple-element.115.refs_2_, bf16[512,2304]{1,0:T(8,128)(2,1)} %get-tuple-element.116.refs_3_, ...), custom_call_target="tpu_custom_call" | custom-call | flops 14495514624 | bytes 18874368 | tf_op jit(solution)/shard_map/ff_grads/pallas_call | solution.py:472
  215.6 17.6 %ff_grads.3 = bf16[8,576,768]{2,1,0:T(8,128)(2,1)} custom-call(s32[1]{0:T(128)} %bitcast.21.s.core_ref, bf16[512,1024]{1,0:T(8,128)(2,1)} %copy-done.27, bf16[512,1024]{1,0:T(8,128)(2,1)} %collective-permute-done.5.refs_0_.refs_1_, bf16[512,2304]{1,0:T(8,128)(2,1)} %get-tuple-element.115.refs_2_, bf16[512,2304]{1,0:T(8,128)(2,1)} %get-tuple-element.116.refs_3_, ...), custom_call_target="tpu_custom_call" | custom-call | flops 14495514624 | bytes 18874368 | tf_op jit(solution)/shard_map/ff_grads/pallas_call | solution.py:472
  233.2 4.9 collective-permute-done.7
  241.7 4.8 collective-permute-start.10
  271.9 5.4 convolution_convert_fusion
  283.7 4.3 take_rows.4
  287.9 4.7 all-to-all-start.2
  295.7 7.7 %fusion.18 = (bf16[1024]{0:T(1024)(128)(2,1)S(1)}, f32[512]{0:T(512)S(1)}, f32[512,1024,1]{1,0,2:T(8,128)}) fusion(f32[528,1024]{1,0:T(8,128)S(1)} %copy-done.8, f32[512]{0:T(512)S(1)} %slice.240, f32[1024]{0:T(1024)S(1)} %copy-done.70, bf16[3,512,1024]{2,1,0:T(8,128)(2,1)} %pad_maximum_fusion, bf16[3,512,512]{2,1,0:T(8,128)(2,1)} %slice.260, ...), kind=kOutput, calls=%fused_computation.52 | convolution fusion | flops 3243244032 | bytes 13641728 | tf_op jit(solution)/shard_map/krc,kdc->rd/dot_general | solution.py:884
  304.1 4.6 pack_conv.2
  317.0 4.7 pack_conv.3
  321.6 4.6 collective-permute-done.17
  327.2 4.3 take_rows.6
  331.5 6.9 %all-to-all-start.3 = ((bf16[16,96,512]{2,1,0:T(8,128)(2,1)}), bf16[16,96,512]{2,1,0:T(8,128)(2,1)}, u32[]{:S(2)}, u32[]{:S(2)}) async-start(bf16[16,96,512]{2,1,0:T(8,128)(2,1)} %bitcast.144), calls=%async_computation.3 | async-start | bytes 3145728 | tf_op jit(solution)/shard_map/all_to_all | solution.py:832
  343.3 31.2 %collective-permute-done.39 = bf16[1,288,768]{2,1,0:T(8,128)(2,1)S(1)} collective-permute-done((bf16[1,288,768]{2,1,0:T(8,128)(2,1)}, bf16[1,288,768]{2,1,0:T(8,128)(2,1)S(1)}, u32[]{:S(2)}, u32[]{:S(2)}) %collective-permute-start.39) | collective-permute-done | bytes 442400 | tf_op jit(solution)/shard_map/ppermute | solution.py:318
  379.1 10.0 %collective-permute-start.41 = (bf16[1,288,768]{2,1,0:T(8,128)(2,1)}, bf16[1,288,768]{2,1,0:T(8,128)(2,1)S(1)}, u32[]{:S(2)}, u32[]{:S(2)}) collective-permute-start(bf16[1,288,768]{2,1,0:T(8,128)(2,1)} %get-tuple-element.140), channel_id=1, source_target_pairs={{0,8},{2,10},{8,16},{10,18},{16,24},{18,26},{24,28},{26,30},{28,20... | collective-permute-start | bytes 1327112 | tf_op jit(solution)/shard_map/ppermute | solution.py:318
  389.1 9.5 %collective-permute-done.41 = bf16[1,288,768]{2,1,0:T(8,128)(2,1)S(1)} collective-permute-done((bf16[1,288,768]{2,1,0:T(8,128)(2,1)}, bf16[1,288,768]{2,1,0:T(8,128)(2,1)S(1)}, u32[]{:S(2)}, u32[]{:S(2)}) %collective-permute-start.41) | collective-permute-done | bytes 442400 | tf_op jit(solution)/shard_map/ppermute | solution.py:318
  409.2 4.5 take_rows.5
  413.7 4.1 collective-permute-done.21
  431.7 6.6 %collective-permute-done.45 = bf16[1,288,768]{2,1,0:T(8,128)(2,1)S(1)} collective-permute-done((bf16[1,288,768]{2,1,0:T(8,128)(2,1)S(1)}, bf16[1,288,768]{2,1,0:T(8,128)(2,1)S(1)}, u32[]{:S(2)}, u32[]{:S(2)}) %collective-permute-start.45) | collective-permute-done | bytes 442400 | tf_op jit(solution)/shard_map/ppermute | solution.py:318
  443.2 4.5 take_rows.7
  453.1 8.0 %collective-permute-done.25 = bf16[1,72,1024]{2,1,0:T(8,128)(2,1)S(1)} collective-permute-done((bf16[1,72,1024]{2,1,0:T(8,128)(2,1)S(1)}, bf16[1,72,1024]{2,1,0:T(8,128)(2,1)S(1)}, u32[]{:S(2)}, u32[]{:S(2)}) %collective-permute-start.25) | collective-permute-done | bytes 147488 | tf_op jit(solution)/shard_map/ppermute | solution.py:318
  467.0 8.0 %collective-permute-done.26 = bf16[1,72,1024]{2,1,0:T(8,128)(2,1)S(1)} collective-permute-done((bf16[1,72,1024]{2,1,0:T(8,128)(2,1)S(1)}, bf16[1,72,1024]{2,1,0:T(8,128)(2,1)S(1)}, u32[]{:S(2)}, u32[]{:S(2)}) %collective-permute-start.26) | collective-permute-done | bytes 147488 | tf_op jit(solution)/shard_map/ppermute | solution.py:318
  480.7 7.8 %collective-permute-done.27 = bf16[1,72,1024]{2,1,0:T(8,128)(2,1)S(1)} collective-permute-done((bf16[1,72,1024]{2,1,0:T(8,128)(2,1)S(1)}, bf16[1,72,1024]{2,1,0:T(8,128)(2,1)S(1)}, u32[]{:S(2)}, u32[]{:S(2)}) %collective-permute-start.27) | collective-permute-done | bytes 147488 | tf_op jit(solution)/shard_map/ppermute | solution.py:318
  494.3 8.8 %collective-permute-done.28 = bf16[1,72,1024]{2,1,0:T(8,128)(2,1)S(1)} collective-permute-done((bf16[1,72,1024]{2,1,0:T(8,128)(2,1)S(1)}, bf16[1,72,1024]{2,1,0:T(8,128)(2,1)S(1)}, u32[]{:S(2)}, u32[]{:S(2)}) %collective-permute-start.28) | collective-permute-done | bytes 147488 | tf_op jit(solution)/shard_map/ppermute | solution.py:318
  508.0 6.0 %collective-permute-done.57 = bf16[1,288,768]{2,1,0:T(8,128)(2,1)S(1)} collective-permute-done((bf16[1,288,768]{2,1,0:T(8,128)(2,1)S(1)}, bf16[1,288,768]{2,1,0:T(8,128)(2,1)S(1)}, u32[]{:S(2)}, u32[]{:S(2)}) %collective-permute-start.57) | collective-permute-done | bytes 442400 | tf_op jit(solution)/shard_map/ppermute | solution.py:318
  517.0 6.4 %gather_pieces.2.refs_0_.refs_1_.refs_2_.refs_3_ = bf16[16,288,768]{2,1,0:T(8,128)(2,1)} custom-call(bf16[288,768]{1,0:T(8,128)(2,1)} %bitcast.143, bf16[288,768]{1,0:T(8,128)(2,1)} %bitcast.148, bf16[288,768]{1,0:T(8,128)(2,1)} %bitcast.150, bf16[288,768]{1,0:T(8,128)(2,1)} %bitcast.152, bf16[288,768]{1,0:T(8,128)(2,1)} %bitcast.154, ...), custom_call_target="tpu_custom_call" | custom-call | bytes 14155776 | tf_op jit(solution)/shard_map/gather_pieces/pallas_call | solution.py:369
  525.8 3.9 collective-permute-done.29
  535.0 5.8 open_ff.4
  543.0 5.8 open_ff.5
  551.0 5.8 open_ff.6
  559.0 5.8 open_ff.7
  577.4 3.3 gather_pieces.3.refs_1_.refs_2_.refs_3_.refs_4_.refs_5_.refs_6_.refs_7_.refs_8_
  580.7 4.7 collective-permute-done.72.refs_9_.refs_10_.refs_11_.refs_12_.refs_13_.refs_14_.refs_15_.refs_16_
  586.9 8.4 %open_conv.1 = (f32[3072,512]{1,0:T(8,128)}, f32[512,1024]{1,0:T(8,128)}, f32[16,16,1024]{2,1,0:T(8,128)}) custom-call(s32[17]{0:T(128)} %pad_add_fusion.1.order.refs_0_, bf16[16,72,1024]{2,1,0:T(8,128)(2,1)} %gather_pieces.3.refs_1_.refs_2_.refs_3_.refs_4_.refs_5_.refs_6_.refs_7_.refs_8_, ...), custom_call_target="tpu_custom_call" | custom-call | bytes 29360128 | tf_op jit(solution)/shard_map/open_conv/pallas_call | solution.py:650
  (380 shorter events, 190.8 us)
Async XLA Ops:
  9.3 41.7 %all-to-all-start = ((bf16[16,104,512]{2,1,0:T(8,128)(2,1)}), bf16[16,104,512]{2,1,0:T(8,128)(2,1)S(1)}, u32[]{:S(2)}, u32[]{:S(2)}) async-start(bf16[16,104,512]{2,1,0:T(8,128)(2,1)} %get-tuple-element.99), calls=%async_computation | async-start | bytes 3407872 | tf_op jit(solution)/shard_map/all_to_all | solution.py:720
  16.7 50.9 %collective-permute-start.1 = (bf16[4,512,512]{2,1,0:T(8,128)(2,1)}, bf16[4,512,512]{2,1,0:T(8,128)(2,1)}, u32[]{:S(2)}, u32[]{:S(2)}) collective-permute-start(bf16[4,512,512]{2,1,0:T(8,128)(2,1)} %pad_maximum_fusion.1), channel_id=1, source_target_pairs={{0,1},{1,0},{2,3},{3,2},{4,5},{5,4},{6,7},{7,6},{8,9},{9,8},{10,11... | collective-permute-start | bytes 6291464 | tf_op jit(solution)/shard_map/ppermute | solution.py:244
  50.9 42.2 %all-to-all-start.1 = ((bf16[16,96,512]{2,1,0:T(8,128)(2,1)}), bf16[16,96,512]{2,1,0:T(8,128)(2,1)}, u32[]{:S(2)}, u32[]{:S(2)}) async-start(bf16[16,96,512]{2,1,0:T(8,128)(2,1)} %send_rows.1), calls=%async_computation.1 | async-start | bytes 3145728 | tf_op jit(solution)/shard_map/all_to_all | solution.py:723
  67.6 17.8 %collective-permute-start.2 = (bf16[4,512,512]{2,1,0:T(8,128)(2,1)}, bf16[4,512,512]{2,1,0:T(8,128)(2,1)}, u32[]{:S(2)}, u32[]{:S(2)}) collective-permute-start(bf16[4,512,512]{2,1,0:T(8,128)(2,1)} %collective-permute-done.1), channel_id=1, source_target_pairs={{0,2},{2,0},{4,6},{6,4},{8,10},{10,8},{12,14},{14,12},{16,18},{18,... | collective-permute-start | bytes 6291464 | tf_op jit(solution)/shard_map/ppermute | solution.py:261
  71.0 14.0 %collective-permute-start = (bf16[528,512]{1,0:T(8,128)(2,1)S(1)}, bf16[528,512]{1,0:T(8,128)(2,1)S(1)}, u32[]{:S(2)}, u32[]{:S(2)}) collective-permute-start(bf16[528,512]{1,0:T(8,128)(2,1)S(1)} %get-tuple-element.238), channel_id=1, source_target_pairs={{0,1},{1,0},{2,3},{3,2},{4,5},{5,4},{6,7},{7,6},{8,9},{9,8},{10,11... | collective-permute-start | bytes 1622024 | tf_op jit(solution)/shard_map/ppermute | solution.py:244
  100.6 14.7 %collective-permute-start.3 = (bf16[512,512]{1,0:T(8,128)(2,1)S(1)}, bf16[512,512]{1,0:T(8,128)(2,1)S(1)}, u32[]{:S(2)}, u32[]{:S(2)}) collective-permute-start(bf16[512,512]{1,0:T(8,128)(2,1)S(1)} %get-tuple-element.246), channel_id=1, source_target_pairs={{0,1},{1,0},{2,3},{3,2},{4,5},{5,4},{6,7},{7,6},{8,9},{9,8},{10,11... | collective-permute-start | bytes 1572872 | tf_op jit(solution)/shard_map/ppermute | solution.py:244
  123.9 38.9 %collective-permute-start.5 = (bf16[512,1024]{1,0:T(8,128)(2,1)S(1)}, bf16[512,1024]{1,0:T(8,128)(2,1)}, u32[]{:S(2)}, u32[]{:S(2)}) collective-permute-start(bf16[512,1024]{1,0:T(8,128)(2,1)S(1)} %multiply_convert_fusion.1.refs_0_), channel_id=1, source_target_pairs={{0,1},{1,0},{2,3},{3,2},{4,5},{5,4},{6,7},{7,6},{8,9},{9,8},{10,11... | collective-permute-start | bytes 3145736 | tf_op jit(solution)/shard_map/ppermute | solution.py:244
  125.4 34.8 %collective-permute-start.6 = (bf16[512,512]{1,0:T(8,128)(2,1)S(1)}, bf16[512,512]{1,0:T(8,128)(2,1)}, u32[]{:S(2)}, u32[]{:S(2)}) collective-permute-start(bf16[512,512]{1,0:T(8,128)(2,1)S(1)} %get-tuple-element.110), channel_id=1, source_target_pairs={{0,1},{1,0},{2,3},{3,2},{4,5},{5,4},{6,7},{7,6},{8,9},{9,8},{10,11... | collective-permute-start | bytes 1572872 | tf_op jit(solution)/shard_map/ppermute | solution.py:244
  208.5 31.6 %collective-permute-start.9 = (bf16[8,576,768]{2,1,0:T(8,128)(2,1)}, bf16[8,576,768]{2,1,0:T(8,128)(2,1)}, u32[]{:S(2)}, u32[]{:S(2)}) collective-permute-start(bf16[8,576,768]{2,1,0:T(8,128)(2,1)} %ff_grads.2), channel_id=1, source_target_pairs={{0,2},{2,0},{4,6},{6,4},{8,10},{10,8},{12,14},{14,12},{16,18},{18,... | collective-permute-start | bytes 21233672 | tf_op jit(solution)/shard_map/ppermute | solution.py:261
  212.1 25.9 %collective-permute-start.7 = (bf16[520,1024]{1,0:T(8,128)(2,1)}, bf16[520,1024]{1,0:T(8,128)(2,1)S(1)}, u32[]{:S(2)}, u32[]{:S(2)}) collective-permute-start(bf16[520,1024]{1,0:T(8,128)(2,1)} %pad_maximum_fusion.2), channel_id=1, source_target_pairs={{0,1},{1,0},{2,3},{3,2},{4,5},{5,4},{6,7},{7,6},{8,9},{9,8},{10,11... | collective-permute-start | bytes 3194888 | tf_op jit(solution)/shard_map/ppermute | solution.py:244
  238.1 32.2 %collective-permute-start.8 = (bf16[512,1024]{1,0:T(8,128)(2,1)}, bf16[512,1024]{1,0:T(8,128)(2,1)S(1)}, u32[]{:S(2)}, u32[]{:S(2)}) collective-permute-start(bf16[512,1024]{1,0:T(8,128)(2,1)} %convert_element_type.498), channel_id=1, source_target_pairs={{0,1},{1,0},{2,3},{3,2},{4,5},{5,4},{6,7},{7,6},{8,9},{9,8},{10,11... | collective-permute-start | bytes 3145736 | tf_op jit(solution)/shard_map/ppermute | solution.py:244
  241.7 13.7 %collective-permute-start.10 = (bf16[1,288,768]{2,1,0:T(8,128)(2,1)S(1)}, bf16[1,288,768]{2,1,0:T(8,128)(2,1)S(1)}, u32[]{:S(2)}, u32[]{:S(2)}) collective-permute-start(bf16[1,288,768]{2,1,0:T(8,128)(2,1)S(1)} %get-tuple-element.214), channel_id=1, source_target_pairs={{0,8},{2,10},{8,16},{10,18},{16,24},{18,26},{24,28},{26,30},{28,20... | collective-permute-start | bytes 1327112 | tf_op jit(solution)/shard_map/ppermute | solution.py:318
  246.5 11.0 %collective-permute-start.11 = (bf16[1,288,768]{2,1,0:T(8,128)(2,1)S(1)}, bf16[1,288,768]{2,1,0:T(8,128)(2,1)S(1)}, u32[]{:S(2)}, u32[]{:S(2)}) collective-permute-start(bf16[1,288,768]{2,1,0:T(8,128)(2,1)S(1)} %get-tuple-element.213), channel_id=1, source_target_pairs={{0,4},{2,6},{8,0},{10,2},{16,8},{18,10},{24,16},{26,18},{28,24},{3... | collective-permute-start | bytes 1327112 | tf_op jit(solution)/shard_map/ppermute | solution.py:318
  259.3 18.0 %collective-permute-start.13 = (bf16[1,288,768]{2,1,0:T(8,128)(2,1)S(1)}, bf16[1,288,768]{2,1,0:T(8,128)(2,1)S(1)}, u32[]{:S(2)}, u32[]{:S(2)}) collective-permute-start(bf16[1,288,768]{2,1,0:T(8,128)(2,1)S(1)} %get-tuple-element.212), channel_id=1, source_target_pairs={{0,8},{2,10},{8,16},{10,18},{16,24},{18,26},{24,28},{26,30},{28,20... | collective-permute-start | bytes 1327112 | tf_op jit(solution)/shard_map/ppermute | solution.py:318
  260.1 17.2 %collective-permute-start.15 = (bf16[1,288,768]{2,1,0:T(8,128)(2,1)S(1)}, bf16[1,288,768]{2,1,0:T(8,128)(2,1)S(1)}, u32[]{:S(2)}, u32[]{:S(2)}) collective-permute-start(bf16[1,288,768]{2,1,0:T(8,128)(2,1)S(1)} %get-tuple-element.211), channel_id=1, source_target_pairs={{0,4},{2,6},{8,0},{10,2},{16,8},{18,10},{24,16},{26,18},{28,24},{3... | collective-permute-start | bytes 1327112 | tf_op jit(solution)/shard_map/ppermute | solution.py:318
  271.3 11.4 %collective-permute-start.12 = (bf16[512,512]{1,0:T(8,128)(2,1)S(1)}, bf16[512,512]{1,0:T(8,128)(2,1)S(1)}, u32[]{:S(2)}, u32[]{:S(2)}) collective-permute-start(bf16[512,512]{1,0:T(8,128)(2,1)S(1)} %get-tuple-element.244), channel_id=1, source_target_pairs={{0,1},{1,0},{2,3},{3,2},{4,5},{5,4},{6,7},{7,6},{8,9},{9,8},{10,11... | collective-permute-start | bytes 1572872 | tf_op jit(solution)/shard_map/ppermute | solution.py:244
  279.9 12.7 %collective-permute-start.14 = (bf16[1,288,768]{2,1,0:T(8,128)(2,1)}, bf16[1,288,768]{2,1,0:T(8,128)(2,1)}, u32[]{:S(2)}, u32[]{:S(2)}) collective-permute-start(bf16[1,288,768]{2,1,0:T(8,128)(2,1)} %get-tuple-element.210), channel_id=1, source_target_pairs={{0,8},{2,10},{8,16},{10,18},{16,24},{18,26},{24,28},{26,30},{28,20... | collective-permute-start | bytes 1327112 | tf_op jit(solution)/shard_map/ppermute | solution.py:318
  280.7 12.0 %collective-permute-start.16 = (bf16[1,288,768]{2,1,0:T(8,128)(2,1)}, bf16[1,288,768]{2,1,0:T(8,128)(2,1)}, u32[]{:S(2)}, u32[]{:S(2)}) collective-permute-start(bf16[1,288,768]{2,1,0:T(8,128)(2,1)} %get-tuple-element.209), channel_id=1, source_target_pairs={{0,4},{2,6},{8,0},{10,2},{16,8},{18,10},{24,16},{26,18},{28,24},{3... | collective-permute-start | bytes 1327112 | tf_op jit(solution)/shard_map/ppermute | solution.py:318
  287.9 39.3 %all-to-all-start.2 = ((bf16[16,96,512]{2,1,0:T(8,128)(2,1)}), bf16[16,96,512]{2,1,0:T(8,128)(2,1)}, u32[]{:S(2)}, u32[]{:S(2)}) async-start(bf16[16,96,512]{2,1,0:T(8,128)(2,1)} %bitcast.145), calls=%async_computation.2 | async-start | bytes 3145728 | tf_op jit(solution)/shard_map/all_to_all | solution.py:832
  311.4 14.8 %collective-permute-start.17 = (bf16[512,512]{1,0:T(8,128)(2,1)S(1)}, bf16[512,512]{1,0:T(8,128)(2,1)S(1)}, u32[]{:S(2)}, u32[]{:S(2)}) collective-permute-start(bf16[512,512]{1,0:T(8,128)(2,1)S(1)} %get-tuple-element.242), channel_id=1, source_target_pairs={{0,1},{1,0},{2,3},{3,2},{4,5},{5,4},{6,7},{7,6},{8,9},{9,8},{10,11... | collective-permute-start | bytes 1572872 | tf_op jit(solution)/shard_map/ppermute | solution.py:244
  312.3 26.2 %collective-permute-start.37 = (bf16[1,288,768]{2,1,0:T(8,128)(2,1)S(1)}, bf16[1,288,768]{2,1,0:T(8,128)(2,1)}, u32[]{:S(2)}, u32[]{:S(2)}) collective-permute-start(bf16[1,288,768]{2,1,0:T(8,128)(2,1)S(1)} %copy-done.49), channel_id=1, source_target_pairs={{0,8},{2,10},{8,16},{10,18},{16,24},{18,26},{24,28},{26,30},{28,20... | collective-permute-start | bytes 1327112 | tf_op jit(solution)/shard_map/ppermute | solution.py:318
  314.0 24.5 %collective-permute-start.38 = (bf16[1,288,768]{2,1,0:T(8,128)(2,1)S(1)}, bf16[1,288,768]{2,1,0:T(8,128)(2,1)}, u32[]{:S(2)}, u32[]{:S(2)}) collective-permute-start(bf16[1,288,768]{2,1,0:T(8,128)(2,1)S(1)} %copy-done.48), channel_id=1, source_target_pairs={{0,4},{2,6},{8,0},{10,2},{16,8},{18,10},{24,16},{26,18},{28,24},{3... | collective-permute-start | bytes 1327112 | tf_op jit(solution)/shard_map/ppermute | solution.py:318
  315.7 86.9 %collective-permute-start.20 = (bf16[8,144,1024]{2,1,0:T(8,128)(2,1)S(1)}, bf16[8,144,1024]{2,1,0:T(8,128)(2,1)}, u32[]{:S(2)}, u32[]{:S(2)}) collective-permute-start(bf16[8,144,1024]{2,1,0:T(8,128)(2,1)S(1)} %add_convert_fusion), channel_id=1, source_target_pairs={{0,1},{1,0},{2,3},{3,2},{4,5},{5,4},{6,7},{7,6},{8,9},{9,8},{10,11... | collective-permute-start | bytes 7077896 | tf_op jit(solution)/shard_map/ppermute | solution.py:244
  321.6 81.0 %collective-permute-start.19 = (bf16[8,144,1024]{2,1,0:T(8,128)(2,1)}, bf16[8,144,1024]{2,1,0:T(8,128)(2,1)}, u32[]{:S(2)}, u32[]{:S(2)}) collective-permute-start(bf16[8,144,1024]{2,1,0:T(8,128)(2,1)} %get-tuple-element.133), channel_id=1, source_target_pairs={{0,2},{2,0},{4,6},{6,4},{8,10},{10,8},{12,14},{14,12},{16,18},{18,... | collective-permute-start | bytes 7077896 | tf_op jit(solution)/shard_map/ppermute | solution.py:261
  331.5 93.6 %all-to-all-start.3 = ((bf16[16,96,512]{2,1,0:T(8,128)(2,1)}), bf16[16,96,512]{2,1,0:T(8,128)(2,1)}, u32[]{:S(2)}, u32[]{:S(2)}) async-start(bf16[16,96,512]{2,1,0:T(8,128)(2,1)} %bitcast.144), calls=%async_computation.3 | async-start | bytes 3145728 | tf_op jit(solution)/shard_map/all_to_all | solution.py:832
  341.3 33.2 %collective-permute-start.39 = (bf16[1,288,768]{2,1,0:T(8,128)(2,1)}, bf16[1,288,768]{2,1,0:T(8,128)(2,1)S(1)}, u32[]{:S(2)}, u32[]{:S(2)}) collective-permute-start(bf16[1,288,768]{2,1,0:T(8,128)(2,1)} %get-tuple-element.138), channel_id=1, source_target_pairs={{0,8},{2,10},{8,16},{10,18},{16,24},{18,26},{24,28},{26,30},{28,20... | collective-permute-start | bytes 1327112 | tf_op jit(solution)/shard_map/ppermute | solution.py:318
  343.3 33.2 %collective-permute-start.40 = (bf16[1,288,768]{2,1,0:T(8,128)(2,1)S(1)}, bf16[1,288,768]{2,1,0:T(8,128)(2,1)}, u32[]{:S(2)}, u32[]{:S(2)}) collective-permute-start(bf16[1,288,768]{2,1,0:T(8,128)(2,1)S(1)} %get-tuple-element.139), channel_id=1, source_target_pairs={{0,4},{2,6},{8,0},{10,2},{16,8},{18,10},{24,16},{26,18},{28,24},{3... | collective-permute-start | bytes 1327112 | tf_op jit(solution)/shard_map/ppermute | solution.py:318
  379.1 19.5 %collective-permute-start.41 = (bf16[1,288,768]{2,1,0:T(8,128)(2,1)}, bf16[1,288,768]{2,1,0:T(8,128)(2,1)S(1)}, u32[]{:S(2)}, u32[]{:S(2)}) collective-permute-start(bf16[1,288,768]{2,1,0:T(8,128)(2,1)} %get-tuple-element.140), channel_id=1, source_target_pairs={{0,8},{2,10},{8,16},{10,18},{16,24},{18,26},{24,28},{26,30},{28,20... | collective-permute-start | bytes 1327112 | tf_op jit(solution)/shard_map/ppermute | solution.py:318
  389.1 11.5 %collective-permute-start.42 = (bf16[1,288,768]{2,1,0:T(8,128)(2,1)S(1)}, bf16[1,288,768]{2,1,0:T(8,128)(2,1)}, u32[]{:S(2)}, u32[]{:S(2)}) collective-permute-start(bf16[1,288,768]{2,1,0:T(8,128)(2,1)S(1)} %get-tuple-element.141), channel_id=1, source_target_pairs={{0,4},{2,6},{8,0},{10,2},{16,8},{18,10},{24,16},{26,18},{28,24},{3... | collective-permute-start | bytes 1327112 | tf_op jit(solution)/shard_map/ppermute | solution.py:318
  404.0 19.0 %collective-permute-start.43 = (bf16[1,288,768]{2,1,0:T(8,128)(2,1)S(1)}, bf16[1,288,768]{2,1,0:T(8,128)(2,1)}, u32[]{:S(2)}, u32[]{:S(2)}) collective-permute-start(bf16[1,288,768]{2,1,0:T(8,128)(2,1)S(1)} %get-tuple-element.142), channel_id=1, source_target_pairs={{0,8},{2,10},{8,16},{10,18},{16,24},{18,26},{24,28},{26,30},{28,20... | collective-permute-start | bytes 1327112 | tf_op jit(solution)/shard_map/ppermute | solution.py:318
  405.2 17.8 %collective-permute-start.44 = (bf16[1,288,768]{2,1,0:T(8,128)(2,1)S(1)}, bf16[1,288,768]{2,1,0:T(8,128)(2,1)}, u32[]{:S(2)}, u32[]{:S(2)}) collective-permute-start(bf16[1,288,768]{2,1,0:T(8,128)(2,1)S(1)} %get-tuple-element.143), channel_id=1, source_target_pairs={{0,4},{2,6},{8,0},{10,2},{16,8},{18,10},{24,16},{26,18},{28,24},{3... | collective-permute-start | bytes 1327112 | tf_op jit(solution)/shard_map/ppermute | solution.py:318
  407.1 10.6 %collective-permute-start.21 = (bf16[1,72,1024]{2,1,0:T(8,128)(2,1)S(1)}, bf16[1,72,1024]{2,1,0:T(8,128)(2,1)S(1)}, u32[]{:S(2)}, u32[]{:S(2)}) collective-permute-start(bf16[1,72,1024]{2,1,0:T(8,128)(2,1)S(1)} %get-tuple-element.230), channel_id=1, source_target_pairs={{0,8},{2,10},{8,16},{10,18},{16,24},{18,26},{24,28},{26,30},{28,20... | collective-permute-start | bytes 442376 | tf_op jit(solution)/shard_map/ppermute | solution.py:318
  408.3 10.7 %collective-permute-start.22 = (bf16[1,72,1024]{2,1,0:T(8,128)(2,1)S(1)}, bf16[1,72,1024]{2,1,0:T(8,128)(2,1)S(1)}, u32[]{:S(2)}, u32[]{:S(2)}) collective-permute-start(bf16[1,72,1024]{2,1,0:T(8,128)(2,1)S(1)} %get-tuple-element.229), channel_id=1, source_target_pairs={{0,4},{2,6},{8,0},{10,2},{16,8},{18,10},{24,16},{26,18},{28,24},{3... | collective-permute-start | bytes 442376 | tf_op jit(solution)/shard_map/ppermute | solution.py:318
  425.1 13.2 %collective-permute-start.45 = (bf16[1,288,768]{2,1,0:T(8,128)(2,1)S(1)}, bf16[1,288,768]{2,1,0:T(8,128)(2,1)S(1)}, u32[]{:S(2)}, u32[]{:S(2)}) collective-permute-start(bf16[1,288,768]{2,1,0:T(8,128)(2,1)S(1)} %get-tuple-element.144), channel_id=1, source_target_pairs={{0,8},{2,10},{8,16},{10,18},{16,24},{18,26},{24,28},{26,30},{28,20... | collective-permute-start | bytes 1327112 | tf_op jit(solution)/shard_map/ppermute | solution.py:318
  425.6 13.1 %collective-permute-start.46 = (bf16[1,288,768]{2,1,0:T(8,128)(2,1)S(1)}, bf16[1,288,768]{2,1,0:T(8,128)(2,1)S(1)}, u32[]{:S(2)}, u32[]{:S(2)}) collective-permute-start(bf16[1,288,768]{2,1,0:T(8,128)(2,1)S(1)} %get-tuple-element.145), channel_id=1, source_target_pairs={{0,4},{2,6},{8,0},{10,2},{16,8},{18,10},{24,16},{26,18},{28,24},{3... | collective-permute-start | bytes 1327112 | tf_op jit(solution)/shard_map/ppermute | solution.py:318
  429.6 11.8 %collective-permute-start.24 = (bf16[1,72,1024]{2,1,0:T(8,128)(2,1)S(1)}, bf16[1,72,1024]{2,1,0:T(8,128)(2,1)S(1)}, u32[]{:S(2)}, u32[]{:S(2)}) collective-permute-start(bf16[1,72,1024]{2,1,0:T(8,128)(2,1)S(1)} %get-tuple-element.226), channel_id=1, source_target_pairs={{0,8},{2,10},{8,16},{10,18},{16,24},{18,26},{24,28},{26,30},{28,20... | collective-permute-start | bytes 442376 | tf_op jit(solution)/shard_map/ppermute | solution.py:318
  430.4 11.5 %collective-permute-start.31 = (bf16[1,72,1024]{2,1,0:T(8,128)(2,1)S(1)}, bf16[1,72,1024]{2,1,0:T(8,128)(2,1)S(1)}, u32[]{:S(2)}, u32[]{:S(2)}) collective-permute-start(bf16[1,72,1024]{2,1,0:T(8,128)(2,1)S(1)} %get-tuple-element.225), channel_id=1, source_target_pairs={{0,4},{2,6},{8,0},{10,2},{16,8},{18,10},{24,16},{26,18},{28,24},{3... | collective-permute-start | bytes 442376 | tf_op jit(solution)/shard_map/ppermute | solution.py:318
  449.0 13.8 %collective-permute-start.49 = (bf16[1,288,768]{2,1,0:T(8,128)(2,1)S(1)}, bf16[1,288,768]{2,1,0:T(8,128)(2,1)S(1)}, u32[]{:S(2)}, u32[]{:S(2)}) collective-permute-start(bf16[1,288,768]{2,1,0:T(8,128)(2,1)S(1)} %collective-permute-done.47), channel_id=1, source_target_pairs={{0,8},{2,10},{8,16},{10,18},{16,24},{18,26},{24,28},{26,30},{28,20... | collective-permute-start | bytes 1327112 | tf_op jit(solution)/shard_map/ppermute | solution.py:318
  449.6 13.3 %collective-permute-start.50 = (bf16[1,288,768]{2,1,0:T(8,128)(2,1)S(1)}, bf16[1,288,768]{2,1,0:T(8,128)(2,1)S(1)}, u32[]{:S(2)}, u32[]{:S(2)}) collective-permute-start(bf16[1,288,768]{2,1,0:T(8,128)(2,1)S(1)} %collective-permute-done.48), channel_id=1, source_target_pairs={{0,4},{2,6},{8,0},{10,2},{16,8},{18,10},{24,16},{26,18},{28,24},{3... | collective-permute-start | bytes 1327112 | tf_op jit(solution)/shard_map/ppermute | solution.py:318
  462.9 13.7 %collective-permute-start.51 = (bf16[1,288,768]{2,1,0:T(8,128)(2,1)S(1)}, bf16[1,288,768]{2,1,0:T(8,128)(2,1)S(1)}, u32[]{:S(2)}, u32[]{:S(2)}) collective-permute-start(bf16[1,288,768]{2,1,0:T(8,128)(2,1)S(1)} %collective-permute-done.49), channel_id=1, source_target_pairs={{0,8},{2,10},{8,16},{10,18},{16,24},{18,26},{24,28},{26,30},{28,20... | collective-permute-start | bytes 1327112 | tf_op jit(solution)/shard_map/ppermute | solution.py:318
  463.4 13.2 %collective-permute-start.52 = (bf16[1,288,768]{2,1,0:T(8,128)(2,1)S(1)}, bf16[1,288,768]{2,1,0:T(8,128)(2,1)S(1)}, u32[]{:S(2)}, u32[]{:S(2)}) collective-permute-start(bf16[1,288,768]{2,1,0:T(8,128)(2,1)S(1)} %collective-permute-done.50), channel_id=1, source_target_pairs={{0,4},{2,6},{8,0},{10,2},{16,8},{18,10},{24,16},{26,18},{28,24},{3... | collective-permute-start | bytes 1327112 | tf_op jit(solution)/shard_map/ppermute | solution.py:318
  476.6 13.2 %collective-permute-start.53 = (bf16[1,288,768]{2,1,0:T(8,128)(2,1)S(1)}, bf16[1,288,768]{2,1,0:T(8,128)(2,1)S(1)}, u32[]{:S(2)}, u32[]{:S(2)}) collective-permute-start(bf16[1,288,768]{2,1,0:T(8,128)(2,1)S(1)} %collective-permute-done.51), channel_id=1, source_target_pairs={{0,8},{2,10},{8,16},{10,18},{16,24},{18,26},{24,28},{26,30},{28,20... | collective-permute-start | bytes 1327112 | tf_op jit(solution)/shard_map/ppermute | solution.py:318
  476.9 13.0 %collective-permute-start.54 = (bf16[1,288,768]{2,1,0:T(8,128)(2,1)S(1)}, bf16[1,288,768]{2,1,0:T(8,128)(2,1)S(1)}, u32[]{:S(2)}, u32[]{:S(2)}) collective-permute-start(bf16[1,288,768]{2,1,0:T(8,128)(2,1)S(1)} %collective-permute-done.52), channel_id=1, source_target_pairs={{0,4},{2,6},{8,0},{10,2},{16,8},{18,10},{24,16},{26,18},{28,24},{3... | collective-permute-start | bytes 1327112 | tf_op jit(solution)/shard_map/ppermute | solution.py:318
  489.9 15.7 %collective-permute-start.55 = (bf16[1,288,768]{2,1,0:T(8,128)(2,1)S(1)}, bf16[1,288,768]{2,1,0:T(8,128)(2,1)S(1)}, u32[]{:S(2)}, u32[]{:S(2)}) collective-permute-start(bf16[1,288,768]{2,1,0:T(8,128)(2,1)S(1)} %collective-permute-done.53), channel_id=1, source_target_pairs={{0,8},{2,10},{8,16},{10,18},{16,24},{18,26},{24,28},{26,30},{28,20... | collective-permute-start | bytes 1327112 | tf_op jit(solution)/shard_map/ppermute | solution.py:318
  491.3 14.3 %collective-permute-start.56 = (bf16[1,288,768]{2,1,0:T(8,128)(2,1)S(1)}, bf16[1,288,768]{2,1,0:T(8,128)(2,1)S(1)}, u32[]{:S(2)}, u32[]{:S(2)}) collective-permute-start(bf16[1,288,768]{2,1,0:T(8,128)(2,1)S(1)} %collective-permute-done.54), channel_id=1, source_target_pairs={{0,4},{2,6},{8,0},{10,2},{16,8},{18,10},{24,16},{26,18},{28,24},{3... | collective-permute-start | bytes 1327112 | tf_op jit(solution)/shard_map/ppermute | solution.py:318
  492.3 10.8 %collective-permute-start.28 = (bf16[1,72,1024]{2,1,0:T(8,128)(2,1)S(1)}, bf16[1,72,1024]{2,1,0:T(8,128)(2,1)S(1)}, u32[]{:S(2)}, u32[]{:S(2)}) collective-permute-start(bf16[1,72,1024]{2,1,0:T(8,128)(2,1)S(1)} %get-tuple-element.218), channel_id=1, source_target_pairs={{0,8},{2,10},{8,16},{10,18},{16,24},{18,26},{24,28},{26,30},{28,20... | collective-permute-start | bytes 442376 | tf_op jit(solution)/shard_map/ppermute | solution.py:318
  493.6 10.6 %collective-permute-start.35 = (bf16[1,72,1024]{2,1,0:T(8,128)(2,1)S(1)}, bf16[1,72,1024]{2,1,0:T(8,128)(2,1)S(1)}, u32[]{:S(2)}, u32[]{:S(2)}) collective-permute-start(bf16[1,72,1024]{2,1,0:T(8,128)(2,1)S(1)} %get-tuple-element.217), channel_id=1, source_target_pairs={{0,4},{2,6},{8,0},{10,2},{16,8},{18,10},{24,16},{26,18},{28,24},{3... | collective-permute-start | bytes 442376 | tf_op jit(solution)/shard_map/ppermute | solution.py:318
  523.4 11.6 %collective-permute-start.61 = (bf16[16,288,768]{2,1,0:T(8,128)(2,1)}, bf16[16,288,768]{2,1,0:T(8,128)(2,1)}, u32[]{:S(2)}, u32[]{:S(2)}) collective-permute-start(bf16[16,288,768]{2,1,0:T(8,128)(2,1)} %gather_pieces.2.refs_0_.refs_1_.refs_2_.refs_3_), channel_id=1, source_target_pairs={{0,2},{2,0},{4,6},{6,4},{8,10},{10,8},{12,14},{14,12},{16,18},{18,... | collective-permute-start | bytes 21233672 | tf_op jit(solution)/shard_map/ppermute | solution.py:261
  (107 other events, 970.5 us)

commit v5 on v4

--- a/solution.py
+++ b/solution.py
@@ -10,7 +10,9 @@
 bf16 = jnp.bfloat16
 halo = 8
 spare = 8
-big_vmem = pltpu.CompilerParams(vmem_limit_bytes=58 << 20)
+small_vmem = pltpu.CompilerParams(vmem_limit_bytes=26 << 20)
+forward_vmem = pltpu.CompilerParams(vmem_limit_bytes=40 << 20)
+big_vmem = pltpu.CompilerParams(vmem_limit_bytes=48 << 20)
 
 
 def cost(flops, moved, transcendentals=0):
@@ -123,7 +125,7 @@
             jax.ShapeDtypeStruct((members, 8, lanes), bf16),
             jax.ShapeDtypeStruct((1, rows), jnp.int32),
         ],
-        compiler_params=big_vmem,
+        compiler_params=small_vmem,
         cost_estimate=cost(2 * members * slots * rows * width, 5 * rows * width),
         name="pack",
     )(route.reshape(1, rows), tokens)
@@ -151,7 +153,7 @@
         ],
         out_specs=pl.BlockSpec((group, slots, width), lambda j: (j, 0, 0)),
         out_shape=jax.ShapeDtypeStruct((members, slots, width), bf16),
-        compiler_params=big_vmem,
+        compiler_params=small_vmem,
         cost_estimate=cost(2 * members * slots * rows * width, 5 * rows * width),
         name="send_rows",
     )(slot_of, source)
@@ -208,7 +210,7 @@
             jax.ShapeDtypeStruct((bases.shape[0], count, width), bf16),
             jax.ShapeDtypeStruct((members, slots), jnp.int32),
         ],
-        compiler_params=big_vmem,
+        compiler_params=small_vmem,
         cost_estimate=cost(0, (bases.shape[0] * count + members * slots) * width // 8),
         name="place_rows",
     )(bases, digits, got)
@@ -234,7 +236,7 @@
         ],
         out_specs=pl.BlockSpec((block, width), lambda i: (i, 0)),
         out_shape=jax.ShapeDtypeStruct((count, width), dtype),
-        compiler_params=big_vmem,
+        compiler_params=small_vmem,
         cost_estimate=cost(2 * count * total * width, 2 * (count + total) * width),
         name="take_rows",
     )(ids, source)
@@ -371,7 +373,7 @@
         in_specs=[vmem] * count,
         out_specs=vmem,
         out_shape=jax.ShapeDtypeStruct((count, *pieces[0].shape), bf16),
-        compiler_params=big_vmem,
+        compiler_params=small_vmem,
         cost_estimate=cost(0, 4 * count * pieces[0].size),
         name="gather_pieces",
     )(*pieces)
@@ -423,7 +425,7 @@
         ],
         out_specs=[whole, whole, wide, wide, wide],
         out_shape=[jax.ShapeDtypeStruct((r, d), f32)] * 2 + [jax.ShapeDtypeStruct((r, hid), bf16)] * 3,
-        compiler_params=big_vmem,
+        compiler_params=forward_vmem,
         cost_estimate=cost(24 * r * d * hid, 6 * (d + r) * hid + 12 * r * d, 2 * r * hid),
         name="feed_forward",
     )(x, g, wg, wu, wd)
@@ -572,7 +574,7 @@
         ),
         out_shape=[jax.ShapeDtypeStruct(shape, f32) for shape in shapes],
         input_output_aliases={1 + 4 * group + k: k for k in range(len(so_far))},
-        compiler_params=big_vmem,
+        compiler_params=small_vmem,
         cost_estimate=cost(0, 24 * width * hidden // steps),
         name="open_ff",
     )(order, *[mine] * (2 * group), *[other] * (2 * group), *so_far)
@@ -616,7 +618,7 @@
             out_specs=[out, out],
         ),
         out_shape=[jax.ShapeDtypeStruct((nodes, count, width), bf16)] * 2,
-        compiler_params=big_vmem,
+        compiler_params=small_vmem,
         cost_estimate=cost(0, 2 * (grad_in.size + grad_out.size)),
         name="pack_conv",
     )(core, grad_in, grad_out, tail)
@@ -666,7 +668,7 @@
             jax.ShapeDtypeStruct((deep_total, width), f32),
             jax.ShapeDtypeStruct((blocks, spared, width), f32),
         ],
-        compiler_params=big_vmem,
+        compiler_params=small_vmem,
         cost_estimate=cost(0, 8 * (total + deep_total) * width),
         name="open_conv",
     )(ring.order(), *[mine] * (2 * group), *[other] * (2 * group))

time: 603 us -> 569 us (0.944)
  Pallas kernels: 175 us -> 127 us
  local copies, waits for them, and re-layouts: 24.3 us -> 34.4 us
  waiting for transfers between devices: 195 us -> 202 us
    unnamed x155 -> x141, local copies, waits for them, and re-layouts: 9.75 us -> 22.9 us
    pallas_call x2, Pallas kernels: 9.71 us -> 0.61 us  [gather_pieces(): pl.pallas_call(gather_kernel, in_specs=[vmem] * count, out_specs=vmem, ou...]
    pallas_call x4, Pallas kernels: 23.4 us -> 15 us  [open_ff(): pl.pallas_call(kernel, grid_spec=pltpu.PrefetchScalarGridSpec(num_scalar_...]
    pallas_call x2, Pallas kernels: 9.3 us -> 2.57 us  [pack_conv(): pl.pallas_call(pack_conv_kernel, grid_spec=pltpu.PrefetchScalarGridSpec(n...]
    pallas_call x2, Pallas kernels: 50.2 us -> 44.1 us  [feed_forward(): pl.pallas_call(lambda *refs: ff_kernel(sub, *refs), grid=(hid // chunk,),...]
  transfers between devices with their start and end apart: 77 -> 77, of which waited for: 40 -> 44; matrix products, arithmetic and copies ran while one was open for 14% -> 14% of each run, Pallas kernels for 17% -> 13%
where the time goes in v5:
time: 569 us; the launch traced here: 565 us
  waiting for transfers between devices  202 us (36%)
  Pallas kernels  127 us (22%)
  starting transfers between devices  116 us (20%)
  other arithmetic  62.2 us (11%)
  local copies, waits for them, and re-layouts  34.4 us (6%)
  matrix products  21.6 us (4%)
    ppermute x56, waiting for transfers between devices, send(): return lax.ppermute(value, 'dp', pairs)  123 us
    ppermute x56, starting transfers between devices, send(): return lax.ppermute(value, 'dp', pairs)  70.2 us
    pallas_call x2, Pallas kernels, feed_forward(): pl.pallas_call(lambda *refs: ff_kernel(sub, *refs), grid=(hid // chunk,),...  44.1 us
    ppermute x11, waiting for transfers between devices, swap_mp(): return lax.ppermute(value, 'mp', [(0, 1), (1, 0)])  41.2 us
    pallas_call x2, Pallas kernels, ff_grads(): pl.pallas_call(lambda s, *refs: grads_kernel(*refs), grid_spec=pltpu.Pref...  33.3 us
    all_to_all x1, waiting for transfers between devices, on_device(): got_rows = lax.all_to_all(sent_rows, 'dp', **over)  29.6 us
    convert_element_type x14, other arithmetic, step(): came = (came.astype(f32) + own).astype(bf16)  26.5 us
    unnamed x141, local copies, waits for them, and re-layouts  22.9 us
  transfers between devices with their start and end apart: 77, of which 44 were waited for; matrix products, arithmetic and copies ran while one was open for 14% of the time, Pallas kernels for 13%

profile of v5, /device:TPU:0, one launch (start us, length us, event | category | flops | bytes accessed | tf_op | source)
XLA Modules:
  0.0 565.4 jit_solution(2948555168647752146)
XLA Ops:
  3.9 4.2 pack.1
  8.1 7.5 %all-to-all-start = ((bf16[16,104,512]{2,1,0:T(8,128)(2,1)}), bf16[16,104,512]{2,1,0:T(8,128)(2,1)S(1)}, u32[]{:S(2)}, u32[]{:S(2)}) async-start(bf16[16,104,512]{2,1,0:T(8,128)(2,1)} %get-tuple-element.99), calls=%async_computation | async-start | bytes 3407872 | tf_op jit(solution)/shard_map/all_to_all | solution.py:722
  20.3 29.6 %all-to-all-done.refs_1_.refs_2_ = bf16[16,104,512]{2,1,0:T(8,128)(2,1)S(1)} async-done(((bf16[16,104,512]{2,1,0:T(8,128)(2,1)}), bf16[16,104,512]{2,1,0:T(8,128)(2,1)S(1)}, u32[]{:S(2)}, u32[]{:S(2)}) %all-to-all-start) | async-done | bytes 1703968 | tf_op jit(solution)/shard_map/all_to_all | solution.py:722
  49.9 10.2 %all-to-all-start.1 = ((bf16[16,96,512]{2,1,0:T(8,128)(2,1)}), bf16[16,96,512]{2,1,0:T(8,128)(2,1)S(1)}, u32[]{:S(2)}, u32[]{:S(2)}) async-start(bf16[16,96,512]{2,1,0:T(8,128)(2,1)} %copy-done.9), calls=%async_computation.1 | async-start | bytes 3145728 | tf_op jit(solution)/shard_map/all_to_all | solution.py:725
  60.1 3.5 place_rows.2
  69.7 13.7 %collective-permute-done = bf16[528,512]{1,0:T(8,128)(2,1)} collective-permute-done((bf16[528,512]{1,0:T(8,128)(2,1)}, bf16[528,512]{1,0:T(8,128)(2,1)}, u32[]{:S(2)}, u32[]{:S(2)}) %collective-permute-start) | collective-permute-done | bytes 540704 | tf_op jit(solution)/shard_map/ppermute | solution.py:246
  83.3 3.0 maximum_select_fusion
  92.4 3.8 place_rows.3
  98.6 3.5 convolution_bitcast_fusion
  102.1 8.7 %collective-permute-done.3 = bf16[512,512]{1,0:T(8,128)(2,1)S(1)} collective-permute-done((bf16[512,512]{1,0:T(8,128)(2,1)S(1)}, bf16[512,512]{1,0:T(8,128)(2,1)S(1)}, u32[]{:S(2)}, u32[]{:S(2)}) %collective-permute-start.3) | collective-permute-done | bytes 524320 | tf_op jit(solution)/shard_map/ppermute | solution.py:246
  112.9 3.4 fusion.3
  122.2 21.8 %feed_forward.2 = (f32[512,1024]{1,0:T(8,128)S(1)}, f32[512,1024]{1,0:T(8,128)S(1)}, bf16[512,2304]{1,0:T(8,128)(2,1)S(1)}, bf16[512,2304]{1,0:T(8,128)(2,1)S(1)}, bf16[512,2304]{1,0:T(8,128)(2,1)S(1)}) custom-call(bf16[512,1024]{1,0:T(8,128)(2,1)S(1)} %multiply_convert_fusion.1.refs_0_, bf16[512,1024]{1,0:T(8,128)(2,1)S(1)} %maximum_select_fusion.1.refs_1_.refs_8_, ...), custom_call_target="tpu_custom_call" | custom-call | flops 28991029248 | bytes 27525120 | tf_op jit(solution)/shard_map/feed_forward/pallas_call | solution.py:416
  149.6 6.3 %collective-permute-done.6 = bf16[512,512]{1,0:T(8,128)(2,1)S(1)} collective-permute-done((bf16[512,512]{1,0:T(8,128)(2,1)S(1)}, bf16[512,512]{1,0:T(8,128)(2,1)S(1)}, u32[]{:S(2)}, u32[]{:S(2)}) %collective-permute-start.6) | collective-permute-done | bytes 524320 | tf_op jit(solution)/shard_map/ppermute | solution.py:246
  156.2 22.4 %feed_forward.3 = (f32[512,1024]{1,0:T(8,128)S(1)}, f32[512,1024]{1,0:T(8,128)S(1)}, bf16[512,2304]{1,0:T(8,128)(2,1)S(1)}, bf16[512,2304]{1,0:T(8,128)(2,1)S(1)}, bf16[512,2304]{1,0:T(8,128)(2,1)S(1)}) custom-call(bf16[512,1024]{1,0:T(8,128)(2,1)S(1)} %collective-permute-done.5.refs_0_.refs_1_, bf16[512,1024]{1,0:T(8,128)(2,1)S(1)} %maximum_select_fusion.2.refs_1_.refs_9_, ...), custom_call_target="tpu_custom_call" | custom-call | flops 28991029248 | bytes 27525120 | tf_op jit(solution)/shard_map/feed_forward/pallas_call | solution.py:416
  183.8 16.8 %ff_grads.2 = bf16[8,576,768]{2,1,0:T(8,128)(2,1)} custom-call(s32[1]{0:T(128)} %bitcast.22.s, bf16[512,1024]{1,0:T(8,128)(2,1)S(1)} %multiply_convert_fusion.1.refs_0_, bf16[512,1024]{1,0:T(8,128)(2,1)S(1)} %collective-permute-done.5.refs_0_.refs_1_, bf16[512,2304]{1,0:T(8,128)(2,1)} %copy-done.26, bf16[512,2304]{1,0:T(8,128)(2,1)} %copy-done.29, ...), custom_call_target="tpu_custom_call" | custom-call | flops 14495514624 | bytes 18874368 | tf_op jit(solution)/shard_map/ff_grads/pallas_call | solution.py:474
  202.7 2.9 convert_element_type.492
  207.6 16.5 %ff_grads.3 = bf16[8,576,768]{2,1,0:T(8,128)(2,1)} custom-call(s32[1]{0:T(128)} %bitcast.21.s.core_ref, bf16[512,1024]{1,0:T(8,128)(2,1)S(1)} %copy-done.14, bf16[512,1024]{1,0:T(8,128)(2,1)S(1)} %copy-done.23, bf16[512,2304]{1,0:T(8,128)(2,1)} %copy-done.26, bf16[512,2304]{1,0:T(8,128)(2,1)} %copy-done.29, bf16[512,2304]{1,0:T(8,128)(2,1)} %copy-done.27, ...), custom_call_target="tpu_custom_call" | custom-call | flops 14495514624 | bytes 18874368 | tf_op jit(solution)/shard_map/ff_grads/pallas_call | solution.py:474
  224.2 7.3 %collective-permute-done.7 = bf16[520,1024]{1,0:T(8,128)(2,1)S(1)} collective-permute-done((bf16[520,1024]{1,0:T(8,128)(2,1)S(1)}, bf16[520,1024]{1,0:T(8,128)(2,1)S(1)}, u32[]{:S(2)}, u32[]{:S(2)}) %collective-permute-start.7) | collective-permute-done | bytes 1064992 | tf_op jit(solution)/shard_map/ppermute | solution.py:246
  235.3 4.8 collective-permute-start.10
  265.5 5.4 convolution_convert_fusion
  279.6 4.4 all-to-all-start.2
  284.8 2.8 add_convert_fusion.10
  287.6 8.8 %fusion.18 = (bf16[1024]{0:T(1024)(128)(2,1)S(1)}, f32[512]{0:T(512)S(1)}, f32[512,1024,1]{1,0,2:T(8,128)}) fusion(f32[528,1024]{1,0:T(8,128)S(1)} %copy-done.40, f32[512]{0:T(512)S(1)} %slice.240, f32[1024]{0:T(1024)S(1)} %copy-done.63, bf16[3,512,1024]{2,1,0:T(8,128)(2,1)} %pad_maximum_fusion, bf16[3,512,512]{2,1,0:T(8,128)(2,1)} %slice.260, ...), kind=kOutput, calls=%fused_computation.52 | convolution fusion | flops 3243244032 | bytes 13641728 | tf_op jit(solution)/shard_map/krc,kdc->rd/dot_general | solution.py:886
  309.4 4.6 collective-permute-done.17
  316.1 2.9 take_rows.6
  319.0 9.4 %all-to-all-start.3 = ((bf16[16,96,512]{2,1,0:T(8,128)(2,1)}), bf16[16,96,512]{2,1,0:T(8,128)(2,1)}, u32[]{:S(2)}, u32[]{:S(2)}) async-start(bf16[16,96,512]{2,1,0:T(8,128)(2,1)} %bitcast.32), calls=%async_computation.3 | async-start | bytes 3145728 | tf_op jit(solution)/shard_map/all_to_all | solution.py:834
  330.5 3.4 collective-permute-start.39
  333.9 30.5 %collective-permute-done.39 = bf16[1,288,768]{2,1,0:T(8,128)(2,1)S(1)} collective-permute-done((bf16[1,288,768]{2,1,0:T(8,128)(2,1)S(1)}, bf16[1,288,768]{2,1,0:T(8,128)(2,1)S(1)}, u32[]{:S(2)}, u32[]{:S(2)}) %collective-permute-start.39) | collective-permute-done | bytes 442400 | tf_op jit(solution)/shard_map/ppermute | solution.py:320
  368.8 10.0 %collective-permute-start.41 = (bf16[1,288,768]{2,1,0:T(8,128)(2,1)}, bf16[1,288,768]{2,1,0:T(8,128)(2,1)S(1)}, u32[]{:S(2)}, u32[]{:S(2)}) collective-permute-start(bf16[1,288,768]{2,1,0:T(8,128)(2,1)} %get-tuple-element.140), channel_id=1, source_target_pairs={{0,8},{2,10},{8,16},{10,18},{16,24},{18,26},{24,28},{26,30},{28,20... | collective-permute-start | bytes 1327112 | tf_op jit(solution)/shard_map/ppermute | solution.py:320
  378.8 9.5 %collective-permute-done.41 = bf16[1,288,768]{2,1,0:T(8,128)(2,1)S(1)} collective-permute-done((bf16[1,288,768]{2,1,0:T(8,128)(2,1)}, bf16[1,288,768]{2,1,0:T(8,128)(2,1)S(1)}, u32[]{:S(2)}, u32[]{:S(2)}) %collective-permute-start.41) | collective-permute-done | bytes 442400 | tf_op jit(solution)/shard_map/ppermute | solution.py:320
  399.5 4.3 take_rows.5
  403.7 5.3 collective-permute-done.21
  422.7 6.5 %collective-permute-done.45 = bf16[1,288,768]{2,1,0:T(8,128)(2,1)S(1)} collective-permute-done((bf16[1,288,768]{2,1,0:T(8,128)(2,1)S(1)}, bf16[1,288,768]{2,1,0:T(8,128)(2,1)S(1)}, u32[]{:S(2)}, u32[]{:S(2)}) %collective-permute-start.45) | collective-permute-done | bytes 442400 | tf_op jit(solution)/shard_map/ppermute | solution.py:320
  434.3 4.5 take_rows.7
  443.9 8.2 %collective-permute-done.25 = bf16[1,72,1024]{2,1,0:T(8,128)(2,1)S(1)} collective-permute-done((bf16[1,72,1024]{2,1,0:T(8,128)(2,1)S(1)}, bf16[1,72,1024]{2,1,0:T(8,128)(2,1)S(1)}, u32[]{:S(2)}, u32[]{:S(2)}) %collective-permute-start.25) | collective-permute-done | bytes 147488 | tf_op jit(solution)/shard_map/ppermute | solution.py:320
  458.0 8.0 %collective-permute-done.26 = bf16[1,72,1024]{2,1,0:T(8,128)(2,1)S(1)} collective-permute-done((bf16[1,72,1024]{2,1,0:T(8,128)(2,1)S(1)}, bf16[1,72,1024]{2,1,0:T(8,128)(2,1)S(1)}, u32[]{:S(2)}, u32[]{:S(2)}) %collective-permute-start.26) | collective-permute-done | bytes 147488 | tf_op jit(solution)/shard_map/ppermute | solution.py:320
  471.8 7.8 %collective-permute-done.27 = bf16[1,72,1024]{2,1,0:T(8,128)(2,1)S(1)} collective-permute-done((bf16[1,72,1024]{2,1,0:T(8,128)(2,1)S(1)}, bf16[1,72,1024]{2,1,0:T(8,128)(2,1)S(1)}, u32[]{:S(2)}, u32[]{:S(2)}) %collective-permute-start.27) | collective-permute-done | bytes 147488 | tf_op jit(solution)/shard_map/ppermute | solution.py:320
  485.4 8.9 %collective-permute-done.28 = bf16[1,72,1024]{2,1,0:T(8,128)(2,1)S(1)} collective-permute-done((bf16[1,72,1024]{2,1,0:T(8,128)(2,1)S(1)}, bf16[1,72,1024]{2,1,0:T(8,128)(2,1)S(1)}, u32[]{:S(2)}, u32[]{:S(2)}) %collective-permute-start.28) | collective-permute-done | bytes 147488 | tf_op jit(solution)/shard_map/ppermute | solution.py:320
  498.8 6.0 %collective-permute-done.57 = bf16[1,288,768]{2,1,0:T(8,128)(2,1)S(1)} collective-permute-done((bf16[1,288,768]{2,1,0:T(8,128)(2,1)S(1)}, bf16[1,288,768]{2,1,0:T(8,128)(2,1)S(1)}, u32[]{:S(2)}, u32[]{:S(2)}) %collective-permute-start.57) | collective-permute-done | bytes 442400 | tf_op jit(solution)/shard_map/ppermute | solution.py:320
  509.7 4.2 collective-permute-done.29
  518.9 3.7 open_ff.4
  524.7 3.7 open_ff.5
  531.8 3.7 open_ff.6
  537.6 3.7 open_ff.7
  544.5 4.6 collective-permute-done.68
  551.1 3.1 collective-permute-done.69
  555.2 4.5 collective-permute-done.72.refs_9_.refs_10_.refs_11_.refs_12_.refs_13_.refs_14_.refs_15_.refs_16_
  559.7 4.2 open_conv.1
  (367 shorter events, 186.7 us)
Async XLA Ops:
  8.1 41.8 %all-to-all-start = ((bf16[16,104,512]{2,1,0:T(8,128)(2,1)}), bf16[16,104,512]{2,1,0:T(8,128)(2,1)S(1)}, u32[]{:S(2)}, u32[]{:S(2)}) async-start(bf16[16,104,512]{2,1,0:T(8,128)(2,1)} %get-tuple-element.99), calls=%async_computation | async-start | bytes 3407872 | tf_op jit(solution)/shard_map/all_to_all | solution.py:722
  15.6 49.0 %collective-permute-start.1 = (bf16[4,512,512]{2,1,0:T(8,128)(2,1)}, bf16[4,512,512]{2,1,0:T(8,128)(2,1)}, u32[]{:S(2)}, u32[]{:S(2)}) collective-permute-start(bf16[4,512,512]{2,1,0:T(8,128)(2,1)} %pad_maximum_fusion.1), channel_id=1, source_target_pairs={{0,1},{1,0},{2,3},{3,2},{4,5},{5,4},{6,7},{7,6},{8,9},{9,8},{10,11... | collective-permute-start | bytes 6291464 | tf_op jit(solution)/shard_map/ppermute | solution.py:246
  49.9 42.5 %all-to-all-start.1 = ((bf16[16,96,512]{2,1,0:T(8,128)(2,1)}), bf16[16,96,512]{2,1,0:T(8,128)(2,1)S(1)}, u32[]{:S(2)}, u32[]{:S(2)}) async-start(bf16[16,96,512]{2,1,0:T(8,128)(2,1)} %copy-done.9), calls=%async_computation.1 | async-start | bytes 3145728 | tf_op jit(solution)/shard_map/all_to_all | solution.py:725
  64.6 21.7 %collective-permute-start.2 = (bf16[4,512,512]{2,1,0:T(8,128)(2,1)}, bf16[4,512,512]{2,1,0:T(8,128)(2,1)}, u32[]{:S(2)}, u32[]{:S(2)}) collective-permute-start(bf16[4,512,512]{2,1,0:T(8,128)(2,1)} %collective-permute-done.1), channel_id=1, source_target_pairs={{0,2},{2,0},{4,6},{6,4},{8,10},{10,8},{12,14},{14,12},{16,18},{18,... | collective-permute-start | bytes 6291464 | tf_op jit(solution)/shard_map/ppermute | solution.py:263
  69.1 14.3 %collective-permute-start = (bf16[528,512]{1,0:T(8,128)(2,1)}, bf16[528,512]{1,0:T(8,128)(2,1)}, u32[]{:S(2)}, u32[]{:S(2)}) collective-permute-start(bf16[528,512]{1,0:T(8,128)(2,1)} %get-tuple-element.238), channel_id=1, source_target_pairs={{0,1},{1,0},{2,3},{3,2},{4,5},{5,4},{6,7},{7,6},{8,9},{9,8},{10,11... | collective-permute-start | bytes 1622024 | tf_op jit(solution)/shard_map/ppermute | solution.py:246
  96.6 14.3 %collective-permute-start.3 = (bf16[512,512]{1,0:T(8,128)(2,1)S(1)}, bf16[512,512]{1,0:T(8,128)(2,1)S(1)}, u32[]{:S(2)}, u32[]{:S(2)}) collective-permute-start(bf16[512,512]{1,0:T(8,128)(2,1)S(1)} %get-tuple-element.246), channel_id=1, source_target_pairs={{0,1},{1,0},{2,3},{3,2},{4,5},{5,4},{6,7},{7,6},{8,9},{9,8},{10,11... | collective-permute-start | bytes 1572872 | tf_op jit(solution)/shard_map/ppermute | solution.py:246
  119.9 36.4 %collective-permute-start.5 = (bf16[512,1024]{1,0:T(8,128)(2,1)S(1)}, bf16[512,1024]{1,0:T(8,128)(2,1)S(1)}, u32[]{:S(2)}, u32[]{:S(2)}) collective-permute-start(bf16[512,1024]{1,0:T(8,128)(2,1)S(1)} %multiply_convert_fusion.1.refs_0_), channel_id=1, source_target_pairs={{0,1},{1,0},{2,3},{3,2},{4,5},{5,4},{6,7},{7,6},{8,9},{9,8},{10,11... | collective-permute-start | bytes 3145736 | tf_op jit(solution)/shard_map/ppermute | solution.py:246
  121.4 34.5 %collective-permute-start.6 = (bf16[512,512]{1,0:T(8,128)(2,1)S(1)}, bf16[512,512]{1,0:T(8,128)(2,1)S(1)}, u32[]{:S(2)}, u32[]{:S(2)}) collective-permute-start(bf16[512,512]{1,0:T(8,128)(2,1)S(1)} %get-tuple-element.110), channel_id=1, source_target_pairs={{0,1},{1,0},{2,3},{3,2},{4,5},{5,4},{6,7},{7,6},{8,9},{9,8},{10,11... | collective-permute-start | bytes 1572872 | tf_op jit(solution)/shard_map/ppermute | solution.py:246
  200.7 32.9 %collective-permute-start.9 = (bf16[8,576,768]{2,1,0:T(8,128)(2,1)}, bf16[8,576,768]{2,1,0:T(8,128)(2,1)}, u32[]{:S(2)}, u32[]{:S(2)}) collective-permute-start(bf16[8,576,768]{2,1,0:T(8,128)(2,1)} %ff_grads.2), channel_id=1, source_target_pairs={{0,2},{2,0},{4,6},{6,4},{8,10},{10,8},{12,14},{14,12},{16,18},{18,... | collective-permute-start | bytes 21233672 | tf_op jit(solution)/shard_map/ppermute | solution.py:263
  205.7 25.7 %collective-permute-start.7 = (bf16[520,1024]{1,0:T(8,128)(2,1)S(1)}, bf16[520,1024]{1,0:T(8,128)(2,1)S(1)}, u32[]{:S(2)}, u32[]{:S(2)}) collective-permute-start(bf16[520,1024]{1,0:T(8,128)(2,1)S(1)} %copy-done.51), channel_id=1, source_target_pairs={{0,1},{1,0},{2,3},{3,2},{4,5},{5,4},{6,7},{7,6},{8,9},{9,8},{10,11... | collective-permute-start | bytes 3194888 | tf_op jit(solution)/shard_map/ppermute | solution.py:246
  231.4 32.5 %collective-permute-start.8 = (bf16[512,1024]{1,0:T(8,128)(2,1)S(1)}, bf16[512,1024]{1,0:T(8,128)(2,1)S(1)}, u32[]{:S(2)}, u32[]{:S(2)}) collective-permute-start(bf16[512,1024]{1,0:T(8,128)(2,1)S(1)} %convert_element_type.498), channel_id=1, source_target_pairs={{0,1},{1,0},{2,3},{3,2},{4,5},{5,4},{6,7},{7,6},{8,9},{9,8},{10,11... | collective-permute-start | bytes 3145736 | tf_op jit(solution)/shard_map/ppermute | solution.py:246
  235.3 13.7 %collective-permute-start.10 = (bf16[1,288,768]{2,1,0:T(8,128)(2,1)S(1)}, bf16[1,288,768]{2,1,0:T(8,128)(2,1)S(1)}, u32[]{:S(2)}, u32[]{:S(2)}) collective-permute-start(bf16[1,288,768]{2,1,0:T(8,128)(2,1)S(1)} %get-tuple-element.214), channel_id=1, source_target_pairs={{0,8},{2,10},{8,16},{10,18},{16,24},{18,26},{24,28},{26,30},{28,20... | collective-permute-start | bytes 1327112 | tf_op jit(solution)/shard_map/ppermute | solution.py:320
  240.2 11.0 %collective-permute-start.11 = (bf16[1,288,768]{2,1,0:T(8,128)(2,1)S(1)}, bf16[1,288,768]{2,1,0:T(8,128)(2,1)S(1)}, u32[]{:S(2)}, u32[]{:S(2)}) collective-permute-start(bf16[1,288,768]{2,1,0:T(8,128)(2,1)S(1)} %get-tuple-element.213), channel_id=1, source_target_pairs={{0,4},{2,6},{8,0},{10,2},{16,8},{18,10},{24,16},{26,18},{28,24},{3... | collective-permute-start | bytes 1327112 | tf_op jit(solution)/shard_map/ppermute | solution.py:320
  252.9 18.0 %collective-permute-start.13 = (bf16[1,288,768]{2,1,0:T(8,128)(2,1)S(1)}, bf16[1,288,768]{2,1,0:T(8,128)(2,1)S(1)}, u32[]{:S(2)}, u32[]{:S(2)}) collective-permute-start(bf16[1,288,768]{2,1,0:T(8,128)(2,1)S(1)} %get-tuple-element.212), channel_id=1, source_target_pairs={{0,8},{2,10},{8,16},{10,18},{16,24},{18,26},{24,28},{26,30},{28,20... | collective-permute-start | bytes 1327112 | tf_op jit(solution)/shard_map/ppermute | solution.py:320
  253.7 17.2 %collective-permute-start.15 = (bf16[1,288,768]{2,1,0:T(8,128)(2,1)S(1)}, bf16[1,288,768]{2,1,0:T(8,128)(2,1)S(1)}, u32[]{:S(2)}, u32[]{:S(2)}) collective-permute-start(bf16[1,288,768]{2,1,0:T(8,128)(2,1)S(1)} %get-tuple-element.211), channel_id=1, source_target_pairs={{0,4},{2,6},{8,0},{10,2},{16,8},{18,10},{24,16},{26,18},{28,24},{3... | collective-permute-start | bytes 1327112 | tf_op jit(solution)/shard_map/ppermute | solution.py:320
  264.9 11.4 %collective-permute-start.12 = (bf16[512,512]{1,0:T(8,128)(2,1)S(1)}, bf16[512,512]{1,0:T(8,128)(2,1)S(1)}, u32[]{:S(2)}, u32[]{:S(2)}) collective-permute-start(bf16[512,512]{1,0:T(8,128)(2,1)S(1)} %get-tuple-element.244), channel_id=1, source_target_pairs={{0,1},{1,0},{2,3},{3,2},{4,5},{5,4},{6,7},{7,6},{8,9},{9,8},{10,11... | collective-permute-start | bytes 1572872 | tf_op jit(solution)/shard_map/ppermute | solution.py:246
  273.6 10.4 %collective-permute-start.14 = (bf16[1,288,768]{2,1,0:T(8,128)(2,1)}, bf16[1,288,768]{2,1,0:T(8,128)(2,1)S(1)}, u32[]{:S(2)}, u32[]{:S(2)}) collective-permute-start(bf16[1,288,768]{2,1,0:T(8,128)(2,1)} %get-tuple-element.210), channel_id=1, source_target_pairs={{0,8},{2,10},{8,16},{10,18},{16,24},{18,26},{24,28},{26,30},{28,20... | collective-permute-start | bytes 1327112 | tf_op jit(solution)/shard_map/ppermute | solution.py:320
  274.4 10.4 %collective-permute-start.16 = (bf16[1,288,768]{2,1,0:T(8,128)(2,1)}, bf16[1,288,768]{2,1,0:T(8,128)(2,1)}, u32[]{:S(2)}, u32[]{:S(2)}) collective-permute-start(bf16[1,288,768]{2,1,0:T(8,128)(2,1)} %get-tuple-element.209), channel_id=1, source_target_pairs={{0,4},{2,6},{8,0},{10,2},{16,8},{18,10},{24,16},{26,18},{28,24},{3... | collective-permute-start | bytes 1327112 | tf_op jit(solution)/shard_map/ppermute | solution.py:320
  279.6 36.5 %all-to-all-start.2 = ((bf16[16,96,512]{2,1,0:T(8,128)(2,1)}), bf16[16,96,512]{2,1,0:T(8,128)(2,1)}, u32[]{:S(2)}, u32[]{:S(2)}) async-start(bf16[16,96,512]{2,1,0:T(8,128)(2,1)} %bitcast.144), calls=%async_computation.2 | async-start | bytes 3145728 | tf_op jit(solution)/shard_map/all_to_all | solution.py:834
  299.2 14.8 %collective-permute-start.17 = (bf16[512,512]{1,0:T(8,128)(2,1)S(1)}, bf16[512,512]{1,0:T(8,128)(2,1)S(1)}, u32[]{:S(2)}, u32[]{:S(2)}) collective-permute-start(bf16[512,512]{1,0:T(8,128)(2,1)S(1)} %get-tuple-element.242), channel_id=1, source_target_pairs={{0,1},{1,0},{2,3},{3,2},{4,5},{5,4},{6,7},{7,6},{8,9},{9,8},{10,11... | collective-permute-start | bytes 1572872 | tf_op jit(solution)/shard_map/ppermute | solution.py:246
  300.2 28.3 %collective-permute-start.37 = (bf16[1,288,768]{2,1,0:T(8,128)(2,1)}, bf16[1,288,768]{2,1,0:T(8,128)(2,1)}, u32[]{:S(2)}, u32[]{:S(2)}) collective-permute-start(bf16[1,288,768]{2,1,0:T(8,128)(2,1)} %get-tuple-element.136), channel_id=1, source_target_pairs={{0,8},{2,10},{8,16},{10,18},{16,24},{18,26},{24,28},{26,30},{28,20... | collective-permute-start | bytes 1327112 | tf_op jit(solution)/shard_map/ppermute | solution.py:320
  302.0 26.5 %collective-permute-start.38 = (bf16[1,288,768]{2,1,0:T(8,128)(2,1)S(1)}, bf16[1,288,768]{2,1,0:T(8,128)(2,1)}, u32[]{:S(2)}, u32[]{:S(2)}) collective-permute-start(bf16[1,288,768]{2,1,0:T(8,128)(2,1)S(1)} %get-tuple-element.137), channel_id=1, source_target_pairs={{0,4},{2,6},{8,0},{10,2},{16,8},{18,10},{24,16},{26,18},{28,24},{3... | collective-permute-start | bytes 1327112 | tf_op jit(solution)/shard_map/ppermute | solution.py:320
  305.0 88.2 %collective-permute-start.20 = (bf16[8,144,1024]{2,1,0:T(8,128)(2,1)}, bf16[8,144,1024]{2,1,0:T(8,128)(2,1)}, u32[]{:S(2)}, u32[]{:S(2)}) collective-permute-start(bf16[8,144,1024]{2,1,0:T(8,128)(2,1)} %add_convert_fusion), channel_id=1, source_target_pairs={{0,1},{1,0},{2,3},{3,2},{4,5},{5,4},{6,7},{7,6},{8,9},{9,8},{10,11... | collective-permute-start | bytes 7077896 | tf_op jit(solution)/shard_map/ppermute | solution.py:246
  309.4 83.7 %collective-permute-start.19 = (bf16[8,144,1024]{2,1,0:T(8,128)(2,1)}, bf16[8,144,1024]{2,1,0:T(8,128)(2,1)}, u32[]{:S(2)}, u32[]{:S(2)}) collective-permute-start(bf16[8,144,1024]{2,1,0:T(8,128)(2,1)} %get-tuple-element.133), channel_id=1, source_target_pairs={{0,2},{2,0},{4,6},{6,4},{8,10},{10,8},{12,14},{14,12},{16,18},{18,... | collective-permute-start | bytes 7077896 | tf_op jit(solution)/shard_map/ppermute | solution.py:263
  319.0 97.0 %all-to-all-start.3 = ((bf16[16,96,512]{2,1,0:T(8,128)(2,1)}), bf16[16,96,512]{2,1,0:T(8,128)(2,1)}, u32[]{:S(2)}, u32[]{:S(2)}) async-start(bf16[16,96,512]{2,1,0:T(8,128)(2,1)} %bitcast.32), calls=%async_computation.3 | async-start | bytes 3145728 | tf_op jit(solution)/shard_map/all_to_all | solution.py:834
  330.5 33.9 %collective-permute-start.39 = (bf16[1,288,768]{2,1,0:T(8,128)(2,1)S(1)}, bf16[1,288,768]{2,1,0:T(8,128)(2,1)S(1)}, u32[]{:S(2)}, u32[]{:S(2)}) collective-permute-start(bf16[1,288,768]{2,1,0:T(8,128)(2,1)S(1)} %get-tuple-element.138), channel_id=1, source_target_pairs={{0,8},{2,10},{8,16},{10,18},{16,24},{18,26},{24,28},{26,30},{28,20... | collective-permute-start | bytes 1327112 | tf_op jit(solution)/shard_map/ppermute | solution.py:320
  333.9 32.4 %collective-permute-start.40 = (bf16[1,288,768]{2,1,0:T(8,128)(2,1)S(1)}, bf16[1,288,768]{2,1,0:T(8,128)(2,1)S(1)}, u32[]{:S(2)}, u32[]{:S(2)}) collective-permute-start(bf16[1,288,768]{2,1,0:T(8,128)(2,1)S(1)} %get-tuple-element.139), channel_id=1, source_target_pairs={{0,4},{2,6},{8,0},{10,2},{16,8},{18,10},{24,16},{26,18},{28,24},{3... | collective-permute-start | bytes 1327112 | tf_op jit(solution)/shard_map/ppermute | solution.py:320
  368.8 19.5 %collective-permute-start.41 = (bf16[1,288,768]{2,1,0:T(8,128)(2,1)}, bf16[1,288,768]{2,1,0:T(8,128)(2,1)S(1)}, u32[]{:S(2)}, u32[]{:S(2)}) collective-permute-start(bf16[1,288,768]{2,1,0:T(8,128)(2,1)} %get-tuple-element.140), channel_id=1, source_target_pairs={{0,8},{2,10},{8,16},{10,18},{16,24},{18,26},{24,28},{26,30},{28,20... | collective-permute-start | bytes 1327112 | tf_op jit(solution)/shard_map/ppermute | solution.py:320
  378.8 11.5 %collective-permute-start.42 = (bf16[1,288,768]{2,1,0:T(8,128)(2,1)S(1)}, bf16[1,288,768]{2,1,0:T(8,128)(2,1)}, u32[]{:S(2)}, u32[]{:S(2)}) collective-permute-start(bf16[1,288,768]{2,1,0:T(8,128)(2,1)S(1)} %get-tuple-element.141), channel_id=1, source_target_pairs={{0,4},{2,6},{8,0},{10,2},{16,8},{18,10},{24,16},{26,18},{28,24},{3... | collective-permute-start | bytes 1327112 | tf_op jit(solution)/shard_map/ppermute | solution.py:320
  395.1 19.0 %collective-permute-start.43 = (bf16[1,288,768]{2,1,0:T(8,128)(2,1)}, bf16[1,288,768]{2,1,0:T(8,128)(2,1)}, u32[]{:S(2)}, u32[]{:S(2)}) collective-permute-start(bf16[1,288,768]{2,1,0:T(8,128)(2,1)} %get-tuple-element.142), channel_id=1, source_target_pairs={{0,8},{2,10},{8,16},{10,18},{16,24},{18,26},{24,28},{26,30},{28,20... | collective-permute-start | bytes 1327112 | tf_op jit(solution)/shard_map/ppermute | solution.py:320
  396.2 17.8 %collective-permute-start.44 = (bf16[1,288,768]{2,1,0:T(8,128)(2,1)S(1)}, bf16[1,288,768]{2,1,0:T(8,128)(2,1)}, u32[]{:S(2)}, u32[]{:S(2)}) collective-permute-start(bf16[1,288,768]{2,1,0:T(8,128)(2,1)S(1)} %get-tuple-element.143), channel_id=1, source_target_pairs={{0,4},{2,6},{8,0},{10,2},{16,8},{18,10},{24,16},{26,18},{28,24},{3... | collective-permute-start | bytes 1327112 | tf_op jit(solution)/shard_map/ppermute | solution.py:320
  397.4 11.6 %collective-permute-start.21 = (bf16[1,72,1024]{2,1,0:T(8,128)(2,1)}, bf16[1,72,1024]{2,1,0:T(8,128)(2,1)S(1)}, u32[]{:S(2)}, u32[]{:S(2)}) collective-permute-start(bf16[1,72,1024]{2,1,0:T(8,128)(2,1)} %get-tuple-element.230), channel_id=1, source_target_pairs={{0,8},{2,10},{8,16},{10,18},{16,24},{18,26},{24,28},{26,30},{28,20... | collective-permute-start | bytes 442376 | tf_op jit(solution)/shard_map/ppermute | solution.py:320
  398.6 11.5 %collective-permute-start.22 = (bf16[1,72,1024]{2,1,0:T(8,128)(2,1)S(1)}, bf16[1,72,1024]{2,1,0:T(8,128)(2,1)S(1)}, u32[]{:S(2)}, u32[]{:S(2)}) collective-permute-start(bf16[1,72,1024]{2,1,0:T(8,128)(2,1)S(1)} %get-tuple-element.229), channel_id=1, source_target_pairs={{0,4},{2,6},{8,0},{10,2},{16,8},{18,10},{24,16},{26,18},{28,24},{3... | collective-permute-start | bytes 442376 | tf_op jit(solution)/shard_map/ppermute | solution.py:320
  416.1 13.2 %collective-permute-start.45 = (bf16[1,288,768]{2,1,0:T(8,128)(2,1)S(1)}, bf16[1,288,768]{2,1,0:T(8,128)(2,1)S(1)}, u32[]{:S(2)}, u32[]{:S(2)}) collective-permute-start(bf16[1,288,768]{2,1,0:T(8,128)(2,1)S(1)} %get-tuple-element.144), channel_id=1, source_target_pairs={{0,8},{2,10},{8,16},{10,18},{16,24},{18,26},{24,28},{26,30},{28,20... | collective-permute-start | bytes 1327112 | tf_op jit(solution)/shard_map/ppermute | solution.py:320
  416.7 13.1 %collective-permute-start.46 = (bf16[1,288,768]{2,1,0:T(8,128)(2,1)S(1)}, bf16[1,288,768]{2,1,0:T(8,128)(2,1)S(1)}, u32[]{:S(2)}, u32[]{:S(2)}) collective-permute-start(bf16[1,288,768]{2,1,0:T(8,128)(2,1)S(1)} %get-tuple-element.145), channel_id=1, source_target_pairs={{0,4},{2,6},{8,0},{10,2},{16,8},{18,10},{24,16},{26,18},{28,24},{3... | collective-permute-start | bytes 1327112 | tf_op jit(solution)/shard_map/ppermute | solution.py:320
  420.7 11.7 %collective-permute-start.24 = (bf16[1,72,1024]{2,1,0:T(8,128)(2,1)S(1)}, bf16[1,72,1024]{2,1,0:T(8,128)(2,1)S(1)}, u32[]{:S(2)}, u32[]{:S(2)}) collective-permute-start(bf16[1,72,1024]{2,1,0:T(8,128)(2,1)S(1)} %get-tuple-element.226), channel_id=1, source_target_pairs={{0,8},{2,10},{8,16},{10,18},{16,24},{18,26},{24,28},{26,30},{28,20... | collective-permute-start | bytes 442376 | tf_op jit(solution)/shard_map/ppermute | solution.py:320
  421.3 11.7 %collective-permute-start.31 = (bf16[1,72,1024]{2,1,0:T(8,128)(2,1)S(1)}, bf16[1,72,1024]{2,1,0:T(8,128)(2,1)S(1)}, u32[]{:S(2)}, u32[]{:S(2)}) collective-permute-start(bf16[1,72,1024]{2,1,0:T(8,128)(2,1)S(1)} %get-tuple-element.225), channel_id=1, source_target_pairs={{0,4},{2,6},{8,0},{10,2},{16,8},{18,10},{24,16},{26,18},{28,24},{3... | collective-permute-start | bytes 442376 | tf_op jit(solution)/shard_map/ppermute | solution.py:320
  439.9 14.0 %collective-permute-start.49 = (bf16[1,288,768]{2,1,0:T(8,128)(2,1)S(1)}, bf16[1,288,768]{2,1,0:T(8,128)(2,1)S(1)}, u32[]{:S(2)}, u32[]{:S(2)}) collective-permute-start(bf16[1,288,768]{2,1,0:T(8,128)(2,1)S(1)} %collective-permute-done.47), channel_id=1, source_target_pairs={{0,8},{2,10},{8,16},{10,18},{16,24},{18,26},{24,28},{26,30},{28,20... | collective-permute-start | bytes 1327112 | tf_op jit(solution)/shard_map/ppermute | solution.py:320
  440.6 13.2 %collective-permute-start.50 = (bf16[1,288,768]{2,1,0:T(8,128)(2,1)S(1)}, bf16[1,288,768]{2,1,0:T(8,128)(2,1)S(1)}, u32[]{:S(2)}, u32[]{:S(2)}) collective-permute-start(bf16[1,288,768]{2,1,0:T(8,128)(2,1)S(1)} %collective-permute-done.48), channel_id=1, source_target_pairs={{0,4},{2,6},{8,0},{10,2},{16,8},{18,10},{24,16},{26,18},{28,24},{3... | collective-permute-start | bytes 1327112 | tf_op jit(solution)/shard_map/ppermute | solution.py:320
  453.9 13.8 %collective-permute-start.51 = (bf16[1,288,768]{2,1,0:T(8,128)(2,1)S(1)}, bf16[1,288,768]{2,1,0:T(8,128)(2,1)S(1)}, u32[]{:S(2)}, u32[]{:S(2)}) collective-permute-start(bf16[1,288,768]{2,1,0:T(8,128)(2,1)S(1)} %collective-permute-done.49), channel_id=1, source_target_pairs={{0,8},{2,10},{8,16},{10,18},{16,24},{18,26},{24,28},{26,30},{28,20... | collective-permute-start | bytes 1327112 | tf_op jit(solution)/shard_map/ppermute | solution.py:320
  454.5 13.2 %collective-permute-start.52 = (bf16[1,288,768]{2,1,0:T(8,128)(2,1)S(1)}, bf16[1,288,768]{2,1,0:T(8,128)(2,1)S(1)}, u32[]{:S(2)}, u32[]{:S(2)}) collective-permute-start(bf16[1,288,768]{2,1,0:T(8,128)(2,1)S(1)} %collective-permute-done.50), channel_id=1, source_target_pairs={{0,4},{2,6},{8,0},{10,2},{16,8},{18,10},{24,16},{26,18},{28,24},{3... | collective-permute-start | bytes 1327112 | tf_op jit(solution)/shard_map/ppermute | solution.py:320
  467.7 13.3 %collective-permute-start.53 = (bf16[1,288,768]{2,1,0:T(8,128)(2,1)S(1)}, bf16[1,288,768]{2,1,0:T(8,128)(2,1)S(1)}, u32[]{:S(2)}, u32[]{:S(2)}) collective-permute-start(bf16[1,288,768]{2,1,0:T(8,128)(2,1)S(1)} %collective-permute-done.51), channel_id=1, source_target_pairs={{0,8},{2,10},{8,16},{10,18},{16,24},{18,26},{24,28},{26,30},{28,20... | collective-permute-start | bytes 1327112 | tf_op jit(solution)/shard_map/ppermute | solution.py:320
  468.0 13.0 %collective-permute-start.54 = (bf16[1,288,768]{2,1,0:T(8,128)(2,1)S(1)}, bf16[1,288,768]{2,1,0:T(8,128)(2,1)S(1)}, u32[]{:S(2)}, u32[]{:S(2)}) collective-permute-start(bf16[1,288,768]{2,1,0:T(8,128)(2,1)S(1)} %collective-permute-done.52), channel_id=1, source_target_pairs={{0,4},{2,6},{8,0},{10,2},{16,8},{18,10},{24,16},{26,18},{28,24},{3... | collective-permute-start | bytes 1327112 | tf_op jit(solution)/shard_map/ppermute | solution.py:320
  481.0 15.4 %collective-permute-start.55 = (bf16[1,288,768]{2,1,0:T(8,128)(2,1)S(1)}, bf16[1,288,768]{2,1,0:T(8,128)(2,1)S(1)}, u32[]{:S(2)}, u32[]{:S(2)}) collective-permute-start(bf16[1,288,768]{2,1,0:T(8,128)(2,1)S(1)} %collective-permute-done.53), channel_id=1, source_target_pairs={{0,8},{2,10},{8,16},{10,18},{16,24},{18,26},{24,28},{26,30},{28,20... | collective-permute-start | bytes 1327112 | tf_op jit(solution)/shard_map/ppermute | solution.py:320
  482.2 14.2 %collective-permute-start.56 = (bf16[1,288,768]{2,1,0:T(8,128)(2,1)S(1)}, bf16[1,288,768]{2,1,0:T(8,128)(2,1)S(1)}, u32[]{:S(2)}, u32[]{:S(2)}) collective-permute-start(bf16[1,288,768]{2,1,0:T(8,128)(2,1)S(1)} %collective-permute-done.54), channel_id=1, source_target_pairs={{0,4},{2,6},{8,0},{10,2},{16,8},{18,10},{24,16},{26,18},{28,24},{3... | collective-permute-start | bytes 1327112 | tf_op jit(solution)/shard_map/ppermute | solution.py:320
  483.4 10.9 %collective-permute-start.28 = (bf16[1,72,1024]{2,1,0:T(8,128)(2,1)S(1)}, bf16[1,72,1024]{2,1,0:T(8,128)(2,1)S(1)}, u32[]{:S(2)}, u32[]{:S(2)}) collective-permute-start(bf16[1,72,1024]{2,1,0:T(8,128)(2,1)S(1)} %get-tuple-element.218), channel_id=1, source_target_pairs={{0,8},{2,10},{8,16},{10,18},{16,24},{18,26},{24,28},{26,30},{28,20... | collective-permute-start | bytes 442376 | tf_op jit(solution)/shard_map/ppermute | solution.py:320
  484.5 10.6 %collective-permute-start.35 = (bf16[1,72,1024]{2,1,0:T(8,128)(2,1)S(1)}, bf16[1,72,1024]{2,1,0:T(8,128)(2,1)S(1)}, u32[]{:S(2)}, u32[]{:S(2)}) collective-permute-start(bf16[1,72,1024]{2,1,0:T(8,128)(2,1)S(1)} %get-tuple-element.217), channel_id=1, source_target_pairs={{0,4},{2,6},{8,0},{10,2},{16,8},{18,10},{24,16},{26,18},{28,24},{3... | collective-permute-start | bytes 442376 | tf_op jit(solution)/shard_map/ppermute | solution.py:320
  507.5 11.3 %collective-permute-start.61 = (bf16[16,288,768]{2,1,0:T(8,128)(2,1)S(1)}, bf16[16,288,768]{2,1,0:T(8,128)(2,1)S(1)}, u32[]{:S(2)}, u32[]{:S(2)}) collective-permute-start(bf16[16,288,768]{2,1,0:T(8,128)(2,1)S(1)} %gather_pieces.2.refs_0_.refs_1_.refs_2_.refs_3_), channel_id=1, source_target_pairs={{0,2},{2,0},{4,6},{6,4},{8,10},{10,8},{12,14},{14,12},{16,18},{18,... | collective-permute-start | bytes 21233672 | tf_op jit(solution)/shard_map/ppermute | solution.py:263
  (100 other events, 622.6 us)

commit v6 on v5

--- a/solution.py
+++ b/solution.py
@@ -11,8 +11,9 @@
 halo = 8
 spare = 8
 small_vmem = pltpu.CompilerParams(vmem_limit_bytes=26 << 20)
-forward_vmem = pltpu.CompilerParams(vmem_limit_bytes=40 << 20)
-big_vmem = pltpu.CompilerParams(vmem_limit_bytes=48 << 20)
+forward_vmem = pltpu.CompilerParams(vmem_limit_bytes=46 << 20)
+tight_vmem = pltpu.CompilerParams(vmem_limit_bytes=20 << 20)
+big_vmem = pltpu.CompilerParams(vmem_limit_bytes=52 << 20)
 
 
 def cost(flops, moved, transcendentals=0):
@@ -373,7 +374,7 @@
         in_specs=[vmem] * count,
         out_specs=vmem,
         out_shape=jax.ShapeDtypeStruct((count, *pieces[0].shape), bf16),
-        compiler_params=small_vmem,
+        compiler_params=tight_vmem,
         cost_estimate=cost(0, 4 * count * pieces[0].size),
         name="gather_pieces",
     )(*pieces)
@@ -574,7 +575,7 @@
         ),
         out_shape=[jax.ShapeDtypeStruct(shape, f32) for shape in shapes],
         input_output_aliases={1 + 4 * group + k: k for k in range(len(so_far))},
-        compiler_params=small_vmem,
+        compiler_params=tight_vmem,
         cost_estimate=cost(0, 24 * width * hidden // steps),
         name="open_ff",
     )(order, *[mine] * (2 * group), *[other] * (2 * group), *so_far)
@@ -618,7 +619,7 @@
             out_specs=[out, out],
         ),
         out_shape=[jax.ShapeDtypeStruct((nodes, count, width), bf16)] * 2,
-        compiler_params=small_vmem,
+        compiler_params=tight_vmem,
         cost_estimate=cost(0, 2 * (grad_in.size + grad_out.size)),
         name="pack_conv",
     )(core, grad_in, grad_out, tail)
@@ -668,7 +669,7 @@
             jax.ShapeDtypeStruct((deep_total, width), f32),
             jax.ShapeDtypeStruct((blocks, spared, width), f32),
         ],
-        compiler_params=small_vmem,
+        compiler_params=tight_vmem,
         cost_estimate=cost(0, 8 * (total + deep_total) * width),
         name="open_conv",
     )(ring.order(), *[mine] * (2 * group), *[other] * (2 * group))

time: 569 us -> 565 us (level)
  local copies, waits for them, and re-layouts: 34.4 us -> 26.2 us
    unnamed x141 -> x127, local copies, waits for them, and re-layouts: 22.9 us -> 16 us
  transfers between devices with their start and end apart: 77 -> 77, of which waited for: 44 -> 44; matrix products, arithmetic and copies ran while one was open for 14% -> 14% of each run, Pallas kernels for 13% -> 14%
where the time goes in v6:
time: 565 us; the launch traced here: 562 us
  waiting for transfers between devices  204 us (36%)
  Pallas kernels  130 us (23%)
  starting transfers between devices  116 us (21%)
  other arithmetic  62.4 us (11%)
  local copies, waits for them, and re-layouts  26.2 us (5%)
  matrix products  21.6 us (4%)
    ppermute x56, waiting for transfers between devices, send(): return lax.ppermute(value, 'dp', pairs)  123 us
    ppermute x56, starting transfers between devices, send(): return lax.ppermute(value, 'dp', pairs)  70.3 us
    pallas_call x2, Pallas kernels, feed_forward(): pl.pallas_call(lambda *refs: ff_kernel(sub, *refs), grid=(hid // chunk,),...  46.1 us
    ppermute x11, waiting for transfers between devices, swap_mp(): return lax.ppermute(value, 'mp', [(0, 1), (1, 0)])  43.4 us
    pallas_call x2, Pallas kernels, ff_grads(): pl.pallas_call(lambda s, *refs: grads_kernel(*refs), grid_spec=pltpu.Pref...  34.5 us
    all_to_all x1, waiting for transfers between devices, on_device(): got_rows = lax.all_to_all(sent_rows, 'dp', **over)  29.6 us
    convert_element_type x14, other arithmetic, step(): came = (came.astype(f32) + own).astype(bf16)  26.6 us
    unnamed x127, local copies, waits for them, and re-layouts  16 us
  transfers between devices with their start and end apart: 77, of which 44 were waited for; matrix products, arithmetic and copies ran while one was open for 14% of the time, Pallas kernels for 14%

profile of v6, /device:TPU:0, one launch (start us, length us, event | category | flops | bytes accessed | tf_op | source)
XLA Modules:
  0.0 562.0 jit_solution(8014274943706019508)
XLA Ops:
  3.9 4.2 pack.1
  8.1 7.5 %all-to-all-start = ((bf16[16,104,512]{2,1,0:T(8,128)(2,1)}), bf16[16,104,512]{2,1,0:T(8,128)(2,1)S(1)}, u32[]{:S(2)}, u32[]{:S(2)}) async-start(bf16[16,104,512]{2,1,0:T(8,128)(2,1)} %get-tuple-element.99), calls=%async_computation | async-start | bytes 3407872 | tf_op jit(solution)/shard_map/all_to_all | solution.py:723
  20.3 29.6 %all-to-all-done.refs_1_.refs_2_ = bf16[16,104,512]{2,1,0:T(8,128)(2,1)S(1)} async-done(((bf16[16,104,512]{2,1,0:T(8,128)(2,1)}), bf16[16,104,512]{2,1,0:T(8,128)(2,1)S(1)}, u32[]{:S(2)}, u32[]{:S(2)}) %all-to-all-start) | async-done | bytes 1703968 | tf_op jit(solution)/shard_map/all_to_all | solution.py:723
  49.9 9.9 %all-to-all-start.1 = ((bf16[16,96,512]{2,1,0:T(8,128)(2,1)}), bf16[16,96,512]{2,1,0:T(8,128)(2,1)S(1)}, u32[]{:S(2)}, u32[]{:S(2)}) async-start(bf16[16,96,512]{2,1,0:T(8,128)(2,1)} %copy-done.11), calls=%async_computation.1 | async-start | bytes 3145728 | tf_op jit(solution)/shard_map/all_to_all | solution.py:726
  59.9 3.5 place_rows.2
  69.4 13.7 %collective-permute-done = bf16[528,512]{1,0:T(8,128)(2,1)} collective-permute-done((bf16[528,512]{1,0:T(8,128)(2,1)}, bf16[528,512]{1,0:T(8,128)(2,1)}, u32[]{:S(2)}, u32[]{:S(2)}) %collective-permute-start) | collective-permute-done | bytes 540704 | tf_op jit(solution)/shard_map/ppermute | solution.py:247
  83.1 3.0 maximum_select_fusion
  92.2 3.8 place_rows.3
  98.4 3.5 convolution_bitcast_fusion
  101.9 8.7 %collective-permute-done.3 = bf16[512,512]{1,0:T(8,128)(2,1)S(1)} collective-permute-done((bf16[512,512]{1,0:T(8,128)(2,1)S(1)}, bf16[512,512]{1,0:T(8,128)(2,1)S(1)}, u32[]{:S(2)}, u32[]{:S(2)}) %collective-permute-start.3) | collective-permute-done | bytes 524320 | tf_op jit(solution)/shard_map/ppermute | solution.py:247
  112.6 3.4 fusion.3
  122.0 22.9 %feed_forward.2 = (f32[512,1024]{1,0:T(8,128)S(1)}, f32[512,1024]{1,0:T(8,128)S(1)}, bf16[512,2304]{1,0:T(8,128)(2,1)}, bf16[512,2304]{1,0:T(8,128)(2,1)}, bf16[512,2304]{1,0:T(8,128)(2,1)}) custom-call(bf16[512,1024]{1,0:T(8,128)(2,1)S(1)} %multiply_convert_fusion.1.refs_0_, bf16[512,1024]{1,0:T(8,128)(2,1)S(1)} %maximum_select_fusion.1.refs_1_.refs_8_, ...), custom_call_target="tpu_custom_call" | custom-call | flops 28991029248 | bytes 27525120 | tf_op jit(solution)/shard_map/feed_forward/pallas_call | solution.py:417
  146.3 9.4 %collective-permute-done.6 = bf16[512,512]{1,0:T(8,128)(2,1)S(1)} collective-permute-done((bf16[512,512]{1,0:T(8,128)(2,1)S(1)}, bf16[512,512]{1,0:T(8,128)(2,1)S(1)}, u32[]{:S(2)}, u32[]{:S(2)}) %collective-permute-start.6) | collective-permute-done | bytes 524320 | tf_op jit(solution)/shard_map/ppermute | solution.py:247
  156.0 23.1 %feed_forward.3 = (f32[512,1024]{1,0:T(8,128)S(1)}, f32[512,1024]{1,0:T(8,128)S(1)}, bf16[512,2304]{1,0:T(8,128)(2,1)}, bf16[512,2304]{1,0:T(8,128)(2,1)}, bf16[512,2304]{1,0:T(8,128)(2,1)}) custom-call(bf16[512,1024]{1,0:T(8,128)(2,1)S(1)} %collective-permute-done.5.refs_0_.refs_1_, bf16[512,1024]{1,0:T(8,128)(2,1)S(1)} %maximum_select_fusion.2.refs_1_.refs_9_, ...), custom_call_target="tpu_custom_call" | custom-call | flops 28991029248 | bytes 27525120 | tf_op jit(solution)/shard_map/feed_forward/pallas_call | solution.py:417
  180.8 17.3 %ff_grads.2 = bf16[8,576,768]{2,1,0:T(8,128)(2,1)} custom-call(s32[1]{0:T(128)} %bitcast.22.s, bf16[512,1024]{1,0:T(8,128)(2,1)S(1)} %multiply_convert_fusion.1.refs_0_, bf16[512,1024]{1,0:T(8,128)(2,1)} %copy-done.22, bf16[512,2304]{1,0:T(8,128)(2,1)} %get-tuple-element.115.refs_2_, bf16[512,2304]{1,0:T(8,128)(2,1)} %get-tuple-element.116.refs_3_, ...), custom_call_target="tpu_custom_call" | custom-call | flops 14495514624 | bytes 18874368 | tf_op jit(solution)/shard_map/ff_grads/pallas_call | solution.py:475
  199.2 3.0 convert_element_type.492
  204.1 17.2 %ff_grads.3 = bf16[8,576,768]{2,1,0:T(8,128)(2,1)} custom-call(s32[1]{0:T(128)} %bitcast.21.s.core_ref, bf16[512,1024]{1,0:T(8,128)(2,1)S(1)} %copy-done.15, bf16[512,1024]{1,0:T(8,128)(2,1)} %copy-done.22, bf16[512,2304]{1,0:T(8,128)(2,1)} %get-tuple-element.115.refs_2_, bf16[512,2304]{1,0:T(8,128)(2,1)} %get-tuple-element.116.refs_3_, ...), custom_call_target="tpu_custom_call" | custom-call | flops 14495514624 | bytes 18874368 | tf_op jit(solution)/shard_map/ff_grads/pallas_call | solution.py:475
  221.3 6.6 %collective-permute-done.7 = bf16[520,1024]{1,0:T(8,128)(2,1)S(1)} collective-permute-done((bf16[520,1024]{1,0:T(8,128)(2,1)S(1)}, bf16[520,1024]{1,0:T(8,128)(2,1)S(1)}, u32[]{:S(2)}, u32[]{:S(2)}) %collective-permute-start.7) | collective-permute-done | bytes 1064992 | tf_op jit(solution)/shard_map/ppermute | solution.py:247
  231.8 4.8 collective-permute-start.10
  262.1 5.4 convolution_convert_fusion
  276.1 4.4 all-to-all-start.2
  284.2 8.8 %fusion.18 = (bf16[1024]{0:T(1024)(128)(2,1)S(1)}, f32[512]{0:T(512)S(1)}, f32[512,1024,1]{1,0,2:T(8,128)}) fusion(f32[528,1024]{1,0:T(8,128)S(1)} %copy-done.33, f32[512]{0:T(512)S(1)} %slice.240, f32[1024]{0:T(1024)S(1)} %copy-done.56, bf16[3,512,1024]{2,1,0:T(8,128)(2,1)} %pad_maximum_fusion, bf16[3,512,512]{2,1,0:T(8,128)(2,1)} %slice.260, ...), kind=kOutput, calls=%fused_computation.52 | convolution fusion | flops 3243244032 | bytes 13641728 | tf_op jit(solution)/shard_map/krc,kdc->rd/dot_general | solution.py:887
  306.2 4.4 collective-permute-done.17
  312.7 2.9 take_rows.6
  315.6 9.4 %all-to-all-start.3 = ((bf16[16,96,512]{2,1,0:T(8,128)(2,1)}), bf16[16,96,512]{2,1,0:T(8,128)(2,1)}, u32[]{:S(2)}, u32[]{:S(2)}) async-start(bf16[16,96,512]{2,1,0:T(8,128)(2,1)} %bitcast.32), calls=%async_computation.3 | async-start | bytes 3145728 | tf_op jit(solution)/shard_map/all_to_all | solution.py:835
  327.1 3.4 collective-permute-start.39
  330.5 30.5 %collective-permute-done.39 = bf16[1,288,768]{2,1,0:T(8,128)(2,1)S(1)} collective-permute-done((bf16[1,288,768]{2,1,0:T(8,128)(2,1)S(1)}, bf16[1,288,768]{2,1,0:T(8,128)(2,1)S(1)}, u32[]{:S(2)}, u32[]{:S(2)}) %collective-permute-start.39) | collective-permute-done | bytes 442400 | tf_op jit(solution)/shard_map/ppermute | solution.py:321
  365.4 10.0 %collective-permute-start.41 = (bf16[1,288,768]{2,1,0:T(8,128)(2,1)}, bf16[1,288,768]{2,1,0:T(8,128)(2,1)S(1)}, u32[]{:S(2)}, u32[]{:S(2)}) collective-permute-start(bf16[1,288,768]{2,1,0:T(8,128)(2,1)} %get-tuple-element.140), channel_id=1, source_target_pairs={{0,8},{2,10},{8,16},{10,18},{16,24},{18,26},{24,28},{26,30},{28,20... | collective-permute-start | bytes 1327112 | tf_op jit(solution)/shard_map/ppermute | solution.py:321
  375.4 9.5 %collective-permute-done.41 = bf16[1,288,768]{2,1,0:T(8,128)(2,1)S(1)} collective-permute-done((bf16[1,288,768]{2,1,0:T(8,128)(2,1)}, bf16[1,288,768]{2,1,0:T(8,128)(2,1)S(1)}, u32[]{:S(2)}, u32[]{:S(2)}) %collective-permute-start.41) | collective-permute-done | bytes 442400 | tf_op jit(solution)/shard_map/ppermute | solution.py:321
  387.0 2.8 add_convert_fusion.4
  396.1 4.3 take_rows.5
  400.4 5.3 collective-permute-done.21
  419.4 6.5 %collective-permute-done.45 = bf16[1,288,768]{2,1,0:T(8,128)(2,1)S(1)} collective-permute-done((bf16[1,288,768]{2,1,0:T(8,128)(2,1)S(1)}, bf16[1,288,768]{2,1,0:T(8,128)(2,1)S(1)}, u32[]{:S(2)}, u32[]{:S(2)}) %collective-permute-start.45) | collective-permute-done | bytes 442400 | tf_op jit(solution)/shard_map/ppermute | solution.py:321
  431.0 4.5 take_rows.7
  440.6 8.2 %collective-permute-done.25 = bf16[1,72,1024]{2,1,0:T(8,128)(2,1)S(1)} collective-permute-done((bf16[1,72,1024]{2,1,0:T(8,128)(2,1)S(1)}, bf16[1,72,1024]{2,1,0:T(8,128)(2,1)S(1)}, u32[]{:S(2)}, u32[]{:S(2)}) %collective-permute-start.25) | collective-permute-done | bytes 147488 | tf_op jit(solution)/shard_map/ppermute | solution.py:321
  454.6 8.0 %collective-permute-done.26 = bf16[1,72,1024]{2,1,0:T(8,128)(2,1)S(1)} collective-permute-done((bf16[1,72,1024]{2,1,0:T(8,128)(2,1)S(1)}, bf16[1,72,1024]{2,1,0:T(8,128)(2,1)S(1)}, u32[]{:S(2)}, u32[]{:S(2)}) %collective-permute-start.26) | collective-permute-done | bytes 147488 | tf_op jit(solution)/shard_map/ppermute | solution.py:321
  468.4 7.8 %collective-permute-done.27 = bf16[1,72,1024]{2,1,0:T(8,128)(2,1)S(1)} collective-permute-done((bf16[1,72,1024]{2,1,0:T(8,128)(2,1)S(1)}, bf16[1,72,1024]{2,1,0:T(8,128)(2,1)S(1)}, u32[]{:S(2)}, u32[]{:S(2)}) %collective-permute-start.27) | collective-permute-done | bytes 147488 | tf_op jit(solution)/shard_map/ppermute | solution.py:321
  482.1 8.9 %collective-permute-done.28 = bf16[1,72,1024]{2,1,0:T(8,128)(2,1)S(1)} collective-permute-done((bf16[1,72,1024]{2,1,0:T(8,128)(2,1)S(1)}, bf16[1,72,1024]{2,1,0:T(8,128)(2,1)S(1)}, u32[]{:S(2)}, u32[]{:S(2)}) %collective-permute-start.28) | collective-permute-done | bytes 147488 | tf_op jit(solution)/shard_map/ppermute | solution.py:321
  495.4 6.0 %collective-permute-done.57 = bf16[1,288,768]{2,1,0:T(8,128)(2,1)S(1)} collective-permute-done((bf16[1,288,768]{2,1,0:T(8,128)(2,1)S(1)}, bf16[1,288,768]{2,1,0:T(8,128)(2,1)S(1)}, u32[]{:S(2)}, u32[]{:S(2)}) %collective-permute-start.57) | collective-permute-done | bytes 442400 | tf_op jit(solution)/shard_map/ppermute | solution.py:321
  506.3 4.2 collective-permute-done.29
  515.5 3.7 open_ff.4
  521.3 3.7 open_ff.5
  528.4 3.7 open_ff.6
  534.3 3.7 open_ff.7
  541.1 4.6 collective-permute-done.68
  547.7 3.1 collective-permute-done.69
  551.8 4.5 collective-permute-done.72.refs_9_.refs_10_.refs_11_.refs_12_.refs_13_.refs_14_.refs_15_.refs_16_
  556.4 4.2 open_conv.1
  (353 shorter events, 178.2 us)
Async XLA Ops:
  8.1 41.8 %all-to-all-start = ((bf16[16,104,512]{2,1,0:T(8,128)(2,1)}), bf16[16,104,512]{2,1,0:T(8,128)(2,1)S(1)}, u32[]{:S(2)}, u32[]{:S(2)}) async-start(bf16[16,104,512]{2,1,0:T(8,128)(2,1)} %get-tuple-element.99), calls=%async_computation | async-start | bytes 3407872 | tf_op jit(solution)/shard_map/all_to_all | solution.py:723
  15.6 48.8 %collective-permute-start.1 = (bf16[4,512,512]{2,1,0:T(8,128)(2,1)}, bf16[4,512,512]{2,1,0:T(8,128)(2,1)}, u32[]{:S(2)}, u32[]{:S(2)}) collective-permute-start(bf16[4,512,512]{2,1,0:T(8,128)(2,1)} %pad_maximum_fusion.1), channel_id=1, source_target_pairs={{0,1},{1,0},{2,3},{3,2},{4,5},{5,4},{6,7},{7,6},{8,9},{9,8},{10,11... | collective-permute-start | bytes 6291464 | tf_op jit(solution)/shard_map/ppermute | solution.py:247
  49.9 42.3 %all-to-all-start.1 = ((bf16[16,96,512]{2,1,0:T(8,128)(2,1)}), bf16[16,96,512]{2,1,0:T(8,128)(2,1)S(1)}, u32[]{:S(2)}, u32[]{:S(2)}) async-start(bf16[16,96,512]{2,1,0:T(8,128)(2,1)} %copy-done.11), calls=%async_computation.1 | async-start | bytes 3145728 | tf_op jit(solution)/shard_map/all_to_all | solution.py:726
  64.4 21.7 %collective-permute-start.2 = (bf16[4,512,512]{2,1,0:T(8,128)(2,1)}, bf16[4,512,512]{2,1,0:T(8,128)(2,1)}, u32[]{:S(2)}, u32[]{:S(2)}) collective-permute-start(bf16[4,512,512]{2,1,0:T(8,128)(2,1)} %collective-permute-done.1), channel_id=1, source_target_pairs={{0,2},{2,0},{4,6},{6,4},{8,10},{10,8},{12,14},{14,12},{16,18},{18,... | collective-permute-start | bytes 6291464 | tf_op jit(solution)/shard_map/ppermute | solution.py:264
  68.8 14.3 %collective-permute-start = (bf16[528,512]{1,0:T(8,128)(2,1)}, bf16[528,512]{1,0:T(8,128)(2,1)}, u32[]{:S(2)}, u32[]{:S(2)}) collective-permute-start(bf16[528,512]{1,0:T(8,128)(2,1)} %get-tuple-element.238), channel_id=1, source_target_pairs={{0,1},{1,0},{2,3},{3,2},{4,5},{5,4},{6,7},{7,6},{8,9},{9,8},{10,11... | collective-permute-start | bytes 1622024 | tf_op jit(solution)/shard_map/ppermute | solution.py:247
  96.4 14.3 %collective-permute-start.3 = (bf16[512,512]{1,0:T(8,128)(2,1)S(1)}, bf16[512,512]{1,0:T(8,128)(2,1)S(1)}, u32[]{:S(2)}, u32[]{:S(2)}) collective-permute-start(bf16[512,512]{1,0:T(8,128)(2,1)S(1)} %get-tuple-element.246), channel_id=1, source_target_pairs={{0,1},{1,0},{2,3},{3,2},{4,5},{5,4},{6,7},{7,6},{8,9},{9,8},{10,11... | collective-permute-start | bytes 1572872 | tf_op jit(solution)/shard_map/ppermute | solution.py:247
  119.6 36.3 %collective-permute-start.5 = (bf16[512,1024]{1,0:T(8,128)(2,1)S(1)}, bf16[512,1024]{1,0:T(8,128)(2,1)S(1)}, u32[]{:S(2)}, u32[]{:S(2)}) collective-permute-start(bf16[512,1024]{1,0:T(8,128)(2,1)S(1)} %multiply_convert_fusion.1.refs_0_), channel_id=1, source_target_pairs={{0,1},{1,0},{2,3},{3,2},{4,5},{5,4},{6,7},{7,6},{8,9},{9,8},{10,11... | collective-permute-start | bytes 3145736 | tf_op jit(solution)/shard_map/ppermute | solution.py:247
  121.2 34.5 %collective-permute-start.6 = (bf16[512,512]{1,0:T(8,128)(2,1)S(1)}, bf16[512,512]{1,0:T(8,128)(2,1)S(1)}, u32[]{:S(2)}, u32[]{:S(2)}) collective-permute-start(bf16[512,512]{1,0:T(8,128)(2,1)S(1)} %get-tuple-element.110), channel_id=1, source_target_pairs={{0,1},{1,0},{2,3},{3,2},{4,5},{5,4},{6,7},{7,6},{8,9},{9,8},{10,11... | collective-permute-start | bytes 1572872 | tf_op jit(solution)/shard_map/ppermute | solution.py:247
  198.0 32.0 %collective-permute-start.9 = (bf16[8,576,768]{2,1,0:T(8,128)(2,1)}, bf16[8,576,768]{2,1,0:T(8,128)(2,1)}, u32[]{:S(2)}, u32[]{:S(2)}) collective-permute-start(bf16[8,576,768]{2,1,0:T(8,128)(2,1)} %ff_grads.2), channel_id=1, source_target_pairs={{0,2},{2,0},{4,6},{6,4},{8,10},{10,8},{12,14},{14,12},{16,18},{18,... | collective-permute-start | bytes 21233672 | tf_op jit(solution)/shard_map/ppermute | solution.py:264
  202.2 25.7 %collective-permute-start.7 = (bf16[520,1024]{1,0:T(8,128)(2,1)S(1)}, bf16[520,1024]{1,0:T(8,128)(2,1)S(1)}, u32[]{:S(2)}, u32[]{:S(2)}) collective-permute-start(bf16[520,1024]{1,0:T(8,128)(2,1)S(1)} %copy-done.44), channel_id=1, source_target_pairs={{0,1},{1,0},{2,3},{3,2},{4,5},{5,4},{6,7},{7,6},{8,9},{9,8},{10,11... | collective-permute-start | bytes 3194888 | tf_op jit(solution)/shard_map/ppermute | solution.py:247
  227.9 32.6 %collective-permute-start.8 = (bf16[512,1024]{1,0:T(8,128)(2,1)S(1)}, bf16[512,1024]{1,0:T(8,128)(2,1)S(1)}, u32[]{:S(2)}, u32[]{:S(2)}) collective-permute-start(bf16[512,1024]{1,0:T(8,128)(2,1)S(1)} %convert_element_type.498), channel_id=1, source_target_pairs={{0,1},{1,0},{2,3},{3,2},{4,5},{5,4},{6,7},{7,6},{8,9},{9,8},{10,11... | collective-permute-start | bytes 3145736 | tf_op jit(solution)/shard_map/ppermute | solution.py:247
  231.8 13.7 %collective-permute-start.10 = (bf16[1,288,768]{2,1,0:T(8,128)(2,1)S(1)}, bf16[1,288,768]{2,1,0:T(8,128)(2,1)S(1)}, u32[]{:S(2)}, u32[]{:S(2)}) collective-permute-start(bf16[1,288,768]{2,1,0:T(8,128)(2,1)S(1)} %get-tuple-element.214), channel_id=1, source_target_pairs={{0,8},{2,10},{8,16},{10,18},{16,24},{18,26},{24,28},{26,30},{28,20... | collective-permute-start | bytes 1327112 | tf_op jit(solution)/shard_map/ppermute | solution.py:321
  236.7 11.0 %collective-permute-start.11 = (bf16[1,288,768]{2,1,0:T(8,128)(2,1)S(1)}, bf16[1,288,768]{2,1,0:T(8,128)(2,1)S(1)}, u32[]{:S(2)}, u32[]{:S(2)}) collective-permute-start(bf16[1,288,768]{2,1,0:T(8,128)(2,1)S(1)} %get-tuple-element.213), channel_id=1, source_target_pairs={{0,4},{2,6},{8,0},{10,2},{16,8},{18,10},{24,16},{26,18},{28,24},{3... | collective-permute-start | bytes 1327112 | tf_op jit(solution)/shard_map/ppermute | solution.py:321
  249.4 18.1 %collective-permute-start.13 = (bf16[1,288,768]{2,1,0:T(8,128)(2,1)S(1)}, bf16[1,288,768]{2,1,0:T(8,128)(2,1)S(1)}, u32[]{:S(2)}, u32[]{:S(2)}) collective-permute-start(bf16[1,288,768]{2,1,0:T(8,128)(2,1)S(1)} %get-tuple-element.212), channel_id=1, source_target_pairs={{0,8},{2,10},{8,16},{10,18},{16,24},{18,26},{24,28},{26,30},{28,20... | collective-permute-start | bytes 1327112 | tf_op jit(solution)/shard_map/ppermute | solution.py:321
  250.2 17.3 %collective-permute-start.15 = (bf16[1,288,768]{2,1,0:T(8,128)(2,1)S(1)}, bf16[1,288,768]{2,1,0:T(8,128)(2,1)S(1)}, u32[]{:S(2)}, u32[]{:S(2)}) collective-permute-start(bf16[1,288,768]{2,1,0:T(8,128)(2,1)S(1)} %get-tuple-element.211), channel_id=1, source_target_pairs={{0,4},{2,6},{8,0},{10,2},{16,8},{18,10},{24,16},{26,18},{28,24},{3... | collective-permute-start | bytes 1327112 | tf_op jit(solution)/shard_map/ppermute | solution.py:321
  261.5 11.4 %collective-permute-start.12 = (bf16[512,512]{1,0:T(8,128)(2,1)S(1)}, bf16[512,512]{1,0:T(8,128)(2,1)S(1)}, u32[]{:S(2)}, u32[]{:S(2)}) collective-permute-start(bf16[512,512]{1,0:T(8,128)(2,1)S(1)} %get-tuple-element.244), channel_id=1, source_target_pairs={{0,1},{1,0},{2,3},{3,2},{4,5},{5,4},{6,7},{7,6},{8,9},{9,8},{10,11... | collective-permute-start | bytes 1572872 | tf_op jit(solution)/shard_map/ppermute | solution.py:247
  270.2 10.4 %collective-permute-start.14 = (bf16[1,288,768]{2,1,0:T(8,128)(2,1)}, bf16[1,288,768]{2,1,0:T(8,128)(2,1)S(1)}, u32[]{:S(2)}, u32[]{:S(2)}) collective-permute-start(bf16[1,288,768]{2,1,0:T(8,128)(2,1)} %get-tuple-element.210), channel_id=1, source_target_pairs={{0,8},{2,10},{8,16},{10,18},{16,24},{18,26},{24,28},{26,30},{28,20... | collective-permute-start | bytes 1327112 | tf_op jit(solution)/shard_map/ppermute | solution.py:321
  270.9 10.4 %collective-permute-start.16 = (bf16[1,288,768]{2,1,0:T(8,128)(2,1)}, bf16[1,288,768]{2,1,0:T(8,128)(2,1)}, u32[]{:S(2)}, u32[]{:S(2)}) collective-permute-start(bf16[1,288,768]{2,1,0:T(8,128)(2,1)} %get-tuple-element.209), channel_id=1, source_target_pairs={{0,4},{2,6},{8,0},{10,2},{16,8},{18,10},{24,16},{26,18},{28,24},{3... | collective-permute-start | bytes 1327112 | tf_op jit(solution)/shard_map/ppermute | solution.py:321
  276.1 36.5 %all-to-all-start.2 = ((bf16[16,96,512]{2,1,0:T(8,128)(2,1)}), bf16[16,96,512]{2,1,0:T(8,128)(2,1)}, u32[]{:S(2)}, u32[]{:S(2)}) async-start(bf16[16,96,512]{2,1,0:T(8,128)(2,1)} %bitcast.144), calls=%async_computation.2 | async-start | bytes 3145728 | tf_op jit(solution)/shard_map/all_to_all | solution.py:835
  295.8 14.8 %collective-permute-start.17 = (bf16[512,512]{1,0:T(8,128)(2,1)S(1)}, bf16[512,512]{1,0:T(8,128)(2,1)S(1)}, u32[]{:S(2)}, u32[]{:S(2)}) collective-permute-start(bf16[512,512]{1,0:T(8,128)(2,1)S(1)} %get-tuple-element.242), channel_id=1, source_target_pairs={{0,1},{1,0},{2,3},{3,2},{4,5},{5,4},{6,7},{7,6},{8,9},{9,8},{10,11... | collective-permute-start | bytes 1572872 | tf_op jit(solution)/shard_map/ppermute | solution.py:247
  296.7 28.3 %collective-permute-start.37 = (bf16[1,288,768]{2,1,0:T(8,128)(2,1)}, bf16[1,288,768]{2,1,0:T(8,128)(2,1)}, u32[]{:S(2)}, u32[]{:S(2)}) collective-permute-start(bf16[1,288,768]{2,1,0:T(8,128)(2,1)} %get-tuple-element.136), channel_id=1, source_target_pairs={{0,8},{2,10},{8,16},{10,18},{16,24},{18,26},{24,28},{26,30},{28,20... | collective-permute-start | bytes 1327112 | tf_op jit(solution)/shard_map/ppermute | solution.py:321
  298.5 26.6 %collective-permute-start.38 = (bf16[1,288,768]{2,1,0:T(8,128)(2,1)S(1)}, bf16[1,288,768]{2,1,0:T(8,128)(2,1)}, u32[]{:S(2)}, u32[]{:S(2)}) collective-permute-start(bf16[1,288,768]{2,1,0:T(8,128)(2,1)S(1)} %get-tuple-element.137), channel_id=1, source_target_pairs={{0,4},{2,6},{8,0},{10,2},{16,8},{18,10},{24,16},{26,18},{28,24},{3... | collective-permute-start | bytes 1327112 | tf_op jit(solution)/shard_map/ppermute | solution.py:321
  301.7 88.1 %collective-permute-start.20 = (bf16[8,144,1024]{2,1,0:T(8,128)(2,1)}, bf16[8,144,1024]{2,1,0:T(8,128)(2,1)}, u32[]{:S(2)}, u32[]{:S(2)}) collective-permute-start(bf16[8,144,1024]{2,1,0:T(8,128)(2,1)} %add_convert_fusion), channel_id=1, source_target_pairs={{0,1},{1,0},{2,3},{3,2},{4,5},{5,4},{6,7},{7,6},{8,9},{9,8},{10,11... | collective-permute-start | bytes 7077896 | tf_op jit(solution)/shard_map/ppermute | solution.py:247
  306.2 83.6 %collective-permute-start.19 = (bf16[8,144,1024]{2,1,0:T(8,128)(2,1)}, bf16[8,144,1024]{2,1,0:T(8,128)(2,1)}, u32[]{:S(2)}, u32[]{:S(2)}) collective-permute-start(bf16[8,144,1024]{2,1,0:T(8,128)(2,1)} %get-tuple-element.133), channel_id=1, source_target_pairs={{0,2},{2,0},{4,6},{6,4},{8,10},{10,8},{12,14},{14,12},{16,18},{18,... | collective-permute-start | bytes 7077896 | tf_op jit(solution)/shard_map/ppermute | solution.py:264
  315.6 97.1 %all-to-all-start.3 = ((bf16[16,96,512]{2,1,0:T(8,128)(2,1)}), bf16[16,96,512]{2,1,0:T(8,128)(2,1)}, u32[]{:S(2)}, u32[]{:S(2)}) async-start(bf16[16,96,512]{2,1,0:T(8,128)(2,1)} %bitcast.32), calls=%async_computation.3 | async-start | bytes 3145728 | tf_op jit(solution)/shard_map/all_to_all | solution.py:835
  327.1 33.9 %collective-permute-start.39 = (bf16[1,288,768]{2,1,0:T(8,128)(2,1)S(1)}, bf16[1,288,768]{2,1,0:T(8,128)(2,1)S(1)}, u32[]{:S(2)}, u32[]{:S(2)}) collective-permute-start(bf16[1,288,768]{2,1,0:T(8,128)(2,1)S(1)} %get-tuple-element.138), channel_id=1, source_target_pairs={{0,8},{2,10},{8,16},{10,18},{16,24},{18,26},{24,28},{26,30},{28,20... | collective-permute-start | bytes 1327112 | tf_op jit(solution)/shard_map/ppermute | solution.py:321
  330.5 32.4 %collective-permute-start.40 = (bf16[1,288,768]{2,1,0:T(8,128)(2,1)S(1)}, bf16[1,288,768]{2,1,0:T(8,128)(2,1)S(1)}, u32[]{:S(2)}, u32[]{:S(2)}) collective-permute-start(bf16[1,288,768]{2,1,0:T(8,128)(2,1)S(1)} %get-tuple-element.139), channel_id=1, source_target_pairs={{0,4},{2,6},{8,0},{10,2},{16,8},{18,10},{24,16},{26,18},{28,24},{3... | collective-permute-start | bytes 1327112 | tf_op jit(solution)/shard_map/ppermute | solution.py:321
  365.4 19.5 %collective-permute-start.41 = (bf16[1,288,768]{2,1,0:T(8,128)(2,1)}, bf16[1,288,768]{2,1,0:T(8,128)(2,1)S(1)}, u32[]{:S(2)}, u32[]{:S(2)}) collective-permute-start(bf16[1,288,768]{2,1,0:T(8,128)(2,1)} %get-tuple-element.140), channel_id=1, source_target_pairs={{0,8},{2,10},{8,16},{10,18},{16,24},{18,26},{24,28},{26,30},{28,20... | collective-permute-start | bytes 1327112 | tf_op jit(solution)/shard_map/ppermute | solution.py:321
  375.4 11.5 %collective-permute-start.42 = (bf16[1,288,768]{2,1,0:T(8,128)(2,1)S(1)}, bf16[1,288,768]{2,1,0:T(8,128)(2,1)}, u32[]{:S(2)}, u32[]{:S(2)}) collective-permute-start(bf16[1,288,768]{2,1,0:T(8,128)(2,1)S(1)} %get-tuple-element.141), channel_id=1, source_target_pairs={{0,4},{2,6},{8,0},{10,2},{16,8},{18,10},{24,16},{26,18},{28,24},{3... | collective-permute-start | bytes 1327112 | tf_op jit(solution)/shard_map/ppermute | solution.py:321
  391.7 18.9 %collective-permute-start.43 = (bf16[1,288,768]{2,1,0:T(8,128)(2,1)}, bf16[1,288,768]{2,1,0:T(8,128)(2,1)}, u32[]{:S(2)}, u32[]{:S(2)}) collective-permute-start(bf16[1,288,768]{2,1,0:T(8,128)(2,1)} %get-tuple-element.142), channel_id=1, source_target_pairs={{0,8},{2,10},{8,16},{10,18},{16,24},{18,26},{24,28},{26,30},{28,20... | collective-permute-start | bytes 1327112 | tf_op jit(solution)/shard_map/ppermute | solution.py:321
  392.9 17.8 %collective-permute-start.44 = (bf16[1,288,768]{2,1,0:T(8,128)(2,1)S(1)}, bf16[1,288,768]{2,1,0:T(8,128)(2,1)}, u32[]{:S(2)}, u32[]{:S(2)}) collective-permute-start(bf16[1,288,768]{2,1,0:T(8,128)(2,1)S(1)} %get-tuple-element.143), channel_id=1, source_target_pairs={{0,4},{2,6},{8,0},{10,2},{16,8},{18,10},{24,16},{26,18},{28,24},{3... | collective-permute-start | bytes 1327112 | tf_op jit(solution)/shard_map/ppermute | solution.py:321
  394.0 11.6 %collective-permute-start.21 = (bf16[1,72,1024]{2,1,0:T(8,128)(2,1)}, bf16[1,72,1024]{2,1,0:T(8,128)(2,1)S(1)}, u32[]{:S(2)}, u32[]{:S(2)}) collective-permute-start(bf16[1,72,1024]{2,1,0:T(8,128)(2,1)} %get-tuple-element.230), channel_id=1, source_target_pairs={{0,8},{2,10},{8,16},{10,18},{16,24},{18,26},{24,28},{26,30},{28,20... | collective-permute-start | bytes 442376 | tf_op jit(solution)/shard_map/ppermute | solution.py:321
  395.2 11.5 %collective-permute-start.22 = (bf16[1,72,1024]{2,1,0:T(8,128)(2,1)S(1)}, bf16[1,72,1024]{2,1,0:T(8,128)(2,1)S(1)}, u32[]{:S(2)}, u32[]{:S(2)}) collective-permute-start(bf16[1,72,1024]{2,1,0:T(8,128)(2,1)S(1)} %get-tuple-element.229), channel_id=1, source_target_pairs={{0,4},{2,6},{8,0},{10,2},{16,8},{18,10},{24,16},{26,18},{28,24},{3... | collective-permute-start | bytes 442376 | tf_op jit(solution)/shard_map/ppermute | solution.py:321
  412.7 13.2 %collective-permute-start.45 = (bf16[1,288,768]{2,1,0:T(8,128)(2,1)S(1)}, bf16[1,288,768]{2,1,0:T(8,128)(2,1)S(1)}, u32[]{:S(2)}, u32[]{:S(2)}) collective-permute-start(bf16[1,288,768]{2,1,0:T(8,128)(2,1)S(1)} %get-tuple-element.144), channel_id=1, source_target_pairs={{0,8},{2,10},{8,16},{10,18},{16,24},{18,26},{24,28},{26,30},{28,20... | collective-permute-start | bytes 1327112 | tf_op jit(solution)/shard_map/ppermute | solution.py:321
  413.4 13.1 %collective-permute-start.46 = (bf16[1,288,768]{2,1,0:T(8,128)(2,1)S(1)}, bf16[1,288,768]{2,1,0:T(8,128)(2,1)S(1)}, u32[]{:S(2)}, u32[]{:S(2)}) collective-permute-start(bf16[1,288,768]{2,1,0:T(8,128)(2,1)S(1)} %get-tuple-element.145), channel_id=1, source_target_pairs={{0,4},{2,6},{8,0},{10,2},{16,8},{18,10},{24,16},{26,18},{28,24},{3... | collective-permute-start | bytes 1327112 | tf_op jit(solution)/shard_map/ppermute | solution.py:321
  417.3 11.7 %collective-permute-start.24 = (bf16[1,72,1024]{2,1,0:T(8,128)(2,1)S(1)}, bf16[1,72,1024]{2,1,0:T(8,128)(2,1)S(1)}, u32[]{:S(2)}, u32[]{:S(2)}) collective-permute-start(bf16[1,72,1024]{2,1,0:T(8,128)(2,1)S(1)} %get-tuple-element.226), channel_id=1, source_target_pairs={{0,8},{2,10},{8,16},{10,18},{16,24},{18,26},{24,28},{26,30},{28,20... | collective-permute-start | bytes 442376 | tf_op jit(solution)/shard_map/ppermute | solution.py:321
  417.9 11.7 %collective-permute-start.31 = (bf16[1,72,1024]{2,1,0:T(8,128)(2,1)S(1)}, bf16[1,72,1024]{2,1,0:T(8,128)(2,1)S(1)}, u32[]{:S(2)}, u32[]{:S(2)}) collective-permute-start(bf16[1,72,1024]{2,1,0:T(8,128)(2,1)S(1)} %get-tuple-element.225), channel_id=1, source_target_pairs={{0,4},{2,6},{8,0},{10,2},{16,8},{18,10},{24,16},{26,18},{28,24},{3... | collective-permute-start | bytes 442376 | tf_op jit(solution)/shard_map/ppermute | solution.py:321
  436.5 14.0 %collective-permute-start.49 = (bf16[1,288,768]{2,1,0:T(8,128)(2,1)S(1)}, bf16[1,288,768]{2,1,0:T(8,128)(2,1)S(1)}, u32[]{:S(2)}, u32[]{:S(2)}) collective-permute-start(bf16[1,288,768]{2,1,0:T(8,128)(2,1)S(1)} %collective-permute-done.47), channel_id=1, source_target_pairs={{0,8},{2,10},{8,16},{10,18},{16,24},{18,26},{24,28},{26,30},{28,20... | collective-permute-start | bytes 1327112 | tf_op jit(solution)/shard_map/ppermute | solution.py:321
  437.3 13.2 %collective-permute-start.50 = (bf16[1,288,768]{2,1,0:T(8,128)(2,1)S(1)}, bf16[1,288,768]{2,1,0:T(8,128)(2,1)S(1)}, u32[]{:S(2)}, u32[]{:S(2)}) collective-permute-start(bf16[1,288,768]{2,1,0:T(8,128)(2,1)S(1)} %collective-permute-done.48), channel_id=1, source_target_pairs={{0,4},{2,6},{8,0},{10,2},{16,8},{18,10},{24,16},{26,18},{28,24},{3... | collective-permute-start | bytes 1327112 | tf_op jit(solution)/shard_map/ppermute | solution.py:321
  450.5 13.8 %collective-permute-start.51 = (bf16[1,288,768]{2,1,0:T(8,128)(2,1)S(1)}, bf16[1,288,768]{2,1,0:T(8,128)(2,1)S(1)}, u32[]{:S(2)}, u32[]{:S(2)}) collective-permute-start(bf16[1,288,768]{2,1,0:T(8,128)(2,1)S(1)} %collective-permute-done.49), channel_id=1, source_target_pairs={{0,8},{2,10},{8,16},{10,18},{16,24},{18,26},{24,28},{26,30},{28,20... | collective-permute-start | bytes 1327112 | tf_op jit(solution)/shard_map/ppermute | solution.py:321
  451.1 13.2 %collective-permute-start.52 = (bf16[1,288,768]{2,1,0:T(8,128)(2,1)S(1)}, bf16[1,288,768]{2,1,0:T(8,128)(2,1)S(1)}, u32[]{:S(2)}, u32[]{:S(2)}) collective-permute-start(bf16[1,288,768]{2,1,0:T(8,128)(2,1)S(1)} %collective-permute-done.50), channel_id=1, source_target_pairs={{0,4},{2,6},{8,0},{10,2},{16,8},{18,10},{24,16},{26,18},{28,24},{3... | collective-permute-start | bytes 1327112 | tf_op jit(solution)/shard_map/ppermute | solution.py:321
  464.3 13.3 %collective-permute-start.53 = (bf16[1,288,768]{2,1,0:T(8,128)(2,1)S(1)}, bf16[1,288,768]{2,1,0:T(8,128)(2,1)S(1)}, u32[]{:S(2)}, u32[]{:S(2)}) collective-permute-start(bf16[1,288,768]{2,1,0:T(8,128)(2,1)S(1)} %collective-permute-done.51), channel_id=1, source_target_pairs={{0,8},{2,10},{8,16},{10,18},{16,24},{18,26},{24,28},{26,30},{28,20... | collective-permute-start | bytes 1327112 | tf_op jit(solution)/shard_map/ppermute | solution.py:321
  464.6 13.0 %collective-permute-start.54 = (bf16[1,288,768]{2,1,0:T(8,128)(2,1)S(1)}, bf16[1,288,768]{2,1,0:T(8,128)(2,1)S(1)}, u32[]{:S(2)}, u32[]{:S(2)}) collective-permute-start(bf16[1,288,768]{2,1,0:T(8,128)(2,1)S(1)} %collective-permute-done.52), channel_id=1, source_target_pairs={{0,4},{2,6},{8,0},{10,2},{16,8},{18,10},{24,16},{26,18},{28,24},{3... | collective-permute-start | bytes 1327112 | tf_op jit(solution)/shard_map/ppermute | solution.py:321
  477.6 15.4 %collective-permute-start.55 = (bf16[1,288,768]{2,1,0:T(8,128)(2,1)S(1)}, bf16[1,288,768]{2,1,0:T(8,128)(2,1)S(1)}, u32[]{:S(2)}, u32[]{:S(2)}) collective-permute-start(bf16[1,288,768]{2,1,0:T(8,128)(2,1)S(1)} %collective-permute-done.53), channel_id=1, source_target_pairs={{0,8},{2,10},{8,16},{10,18},{16,24},{18,26},{24,28},{26,30},{28,20... | collective-permute-start | bytes 1327112 | tf_op jit(solution)/shard_map/ppermute | solution.py:321
  478.8 14.2 %collective-permute-start.56 = (bf16[1,288,768]{2,1,0:T(8,128)(2,1)S(1)}, bf16[1,288,768]{2,1,0:T(8,128)(2,1)S(1)}, u32[]{:S(2)}, u32[]{:S(2)}) collective-permute-start(bf16[1,288,768]{2,1,0:T(8,128)(2,1)S(1)} %collective-permute-done.54), channel_id=1, source_target_pairs={{0,4},{2,6},{8,0},{10,2},{16,8},{18,10},{24,16},{26,18},{28,24},{3... | collective-permute-start | bytes 1327112 | tf_op jit(solution)/shard_map/ppermute | solution.py:321
  480.0 10.9 %collective-permute-start.28 = (bf16[1,72,1024]{2,1,0:T(8,128)(2,1)S(1)}, bf16[1,72,1024]{2,1,0:T(8,128)(2,1)S(1)}, u32[]{:S(2)}, u32[]{:S(2)}) collective-permute-start(bf16[1,72,1024]{2,1,0:T(8,128)(2,1)S(1)} %get-tuple-element.218), channel_id=1, source_target_pairs={{0,8},{2,10},{8,16},{10,18},{16,24},{18,26},{24,28},{26,30},{28,20... | collective-permute-start | bytes 442376 | tf_op jit(solution)/shard_map/ppermute | solution.py:321
  481.1 10.6 %collective-permute-start.35 = (bf16[1,72,1024]{2,1,0:T(8,128)(2,1)S(1)}, bf16[1,72,1024]{2,1,0:T(8,128)(2,1)S(1)}, u32[]{:S(2)}, u32[]{:S(2)}) collective-permute-start(bf16[1,72,1024]{2,1,0:T(8,128)(2,1)S(1)} %get-tuple-element.217), channel_id=1, source_target_pairs={{0,4},{2,6},{8,0},{10,2},{16,8},{18,10},{24,16},{26,18},{28,24},{3... | collective-permute-start | bytes 442376 | tf_op jit(solution)/shard_map/ppermute | solution.py:321
  504.1 11.3 %collective-permute-start.61 = (bf16[16,288,768]{2,1,0:T(8,128)(2,1)S(1)}, bf16[16,288,768]{2,1,0:T(8,128)(2,1)S(1)}, u32[]{:S(2)}, u32[]{:S(2)}) collective-permute-start(bf16[16,288,768]{2,1,0:T(8,128)(2,1)S(1)} %gather_pieces.2.refs_0_.refs_1_.refs_2_.refs_3_), channel_id=1, source_target_pairs={{0,2},{2,0},{4,6},{6,4},{8,10},{10,8},{12,14},{14,12},{16,18},{18,... | collective-permute-start | bytes 21233672 | tf_op jit(solution)/shard_map/ppermute | solution.py:264
  (93 other events, 619.0 us)

commit v7 on v6

--- a/solution.py
+++ b/solution.py
@@ -11,7 +11,7 @@
 halo = 8
 spare = 8
 small_vmem = pltpu.CompilerParams(vmem_limit_bytes=26 << 20)
-forward_vmem = pltpu.CompilerParams(vmem_limit_bytes=46 << 20)
+forward_vmem = pltpu.CompilerParams(vmem_limit_bytes=43 << 20)
 tight_vmem = pltpu.CompilerParams(vmem_limit_bytes=20 << 20)
 big_vmem = pltpu.CompilerParams(vmem_limit_bytes=52 << 20)
 

time: 565 us -> 568 us (level)
    unnamed x127 -> x135, local copies, waits for them, and re-layouts: 16 us -> 21.1 us
where the time goes in v7:
time: 568 us; the launch traced here: 564 us
  waiting for transfers between devices  202 us (36%)
  Pallas kernels  130 us (23%)
  starting transfers between devices  116 us (20%)
  other arithmetic  62.3 us (11%)
  local copies, waits for them, and re-layouts  31.3 us (6%)
  matrix products  21.6 us (4%)
    ppermute x56, waiting for transfers between devices, send(): return lax.ppermute(value, 'dp', pairs)  123 us
    ppermute x56, starting transfers between devices, send(): return lax.ppermute(value, 'dp', pairs)  70.2 us
    pallas_call x2, Pallas kernels, feed_forward(): pl.pallas_call(lambda *refs: ff_kernel(sub, *refs), grid=(hid // chunk,),...  45.5 us
    ppermute x11, waiting for transfers between devices, swap_mp(): return lax.ppermute(value, 'mp', [(0, 1), (1, 0)])  41.1 us
    pallas_call x2, Pallas kernels, ff_grads(): pl.pallas_call(lambda s, *refs: grads_kernel(*refs), grid_spec=pltpu.Pref...  34.7 us
    all_to_all x1, waiting for transfers between devices, on_device(): got_rows = lax.all_to_all(sent_rows, 'dp', **over)  29.6 us
    convert_element_type x14, other arithmetic, step(): came = (came.astype(f32) + own).astype(bf16)  26.5 us
    unnamed x135, local copies, waits for them, and re-layouts  21.1 us
  transfers between devices with their start and end apart: 77, of which 44 were waited for; matrix products, arithmetic and copies ran while one was open for 14% of the time, Pallas kernels for 14%

profile of v7, /device:TPU:0, one launch (start us, length us, event | category | flops | bytes accessed | tf_op | source)
XLA Modules:
  0.0 564.4 jit_solution(6244897987976184552)
XLA Ops:
  3.9 4.2 pack.1
  8.1 7.5 %all-to-all-start = ((bf16[16,104,512]{2,1,0:T(8,128)(2,1)}), bf16[16,104,512]{2,1,0:T(8,128)(2,1)S(1)}, u32[]{:S(2)}, u32[]{:S(2)}) async-start(bf16[16,104,512]{2,1,0:T(8,128)(2,1)} %get-tuple-element.99), calls=%async_computation | async-start | bytes 3407872 | tf_op jit(solution)/shard_map/all_to_all | solution.py:723
  20.3 29.6 %all-to-all-done.refs_1_.refs_2_ = bf16[16,104,512]{2,1,0:T(8,128)(2,1)S(1)} async-done(((bf16[16,104,512]{2,1,0:T(8,128)(2,1)}), bf16[16,104,512]{2,1,0:T(8,128)(2,1)S(1)}, u32[]{:S(2)}, u32[]{:S(2)}) %all-to-all-start) | async-done | bytes 1703968 | tf_op jit(solution)/shard_map/all_to_all | solution.py:723
  49.9 10.2 %all-to-all-start.1 = ((bf16[16,96,512]{2,1,0:T(8,128)(2,1)}), bf16[16,96,512]{2,1,0:T(8,128)(2,1)S(1)}, u32[]{:S(2)}, u32[]{:S(2)}) async-start(bf16[16,96,512]{2,1,0:T(8,128)(2,1)} %copy-done.11), calls=%async_computation.1 | async-start | bytes 3145728 | tf_op jit(solution)/shard_map/all_to_all | solution.py:726
  60.1 3.5 place_rows.2
  69.7 13.7 %collective-permute-done = bf16[528,512]{1,0:T(8,128)(2,1)} collective-permute-done((bf16[528,512]{1,0:T(8,128)(2,1)}, bf16[528,512]{1,0:T(8,128)(2,1)}, u32[]{:S(2)}, u32[]{:S(2)}) %collective-permute-start) | collective-permute-done | bytes 540704 | tf_op jit(solution)/shard_map/ppermute | solution.py:247
  83.3 3.0 maximum_select_fusion
  92.4 3.8 place_rows.3
  98.6 3.5 convolution_bitcast_fusion
  102.1 8.7 %collective-permute-done.3 = bf16[512,512]{1,0:T(8,128)(2,1)S(1)} collective-permute-done((bf16[512,512]{1,0:T(8,128)(2,1)S(1)}, bf16[512,512]{1,0:T(8,128)(2,1)S(1)}, u32[]{:S(2)}, u32[]{:S(2)}) %collective-permute-start.3) | collective-permute-done | bytes 524320 | tf_op jit(solution)/shard_map/ppermute | solution.py:247
  112.8 3.4 fusion.3
  122.3 22.6 %feed_forward.2 = (f32[512,1024]{1,0:T(8,128)S(1)}, f32[512,1024]{1,0:T(8,128)S(1)}, bf16[512,2304]{1,0:T(8,128)(2,1)S(1)}, bf16[512,2304]{1,0:T(8,128)(2,1)S(1)}, bf16[512,2304]{1,0:T(8,128)(2,1)}) custom-call(bf16[512,1024]{1,0:T(8,128)(2,1)S(1)} %multiply_convert_fusion.1.refs_0_, bf16[512,1024]{1,0:T(8,128)(2,1)S(1)} %maximum_select_fusion.1.refs_1_.refs_8_, ...), custom_call_target="tpu_custom_call" | custom-call | flops 28991029248 | bytes 27525120 | tf_op jit(solution)/shard_map/feed_forward/pallas_call | solution.py:417
  149.0 6.9 %collective-permute-done.6 = bf16[512,512]{1,0:T(8,128)(2,1)S(1)} collective-permute-done((bf16[512,512]{1,0:T(8,128)(2,1)S(1)}, bf16[512,512]{1,0:T(8,128)(2,1)S(1)}, u32[]{:S(2)}, u32[]{:S(2)}) %collective-permute-start.6) | collective-permute-done | bytes 524320 | tf_op jit(solution)/shard_map/ppermute | solution.py:247
  156.2 23.0 %feed_forward.3 = (f32[512,1024]{1,0:T(8,128)S(1)}, f32[512,1024]{1,0:T(8,128)S(1)}, bf16[512,2304]{1,0:T(8,128)(2,1)S(1)}, bf16[512,2304]{1,0:T(8,128)(2,1)S(1)}, bf16[512,2304]{1,0:T(8,128)(2,1)}) custom-call(bf16[512,1024]{1,0:T(8,128)(2,1)S(1)} %collective-permute-done.5.refs_0_.refs_1_, bf16[512,1024]{1,0:T(8,128)(2,1)S(1)} %maximum_select_fusion.2.refs_1_.refs_9_, ...), custom_call_target="tpu_custom_call" | custom-call | flops 28991029248 | bytes 27525120 | tf_op jit(solution)/shard_map/feed_forward/pallas_call | solution.py:417
  183.0 17.5 %ff_grads.2 = bf16[8,576,768]{2,1,0:T(8,128)(2,1)} custom-call(s32[1]{0:T(128)} %bitcast.22.s, bf16[512,1024]{1,0:T(8,128)(2,1)S(1)} %multiply_convert_fusion.1.refs_0_, bf16[512,1024]{1,0:T(8,128)(2,1)} %copy-done.22, bf16[512,2304]{1,0:T(8,128)(2,1)} %copy-done.25, bf16[512,2304]{1,0:T(8,128)(2,1)} %copy-done.27, ...), custom_call_target="tpu_custom_call" | custom-call | flops 14495514624 | bytes 18874368 | tf_op jit(solution)/shard_map/ff_grads/pallas_call | solution.py:475
  201.6 3.0 convert_element_type.492
  206.6 17.2 %ff_grads.3 = bf16[8,576,768]{2,1,0:T(8,128)(2,1)} custom-call(s32[1]{0:T(128)} %bitcast.21.s.core_ref, bf16[512,1024]{1,0:T(8,128)(2,1)S(1)} %copy-done.15, bf16[512,1024]{1,0:T(8,128)(2,1)} %copy-done.22, bf16[512,2304]{1,0:T(8,128)(2,1)} %copy-done.25, bf16[512,2304]{1,0:T(8,128)(2,1)} %copy-done.27, bf16[512,2304]{1,0:T(8,128)(2,1)} %get-tuple-element.117.refs_4_, ...), custom_call_target="tpu_custom_call" | custom-call | flops 14495514624 | bytes 18874368 | tf_op jit(solution)/shard_map/ff_grads/pallas_call | solution.py:475
  223.8 6.6 %collective-permute-done.7 = bf16[520,1024]{1,0:T(8,128)(2,1)S(1)} collective-permute-done((bf16[520,1024]{1,0:T(8,128)(2,1)S(1)}, bf16[520,1024]{1,0:T(8,128)(2,1)S(1)}, u32[]{:S(2)}, u32[]{:S(2)}) %collective-permute-start.7) | collective-permute-done | bytes 1064992 | tf_op jit(solution)/shard_map/ppermute | solution.py:247
  234.3 4.8 collective-permute-start.10
  264.5 5.4 convolution_convert_fusion
  278.5 4.4 all-to-all-start.2
  283.8 2.8 add_convert_fusion.10
  286.6 8.8 %fusion.18 = (bf16[1024]{0:T(1024)(128)(2,1)S(1)}, f32[512]{0:T(512)S(1)}, f32[512,1024,1]{1,0,2:T(8,128)}) fusion(f32[528,1024]{1,0:T(8,128)S(1)} %copy-done.37, f32[512]{0:T(512)S(1)} %slice.240, f32[1024]{0:T(1024)S(1)} %copy-done.60, bf16[3,512,1024]{2,1,0:T(8,128)(2,1)} %pad_maximum_fusion, bf16[3,512,512]{2,1,0:T(8,128)(2,1)} %slice.260, ...), kind=kOutput, calls=%fused_computation.52 | convolution fusion | flops 3243244032 | bytes 13641728 | tf_op jit(solution)/shard_map/krc,kdc->rd/dot_general | solution.py:887
  308.4 4.6 collective-permute-done.17
  315.1 2.9 take_rows.6
  318.0 9.4 %all-to-all-start.3 = ((bf16[16,96,512]{2,1,0:T(8,128)(2,1)}), bf16[16,96,512]{2,1,0:T(8,128)(2,1)}, u32[]{:S(2)}, u32[]{:S(2)}) async-start(bf16[16,96,512]{2,1,0:T(8,128)(2,1)} %bitcast.32), calls=%async_computation.3 | async-start | bytes 3145728 | tf_op jit(solution)/shard_map/all_to_all | solution.py:835
  329.5 3.4 collective-permute-start.39
  332.9 30.5 %collective-permute-done.39 = bf16[1,288,768]{2,1,0:T(8,128)(2,1)S(1)} collective-permute-done((bf16[1,288,768]{2,1,0:T(8,128)(2,1)S(1)}, bf16[1,288,768]{2,1,0:T(8,128)(2,1)S(1)}, u32[]{:S(2)}, u32[]{:S(2)}) %collective-permute-start.39) | collective-permute-done | bytes 442400 | tf_op jit(solution)/shard_map/ppermute | solution.py:321
  367.8 10.0 %collective-permute-start.41 = (bf16[1,288,768]{2,1,0:T(8,128)(2,1)}, bf16[1,288,768]{2,1,0:T(8,128)(2,1)S(1)}, u32[]{:S(2)}, u32[]{:S(2)}) collective-permute-start(bf16[1,288,768]{2,1,0:T(8,128)(2,1)} %get-tuple-element.140), channel_id=1, source_target_pairs={{0,8},{2,10},{8,16},{10,18},{16,24},{18,26},{24,28},{26,30},{28,20... | collective-permute-start | bytes 1327112 | tf_op jit(solution)/shard_map/ppermute | solution.py:321
  377.8 9.5 %collective-permute-done.41 = bf16[1,288,768]{2,1,0:T(8,128)(2,1)S(1)} collective-permute-done((bf16[1,288,768]{2,1,0:T(8,128)(2,1)}, bf16[1,288,768]{2,1,0:T(8,128)(2,1)S(1)}, u32[]{:S(2)}, u32[]{:S(2)}) %collective-permute-start.41) | collective-permute-done | bytes 442400 | tf_op jit(solution)/shard_map/ppermute | solution.py:321
  398.4 4.3 take_rows.5
  402.7 5.3 collective-permute-done.21
  421.7 6.5 %collective-permute-done.45 = bf16[1,288,768]{2,1,0:T(8,128)(2,1)S(1)} collective-permute-done((bf16[1,288,768]{2,1,0:T(8,128)(2,1)S(1)}, bf16[1,288,768]{2,1,0:T(8,128)(2,1)S(1)}, u32[]{:S(2)}, u32[]{:S(2)}) %collective-permute-start.45) | collective-permute-done | bytes 442400 | tf_op jit(solution)/shard_map/ppermute | solution.py:321
  433.3 4.5 take_rows.7
  442.9 8.2 %collective-permute-done.25 = bf16[1,72,1024]{2,1,0:T(8,128)(2,1)S(1)} collective-permute-done((bf16[1,72,1024]{2,1,0:T(8,128)(2,1)S(1)}, bf16[1,72,1024]{2,1,0:T(8,128)(2,1)S(1)}, u32[]{:S(2)}, u32[]{:S(2)}) %collective-permute-start.25) | collective-permute-done | bytes 147488 | tf_op jit(solution)/shard_map/ppermute | solution.py:321
  457.0 8.0 %collective-permute-done.26 = bf16[1,72,1024]{2,1,0:T(8,128)(2,1)S(1)} collective-permute-done((bf16[1,72,1024]{2,1,0:T(8,128)(2,1)S(1)}, bf16[1,72,1024]{2,1,0:T(8,128)(2,1)S(1)}, u32[]{:S(2)}, u32[]{:S(2)}) %collective-permute-start.26) | collective-permute-done | bytes 147488 | tf_op jit(solution)/shard_map/ppermute | solution.py:321
  470.8 7.8 %collective-permute-done.27 = bf16[1,72,1024]{2,1,0:T(8,128)(2,1)S(1)} collective-permute-done((bf16[1,72,1024]{2,1,0:T(8,128)(2,1)S(1)}, bf16[1,72,1024]{2,1,0:T(8,128)(2,1)S(1)}, u32[]{:S(2)}, u32[]{:S(2)}) %collective-permute-start.27) | collective-permute-done | bytes 147488 | tf_op jit(solution)/shard_map/ppermute | solution.py:321
  484.4 8.9 %collective-permute-done.28 = bf16[1,72,1024]{2,1,0:T(8,128)(2,1)S(1)} collective-permute-done((bf16[1,72,1024]{2,1,0:T(8,128)(2,1)S(1)}, bf16[1,72,1024]{2,1,0:T(8,128)(2,1)S(1)}, u32[]{:S(2)}, u32[]{:S(2)}) %collective-permute-start.28) | collective-permute-done | bytes 147488 | tf_op jit(solution)/shard_map/ppermute | solution.py:321
  497.7 6.0 %collective-permute-done.57 = bf16[1,288,768]{2,1,0:T(8,128)(2,1)S(1)} collective-permute-done((bf16[1,288,768]{2,1,0:T(8,128)(2,1)S(1)}, bf16[1,288,768]{2,1,0:T(8,128)(2,1)S(1)}, u32[]{:S(2)}, u32[]{:S(2)}) %collective-permute-start.57) | collective-permute-done | bytes 442400 | tf_op jit(solution)/shard_map/ppermute | solution.py:321
  508.7 4.2 collective-permute-done.29
  517.9 3.7 open_ff.4
  523.7 3.7 open_ff.5
  530.8 3.7 open_ff.6
  536.6 3.7 open_ff.7
  543.5 4.6 collective-permute-done.68
  550.1 3.1 collective-permute-done.69
  554.2 4.5 collective-permute-done.72.refs_9_.refs_10_.refs_11_.refs_12_.refs_13_.refs_14_.refs_15_.refs_16_
  558.7 4.2 open_conv.1
  (361 shorter events, 183.0 us)
Async XLA Ops:
  8.1 41.8 %all-to-all-start = ((bf16[16,104,512]{2,1,0:T(8,128)(2,1)}), bf16[16,104,512]{2,1,0:T(8,128)(2,1)S(1)}, u32[]{:S(2)}, u32[]{:S(2)}) async-start(bf16[16,104,512]{2,1,0:T(8,128)(2,1)} %get-tuple-element.99), calls=%async_computation | async-start | bytes 3407872 | tf_op jit(solution)/shard_map/all_to_all | solution.py:723
  15.6 49.0 %collective-permute-start.1 = (bf16[4,512,512]{2,1,0:T(8,128)(2,1)}, bf16[4,512,512]{2,1,0:T(8,128)(2,1)}, u32[]{:S(2)}, u32[]{:S(2)}) collective-permute-start(bf16[4,512,512]{2,1,0:T(8,128)(2,1)} %pad_maximum_fusion.1), channel_id=1, source_target_pairs={{0,1},{1,0},{2,3},{3,2},{4,5},{5,4},{6,7},{7,6},{8,9},{9,8},{10,11... | collective-permute-start | bytes 6291464 | tf_op jit(solution)/shard_map/ppermute | solution.py:247
  49.9 42.5 %all-to-all-start.1 = ((bf16[16,96,512]{2,1,0:T(8,128)(2,1)}), bf16[16,96,512]{2,1,0:T(8,128)(2,1)S(1)}, u32[]{:S(2)}, u32[]{:S(2)}) async-start(bf16[16,96,512]{2,1,0:T(8,128)(2,1)} %copy-done.11), calls=%async_computation.1 | async-start | bytes 3145728 | tf_op jit(solution)/shard_map/all_to_all | solution.py:726
  64.6 21.7 %collective-permute-start.2 = (bf16[4,512,512]{2,1,0:T(8,128)(2,1)}, bf16[4,512,512]{2,1,0:T(8,128)(2,1)}, u32[]{:S(2)}, u32[]{:S(2)}) collective-permute-start(bf16[4,512,512]{2,1,0:T(8,128)(2,1)} %collective-permute-done.1), channel_id=1, source_target_pairs={{0,2},{2,0},{4,6},{6,4},{8,10},{10,8},{12,14},{14,12},{16,18},{18,... | collective-permute-start | bytes 6291464 | tf_op jit(solution)/shard_map/ppermute | solution.py:264
  69.1 14.3 %collective-permute-start = (bf16[528,512]{1,0:T(8,128)(2,1)}, bf16[528,512]{1,0:T(8,128)(2,1)}, u32[]{:S(2)}, u32[]{:S(2)}) collective-permute-start(bf16[528,512]{1,0:T(8,128)(2,1)} %get-tuple-element.238), channel_id=1, source_target_pairs={{0,1},{1,0},{2,3},{3,2},{4,5},{5,4},{6,7},{7,6},{8,9},{9,8},{10,11... | collective-permute-start | bytes 1622024 | tf_op jit(solution)/shard_map/ppermute | solution.py:247
  96.6 14.3 %collective-permute-start.3 = (bf16[512,512]{1,0:T(8,128)(2,1)S(1)}, bf16[512,512]{1,0:T(8,128)(2,1)S(1)}, u32[]{:S(2)}, u32[]{:S(2)}) collective-permute-start(bf16[512,512]{1,0:T(8,128)(2,1)S(1)} %get-tuple-element.246), channel_id=1, source_target_pairs={{0,1},{1,0},{2,3},{3,2},{4,5},{5,4},{6,7},{7,6},{8,9},{9,8},{10,11... | collective-permute-start | bytes 1572872 | tf_op jit(solution)/shard_map/ppermute | solution.py:247
  119.9 36.4 %collective-permute-start.5 = (bf16[512,1024]{1,0:T(8,128)(2,1)S(1)}, bf16[512,1024]{1,0:T(8,128)(2,1)S(1)}, u32[]{:S(2)}, u32[]{:S(2)}) collective-permute-start(bf16[512,1024]{1,0:T(8,128)(2,1)S(1)} %multiply_convert_fusion.1.refs_0_), channel_id=1, source_target_pairs={{0,1},{1,0},{2,3},{3,2},{4,5},{5,4},{6,7},{7,6},{8,9},{9,8},{10,11... | collective-permute-start | bytes 3145736 | tf_op jit(solution)/shard_map/ppermute | solution.py:247
  121.4 34.5 %collective-permute-start.6 = (bf16[512,512]{1,0:T(8,128)(2,1)S(1)}, bf16[512,512]{1,0:T(8,128)(2,1)S(1)}, u32[]{:S(2)}, u32[]{:S(2)}) collective-permute-start(bf16[512,512]{1,0:T(8,128)(2,1)S(1)} %get-tuple-element.110), channel_id=1, source_target_pairs={{0,1},{1,0},{2,3},{3,2},{4,5},{5,4},{6,7},{7,6},{8,9},{9,8},{10,11... | collective-permute-start | bytes 1572872 | tf_op jit(solution)/shard_map/ppermute | solution.py:247
  200.5 32.0 %collective-permute-start.9 = (bf16[8,576,768]{2,1,0:T(8,128)(2,1)}, bf16[8,576,768]{2,1,0:T(8,128)(2,1)}, u32[]{:S(2)}, u32[]{:S(2)}) collective-permute-start(bf16[8,576,768]{2,1,0:T(8,128)(2,1)} %ff_grads.2), channel_id=1, source_target_pairs={{0,2},{2,0},{4,6},{6,4},{8,10},{10,8},{12,14},{14,12},{16,18},{18,... | collective-permute-start | bytes 21233672 | tf_op jit(solution)/shard_map/ppermute | solution.py:264
  204.6 25.7 %collective-permute-start.7 = (bf16[520,1024]{1,0:T(8,128)(2,1)S(1)}, bf16[520,1024]{1,0:T(8,128)(2,1)S(1)}, u32[]{:S(2)}, u32[]{:S(2)}) collective-permute-start(bf16[520,1024]{1,0:T(8,128)(2,1)S(1)} %copy-done.48), channel_id=1, source_target_pairs={{0,1},{1,0},{2,3},{3,2},{4,5},{5,4},{6,7},{7,6},{8,9},{9,8},{10,11... | collective-permute-start | bytes 3194888 | tf_op jit(solution)/shard_map/ppermute | solution.py:247
  230.4 32.5 %collective-permute-start.8 = (bf16[512,1024]{1,0:T(8,128)(2,1)S(1)}, bf16[512,1024]{1,0:T(8,128)(2,1)S(1)}, u32[]{:S(2)}, u32[]{:S(2)}) collective-permute-start(bf16[512,1024]{1,0:T(8,128)(2,1)S(1)} %convert_element_type.498), channel_id=1, source_target_pairs={{0,1},{1,0},{2,3},{3,2},{4,5},{5,4},{6,7},{7,6},{8,9},{9,8},{10,11... | collective-permute-start | bytes 3145736 | tf_op jit(solution)/shard_map/ppermute | solution.py:247
  234.3 13.7 %collective-permute-start.10 = (bf16[1,288,768]{2,1,0:T(8,128)(2,1)S(1)}, bf16[1,288,768]{2,1,0:T(8,128)(2,1)S(1)}, u32[]{:S(2)}, u32[]{:S(2)}) collective-permute-start(bf16[1,288,768]{2,1,0:T(8,128)(2,1)S(1)} %get-tuple-element.214), channel_id=1, source_target_pairs={{0,8},{2,10},{8,16},{10,18},{16,24},{18,26},{24,28},{26,30},{28,20... | collective-permute-start | bytes 1327112 | tf_op jit(solution)/shard_map/ppermute | solution.py:321
  239.1 11.0 %collective-permute-start.11 = (bf16[1,288,768]{2,1,0:T(8,128)(2,1)S(1)}, bf16[1,288,768]{2,1,0:T(8,128)(2,1)S(1)}, u32[]{:S(2)}, u32[]{:S(2)}) collective-permute-start(bf16[1,288,768]{2,1,0:T(8,128)(2,1)S(1)} %get-tuple-element.213), channel_id=1, source_target_pairs={{0,4},{2,6},{8,0},{10,2},{16,8},{18,10},{24,16},{26,18},{28,24},{3... | collective-permute-start | bytes 1327112 | tf_op jit(solution)/shard_map/ppermute | solution.py:321
  251.9 18.0 %collective-permute-start.13 = (bf16[1,288,768]{2,1,0:T(8,128)(2,1)S(1)}, bf16[1,288,768]{2,1,0:T(8,128)(2,1)S(1)}, u32[]{:S(2)}, u32[]{:S(2)}) collective-permute-start(bf16[1,288,768]{2,1,0:T(8,128)(2,1)S(1)} %get-tuple-element.212), channel_id=1, source_target_pairs={{0,8},{2,10},{8,16},{10,18},{16,24},{18,26},{24,28},{26,30},{28,20... | collective-permute-start | bytes 1327112 | tf_op jit(solution)/shard_map/ppermute | solution.py:321
  252.7 17.2 %collective-permute-start.15 = (bf16[1,288,768]{2,1,0:T(8,128)(2,1)S(1)}, bf16[1,288,768]{2,1,0:T(8,128)(2,1)S(1)}, u32[]{:S(2)}, u32[]{:S(2)}) collective-permute-start(bf16[1,288,768]{2,1,0:T(8,128)(2,1)S(1)} %get-tuple-element.211), channel_id=1, source_target_pairs={{0,4},{2,6},{8,0},{10,2},{16,8},{18,10},{24,16},{26,18},{28,24},{3... | collective-permute-start | bytes 1327112 | tf_op jit(solution)/shard_map/ppermute | solution.py:321
  263.9 11.4 %collective-permute-start.12 = (bf16[512,512]{1,0:T(8,128)(2,1)S(1)}, bf16[512,512]{1,0:T(8,128)(2,1)S(1)}, u32[]{:S(2)}, u32[]{:S(2)}) collective-permute-start(bf16[512,512]{1,0:T(8,128)(2,1)S(1)} %get-tuple-element.244), channel_id=1, source_target_pairs={{0,1},{1,0},{2,3},{3,2},{4,5},{5,4},{6,7},{7,6},{8,9},{9,8},{10,11... | collective-permute-start | bytes 1572872 | tf_op jit(solution)/shard_map/ppermute | solution.py:247
  272.6 10.4 %collective-permute-start.14 = (bf16[1,288,768]{2,1,0:T(8,128)(2,1)}, bf16[1,288,768]{2,1,0:T(8,128)(2,1)S(1)}, u32[]{:S(2)}, u32[]{:S(2)}) collective-permute-start(bf16[1,288,768]{2,1,0:T(8,128)(2,1)} %get-tuple-element.210), channel_id=1, source_target_pairs={{0,8},{2,10},{8,16},{10,18},{16,24},{18,26},{24,28},{26,30},{28,20... | collective-permute-start | bytes 1327112 | tf_op jit(solution)/shard_map/ppermute | solution.py:321
  273.3 10.4 %collective-permute-start.16 = (bf16[1,288,768]{2,1,0:T(8,128)(2,1)}, bf16[1,288,768]{2,1,0:T(8,128)(2,1)}, u32[]{:S(2)}, u32[]{:S(2)}) collective-permute-start(bf16[1,288,768]{2,1,0:T(8,128)(2,1)} %get-tuple-element.209), channel_id=1, source_target_pairs={{0,4},{2,6},{8,0},{10,2},{16,8},{18,10},{24,16},{26,18},{28,24},{3... | collective-permute-start | bytes 1327112 | tf_op jit(solution)/shard_map/ppermute | solution.py:321
  278.5 36.5 %all-to-all-start.2 = ((bf16[16,96,512]{2,1,0:T(8,128)(2,1)}), bf16[16,96,512]{2,1,0:T(8,128)(2,1)}, u32[]{:S(2)}, u32[]{:S(2)}) async-start(bf16[16,96,512]{2,1,0:T(8,128)(2,1)} %bitcast.144), calls=%async_computation.2 | async-start | bytes 3145728 | tf_op jit(solution)/shard_map/all_to_all | solution.py:835
  298.2 14.8 %collective-permute-start.17 = (bf16[512,512]{1,0:T(8,128)(2,1)S(1)}, bf16[512,512]{1,0:T(8,128)(2,1)S(1)}, u32[]{:S(2)}, u32[]{:S(2)}) collective-permute-start(bf16[512,512]{1,0:T(8,128)(2,1)S(1)} %get-tuple-element.242), channel_id=1, source_target_pairs={{0,1},{1,0},{2,3},{3,2},{4,5},{5,4},{6,7},{7,6},{8,9},{9,8},{10,11... | collective-permute-start | bytes 1572872 | tf_op jit(solution)/shard_map/ppermute | solution.py:247
  299.1 28.3 %collective-permute-start.37 = (bf16[1,288,768]{2,1,0:T(8,128)(2,1)}, bf16[1,288,768]{2,1,0:T(8,128)(2,1)}, u32[]{:S(2)}, u32[]{:S(2)}) collective-permute-start(bf16[1,288,768]{2,1,0:T(8,128)(2,1)} %get-tuple-element.136), channel_id=1, source_target_pairs={{0,8},{2,10},{8,16},{10,18},{16,24},{18,26},{24,28},{26,30},{28,20... | collective-permute-start | bytes 1327112 | tf_op jit(solution)/shard_map/ppermute | solution.py:321
  300.9 26.6 %collective-permute-start.38 = (bf16[1,288,768]{2,1,0:T(8,128)(2,1)S(1)}, bf16[1,288,768]{2,1,0:T(8,128)(2,1)}, u32[]{:S(2)}, u32[]{:S(2)}) collective-permute-start(bf16[1,288,768]{2,1,0:T(8,128)(2,1)S(1)} %get-tuple-element.137), channel_id=1, source_target_pairs={{0,4},{2,6},{8,0},{10,2},{16,8},{18,10},{24,16},{26,18},{28,24},{3... | collective-permute-start | bytes 1327112 | tf_op jit(solution)/shard_map/ppermute | solution.py:321
  303.9 88.3 %collective-permute-start.20 = (bf16[8,144,1024]{2,1,0:T(8,128)(2,1)}, bf16[8,144,1024]{2,1,0:T(8,128)(2,1)}, u32[]{:S(2)}, u32[]{:S(2)}) collective-permute-start(bf16[8,144,1024]{2,1,0:T(8,128)(2,1)} %add_convert_fusion), channel_id=1, source_target_pairs={{0,1},{1,0},{2,3},{3,2},{4,5},{5,4},{6,7},{7,6},{8,9},{9,8},{10,11... | collective-permute-start | bytes 7077896 | tf_op jit(solution)/shard_map/ppermute | solution.py:247
  308.4 83.7 %collective-permute-start.19 = (bf16[8,144,1024]{2,1,0:T(8,128)(2,1)}, bf16[8,144,1024]{2,1,0:T(8,128)(2,1)}, u32[]{:S(2)}, u32[]{:S(2)}) collective-permute-start(bf16[8,144,1024]{2,1,0:T(8,128)(2,1)} %get-tuple-element.133), channel_id=1, source_target_pairs={{0,2},{2,0},{4,6},{6,4},{8,10},{10,8},{12,14},{14,12},{16,18},{18,... | collective-permute-start | bytes 7077896 | tf_op jit(solution)/shard_map/ppermute | solution.py:264
  318.0 97.1 %all-to-all-start.3 = ((bf16[16,96,512]{2,1,0:T(8,128)(2,1)}), bf16[16,96,512]{2,1,0:T(8,128)(2,1)}, u32[]{:S(2)}, u32[]{:S(2)}) async-start(bf16[16,96,512]{2,1,0:T(8,128)(2,1)} %bitcast.32), calls=%async_computation.3 | async-start | bytes 3145728 | tf_op jit(solution)/shard_map/all_to_all | solution.py:835
  329.5 33.9 %collective-permute-start.39 = (bf16[1,288,768]{2,1,0:T(8,128)(2,1)S(1)}, bf16[1,288,768]{2,1,0:T(8,128)(2,1)S(1)}, u32[]{:S(2)}, u32[]{:S(2)}) collective-permute-start(bf16[1,288,768]{2,1,0:T(8,128)(2,1)S(1)} %get-tuple-element.138), channel_id=1, source_target_pairs={{0,8},{2,10},{8,16},{10,18},{16,24},{18,26},{24,28},{26,30},{28,20... | collective-permute-start | bytes 1327112 | tf_op jit(solution)/shard_map/ppermute | solution.py:321
  332.9 32.4 %collective-permute-start.40 = (bf16[1,288,768]{2,1,0:T(8,128)(2,1)S(1)}, bf16[1,288,768]{2,1,0:T(8,128)(2,1)S(1)}, u32[]{:S(2)}, u32[]{:S(2)}) collective-permute-start(bf16[1,288,768]{2,1,0:T(8,128)(2,1)S(1)} %get-tuple-element.139), channel_id=1, source_target_pairs={{0,4},{2,6},{8,0},{10,2},{16,8},{18,10},{24,16},{26,18},{28,24},{3... | collective-permute-start | bytes 1327112 | tf_op jit(solution)/shard_map/ppermute | solution.py:321
  367.8 19.5 %collective-permute-start.41 = (bf16[1,288,768]{2,1,0:T(8,128)(2,1)}, bf16[1,288,768]{2,1,0:T(8,128)(2,1)S(1)}, u32[]{:S(2)}, u32[]{:S(2)}) collective-permute-start(bf16[1,288,768]{2,1,0:T(8,128)(2,1)} %get-tuple-element.140), channel_id=1, source_target_pairs={{0,8},{2,10},{8,16},{10,18},{16,24},{18,26},{24,28},{26,30},{28,20... | collective-permute-start | bytes 1327112 | tf_op jit(solution)/shard_map/ppermute | solution.py:321
  377.8 11.5 %collective-permute-start.42 = (bf16[1,288,768]{2,1,0:T(8,128)(2,1)S(1)}, bf16[1,288,768]{2,1,0:T(8,128)(2,1)}, u32[]{:S(2)}, u32[]{:S(2)}) collective-permute-start(bf16[1,288,768]{2,1,0:T(8,128)(2,1)S(1)} %get-tuple-element.141), channel_id=1, source_target_pairs={{0,4},{2,6},{8,0},{10,2},{16,8},{18,10},{24,16},{26,18},{28,24},{3... | collective-permute-start | bytes 1327112 | tf_op jit(solution)/shard_map/ppermute | solution.py:321
  394.1 19.0 %collective-permute-start.43 = (bf16[1,288,768]{2,1,0:T(8,128)(2,1)}, bf16[1,288,768]{2,1,0:T(8,128)(2,1)}, u32[]{:S(2)}, u32[]{:S(2)}) collective-permute-start(bf16[1,288,768]{2,1,0:T(8,128)(2,1)} %get-tuple-element.142), channel_id=1, source_target_pairs={{0,8},{2,10},{8,16},{10,18},{16,24},{18,26},{24,28},{26,30},{28,20... | collective-permute-start | bytes 1327112 | tf_op jit(solution)/shard_map/ppermute | solution.py:321
  395.2 17.8 %collective-permute-start.44 = (bf16[1,288,768]{2,1,0:T(8,128)(2,1)S(1)}, bf16[1,288,768]{2,1,0:T(8,128)(2,1)}, u32[]{:S(2)}, u32[]{:S(2)}) collective-permute-start(bf16[1,288,768]{2,1,0:T(8,128)(2,1)S(1)} %get-tuple-element.143), channel_id=1, source_target_pairs={{0,4},{2,6},{8,0},{10,2},{16,8},{18,10},{24,16},{26,18},{28,24},{3... | collective-permute-start | bytes 1327112 | tf_op jit(solution)/shard_map/ppermute | solution.py:321
  396.4 11.6 %collective-permute-start.21 = (bf16[1,72,1024]{2,1,0:T(8,128)(2,1)}, bf16[1,72,1024]{2,1,0:T(8,128)(2,1)S(1)}, u32[]{:S(2)}, u32[]{:S(2)}) collective-permute-start(bf16[1,72,1024]{2,1,0:T(8,128)(2,1)} %get-tuple-element.230), channel_id=1, source_target_pairs={{0,8},{2,10},{8,16},{10,18},{16,24},{18,26},{24,28},{26,30},{28,20... | collective-permute-start | bytes 442376 | tf_op jit(solution)/shard_map/ppermute | solution.py:321
  397.6 11.5 %collective-permute-start.22 = (bf16[1,72,1024]{2,1,0:T(8,128)(2,1)S(1)}, bf16[1,72,1024]{2,1,0:T(8,128)(2,1)S(1)}, u32[]{:S(2)}, u32[]{:S(2)}) collective-permute-start(bf16[1,72,1024]{2,1,0:T(8,128)(2,1)S(1)} %get-tuple-element.229), channel_id=1, source_target_pairs={{0,4},{2,6},{8,0},{10,2},{16,8},{18,10},{24,16},{26,18},{28,24},{3... | collective-permute-start | bytes 442376 | tf_op jit(solution)/shard_map/ppermute | solution.py:321
  415.1 13.2 %collective-permute-start.45 = (bf16[1,288,768]{2,1,0:T(8,128)(2,1)S(1)}, bf16[1,288,768]{2,1,0:T(8,128)(2,1)S(1)}, u32[]{:S(2)}, u32[]{:S(2)}) collective-permute-start(bf16[1,288,768]{2,1,0:T(8,128)(2,1)S(1)} %get-tuple-element.144), channel_id=1, source_target_pairs={{0,8},{2,10},{8,16},{10,18},{16,24},{18,26},{24,28},{26,30},{28,20... | collective-permute-start | bytes 1327112 | tf_op jit(solution)/shard_map/ppermute | solution.py:321
  415.7 13.1 %collective-permute-start.46 = (bf16[1,288,768]{2,1,0:T(8,128)(2,1)S(1)}, bf16[1,288,768]{2,1,0:T(8,128)(2,1)S(1)}, u32[]{:S(2)}, u32[]{:S(2)}) collective-permute-start(bf16[1,288,768]{2,1,0:T(8,128)(2,1)S(1)} %get-tuple-element.145), channel_id=1, source_target_pairs={{0,4},{2,6},{8,0},{10,2},{16,8},{18,10},{24,16},{26,18},{28,24},{3... | collective-permute-start | bytes 1327112 | tf_op jit(solution)/shard_map/ppermute | solution.py:321
  419.6 11.7 %collective-permute-start.24 = (bf16[1,72,1024]{2,1,0:T(8,128)(2,1)S(1)}, bf16[1,72,1024]{2,1,0:T(8,128)(2,1)S(1)}, u32[]{:S(2)}, u32[]{:S(2)}) collective-permute-start(bf16[1,72,1024]{2,1,0:T(8,128)(2,1)S(1)} %get-tuple-element.226), channel_id=1, source_target_pairs={{0,8},{2,10},{8,16},{10,18},{16,24},{18,26},{24,28},{26,30},{28,20... | collective-permute-start | bytes 442376 | tf_op jit(solution)/shard_map/ppermute | solution.py:321
  420.3 11.7 %collective-permute-start.31 = (bf16[1,72,1024]{2,1,0:T(8,128)(2,1)S(1)}, bf16[1,72,1024]{2,1,0:T(8,128)(2,1)S(1)}, u32[]{:S(2)}, u32[]{:S(2)}) collective-permute-start(bf16[1,72,1024]{2,1,0:T(8,128)(2,1)S(1)} %get-tuple-element.225), channel_id=1, source_target_pairs={{0,4},{2,6},{8,0},{10,2},{16,8},{18,10},{24,16},{26,18},{28,24},{3... | collective-permute-start | bytes 442376 | tf_op jit(solution)/shard_map/ppermute | solution.py:321
  438.9 14.0 %collective-permute-start.49 = (bf16[1,288,768]{2,1,0:T(8,128)(2,1)S(1)}, bf16[1,288,768]{2,1,0:T(8,128)(2,1)S(1)}, u32[]{:S(2)}, u32[]{:S(2)}) collective-permute-start(bf16[1,288,768]{2,1,0:T(8,128)(2,1)S(1)} %collective-permute-done.47), channel_id=1, source_target_pairs={{0,8},{2,10},{8,16},{10,18},{16,24},{18,26},{24,28},{26,30},{28,20... | collective-permute-start | bytes 1327112 | tf_op jit(solution)/shard_map/ppermute | solution.py:321
  439.6 13.2 %collective-permute-start.50 = (bf16[1,288,768]{2,1,0:T(8,128)(2,1)S(1)}, bf16[1,288,768]{2,1,0:T(8,128)(2,1)S(1)}, u32[]{:S(2)}, u32[]{:S(2)}) collective-permute-start(bf16[1,288,768]{2,1,0:T(8,128)(2,1)S(1)} %collective-permute-done.48), channel_id=1, source_target_pairs={{0,4},{2,6},{8,0},{10,2},{16,8},{18,10},{24,16},{26,18},{28,24},{3... | collective-permute-start | bytes 1327112 | tf_op jit(solution)/shard_map/ppermute | solution.py:321
  452.9 13.8 %collective-permute-start.51 = (bf16[1,288,768]{2,1,0:T(8,128)(2,1)S(1)}, bf16[1,288,768]{2,1,0:T(8,128)(2,1)S(1)}, u32[]{:S(2)}, u32[]{:S(2)}) collective-permute-start(bf16[1,288,768]{2,1,0:T(8,128)(2,1)S(1)} %collective-permute-done.49), channel_id=1, source_target_pairs={{0,8},{2,10},{8,16},{10,18},{16,24},{18,26},{24,28},{26,30},{28,20... | collective-permute-start | bytes 1327112 | tf_op jit(solution)/shard_map/ppermute | solution.py:321
  453.5 13.2 %collective-permute-start.52 = (bf16[1,288,768]{2,1,0:T(8,128)(2,1)S(1)}, bf16[1,288,768]{2,1,0:T(8,128)(2,1)S(1)}, u32[]{:S(2)}, u32[]{:S(2)}) collective-permute-start(bf16[1,288,768]{2,1,0:T(8,128)(2,1)S(1)} %collective-permute-done.50), channel_id=1, source_target_pairs={{0,4},{2,6},{8,0},{10,2},{16,8},{18,10},{24,16},{26,18},{28,24},{3... | collective-permute-start | bytes 1327112 | tf_op jit(solution)/shard_map/ppermute | solution.py:321
  466.7 13.3 %collective-permute-start.53 = (bf16[1,288,768]{2,1,0:T(8,128)(2,1)S(1)}, bf16[1,288,768]{2,1,0:T(8,128)(2,1)S(1)}, u32[]{:S(2)}, u32[]{:S(2)}) collective-permute-start(bf16[1,288,768]{2,1,0:T(8,128)(2,1)S(1)} %collective-permute-done.51), channel_id=1, source_target_pairs={{0,8},{2,10},{8,16},{10,18},{16,24},{18,26},{24,28},{26,30},{28,20... | collective-permute-start | bytes 1327112 | tf_op jit(solution)/shard_map/ppermute | solution.py:321
  466.9 13.0 %collective-permute-start.54 = (bf16[1,288,768]{2,1,0:T(8,128)(2,1)S(1)}, bf16[1,288,768]{2,1,0:T(8,128)(2,1)S(1)}, u32[]{:S(2)}, u32[]{:S(2)}) collective-permute-start(bf16[1,288,768]{2,1,0:T(8,128)(2,1)S(1)} %collective-permute-done.52), channel_id=1, source_target_pairs={{0,4},{2,6},{8,0},{10,2},{16,8},{18,10},{24,16},{26,18},{28,24},{3... | collective-permute-start | bytes 1327112 | tf_op jit(solution)/shard_map/ppermute | solution.py:321
  480.0 15.4 %collective-permute-start.55 = (bf16[1,288,768]{2,1,0:T(8,128)(2,1)S(1)}, bf16[1,288,768]{2,1,0:T(8,128)(2,1)S(1)}, u32[]{:S(2)}, u32[]{:S(2)}) collective-permute-start(bf16[1,288,768]{2,1,0:T(8,128)(2,1)S(1)} %collective-permute-done.53), channel_id=1, source_target_pairs={{0,8},{2,10},{8,16},{10,18},{16,24},{18,26},{24,28},{26,30},{28,20... | collective-permute-start | bytes 1327112 | tf_op jit(solution)/shard_map/ppermute | solution.py:321
  481.2 14.2 %collective-permute-start.56 = (bf16[1,288,768]{2,1,0:T(8,128)(2,1)S(1)}, bf16[1,288,768]{2,1,0:T(8,128)(2,1)S(1)}, u32[]{:S(2)}, u32[]{:S(2)}) collective-permute-start(bf16[1,288,768]{2,1,0:T(8,128)(2,1)S(1)} %collective-permute-done.54), channel_id=1, source_target_pairs={{0,4},{2,6},{8,0},{10,2},{16,8},{18,10},{24,16},{26,18},{28,24},{3... | collective-permute-start | bytes 1327112 | tf_op jit(solution)/shard_map/ppermute | solution.py:321
  482.4 10.9 %collective-permute-start.28 = (bf16[1,72,1024]{2,1,0:T(8,128)(2,1)S(1)}, bf16[1,72,1024]{2,1,0:T(8,128)(2,1)S(1)}, u32[]{:S(2)}, u32[]{:S(2)}) collective-permute-start(bf16[1,72,1024]{2,1,0:T(8,128)(2,1)S(1)} %get-tuple-element.218), channel_id=1, source_target_pairs={{0,8},{2,10},{8,16},{10,18},{16,24},{18,26},{24,28},{26,30},{28,20... | collective-permute-start | bytes 442376 | tf_op jit(solution)/shard_map/ppermute | solution.py:321
  483.5 10.6 %collective-permute-start.35 = (bf16[1,72,1024]{2,1,0:T(8,128)(2,1)S(1)}, bf16[1,72,1024]{2,1,0:T(8,128)(2,1)S(1)}, u32[]{:S(2)}, u32[]{:S(2)}) collective-permute-start(bf16[1,72,1024]{2,1,0:T(8,128)(2,1)S(1)} %get-tuple-element.217), channel_id=1, source_target_pairs={{0,4},{2,6},{8,0},{10,2},{16,8},{18,10},{24,16},{26,18},{28,24},{3... | collective-permute-start | bytes 442376 | tf_op jit(solution)/shard_map/ppermute | solution.py:321
  506.5 11.3 %collective-permute-start.61 = (bf16[16,288,768]{2,1,0:T(8,128)(2,1)S(1)}, bf16[16,288,768]{2,1,0:T(8,128)(2,1)S(1)}, u32[]{:S(2)}, u32[]{:S(2)}) collective-permute-start(bf16[16,288,768]{2,1,0:T(8,128)(2,1)S(1)} %gather_pieces.2.refs_0_.refs_1_.refs_2_.refs_3_), channel_id=1, source_target_pairs={{0,2},{2,0},{4,6},{6,4},{8,10},{10,8},{12,14},{14,12},{16,18},{18,... | collective-permute-start | bytes 21233672 | tf_op jit(solution)/shard_map/ppermute | solution.py:264
  (97 other events, 624.2 us)
